TPU v7x, 128 devices: a whole 4x4x4 slice. The times are simulated.
128 devices in a mesh: mesh: 16 (over z, x), bg: 8 (over y, core).
Axes of the slice: x: 4, y: 4, z: 4, core: 2. Of those that a mesh axis runs over, the one named last changes fastest.
Arguments:
- displacement: float32 [3, 64, 32, 128], P(None, 'mesh', 'bg'), may hold values from -0.4 to 0.4
- bg_coef: float32 [8, 2097152], P(None, ('mesh', 'bg')), may hold values from -0.3 to 0.3
- query_elem: int32 [128, 128, 136], P(('mesh', 'bg')), may hold values from 0 to 16383
- query_point: int32 [128, 128, 136], P(('mesh', 'bg')), may hold values from 0 to 6912, as said below
- query_coord: float32 [128, 128, 3, 136], P(('mesh', 'bg')), may hold values from 0 to 1
Outputs:
- new_displacement: float32 [3, 64, 32, 128], P(None, 'mesh', 'bg')
- line_coeffs: float32 [2, 5], replicated
Inputs may be any that keep to these rules, and one draw needn't show every extreme that they name: `query_point`: in each row every quadrature point 0 to 6911 of the row's device fills exactly one slot; all other slots hold 6912 and are empty. In every draw some owner's bucket is full in every row.
All inputs are finite; a program needn't handle non-finite values.
Results may differ from a plain program's by a relative error of at most 0.0003.
Values sent between devices are 32-bit elements; how exact they have to be, the bound alone decides.
No kernel may reach another device: no remote copies, remote signals or barrier semaphores. Data moves between devices by JAX's collectives and lax.ppermute only.
A program may use at most 64 MiB of HBM per device.

v0:
```python
import jax
import jax.numpy as jnp
import numpy as np
from jax import lax
from jax.sharding import PartitionSpec as P

PASSES = 2
LS_STEPS = 4


GAUSS_POINTS = np.array([0.5 - 0.5 * np.sqrt(0.6), 0.5, 0.5 + 0.5 * np.sqrt(0.6)])
GAUSS_WEIGHTS = np.array([5.0 / 18.0, 8.0 / 18.0, 5.0 / 18.0])


def extended(block, sides, width):
    for axis, dim in sides:
        count = lax.axis_size(axis)
        forward = [(i, i + 1) for i in range(count - 1)]
        forward.append((count - 1, 0))
        backward = [(target, source) for source, target in forward]
        low = lax.ppermute(
            lax.slice_in_dim(block, block.shape[dim] - width, None, axis=dim), axis, forward
        )
        high = lax.ppermute(lax.slice_in_dim(block, 0, width, axis=dim), axis, backward)
        block = jnp.concatenate([low, block, high], axis=dim)
    return block


def basis_tables(elements, periodic):
    node_count = 2 * elements if periodic else 2 * elements + 1
    values = np.zeros((node_count, 3 * elements))
    slopes = np.zeros((node_count, 3 * elements))
    points = GAUSS_POINTS
    shape_values = [
        2.0 * (points - 0.5) * (points - 1.0),
        -4.0 * points * (points - 1.0),
        2.0 * points * (points - 0.5),
    ]
    shape_slopes = [4.0 * points - 3.0, 4.0 - 8.0 * points, 4.0 * points - 1.0]
    for offset in range(3):
        node_rows = (2 * np.arange(elements) + offset) % node_count
        for gauss_index in range(3):
            columns = 3 * np.arange(elements) + gauss_index
            values[node_rows, columns] += shape_values[offset][gauss_index]
            slopes[node_rows, columns] += shape_slopes[offset][gauss_index]
    return (jnp.asarray(values, dtype=jnp.float32), jnp.asarray(slopes, dtype=jnp.float32))


def quad_weights(z_elems, y_elems, x_elems):
    along_z = jnp.asarray(np.tile(GAUSS_WEIGHTS, z_elems), dtype=jnp.float32)
    along_y = jnp.asarray(np.tile(GAUSS_WEIGHTS, y_elems), dtype=jnp.float32)
    along_x = jnp.asarray(np.tile(GAUSS_WEIGHTS, x_elems), dtype=jnp.float32)
    return along_z[:, None, None] * along_y[None, :, None] * along_x[None, None, :]


def gradients(node_field, tables):
    z_value, z_slope, y_value, y_slope, value_along_x, x_slope = tables
    highest = lax.Precision.HIGHEST
    value_z = jnp.einsum("czyx,zk->ckyx", node_field, z_value, precision=highest)
    slope_z = jnp.einsum("czyx,zk->ckyx", node_field, z_slope, precision=highest)
    value_zy = jnp.einsum("ckyx,yl->cklx", value_z, y_value, precision=highest)
    slope_y = jnp.einsum("ckyx,yl->cklx", value_z, y_slope, precision=highest)
    slope_zy = jnp.einsum("ckyx,yl->cklx", slope_z, y_value, precision=highest)
    deriv_x = jnp.einsum("cklx,xm->cklm", value_zy, x_slope, precision=highest)
    deriv_y = jnp.einsum("cklx,xm->cklm", slope_y, value_along_x, precision=highest)
    deriv_z = jnp.einsum("cklx,xm->cklm", slope_zy, value_along_x, precision=highest)
    return jnp.stack([deriv_x, deriv_y, deriv_z], axis=1)


def identity_block():
    return jnp.eye(3, dtype=jnp.float32)[:, :, None, None, None]


def gram(left_part, right_part):
    return jnp.sum(left_part[:, :, None] * right_part[:, None, :], axis=0)


def energy(node_field, tables, target_size_scale, weights):
    jacobian = gradients(node_field, tables) + identity_block()
    strain = gram(jacobian, jacobian) * target_size_scale - identity_block()
    return jnp.sum(weights * jnp.sum(strain * strain, axis=(0, 1)))


def line_terms(node_field, direction, tables, target_size_scale, weights):
    jacobian = gradients(node_field, tables) + identity_block()
    motion = gradients(direction, tables)
    strain_zero = gram(jacobian, jacobian) * target_size_scale - identity_block()
    mixed = gram(jacobian, motion)
    strain_one = (mixed + jnp.swapaxes(mixed, 0, 1)) * target_size_scale
    strain_two = gram(motion, motion) * target_size_scale

    def weighted(first_part, latter_portion):
        return jnp.sum(weights * jnp.sum(first_part * latter_portion, axis=(0, 1)))

    zero_zero = weighted(strain_zero, strain_zero)
    zero_one = weighted(strain_zero, strain_one)
    zero_two = weighted(strain_zero, strain_two)
    one_two = weighted(strain_one, strain_two)
    two_two = weighted(strain_two, strain_two)
    gauss_newton = weighted(strain_one, strain_one)
    return (
        zero_zero,
        2.0 * zero_one,
        gauss_newton + 2.0 * zero_two,
        2.0 * one_two,
        two_two,
        gauss_newton,
    )


def line_search(terms):
    const_term, linear, quadratic, cubic_term, quartic, gauss_newton = terms
    step_len = jnp.zeros((), jnp.float32)
    for search_turn in range(LS_STEPS):
        slope = linear + step_len * (
            2.0 * quadratic + step_len * (3.0 * cubic_term + step_len * 4.0 * quartic)
        )
        curvature = 2.0 * quadratic + step_len * (6.0 * cubic_term + step_len * 12.0 * quartic)
        step_len = step_len - slope / jnp.maximum(curvature, gauss_newton + 1e-06)
    return step_len


def inverse_square(coefs, coords):
    along_x = coords[:, 0]
    along_y = coords[:, 1]
    along_z = coords[:, 2]
    summed = jnp.zeros_like(along_x)
    for corner in range(8):
        weight_x = along_x if corner & 1 else 1.0 - along_x
        weight_y = along_y if corner & 2 else 1.0 - along_y
        weight_z = along_z if corner & 4 else 1.0 - along_z
        summed = summed + weight_x * weight_y * weight_z * coefs[:, corner]
    return jnp.exp(-2.0 * summed)


def gather_coefs(table, elem_ids):
    index_rows = elem_ids[:, 0, :]
    corner_rows = jnp.take(jnp.transpose(table), index_rows, axis=0)
    return jnp.moveaxis(corner_rows, 2, 1)


def answer(reply):
    return lax.all_to_all(reply, ("mesh", "bg"), split_axis=0, concat_axis=0, tiled=True)


def assemble(local_part):
    padded_z = extended(local_part, (("mesh", 1),), 1)
    partial_sum = local_part.at[:, 0].add(padded_z[:, 0]).at[:, -1].add(padded_z[:, -1])
    padded_y = extended(partial_sum, (("bg", 2),), 1)
    summed = partial_sum.at[:, :, 0].add(padded_y[:, :, 0]).at[:, :, -1].add(padded_y[:, :, -1])
    return summed


def shards(displacement, bg_coef, query_elem, query_point, query_coord):
    devices = lax.axis_size("mesh") * lax.axis_size("bg")
    z_elems = displacement.shape[1] // 2
    y_elems = displacement.shape[2] // 2
    x_elems = displacement.shape[3] // 2
    tables = (
        basis_tables(z_elems, False) + basis_tables(y_elems, False) + basis_tables(x_elems, True)
    )
    weights = quad_weights(z_elems, y_elems, x_elems)
    point_count = 27 * z_elems * y_elems * x_elems
    elem_ids = query_elem.reshape(devices, 1, -1)
    coords = query_coord.reshape(devices, 3, -1)
    fetched = answer(
        gather_coefs(
            bg_coef,
            lax.all_to_all(elem_ids, ("mesh", "bg"), split_axis=0, concat_axis=0, tiled=True),
        )
    )
    found_vals = inverse_square(fetched, coords).reshape(-1)
    target_size_scale = (
        jnp.zeros((point_count,), jnp.float32)
        .at[query_point.reshape(-1)]
        .set(found_vals, mode="drop")
    )
    target_size_scale = target_size_scale.reshape(3 * z_elems, 3 * y_elems, 3 * x_elems)

    def local_energy(values):
        return energy(values, tables, target_size_scale, weights)

    node_field = assemble(jnp.pad(displacement, ((0, 0), (0, 1), (0, 1), (0, 0))))
    history = []
    for newton_pass in range(PASSES):
        direction = -assemble(jax.grad(local_energy)(node_field))
        partial_terms = jnp.stack(
            line_terms(node_field, direction, tables, target_size_scale, weights)
        )
        totals = lax.psum(partial_terms, ("mesh", "bg"))
        step_len = line_search(totals)
        node_field = node_field + step_len * direction
        history.append(totals[:5] / (devices * z_elems * y_elems * x_elems))
    return (node_field[:, :-1, :-1], jnp.stack(history))


def solution(mesh):
    in_specs = (
        P(None, "mesh", "bg", None),
        P(None, ("mesh", "bg")),
        P(("mesh", "bg"), None, None),
        P(("mesh", "bg"), None, None),
        P(("mesh", "bg"), None, None, None),
    )
    out_specs = (P(None, "mesh", "bg", None), P())
    return jax.shard_map(shards, mesh=mesh, in_specs=in_specs, out_specs=out_specs, check_vma=False)
```

profile of v0, /device:TPU:1, one launch (start us, length us, event | category | flops | bytes accessed | tf_op | source)
XLA Modules:
  0.0 415.2 jit_solution(10419066818697922350)
XLA Ops:
  0.7 2.1 collective-permute-start
  2.8 1.6 copy.164
  4.4 10.7 %all-to-all-start = ((s32[128,1,136]{2,1,0:T(1,128)}), s32[128,1,136]{2,1,0:T(1,128)S(1)}, u32[]{:S(2)}, u32[]{:S(2)}) async-start(s32[128,1,136]{2,1,0:T(1,128)} %bitcast.21), calls=%async_computation | async-start | bytes 262144 | tf_op jit(solution)/shard_map/all_to_all | solution.py:169
  15.1 1.0 copy.160
  16.9 1.0 fusion.53
  18.0 5.5 %collective-permute-start.1 = (f32[3,1,5,128]{3,1,2,0:T(1,128)S(1)}, f32[3,1,5,128]{3,1,2,0:T(1,128)S(1)}, u32[]{:S(2)}, u32[]{:S(2)}) collective-permute-start(f32[3,1,5,128]{3,1,2,0:T(1,128)S(1)} %get-tuple-element.209), channel_id=1, source_target_pairs={{8,0},{16,8},{24,16},{32,24},{40,32},{48,40},{56,48},{64,56},{72,6... | collective-permute-start | bytes 23048 | tf_op jit(solution)/shard_map/ppermute | solution.py:24
  24.3 2.4 collective-permute-start.2
  27.5 2.4 collective-permute-start.3
  29.9 5.3 %copy.167 = f32[8,16384]{0,1:T(8,128)} copy(f32[8,16384]{1,0:T(8,128)S(1)} %copy-done.4) | data formatting | bytes 1048576 | tf_op args[1]
  37.8 61.3 %gather_fusion = f32[17408,8]{1,0:T(8,128)} fusion(f32[16384,8]{1,0:T(8,128)} %bitcast.265, s32[17408]{0:T(1024)S(1)} %broadcast_clamp_fusion), kind=kCustom, calls=%fused_computation | custom fusion | bytes 1183744 | tf_op jit(solution)/shard_map/jit(_take)/gather | solution.py:138
  99.1 6.7 %copy.168 = f32[128,136,8]{1,2,0:T(8,128)S(1)} copy(f32[128,136,8]{2,1,0:T(8,128)} %bitcast.266) | data formatting | bytes 1114112 | tf_op jit(solution)/shard_map/jit(_take)/gather | solution.py:138
  106.1 1.1 select_bitcast_fusion
  107.2 7.9 %all-to-all-start.1 = ((f32[128,8,136]{2,1,0:T(8,128)}), f32[128,8,136]{2,1,0:T(8,128)S(1)}, u32[]{:S(2)}, u32[]{:S(2)}) async-start(f32[128,8,136]{2,1,0:T(8,128)} %select_bitcast_fusion), calls=%async_computation.1 | async-start | bytes 2097152 | tf_op jit(solution)/shard_map/all_to_all | solution.py:143
  116.3 17.6 %all-to-all-done.1 = f32[128,8,136]{2,1,0:T(8,128)S(1)} async-done(((f32[128,8,136]{2,1,0:T(8,128)}), f32[128,8,136]{2,1,0:T(8,128)S(1)}, u32[]{:S(2)}, u32[]{:S(2)}) %all-to-all-start.1) | async-done | bytes 557088 | tf_op jit(solution)/shard_map/all_to_all | solution.py:143
  133.9 2.9 slice_reduce_fusion.6
  137.9 64.3 %scatter_custom_fusion = f32[6912]{0:T(1024)S(1)} fusion(s32[17408]{0:T(1024)} %bitcast.268, f32[17408]{0:T(1024)S(1)} %multiply_exponential_fusion, f32[]{:T(128)} %constant.313.clone.1), kind=kCustom, calls=%fused_computation.166 | custom fusion | bytes 28160 | tf_op jit(solution)/shard_map/scatter | solution.py:176
  205.6 5.3 %collective-permute-done.4 = f32[3,1,5,128]{3,1,2,0:T(1,128)S(1)} collective-permute-done((f32[3,1,5,128]{3,1,2,0:T(1,128)S(1)}, f32[3,1,5,128]{3,1,2,0:T(1,128)S(1)}, u32[]{:S(2)}, u32[]{:S(2)}) %collective-permute-start.4) | collective-permute-done | bytes 7712 | tf_op jit(solution)/shard_map/ppermute | solution.py:21
  211.1 2.4 collective-permute-done.5
  213.7 3.6 collective-permute-start.6
  217.3 0.8 collective-permute-done.6
  218.1 3.5 collective-permute-start.7
  221.7 0.8 collective-permute-done.7
  228.9 2.0 stack.121
  230.9 65.5 %psum.14 = f32[6]{0:T(128)S(1)} all-reduce(f32[6]{0:T(128)S(1)} %stack.121), channel_id=1, replica_groups=mesh['mesh'=16,'bg'=8] {'mesh','bg'}, use_global_device_ids=true, to_apply=%region_18.19 | all-reduce | flops 6 | bytes 48 | tf_op jit(solution)/shard_map/psum | solution.py:190
  312.5 5.8 %collective-permute-done.8 = f32[3,1,5,128]{3,1,2,0:T(1,128)S(1)} collective-permute-done((f32[3,1,5,128]{3,1,2,0:T(1,128)S(1)}, f32[3,1,5,128]{3,1,2,0:T(1,128)S(1)}, u32[]{:S(2)}, u32[]{:S(2)}) %collective-permute-start.8) | collective-permute-done | bytes 7712 | tf_op jit(solution)/shard_map/ppermute | solution.py:21
  318.5 2.4 collective-permute-done.9
  321.0 1.8 collective-permute-start.10
  322.8 2.2 collective-permute-done.10
  325.1 3.7 collective-permute-start.11
  328.7 0.8 collective-permute-done.11
  336.0 2.0 stack.136
  338.0 65.3 %psum.15 = f32[6]{0:T(128)S(1)} all-reduce(f32[6]{0:T(128)S(1)} %stack.136), channel_id=1, replica_groups=mesh['mesh'=16,'bg'=8] {'mesh','bg'}, use_global_device_ids=true, to_apply=%region_36.37 | all-reduce | flops 6 | bytes 48 | tf_op jit(solution)/shard_map/psum | solution.py:190
  (149 shorter events, 26.8 us)
Async XLA Ops:
  0.6 22.8 %copy-start.7 = (f32[6]{0:T(128)S(1)}, f32[6]{0:T(128)}, u32[]{:S(2)}) copy-start(f32[6]{0:T(128)} %constant.334.clone) | copy-start | bytes 76
  0.6 26.0 %copy-start.6 = (f32[192]{0:T(256)S(1)}, f32[192]{0:T(256)}, u32[]{:S(2)}) copy-start(f32[192]{0:T(256)} %constant.335.clone) | copy-start | bytes 2308
  0.7 17.2 %copy-start.5 = (f32[3,4,4,128]{3,2,1,0:T(4,128)S(1)}, f32[3,4,4,128]{3,2,1,0:T(4,128)}, u32[]{:S(2)}) copy-start(f32[3,4,4,128]{3,2,1,0:T(4,128)} %param.38) | copy-start | bytes 73732
  0.7 29.2 %copy-start.4 = (f32[8,16384]{1,0:T(8,128)S(1)}, f32[8,16384]{1,0:T(8,128)}, u32[]{:S(2)}) copy-start(f32[8,16384]{1,0:T(8,128)} %param.39) | copy-start | bytes 1572868
  0.7 17.2 %collective-permute-start = (f32[3,1,5,128]{3,1,2,0:T(1,128)S(1)}, f32[3,1,5,128]{3,1,2,0:T(1,128)S(1)}, u32[]{:S(2)}, u32[]{:S(2)}) collective-permute-start(f32[3,1,5,128]{3,1,2,0:T(1,128)S(1)} %slice.391), channel_id=1, source_target_pairs={{0,8},{8,16},{16,24},{24,32},{32,40},{40,48},{48,56},{56,64},{64,7... | collective-permute-start | bytes 23048 | tf_op jit(solution)/shard_map/ppermute | solution.py:21
  4.4 32.8 %all-to-all-start = ((s32[128,1,136]{2,1,0:T(1,128)}), s32[128,1,136]{2,1,0:T(1,128)S(1)}, u32[]{:S(2)}, u32[]{:S(2)}) async-start(s32[128,1,136]{2,1,0:T(1,128)} %bitcast.21), calls=%async_computation | async-start | bytes 262144 | tf_op jit(solution)/shard_map/all_to_all | solution.py:169
  18.0 6.2 %collective-permute-start.1 = (f32[3,1,5,128]{3,1,2,0:T(1,128)S(1)}, f32[3,1,5,128]{3,1,2,0:T(1,128)S(1)}, u32[]{:S(2)}, u32[]{:S(2)}) collective-permute-start(f32[3,1,5,128]{3,1,2,0:T(1,128)S(1)} %get-tuple-element.209), channel_id=1, source_target_pairs={{8,0},{16,8},{24,16},{32,24},{40,32},{48,40},{56,48},{64,56},{72,6... | collective-permute-start | bytes 23048 | tf_op jit(solution)/shard_map/ppermute | solution.py:24
  24.3 3.2 collective-permute-start.2
  27.5 8.3 %collective-permute-start.3 = (f32[3,5,1,128]{3,1,2,0:T(8,128)S(1)}, f32[3,5,1,128]{3,1,2,0:T(8,128)S(1)}, u32[]{:S(2)}, u32[]{:S(2)}) collective-permute-start(f32[3,5,1,128]{3,1,2,0:T(8,128)S(1)} %get-tuple-element.207), channel_id=1, source_target_pairs={{1,0},{2,1},{3,2},{4,3},{5,4},{6,5},{7,6},{0,7},{9,8},{10,9},{11,1... | collective-permute-start | bytes 23048 | tf_op jit(solution)/shard_map/ppermute | solution.py:24
  29.9 6.0 %copy-start.3 = (f32[5,6,1,1]{0,1,3,2:T(8,128)S(1)}, f32[5,6,1,1]{0,1,3,2:T(8,128)}, u32[]{:S(2)}) copy-start(f32[5,6,1,1]{0,1,3,2:T(8,128)} %constant.344) | copy-start | bytes 364
  35.2 0.9 copy-start.2
  35.2 1.7 copy-start
  107.2 8.3 %copy-start.1 = (f32[128,192,1,1]{0,1,3,2:T(8,128)S(1)}, f32[128,192,1,1]{0,1,3,2:T(8,128)}, u32[]{:S(2)}) copy-start(f32[128,192,1,1]{0,1,3,2:T(8,128)} %constant.343) | copy-start | bytes 294916
  107.2 26.7 %all-to-all-start.1 = ((f32[128,8,136]{2,1,0:T(8,128)}), f32[128,8,136]{2,1,0:T(8,128)S(1)}, u32[]{:S(2)}, u32[]{:S(2)}) async-start(f32[128,8,136]{2,1,0:T(8,128)} %select_bitcast_fusion), calls=%async_computation.1 | async-start | bytes 2097152 | tf_op jit(solution)/shard_map/all_to_all | solution.py:143
  205.1 5.9 %collective-permute-start.4 = (f32[3,1,5,128]{3,1,2,0:T(1,128)S(1)}, f32[3,1,5,128]{3,1,2,0:T(1,128)S(1)}, u32[]{:S(2)}, u32[]{:S(2)}) collective-permute-start(f32[3,1,5,128]{3,1,2,0:T(1,128)S(1)} %slice.440), channel_id=1, source_target_pairs={{0,8},{8,16},{16,24},{24,32},{32,40},{40,48},{48,56},{56,64},{64,7... | collective-permute-start | bytes 23048 | tf_op jit(solution)/shard_map/ppermute | solution.py:21
  211.0 2.6 collective-permute-start.5
  213.7 4.5 %collective-permute-start.6 = (f32[3,5,1,128]{3,1,2,0:T(8,128)S(1)}, f32[3,5,1,128]{3,1,2,0:T(8,128)S(1)}, u32[]{:S(2)}, u32[]{:S(2)}) collective-permute-start(f32[3,5,1,128]{3,1,2,0:T(8,128)S(1)} %slice.443), channel_id=1, source_target_pairs={{0,1},{1,2},{2,3},{3,4},{4,5},{5,6},{6,7},{7,0},{8,9},{9,10},{10,1... | collective-permute-start | bytes 23048 | tf_op jit(solution)/shard_map/ppermute | solution.py:21
  218.1 4.3 %collective-permute-start.7 = (f32[3,5,1,128]{3,1,2,0:T(8,128)S(1)}, f32[3,5,1,128]{3,1,2,0:T(8,128)S(1)}, u32[]{:S(2)}, u32[]{:S(2)}) collective-permute-start(f32[3,5,1,128]{3,1,2,0:T(8,128)S(1)} %get-tuple-element.203), channel_id=1, source_target_pairs={{1,0},{2,1},{3,2},{4,3},{5,4},{6,5},{7,6},{0,7},{9,8},{10,9},{11,1... | collective-permute-start | bytes 23048 | tf_op jit(solution)/shard_map/ppermute | solution.py:24
  312.4 5.9 %collective-permute-start.8 = (f32[3,1,5,128]{3,1,2,0:T(1,128)S(1)}, f32[3,1,5,128]{3,1,2,0:T(1,128)S(1)}, u32[]{:S(2)}, u32[]{:S(2)}) collective-permute-start(f32[3,1,5,128]{3,1,2,0:T(1,128)S(1)} %slice.446), channel_id=1, source_target_pairs={{0,8},{8,16},{16,24},{24,32},{32,40},{40,48},{48,56},{56,64},{64,7... | collective-permute-start | bytes 23048 | tf_op jit(solution)/shard_map/ppermute | solution.py:21
  318.3 2.6 collective-permute-start.9
  321.0 4.1 collective-permute-start.10
  325.1 4.5 %collective-permute-start.11 = (f32[3,5,1,128]{3,1,2,0:T(8,128)S(1)}, f32[3,5,1,128]{3,1,2,0:T(8,128)S(1)}, u32[]{:S(2)}, u32[]{:S(2)}) collective-permute-start(f32[3,5,1,128]{3,1,2,0:T(8,128)S(1)} %get-tuple-element.199), channel_id=1, source_target_pairs={{1,0},{2,1},{3,2},{4,3},{5,4},{6,5},{7,6},{0,7},{9,8},{10,9},{11,1... | collective-permute-start | bytes 23048 | tf_op jit(solution)/shard_map/ppermute | solution.py:24
where the time goes:
time: 416 us; the launch traced here: 415 us
  local copies, waits for them, and re-layouts  153 us (37%)
  blocking collectives  131 us (31%)
  starting transfers between devices  44.3 us (11%)
  waiting for transfers between devices  39.7 us (10%)
  between operations  26.7 us (6%)
  matrix products  12.1 us (3%)
  other arithmetic  9.06 us (2%)
    psum x2, blocking collectives, shards(): totals = lax.psum(partial_terms, ('mesh', 'bg'))  131 us
    gather x2, local copies, waits for them, and re-layouts, gather_coefs(): corner_rows = jnp.take(jnp.transpose(table), index_rows, axis=0)  68 us
    scatter x1, local copies, waits for them, and re-layouts, shards(): target_size_scale = jnp.zeros((point_count,), jnp.float32).at[query_point...  64.3 us
    all_to_all x1, waiting for transfers between devices, answer(): lax.all_to_all(reply, ('mesh', 'bg'), split_axis=0, concat_axis=0, tiled=...  17.6 us
    ppermute x6, starting transfers between devices, extended(): lax.ppermute(lax.slice_in_dim(block, 0, width, axis=dim), axis, backward)  15.1 us
    ppermute x6, waiting for transfers between devices, extended(): lax.ppermute(lax.slice_in_dim(block, block.shape[dim] - width, None, axis...  15 us
    all_to_all x1, starting transfers between devices, shards(): lax.all_to_all(elem_ids, ('mesh', 'bg'), split_axis=0, concat_axis=0, til...  10.7 us
    ppermute x6, starting transfers between devices, extended(): lax.ppermute(lax.slice_in_dim(block, block.shape[dim] - width, None, axis...  10.6 us
  transfers between devices with their start and end apart: 14, of which 11 were waited for; matrix products, arithmetic and copies ran while one was open for 3% of the time, Pallas kernels for 0%

commit v1 on v0

v1 whole, which is shorter than its diff:
```python
import functools

import jax
import jax.numpy as jnp
import numpy as np
from jax import lax
from jax.experimental import pallas as pl
from jax.experimental.pallas import tpu as pltpu
from jax.sharding import PartitionSpec as P

SRC = 128
SLOTS = 136
TABLE = 16384
COLS = 256


def lookup_kernel(asked_ref, table_ref, found_ref, split_ref, turned_ref, result_ref):
    for block in range(5):
        lanes = slice(block * 128, block * 128 + 128)
        turned_ref[lanes, :] = asked_ref[:, lanes].T
    for pair in range(TABLE // (2 * COLS)):
        start = pair * 2 * COLS
        rows = jnp.concatenate(
            [table_ref[:, start : start + COLS], table_ref[:, start + COLS : start + 2 * COLS]], axis=0
        )
        upper = rows.astype(jnp.bfloat16)
        split_ref[pair * 16 : pair * 16 + 16, :COLS] = upper
        split_ref[pair * 16 : pair * 16 + 16, COLS:] = (rows - upper.astype(jnp.float32)).astype(jnp.bfloat16)

    corner = lax.broadcasted_iota(jnp.int32, (8, 256), 0)
    bit_x = (corner & 1) == 1
    bit_y = (corner & 2) == 2
    bit_z = (corner & 4) == 4
    column_at = lax.broadcasted_iota(jnp.int32, (COLS, 256), 0)

    def group(main, tail, at):
        ids = turned_ref[pl.ds(main[0], 8), :].astype(jnp.int32)
        xs, ys, zs = (turned_ref[pl.ds(main[j], 8), :] for j in (1, 2, 3))
        for pair in range(4):
            def both(values):
                return jnp.concatenate([values[2 * pair : 2 * pair + 1], values[2 * pair + 1 : 2 * pair + 2]], axis=1)
            pair_ids = both(ids)
            column = pair_ids & (COLS - 1)
            row8 = jnp.broadcast_to(pair_ids >> 8, (8, 256))
            chosen = (column_at == column).astype(jnp.float32).astype(jnp.bfloat16)
            picked = jnp.dot(split_ref[:, :COLS], chosen, preferred_element_type=jnp.float32) + jnp.dot(
                split_ref[:, COLS:], chosen, preferred_element_type=jnp.float32
            )
            coefs = [jnp.zeros((8, 256), jnp.float32) for _ in range(4)]
            for row in range(TABLE // COLS):
                coefs[row % 4] = jnp.where(row8 == row, picked[row * 8 : row * 8 + 8], coefs[row % 4])
            coef = (coefs[0] + coefs[1]) + (coefs[2] + coefs[3])
            px, py, pz = both(xs), both(ys), both(zs)
            weight = jnp.where(bit_x, px, 1.0 - px) * jnp.where(bit_y, py, 1.0 - py) * jnp.where(bit_z, pz, 1.0 - pz)
            lsize = jnp.sum(weight * coef, axis=0, keepdims=True)
            value = jnp.exp(-2.0 * lsize)
            result_ref[pl.ds(at + 2 * pair, 1), :] = value[:, :128]
            result_ref[pl.ds(at + 2 * pair + 1, 1), :] = value[:, 128:]

    def step(i, carry):
        base = pl.multiple_of(i * 8, 8)
        group([base, base + 128, base + 256, base + 384], None, base)
        return carry

    lax.fori_loop(0, 16, step, 0)
    group([512, 520, 528, 536], None, 128)
    found_ref[:, :128] = result_ref[:128, :].T
    found_ref[:, 128:] = result_ref[128:, :].T


def lookup(asked, table):
    return pl.pallas_call(
        lookup_kernel,
        out_shape=jax.ShapeDtypeStruct((SRC, SLOTS), jnp.float32),
        scratch_shapes=[
            pltpu.VMEM((8 * TABLE // COLS, 2 * COLS), jnp.bfloat16),
            pltpu.VMEM((640, 128), jnp.float32),
            pltpu.VMEM((SLOTS, 128), jnp.float32),
        ],
        name="lookup",
    )(asked, table)


def place_kernel(found_ref, point_ref, size_ref, value_ref, row_ref, lane_ref):
    value_ref[:128, :] = found_ref[:, :128].T
    value_ref[128:, :] = found_ref[:, 128:].T
    point = jnp.concatenate([point_ref[:, :128].T, point_ref[:, 128:].T], axis=0)
    line = (point * 10923) >> 21
    qx = point - line * 192
    qz = (line * 43) >> 8
    qy = line - qz * 6
    ex = (qx * 171) >> 9
    jx = qx - ex * 3
    ey = (qy * 11) >> 5
    jy = qy - ey * 3
    ez = (qz * 11) >> 5
    jz = qz - ez * 3
    row_ref[...] = ((jz * 3 + jy) * 3 + jx) * 2 + ey
    lane_ref[...] = ez * 64 + ex
    lane_at = lax.broadcasted_iota(jnp.int32, (128, 128), 0)
    row_at = lax.broadcasted_iota(jnp.int32, (56, 128), 0)

    def step(i, total):
        base = pl.multiple_of(i * 8, 8)
        values = value_ref[pl.ds(base, 8), :]
        rows = row_ref[pl.ds(base, 8), :]
        lanes = lane_ref[pl.ds(base, 8), :]
        left, right = [], []
        for r in range(8):
            value = values[r : r + 1]
            placed = jnp.where(row_at == rows[r : r + 1], jnp.broadcast_to(value, (56, 128)), 0.0)
            upper = placed.astype(jnp.bfloat16).astype(jnp.float32)
            left.append(jnp.concatenate([upper, placed - upper], axis=0).astype(jnp.bfloat16))
            right.append((lane_at == lanes[r : r + 1]).astype(jnp.float32).astype(jnp.bfloat16))
        left = jnp.concatenate(left, axis=1)
        right = jnp.concatenate(right, axis=1)
        return total + lax.dot_general(left, right, (((1,), (1,)), ((), ())), preferred_element_type=jnp.float32)

    total = lax.fori_loop(0, SLOTS // 8, step, jnp.zeros((112, 128), jnp.float32))
    size_ref[...] = (total[:56] + total[56:])[:54]


def place(found, point):
    return pl.pallas_call(
        place_kernel,
        out_shape=jax.ShapeDtypeStruct((54, 128), jnp.float32),
        scratch_shapes=[
            pltpu.VMEM((SLOTS, 128), jnp.float32),
            pltpu.VMEM((SLOTS, 128), jnp.int32),
            pltpu.VMEM((SLOTS, 128), jnp.int32),
        ],
        name="place",
    )(found, point)


HALF_GAP = float(np.sqrt(0.15))
OUTER, MIDDLE = 5.0 / 18.0, 8.0 / 18.0
NEIGHBOURS = [(z, y) for z in (-1, 0, 1) for y in (-1, 0, 1)]


def lane_index():
    return lax.broadcasted_iota(jnp.int32, (8, 128), 1)


def x_up(v):
    return jnp.where((lane_index() & 63) == 63, pltpu.roll(v, 63, 1), pltpu.roll(v, 127, 1))


def x_down(v):
    return jnp.where((lane_index() & 63) == 0, pltpu.roll(v, 65, 1), pltpu.roll(v, 1, 1))


def z_up(v):
    turned = pltpu.roll(v, 64, 1)
    return jnp.where(lane_index() < 64, turned, pltpu.roll(turned, 4, 0))


def z_down(v):
    turned = pltpu.roll(v, 64, 1)
    return jnp.where(lane_index() < 64, pltpu.roll(turned, 4, 0), turned)


def y_up(v):
    return pltpu.roll(v, 7, 0)


def y_down(v):
    return pltpu.roll(v, 1, 0)


def spread(low, mid, high, slopes=True, values=True):
    bend = (low + high) - 2.0 * mid
    rise = high - low
    vals = slps = None
    if values:
        centre = mid + (2.0 * HALF_GAP * HALF_GAP) * bend
        lean = HALF_GAP * rise
        vals = (centre - lean, mid, centre + lean)
    if slopes:
        change = (4.0 * HALF_GAP) * bend
        slps = (rise - change, rise, rise + change)
    return vals, slps


def collect(vals, slps):
    bend = rise = mid = None
    if vals is not None:
        outer = vals[0] + vals[2]
        bend = (2.0 * HALF_GAP * HALF_GAP) * outer
        rise = HALF_GAP * (vals[2] - vals[0])
        mid = outer + vals[1]
    if slps is not None:
        slope_bend = (4.0 * HALF_GAP) * (slps[2] - slps[0])
        slope_rise = (slps[0] + slps[2]) + slps[1]
        bend = slope_bend if bend is None else bend + slope_bend
        rise = slope_rise if rise is None else rise + slope_rise
    twice = -2.0 * bend
    return bend - rise, twice if mid is None else mid + twice, bend + rise


def at_point(c, k, jz, jy, jx):
    row = (((jz * 3 + jy) * 3 + jx) * 9 + k) * 8
    return pl.ds(pl.multiple_of(row + c * 24, 8), 8)


def forward(c, local, out_ref):
    along_z = [[spread(local(0, y, x), local(1, y, x), local(2, y, x)) for x in range(3)] for y in range(3)]
    for jz in range(3):
        value = [[along_z[y][x][0][jz] for x in range(3)] for y in range(3)]
        slope = [[along_z[y][x][1][jz] for x in range(3)] for y in range(3)]
        plain = [spread(value[0][x], value[1][x], value[2][x]) for x in range(3)]
        steep = [spread(slope[0][x], slope[1][x], slope[2][x], slopes=False)[0] for x in range(3)]
        for jy in range(3):
            dx = spread(*(plain[x][0][jy] for x in range(3)), values=False)[1]
            dy = spread(*(plain[x][1][jy] for x in range(3)), slopes=False)[0]
            dz = spread(*(steep[x][jy] for x in range(3)), slopes=False)[0]
            for jx in range(3):
                for k, part in enumerate((dx, dy, dz)):
                    out_ref[at_point(c, k, jz, jy, jx), :] = part[jx]


def backward(c, from_ref, out_ref):
    planes = []
    for jz in range(3):
        lines = []
        for jy in range(3):
            dx, dy, dz = (
                tuple(from_ref[at_point(c, k, jz, jy, jx), :] for jx in range(3)) for k in range(3)
            )
            lines.append((collect(None, dx), collect(dy, None), collect(dz, None)))
        value = [
            collect(tuple(lines[jy][0][x] for jy in range(3)), tuple(lines[jy][1][x] for jy in range(3)))
            for x in range(3)
        ]
        slope = [collect(tuple(lines[jy][2][x] for jy in range(3)), None) for x in range(3)]
        planes.append((value, slope))
    whole = [
        [
            collect(
                tuple(planes[jz][0][x][y] for jz in range(3)), tuple(planes[jz][1][x][y] for jz in range(3))
            )
            for x in range(3)
        ]
        for y in range(3)
    ]
    folded_x = [[(whole[y][0][z] + x_down(whole[y][2][z]), whole[y][1][z]) for z in range(3)] for y in range(3)]
    for x in range(2):
        folded = [(folded_x[0][z][x] + y_down(folded_x[2][z][x]), folded_x[1][z][x]) for z in range(3)]
        for y in range(2):
            for z, node in enumerate((folded[0][y] + z_down(folded[2][y]), folded[1][y])):
                row = (z * 4 + y * 2 + x) * 8
                out_ref[pl.ds(pl.multiple_of(row + c * 64, 8), 8), :] = node


def symmetric(build):
    upper = {(k, l): build(k, l) for k in range(3) for l in range(k, 3)}
    return {(k, l): upper[min(k, l), max(k, l)] for k in range(3) for l in range(3)}


def inner(a, b):
    square = (a[0, 0] * b[0, 0] + a[1, 1] * b[1, 1]) + a[2, 2] * b[2, 2]
    cross = (a[0, 1] * b[0, 1] + a[0, 2] * b[0, 2]) + a[1, 2] * b[1, 2]
    return square + 2.0 * cross


def column_dot(a, b, k, l):
    return (a[0][k] * b[0][l] + a[1][k] * b[1][l]) + a[2][k] * b[2][l]


def load_tensor(ref, jz, jy, jx):
    tensor = [[ref[at_point(c, k, jz, jy, jx), :] for k in range(3)] for c in range(3)]
    return tensor


def jacobian_at(ref, jz, jy, jx):
    tensor = load_tensor(ref, jz, jy, jx)
    return [[tensor[c][k] + 1.0 if c == k else tensor[c][k] for k in range(3)] for c in range(3)]


def strain_of(jac, size):
    return symmetric(lambda k, l: column_dot(jac, jac, k, l) * size - (1.0 if k == l else 0.0))


def weight_at(jz, jy, jx):
    along_z = jnp.where(jz == 1, MIDDLE, OUTER).astype(jnp.float32)
    return along_z * ((MIDDLE if jy == 1 else OUTER) * (MIDDLE if jx == 1 else OUTER))


def newton_step(totals):
    _, linear, quadratic, cubic, quartic, floor = (totals[:, i : i + 1] for i in range(6))
    step = jnp.zeros_like(linear)
    for _ in range(4):
        slope = linear + step * (2.0 * quadratic + step * (3.0 * cubic + step * 4.0 * quartic))
        curvature = 2.0 * quadratic + step * (6.0 * cubic + step * 12.0 * quartic)
        step = step - slope / jnp.maximum(curvature, floor + 1e-06)
    return step


def add_up(terms_ref):
    return jnp.sum(terms_ref[...], axis=0, keepdims=True)


def ring(pieces, count, out_ref, out_at, z_shift, y_shift):
    low = lax.broadcasted_iota(jnp.int32, (count, 128), 1) < 64
    places = ((-1, 1), (0, 0), (0, 1), (1, 0)) if not y_shift else ((0, 0), (0, 1), (1, 0), (1, 1))
    for upper in range(2):
        for y, (piece_y, row) in enumerate(places):
            rows = pl.ds(row, count, stride=2)
            here = pieces[0, piece_y]
            above = pieces[1, piece_y]
            if z_shift:
                here = pltpu.roll(here[rows, :], 64, 1)
                above = pltpu.roll(above[rows, :], 64, 1)
                value = jnp.where(low, above, here) if upper else jnp.where(low, here, above)
            elif upper:
                value = jnp.where(low, above[rows, :], pieces[-1, piece_y][rows, :])
            else:
                value = here[rows, :]
            out_ref[pl.ds(out_at + upper * 4 + y, count, stride=8), :] = value


def pass_kernel(first, *refs):
    refs = list(refs)
    field = {at: refs.pop(0) for at in NEIGHBOURS}
    if not first:
        shift = {at: refs.pop(0) for at in NEIGHBOURS}
    sizes = {at: refs.pop(0) for at in NEIGHBOURS}
    if first:
        move_ref, terms_out, nodes_ref, size_ref, jac_ref, part_ref, turn_ref = refs
    else:
        terms_in, move_ref, terms_out, own_ref, nodes_ref, size_ref, jac_ref, part_ref, turn_ref, sum_ref = refs
        step = newton_step(add_up(terms_in))
        for i, at in enumerate(NEIGHBOURS):
            sum_ref[i] = field[at][...] + step * shift[at][...]
        field = {at: sum_ref.at[i] for i, at in enumerate(NEIGHBOURS)}
        own_ref[...] = field[0, 0][...]
    for z_shift in range(2):
        for y_shift in range(2):
            ring(field, 24, nodes_ref, (z_shift * 2 + y_shift) * 192, z_shift, y_shift)
    ring(sizes, 27, size_ref, 0, 0, 0)

    def known(c):
        def local(z, y, x):
            row = ((z == 2) * 2 + (y == 2)) * 192 + ((z % 2) * 4 + (y % 2) * 2 + x % 2) * 8
            value = nodes_ref[pl.ds(pl.multiple_of(row + c * 64, 8), 8), :]
            return x_up(value) if x == 2 else value
        return local

    def sought(c):
        def local(z, y, x):
            row = ((z % 2) * 4 + (y % 2) * 2 + x % 2) * 8
            value = turn_ref[pl.ds(pl.multiple_of(row + c * 64, 8), 8), :]
            if x == 2:
                value = x_up(value)
            if y == 2:
                value = y_up(value)
            return z_up(value) if z == 2 else value
        return local

    def each(body):
        def run(i, carry):
            body(i)
            return carry
        lax.fori_loop(0, 3, run, 0)

    def size_at(jz, jy, jx):
        return size_ref[pl.ds(pl.multiple_of((jz * 9 + jy * 3 + jx) * 8, 8), 8), :]

    each(lambda c: forward(c, known(c), jac_ref))

    def stress(jz):
        for jy in range(3):
            for jx in range(3):
                jac = jacobian_at(jac_ref, jz, jy, jx)
                size = size_at(jz, jy, jx)
                strain = strain_of(jac, size)
                scale = size * (-4.0 * weight_at(jz, jy, jx))
                for c in range(3):
                    for k in range(3):
                        part = (strain[k, 0] * jac[c][0] + strain[k, 1] * jac[c][1]) + strain[k, 2] * jac[c][2]
                        part_ref[at_point(c, k, jz, jy, jx), :] = part * scale

    each(stress)
    each(lambda c: backward(c, part_ref, turn_ref))
    for row in range(2):
        move_ref[pl.ds(row, 24, stride=2), :] = turn_ref[pl.ds(row + 1, 24, stride=8), :]
    each(lambda c: forward(c, sought(c), part_ref))

    def line(jz, sums):
        for jy in range(3):
            for jx in range(3):
                jac = jacobian_at(jac_ref, jz, jy, jx)
                motion = load_tensor(part_ref, jz, jy, jx)
                size = size_at(jz, jy, jx)
                weight = weight_at(jz, jy, jx)
                zero = strain_of(jac, size)
                one = symmetric(lambda k, l: (column_dot(jac, motion, k, l) + column_dot(motion, jac, k, l)) * size)
                two = symmetric(lambda k, l: column_dot(motion, motion, k, l) * size)
                pairs = ((zero, zero), (zero, one), (zero, two), (one, two), (two, two), (one, one))
                sums = tuple(total + weight * inner(*pair) for total, pair in zip(sums, pairs))
        return sums

    sums = lax.fori_loop(0, 3, line, tuple(jnp.zeros((8, 128), jnp.float32) for _ in range(6)))
    sub = lax.broadcasted_iota(jnp.int32, (8, 128), 0)
    own = (sub == 1) | (sub == 2)
    zz, zo, zt, ot, tt, gn = (jnp.sum(jnp.where(own, total, 0.0), keepdims=True) for total in sums)
    lane = lax.broadcasted_iota(jnp.int32, (1, 128), 1)
    terms = jnp.zeros((1, 128), jnp.float32)
    for i, term in enumerate((zz, 2.0 * zo, gn + 2.0 * zt, 2.0 * ot, tt, gn)):
        terms = jnp.where(lane == i, term, terms)
    terms_out[...] = jnp.broadcast_to(terms, (SRC, 128))


def newton_pass(field, shift, sizes, terms):
    first = shift is None
    node = jax.ShapeDtypeStruct((48, 128), jnp.float32)
    outs = [node, jax.ShapeDtypeStruct((SRC, 128), jnp.float32)] + ([] if first else [node])
    scratch = [
        pltpu.VMEM((4 * 192, 128), jnp.float32),
        pltpu.VMEM((27 * 8, 128), jnp.float32),
        pltpu.VMEM((243 * 8, 128), jnp.float32),
        pltpu.VMEM((243 * 8, 128), jnp.float32),
        pltpu.VMEM((24 * 8, 128), jnp.float32),
    ] + ([] if first else [pltpu.VMEM((9, 48, 128), jnp.float32)])
    args = list(field) + ([] if first else list(shift)) + list(sizes) + ([] if first else [terms])
    return pl.pallas_call(
        functools.partial(pass_kernel, first),
        out_shape=outs,
        scratch_shapes=scratch,
        name="pass_one" if first else "pass_two",
    )(*args)


def interleave(back):
    row = lax.broadcasted_iota(jnp.int32, (128, 128), 0)
    col = lax.broadcasted_iota(jnp.int32, (128, 128), 1)
    if back:
        row, col = col, row
    return (col == (row & 1) * 64 + (row >> 1)).astype(jnp.float32)


def split_kernel(nodes_ref, out_ref, rows_ref):
    rows = nodes_ref[...].reshape(48, 128)
    rows_ref[...] = jnp.dot(rows, interleave(False), precision=lax.Precision.HIGHEST, preferred_element_type=jnp.float32)
    low = lax.broadcasted_iota(jnp.int32, (1, 128), 1) < 64
    for c in range(3):
        for az in range(2):
            for ay in range(2):
                for ey in range(2):
                    at = c * 16 + az * 4 + ey * 2 + ay
                    first = rows_ref[at : at + 1, :]
                    second = rows_ref[at + 8 : at + 9, :]
                    to = (c * 8 + az * 4 + ay * 2) * 2 + ey
                    out_ref[to : to + 1, :] = jnp.where(low, first, pltpu.roll(second, 64, 1))
                    out_ref[to + 2 : to + 3, :] = jnp.where(low, pltpu.roll(first, 64, 1), second)


def split_nodes(nodes):
    return pl.pallas_call(
        split_kernel,
        out_shape=jax.ShapeDtypeStruct((48, 128), jnp.float32),
        scratch_shapes=[pltpu.VMEM((48, 128), jnp.float32)],
        name="split_nodes",
    )(nodes)


def finish_kernel(own_ref, move_ref, first_ref, second_ref, out_ref, coeff_ref, rows_ref, new_ref):
    first = add_up(first_ref)
    second = add_up(second_ref)
    new_ref[...] = own_ref[...] + newton_step(second) * move_ref[...]
    low = lax.broadcasted_iota(jnp.int32, (1, 128), 1) < 64
    for c in range(3):
        for az in range(2):
            for ay in range(2):
                for ey in range(2):
                    at = (c * 8 + az * 4 + ay * 2) * 2 + ey
                    even = new_ref[at : at + 1, :]
                    odd = new_ref[at + 2 : at + 3, :]
                    to = c * 16 + az * 4 + ey * 2 + ay
                    rows_ref[to : to + 1, :] = jnp.where(low, even, pltpu.roll(odd, 64, 1))
                    rows_ref[to + 8 : to + 9, :] = jnp.where(low, pltpu.roll(even, 64, 1), odd)
    rows = jnp.dot(rows_ref[...], interleave(True), precision=lax.Precision.HIGHEST, preferred_element_type=jnp.float32)
    out_ref[...] = rows.reshape(3, 4, 4, 128)
    coeff_ref[0:1, :] = first[:, :5] * (1.0 / 32768.0)
    coeff_ref[1:2, :] = second[:, :5] * (1.0 / 32768.0)


def finish(own, move, first, second):
    return pl.pallas_call(
        finish_kernel,
        out_shape=[jax.ShapeDtypeStruct((3, 4, 4, 128), jnp.float32), jax.ShapeDtypeStruct((2, 5), jnp.float32)],
        scratch_shapes=[pltpu.VMEM((48, 128), jnp.float32), pltpu.VMEM((48, 128), jnp.float32)],
        name="finish",
    )(own, move, first, second)


def pack_kernel(elem_ref, coord_ref, out_ref):
    elem = elem_ref[...].astype(jnp.float32)
    out_ref[:, :128] = elem[:, :128]
    tails = [elem[:, 128:]]
    for j in range(3):
        coord = coord_ref[:, j, :]
        out_ref[:, 128 + j * 128 : 256 + j * 128] = coord[:, :128]
        tails.append(coord[:, 128:])
    out_ref[:, 512:] = jnp.concatenate(tails + [jnp.zeros((SRC, 96), jnp.float32)], axis=1)


def pack(elem, coord):
    return pl.pallas_call(
        pack_kernel, out_shape=jax.ShapeDtypeStruct((SRC, 640), jnp.float32), name="pack"
    )(elem, coord)


def exchange(values):
    return lax.all_to_all(values, ("mesh", "bg"), split_axis=0, concat_axis=0, tiled=True)


def around(block):
    def moved(values, axis, by):
        count = lax.axis_size(axis)
        return lax.ppermute(values, axis, [(i, (i - by) % count) for i in range(count)])

    pieces = {(0, 0): block}
    for z in (-1, 1):
        pieces[z, 0] = moved(block, "mesh", z)
    for z in (0, -1, 1):
        for y in (-1, 1):
            pieces[z, y] = moved(pieces[z, 0], "bg", y)
    return [pieces[at] for at in NEIGHBOURS]


def shards(displacement, bg_coef, query_elem, query_point, query_coord):
    own = split_nodes(displacement)
    asked = exchange(pack(query_elem.reshape(SRC, SLOTS), query_coord.reshape(SRC, 3, SLOTS)))
    field = around(own)
    found = exchange(lookup(asked, bg_coef))
    sizes = around(place(found, query_point.reshape(SRC, SLOTS)))
    move, terms = newton_pass(field, None, sizes, None)
    first_terms = exchange(terms)
    last_move, last_terms, last_own = newton_pass(field, around(move), sizes, first_terms)
    return finish(last_own, last_move, first_terms, exchange(last_terms))


def solution(mesh):
    in_specs = (
        P(None, "mesh", "bg", None),
        P(None, ("mesh", "bg")),
        P(("mesh", "bg"), None, None),
        P(("mesh", "bg"), None, None),
        P(("mesh", "bg"), None, None, None),
    )
    out_specs = (P(None, "mesh", "bg", None), P())
    return jax.shard_map(shards, mesh=mesh, in_specs=in_specs, out_specs=out_specs, check_vma=False)
```

time: 416 us -> 143 us (0.34)
  local copies, waits for them, and re-layouts: 153 us -> 9.61 us
  blocking collectives: 131 us -> 40.8 us
  Pallas kernels: 0 us -> 38.5 us
  waiting for transfers between devices: 39.7 us -> 4.19 us
  between operations: 26.7 us -> 0.93 us
  matrix products: 12.1 us -> 0 us
  other arithmetic: 9.06 us -> 0 us
    psum x2 -> x0, blocking collectives: 131 us -> none  [shards(): totals = lax.psum(partial_terms, ('mesh', 'bg'))]
    gather x2 -> x0, local copies, waits for them, and re-layouts: 68 us -> none  [gather_coefs(): corner_rows = jnp.take(jnp.transpose(table), index_rows, axis=0)]
    scatter x1 -> x0, local copies, waits for them, and re-layouts: 64.3 us -> none  [shards(): target_size_scale = jnp.zeros((point_count,), jnp.float32).at[query_point...]
    all_to_all x0 -> x2, blocking collectives: none -> 40.8 us  [exchange(): lax.all_to_all(values, ('mesh', 'bg'), split_axis=0, concat_axis=0, tiled...]
    pallas_call x0 -> x7, Pallas kernels: none -> 38.5 us  [the longest x1 15.1 us: lookup(): pl.pallas_call(lookup_kernel, out_shape=jax.ShapeDtypeStruct((SRC, SLOTS)...]
    ppermute x12 -> x24, waiting for transfers between devices: 22.2 us -> 4.18 us  [moved(): lax.ppermute(values, axis, [(i, (i - by) % count) for i in range(count)])]
    all_to_all x2, waiting for transfers between devices: 17.6 us -> 0.01 us  [exchange(): lax.all_to_all(values, ('mesh', 'bg'), split_axis=0, concat_axis=0, tiled...]
    ppermute x12 -> x24, starting transfers between devices: 25.7 us -> 37.9 us  [moved(): lax.ppermute(values, axis, [(i, (i - by) % count) for i in range(count)])]
  transfers between devices with their start and end apart: 14 -> 26, of which waited for: 11 -> 5; matrix products, arithmetic and copies ran while one was open for 3% -> 1% of each run, Pallas kernels for 0% -> 6%
where the time goes in v1:
time: 143 us; the launch traced here: 142 us
  starting transfers between devices  47.9 us (33%)
  blocking collectives  40.8 us (29%)
  Pallas kernels  38.5 us (27%)
  local copies, waits for them, and re-layouts  9.61 us (7%)
  waiting for transfers between devices  4.19 us (3%)
    all_to_all x2, blocking collectives, exchange(): lax.all_to_all(values, ('mesh', 'bg'), split_axis=0, concat_axis=0, tiled...  40.8 us
    ppermute x24, starting transfers between devices, moved(): lax.ppermute(values, axis, [(i, (i - by) % count) for i in range(count)])  37.9 us
    pallas_call x1, Pallas kernels, lookup(): pl.pallas_call(lookup_kernel, out_shape=jax.ShapeDtypeStruct((SRC, SLOTS)...  15.1 us
    pallas_call x2, Pallas kernels, newton_pass(): pl.pallas_call(functools.partial(pass_kernel, first), out_shape=outs, scr...  10.5 us
    all_to_all x2, starting transfers between devices, exchange(): lax.all_to_all(values, ('mesh', 'bg'), split_axis=0, concat_axis=0, tiled...  9.98 us
    pallas_call x1, Pallas kernels, place(): pl.pallas_call(place_kernel, out_shape=jax.ShapeDtypeStruct((54, 128), jn...  6.28 us
    unnamed x60, local copies, waits for them, and re-layouts  5.95 us
    ppermute x24, waiting for transfers between devices, moved(): lax.ppermute(values, axis, [(i, (i - by) % count) for i in range(count)])  4.18 us
  transfers between devices with their start and end apart: 26, of which 5 were waited for; matrix products, arithmetic and copies ran while one was open for 1% of the time, Pallas kernels for 6%

profile of v1, /device:TPU:1, one launch (start us, length us, event | category | flops | bytes accessed | tf_op | source)
XLA Modules:
  0.0 141.9 jit_solution(7999408066513177827)
XLA Ops:
  0.6 2.0 %copy.18 = f32[1,128,3,136]{3,2,1,0:T(4,128)} copy(f32[1,128,3,136]{1,3,2,0:T(8,128)} %param.9) | data formatting | bytes 417792 | tf_op args[4]
  3.4 2.0 %pack.1 = f32[128,640]{1,0:T(8,128)} custom-call(s32[128,136]{1,0:T(8,128)} %bitcast.25, f32[128,3,136]{2,1,0:T(4,128)} %bitcast.20), custom_call_target="tpu_custom_call" | custom-call | tf_op jit(solution)/shard_map/pack/pallas_call | solution.py:509
  5.4 1.3 copy.19
  6.7 22.9 %all_to_all.44 = f32[128,1,640]{2,1,0:T(1,128)S(1)} all-to-all(f32[128,1,640]{2,1,0:T(1,128)S(1)} %copy.19), channel_id=1, replica_groups=mesh['mesh'=16,'bg'=8] {'mesh','bg'}, dimensions={0} | all-to-all | bytes 655360 | tf_op jit(solution)/shard_map/all_to_all | solution.py:515
  30.4 15.1 %lookup.1 = f32[128,136]{1,0:T(8,128)} custom-call(f32[128,640]{1,0:T(8,128)} %bitcast.22, f32[8,16384]{1,0:T(8,128)} %table_ref.1), custom_call_target="tpu_custom_call" | custom-call | tf_op jit(solution)/shard_map/lookup/pallas_call | solution.py:72
  45.4 1.7 %copy.20 = f32[128,1,136]{2,1,0:T(1,128)} copy(f32[128,1,136]{2,0,1:T(8,128)} %bitcast.26) | data formatting | bytes 139264 | tf_op jit(solution)/shard_map/all_to_all | solution.py:515
  47.1 4.4 %all-to-all-start.1 = ((f32[128,1,136]{2,1,0:T(1,128)}), f32[128,1,136]{2,1,0:T(1,128)S(1)}, u32[]{:S(2)}, u32[]{:S(2)}) async-start(f32[128,1,136]{2,1,0:T(1,128)} %copy.20), calls=%async_computation.1 | async-start | bytes 262144 | tf_op jit(solution)/shard_map/all_to_all | solution.py:515
  51.6 1.6 %split_nodes.1.refs_4_ = f32[48,128]{1,0:T(8,128)} custom-call(f32[3,4,4,128]{3,2,1,0:T(4,128)} %nodes_ref.1), custom_call_target="tpu_custom_call" | custom-call | tf_op jit(solution)/shard_map/split_nodes/pallas_call | solution.py:459
  53.2 1.4 collective-permute-start
  54.5 4.1 %collective-permute-start.5 = (f32[48,128]{1,0:T(8,128)}, f32[48,128]{1,0:T(8,128)S(1)}, u32[]{:S(2)}, u32[]{:S(2)}) collective-permute-start(f32[48,128]{1,0:T(8,128)} %split_nodes.1.refs_4_), channel_id=1, source_target_pairs={{0,120},{8,0},{16,8},{24,16},{32,24},{40,32},{48,40},{56,48},{64,5... | collective-permute-start | bytes 73736 | tf_op jit(solution)/shard_map/ppermute | solution.py:521
  58.7 1.8 %collective-permute-start.3 = (f32[48,128]{1,0:T(8,128)}, f32[48,128]{1,0:T(8,128)S(1)}, u32[]{:S(2)}, u32[]{:S(2)}) collective-permute-start(f32[48,128]{1,0:T(8,128)} %split_nodes.1.refs_4_), channel_id=1, source_target_pairs={{0,1},{1,2},{2,3},{3,4},{4,5},{5,6},{6,7},{7,0},{8,9},{9,10},{10,1... | collective-permute-start | bytes 73736 | tf_op jit(solution)/shard_map/ppermute | solution.py:521
  60.5 2.0 %collective-permute-start.1 = (f32[48,128]{1,0:T(8,128)S(1)}, f32[48,128]{1,0:T(8,128)S(1)}, u32[]{:S(2)}, u32[]{:S(2)}) collective-permute-start(f32[48,128]{1,0:T(8,128)S(1)} %collective-permute-done.refs_1_), channel_id=1, source_target_pairs={{0,1},{1,2},{2,3},{3,4},{4,5},{5,6},{6,7},{7,0},{8,9},{9,10},{10,1... | collective-permute-start | bytes 73736 | tf_op jit(solution)/shard_map/ppermute | solution.py:521
  64.1 6.3 %place.1.refs_13_.refs_22_ = f32[54,128]{1,0:T(8,128)} custom-call(f32[128,136]{1,0:T(8,128)} %bitcast.28, s32[128,136]{1,0:T(8,128)} %bitcast.27), custom_call_target="tpu_custom_call" | custom-call | tf_op jit(solution)/shard_map/place/pallas_call | solution.py:124
  70.4 4.8 %collective-permute-start.13 = (f32[54,128]{1,0:T(8,128)}, f32[54,128]{1,0:T(8,128)S(1)}, u32[]{:S(2)}, u32[]{:S(2)}) collective-permute-start(f32[54,128]{1,0:T(8,128)} %place.1.refs_13_.refs_22_), channel_id=1, source_target_pairs={{0,120},{8,0},{16,8},{24,16},{32,24},{40,32},{48,40},{56,48},{64,5... | collective-permute-start | bytes 82952 | tf_op jit(solution)/shard_map/ppermute | solution.py:521
  75.2 2.2 %collective-permute-start.11 = (f32[54,128]{1,0:T(8,128)}, f32[54,128]{1,0:T(8,128)S(1)}, u32[]{:S(2)}, u32[]{:S(2)}) collective-permute-start(f32[54,128]{1,0:T(8,128)} %place.1.refs_13_.refs_22_), channel_id=1, source_target_pairs={{0,1},{1,2},{2,3},{3,4},{4,5},{5,6},{6,7},{7,0},{8,9},{9,10},{10,1... | collective-permute-start | bytes 82952 | tf_op jit(solution)/shard_map/ppermute | solution.py:521
  77.4 1.4 collective-permute-start.7
  79.6 4.0 %collective-permute-start.12 = (f32[54,128]{1,0:T(8,128)}, f32[54,128]{1,0:T(8,128)S(1)}, u32[]{:S(2)}, u32[]{:S(2)}) collective-permute-start(f32[54,128]{1,0:T(8,128)} %place.1.refs_13_.refs_22_), channel_id=1, source_target_pairs={{0,7},{1,0},{2,1},{3,2},{4,3},{5,4},{6,5},{7,6},{8,15},{9,8},{10,9... | collective-permute-start | bytes 82952 | tf_op jit(solution)/shard_map/ppermute | solution.py:521
  83.7 1.7 %collective-permute-start.14 = (f32[54,128]{1,0:T(8,128)S(1)}, f32[54,128]{1,0:T(8,128)S(1)}, u32[]{:S(2)}, u32[]{:S(2)}) collective-permute-start(f32[54,128]{1,0:T(8,128)S(1)} %collective-permute-done.13.refs_16_.refs_25_), channel_id=1, source_target_pairs={{0,1},{1,2},{2,3},{3,4},{4,5},{5,6},{6,7},{7,0},{8,9},{9,10},{10,1... | collective-permute-start | bytes 82952 | tf_op jit(solution)/shard_map/ppermute | solution.py:521
  85.5 1.7 %collective-permute-start.9 = (f32[54,128]{1,0:T(8,128)S(1)}, f32[54,128]{1,0:T(8,128)S(1)}, u32[]{:S(2)}, u32[]{:S(2)}) collective-permute-start(f32[54,128]{1,0:T(8,128)S(1)} %collective-permute-done.8.refs_10_.refs_19_), channel_id=1, source_target_pairs={{0,1},{1,2},{2,3},{3,4},{4,5},{5,6},{6,7},{7,0},{8,9},{9,10},{10,1... | collective-permute-start | bytes 82952 | tf_op jit(solution)/shard_map/ppermute | solution.py:521
  87.3 1.5 %collective-permute-done.15.refs_17_.refs_26_ = f32[54,128]{1,0:T(8,128)S(1)} collective-permute-done((f32[54,128]{1,0:T(8,128)S(1)}, f32[54,128]{1,0:T(8,128)S(1)}, u32[]{:S(2)}, u32[]{:S(2)}) %collective-permute-start.15) | collective-permute-done | bytes 27680 | tf_op jit(solution)/shard_map/ppermute | solution.py:521
  89.9 4.5 %pass_one.1 = (f32[48,128]{1,0:T(8,128)}, f32[128,128]{1,0:T(8,128)}) custom-call(f32[48,128]{1,0:T(8,128)} %copy-done.13, f32[48,128]{1,0:T(8,128)} %copy-done.9, f32[48,128]{1,0:T(8,128)} %copy-done.14, f32[48,128]{1,0:T(8,128)} %copy-done.11, f32[48,128]{1,0:T(8,128)} %split_nodes.1.refs_4_, f32[48,128]{1,0:T(8,128)} %copy-done.12, f32[48,128]{1,0:T(8,128)} %copy-done.15, ...), custom_call_target="tpu_custom_call" | custom-call | tf_op jit(solution)/shard_map/pass_one/pallas_call | solution.py:426
  94.5 5.5 %all-to-all-start.2 = ((f32[128,1,128]{2,1,0:T(1,128)}), f32[128,1,128]{2,1,0:T(1,128)S(1)}, u32[]{:S(2)}, u32[]{:S(2)}) async-start(f32[128,1,128]{2,1,0:T(1,128)} %bitcast.30), calls=%async_computation.2 | async-start | bytes 131072 | tf_op jit(solution)/shard_map/all_to_all | solution.py:515
  100.0 1.4 %collective-permute-start.16 = (f32[48,128]{1,0:T(8,128)S(1)}, f32[48,128]{1,0:T(8,128)S(1)}, u32[]{:S(2)}, u32[]{:S(2)}) collective-permute-start(f32[48,128]{1,0:T(8,128)S(1)} %copy-done.19), channel_id=1, source_target_pairs={{0,8},{8,16},{16,24},{24,32},{32,40},{40,48},{48,56},{56,64},{64,7... | collective-permute-start | bytes 73736 | tf_op jit(solution)/shard_map/ppermute | solution.py:521
  101.5 4.2 %collective-permute-start.21 = (f32[48,128]{1,0:T(8,128)S(1)}, f32[48,128]{1,0:T(8,128)S(1)}, u32[]{:S(2)}, u32[]{:S(2)}) collective-permute-start(f32[48,128]{1,0:T(8,128)S(1)} %copy-done.19), channel_id=1, source_target_pairs={{0,120},{8,0},{16,8},{24,16},{32,24},{40,32},{48,40},{56,48},{64,5... | collective-permute-start | bytes 73736 | tf_op jit(solution)/shard_map/ppermute | solution.py:521
  105.7 1.8 %collective-permute-start.19 = (f32[48,128]{1,0:T(8,128)S(1)}, f32[48,128]{1,0:T(8,128)S(1)}, u32[]{:S(2)}, u32[]{:S(2)}) collective-permute-start(f32[48,128]{1,0:T(8,128)S(1)} %copy-done.19), channel_id=1, source_target_pairs={{0,1},{1,2},{2,3},{3,4},{4,5},{5,6},{6,7},{7,0},{8,9},{9,10},{10,1... | collective-permute-start | bytes 73736 | tf_op jit(solution)/shard_map/ppermute | solution.py:521
  107.5 1.9 %collective-permute-start.17 = (f32[48,128]{1,0:T(8,128)S(1)}, f32[48,128]{1,0:T(8,128)S(1)}, u32[]{:S(2)}, u32[]{:S(2)}) collective-permute-start(f32[48,128]{1,0:T(8,128)S(1)} %collective-permute-done.16.refs_10_), channel_id=1, source_target_pairs={{0,1},{1,2},{2,3},{3,4},{4,5},{5,6},{6,7},{7,0},{8,9},{9,10},{10,1... | collective-permute-start | bytes 73736 | tf_op jit(solution)/shard_map/ppermute | solution.py:521
  109.7 1.5 %collective-permute-start.22 = (f32[48,128]{1,0:T(8,128)S(1)}, f32[48,128]{1,0:T(8,128)S(1)}, u32[]{:S(2)}, u32[]{:S(2)}) collective-permute-start(f32[48,128]{1,0:T(8,128)S(1)} %collective-permute-done.21.refs_16_), channel_id=1, source_target_pairs={{0,1},{1,2},{2,3},{3,4},{4,5},{5,6},{6,7},{7,0},{8,9},{9,10},{10,1... | collective-permute-start | bytes 73736 | tf_op jit(solution)/shard_map/ppermute | solution.py:521
  111.2 1.5 %collective-permute-start.23 = (f32[48,128]{1,0:T(8,128)S(1)}, f32[48,128]{1,0:T(8,128)S(1)}, u32[]{:S(2)}, u32[]{:S(2)}) collective-permute-start(f32[48,128]{1,0:T(8,128)S(1)} %collective-permute-done.21.refs_16_), channel_id=1, source_target_pairs={{0,7},{1,0},{2,1},{3,2},{4,3},{5,4},{6,5},{7,6},{8,15},{9,8},{10,9... | collective-permute-start | bytes 73736 | tf_op jit(solution)/shard_map/ppermute | solution.py:521
  113.3 1.1 collective-permute-done.23.refs_17_
  115.1 5.9 %pass_two.1 = (f32[48,128]{1,0:T(8,128)}, f32[128,128]{1,0:T(8,128)}, f32[48,128]{1,0:T(8,128)}) custom-call(f32[48,128]{1,0:T(8,128)} %copy-done.13, f32[48,128]{1,0:T(8,128)} %copy-done.9, f32[48,128]{1,0:T(8,128)} %copy-done.14, f32[48,128]{1,0:T(8,128)} %copy-done.11, f32[48,128]{1,0:T(8,128)} %split_nodes.1.refs_4_, f32[48,128]{1,0:T(8,128)} %copy-done.12, ...), custom_call_target="tpu_custom_call" | custom-call | tf_op jit(solution)/shard_map/pass_two/pallas_call | solution.py:426
  121.0 17.9 %all_to_all.45 = f32[128,1,128]{2,1,0:T(1,128)} all-to-all(f32[128,1,128]{2,1,0:T(1,128)} %bitcast.31), channel_id=1, replica_groups=mesh['mesh'=16,'bg'=8] {'mesh','bg'}, dimensions={0} | all-to-all | bytes 131072 | tf_op jit(solution)/shard_map/all_to_all | solution.py:515
  138.9 3.0 %finish.1 = (f32[3,4,4,128]{3,2,1,0:T(4,128)}, f32[2,5]{1,0:T(2,128)}) custom-call(f32[48,128]{1,0:T(8,128)} %get-tuple-element.9.own_ref, f32[48,128]{1,0:T(8,128)} %get-tuple-element.10.move_ref, f32[128,128]{1,0:T(8,128)} %bitcast.24, f32[128,128]{1,0:T(8,128)} %bitcast.29), custom_call_target="tpu_custom_call" | custom-call | tf_op jit(solution)/shard_map/finish/pallas_call | solution.py:489
  (92 shorter events, 6.7 us)
Async XLA Ops:
  47.1 15.6 %copy-start.18 = (s32[1,128,136]{1,2,0:T(8,128)S(1)}, s32[1,128,136]{1,2,0:T(8,128)}, u32[]{:S(2)}) copy-start(s32[1,128,136]{1,2,0:T(8,128)} %param.8) | copy-start | bytes 208900
  47.1 16.3 %all-to-all-start.1 = ((f32[128,1,136]{2,1,0:T(1,128)}), f32[128,1,136]{2,1,0:T(1,128)S(1)}, u32[]{:S(2)}, u32[]{:S(2)}) async-start(f32[128,1,136]{2,1,0:T(1,128)} %copy.20), calls=%async_computation.1 | async-start | bytes 262144 | tf_op jit(solution)/shard_map/all_to_all | solution.py:515
  53.2 7.3 %collective-permute-start = (f32[48,128]{1,0:T(8,128)}, f32[48,128]{1,0:T(8,128)S(1)}, u32[]{:S(2)}, u32[]{:S(2)}) collective-permute-start(f32[48,128]{1,0:T(8,128)} %split_nodes.1.refs_4_), channel_id=1, source_target_pairs={{0,8},{8,16},{16,24},{24,32},{32,40},{40,48},{48,56},{56,64},{64,7... | collective-permute-start | bytes 73736 | tf_op jit(solution)/shard_map/ppermute | solution.py:521
  54.5 15.8 %collective-permute-start.5 = (f32[48,128]{1,0:T(8,128)}, f32[48,128]{1,0:T(8,128)S(1)}, u32[]{:S(2)}, u32[]{:S(2)}) collective-permute-start(f32[48,128]{1,0:T(8,128)} %split_nodes.1.refs_4_), channel_id=1, source_target_pairs={{0,120},{8,0},{16,8},{24,16},{32,24},{40,32},{48,40},{56,48},{64,5... | collective-permute-start | bytes 73736 | tf_op jit(solution)/shard_map/ppermute | solution.py:521
  58.7 11.7 %collective-permute-start.3 = (f32[48,128]{1,0:T(8,128)}, f32[48,128]{1,0:T(8,128)S(1)}, u32[]{:S(2)}, u32[]{:S(2)}) collective-permute-start(f32[48,128]{1,0:T(8,128)} %split_nodes.1.refs_4_), channel_id=1, source_target_pairs={{0,1},{1,2},{2,3},{3,4},{4,5},{5,6},{6,7},{7,0},{8,9},{9,10},{10,1... | collective-permute-start | bytes 73736 | tf_op jit(solution)/shard_map/ppermute | solution.py:521
  60.5 14.7 %collective-permute-start.4 = (f32[48,128]{1,0:T(8,128)}, f32[48,128]{1,0:T(8,128)S(1)}, u32[]{:S(2)}, u32[]{:S(2)}) collective-permute-start(f32[48,128]{1,0:T(8,128)} %split_nodes.1.refs_4_), channel_id=1, source_target_pairs={{0,7},{1,0},{2,1},{3,2},{4,3},{5,4},{6,5},{7,6},{8,15},{9,8},{10,9... | collective-permute-start | bytes 73736 | tf_op jit(solution)/shard_map/ppermute | solution.py:521
  60.5 16.8 %collective-permute-start.1 = (f32[48,128]{1,0:T(8,128)S(1)}, f32[48,128]{1,0:T(8,128)S(1)}, u32[]{:S(2)}, u32[]{:S(2)}) collective-permute-start(f32[48,128]{1,0:T(8,128)S(1)} %collective-permute-done.refs_1_), channel_id=1, source_target_pairs={{0,1},{1,2},{2,3},{3,4},{4,5},{5,6},{6,7},{7,0},{8,9},{9,10},{10,1... | collective-permute-start | bytes 73736 | tf_op jit(solution)/shard_map/ppermute | solution.py:521
  62.5 14.8 %collective-permute-start.2 = (f32[48,128]{1,0:T(8,128)S(1)}, f32[48,128]{1,0:T(8,128)S(1)}, u32[]{:S(2)}, u32[]{:S(2)}) collective-permute-start(f32[48,128]{1,0:T(8,128)S(1)} %collective-permute-done.refs_1_), channel_id=1, source_target_pairs={{0,7},{1,0},{2,1},{3,2},{4,3},{5,4},{6,5},{7,6},{8,15},{9,8},{10,9... | collective-permute-start | bytes 73736 | tf_op jit(solution)/shard_map/ppermute | solution.py:521
  70.4 18.4 %copy-start.10 = (f32[48,128]{1,0:T(8,128)}, f32[48,128]{1,0:T(8,128)S(1)}, u32[]{:S(2)}) copy-start(f32[48,128]{1,0:T(8,128)S(1)} %collective-permute-done.5.refs_7_) | copy-start | bytes 73732
  70.4 13.3 %collective-permute-start.8 = (f32[54,128]{1,0:T(8,128)}, f32[54,128]{1,0:T(8,128)S(1)}, u32[]{:S(2)}, u32[]{:S(2)}) collective-permute-start(f32[54,128]{1,0:T(8,128)} %place.1.refs_13_.refs_22_), channel_id=1, source_target_pairs={{0,8},{8,16},{16,24},{24,32},{32,40},{40,48},{48,56},{56,64},{64,7... | collective-permute-start | bytes 82952 | tf_op jit(solution)/shard_map/ppermute | solution.py:521
  70.4 18.3 %copy-start.11 = (f32[48,128]{1,0:T(8,128)}, f32[48,128]{1,0:T(8,128)S(1)}, u32[]{:S(2)}) copy-start(f32[48,128]{1,0:T(8,128)S(1)} %collective-permute-done.3.refs_3_) | copy-start | bytes 73732
  70.4 13.3 %collective-permute-start.13 = (f32[54,128]{1,0:T(8,128)}, f32[54,128]{1,0:T(8,128)S(1)}, u32[]{:S(2)}, u32[]{:S(2)}) collective-permute-start(f32[54,128]{1,0:T(8,128)} %place.1.refs_13_.refs_22_), channel_id=1, source_target_pairs={{0,120},{8,0},{16,8},{24,16},{32,24},{40,32},{48,40},{56,48},{64,5... | collective-permute-start | bytes 82952 | tf_op jit(solution)/shard_map/ppermute | solution.py:521
  75.2 13.6 %copy-start.12 = (f32[48,128]{1,0:T(8,128)}, f32[48,128]{1,0:T(8,128)S(1)}, u32[]{:S(2)}) copy-start(f32[48,128]{1,0:T(8,128)S(1)} %collective-permute-done.4.refs_5_) | copy-start | bytes 73732
  75.2 10.3 %collective-permute-start.11 = (f32[54,128]{1,0:T(8,128)}, f32[54,128]{1,0:T(8,128)S(1)}, u32[]{:S(2)}, u32[]{:S(2)}) collective-permute-start(f32[54,128]{1,0:T(8,128)} %place.1.refs_13_.refs_22_), channel_id=1, source_target_pairs={{0,1},{1,2},{2,3},{3,4},{4,5},{5,6},{6,7},{7,0},{8,9},{9,10},{10,1... | collective-permute-start | bytes 82952 | tf_op jit(solution)/shard_map/ppermute | solution.py:521
  77.3 11.4 %copy-start.13 = (f32[48,128]{1,0:T(8,128)}, f32[48,128]{1,0:T(8,128)S(1)}, u32[]{:S(2)}) copy-start(f32[48,128]{1,0:T(8,128)S(1)} %collective-permute-done.1.refs_0_) | copy-start | bytes 73732
  77.3 2.3 %collective-permute-start.6 = (f32[48,128]{1,0:T(8,128)S(1)}, f32[48,128]{1,0:T(8,128)S(1)}, u32[]{:S(2)}, u32[]{:S(2)}) collective-permute-start(f32[48,128]{1,0:T(8,128)S(1)} %collective-permute-done.5.refs_7_), channel_id=1, source_target_pairs={{0,1},{1,2},{2,3},{3,4},{4,5},{5,6},{6,7},{7,0},{8,9},{9,10},{10,1... | collective-permute-start | bytes 73736 | tf_op jit(solution)/shard_map/ppermute | solution.py:521
  77.4 11.4 %copy-start.14 = (f32[48,128]{1,0:T(8,128)}, f32[48,128]{1,0:T(8,128)S(1)}, u32[]{:S(2)}) copy-start(f32[48,128]{1,0:T(8,128)S(1)} %collective-permute-done.2.refs_2_) | copy-start | bytes 73732
  77.4 8.0 %collective-permute-start.7 = (f32[48,128]{1,0:T(8,128)S(1)}, f32[48,128]{1,0:T(8,128)S(1)}, u32[]{:S(2)}, u32[]{:S(2)}) collective-permute-start(f32[48,128]{1,0:T(8,128)S(1)} %collective-permute-done.5.refs_7_), channel_id=1, source_target_pairs={{0,7},{1,0},{2,1},{3,2},{4,3},{5,4},{6,5},{7,6},{8,15},{9,8},{10,9... | collective-permute-start | bytes 73736 | tf_op jit(solution)/shard_map/ppermute | solution.py:521
  79.6 7.6 %collective-permute-start.12 = (f32[54,128]{1,0:T(8,128)}, f32[54,128]{1,0:T(8,128)S(1)}, u32[]{:S(2)}, u32[]{:S(2)}) collective-permute-start(f32[54,128]{1,0:T(8,128)} %place.1.refs_13_.refs_22_), channel_id=1, source_target_pairs={{0,7},{1,0},{2,1},{3,2},{4,3},{5,4},{6,5},{7,6},{8,15},{9,8},{10,9... | collective-permute-start | bytes 82952 | tf_op jit(solution)/shard_map/ppermute | solution.py:521
  83.7 3.6 %collective-permute-start.10 = (f32[54,128]{1,0:T(8,128)S(1)}, f32[54,128]{1,0:T(8,128)S(1)}, u32[]{:S(2)}, u32[]{:S(2)}) collective-permute-start(f32[54,128]{1,0:T(8,128)S(1)} %collective-permute-done.8.refs_10_.refs_19_), channel_id=1, source_target_pairs={{0,7},{1,0},{2,1},{3,2},{4,3},{5,4},{6,5},{7,6},{8,15},{9,8},{10,9... | collective-permute-start | bytes 82952 | tf_op jit(solution)/shard_map/ppermute | solution.py:521
  83.7 3.6 %collective-permute-start.14 = (f32[54,128]{1,0:T(8,128)S(1)}, f32[54,128]{1,0:T(8,128)S(1)}, u32[]{:S(2)}, u32[]{:S(2)}) collective-permute-start(f32[54,128]{1,0:T(8,128)S(1)} %collective-permute-done.13.refs_16_.refs_25_), channel_id=1, source_target_pairs={{0,1},{1,2},{2,3},{3,4},{4,5},{5,6},{6,7},{7,0},{8,9},{9,10},{10,1... | collective-permute-start | bytes 82952 | tf_op jit(solution)/shard_map/ppermute | solution.py:521
  85.4 3.3 %collective-permute-start.15 = (f32[54,128]{1,0:T(8,128)S(1)}, f32[54,128]{1,0:T(8,128)S(1)}, u32[]{:S(2)}, u32[]{:S(2)}) collective-permute-start(f32[54,128]{1,0:T(8,128)S(1)} %collective-permute-done.13.refs_16_.refs_25_), channel_id=1, source_target_pairs={{0,7},{1,0},{2,1},{3,2},{4,3},{5,4},{6,5},{7,6},{8,15},{9,8},{10,9... | collective-permute-start | bytes 82952 | tf_op jit(solution)/shard_map/ppermute | solution.py:521
  85.5 3.3 %collective-permute-start.9 = (f32[54,128]{1,0:T(8,128)S(1)}, f32[54,128]{1,0:T(8,128)S(1)}, u32[]{:S(2)}, u32[]{:S(2)}) collective-permute-start(f32[54,128]{1,0:T(8,128)S(1)} %collective-permute-done.8.refs_10_.refs_19_), channel_id=1, source_target_pairs={{0,1},{1,2},{2,3},{3,4},{4,5},{5,6},{6,7},{7,0},{8,9},{9,10},{10,1... | collective-permute-start | bytes 82952 | tf_op jit(solution)/shard_map/ppermute | solution.py:521
  94.5 19.9 %all-to-all-start.2 = ((f32[128,1,128]{2,1,0:T(1,128)}), f32[128,1,128]{2,1,0:T(1,128)S(1)}, u32[]{:S(2)}, u32[]{:S(2)}) async-start(f32[128,1,128]{2,1,0:T(1,128)} %bitcast.30), calls=%async_computation.2 | async-start | bytes 131072 | tf_op jit(solution)/shard_map/all_to_all | solution.py:515
  100.0 7.5 %collective-permute-start.16 = (f32[48,128]{1,0:T(8,128)S(1)}, f32[48,128]{1,0:T(8,128)S(1)}, u32[]{:S(2)}, u32[]{:S(2)}) collective-permute-start(f32[48,128]{1,0:T(8,128)S(1)} %copy-done.19), channel_id=1, source_target_pairs={{0,8},{8,16},{16,24},{24,32},{32,40},{40,48},{48,56},{56,64},{64,7... | collective-permute-start | bytes 73736 | tf_op jit(solution)/shard_map/ppermute | solution.py:521
  101.5 8.2 %collective-permute-start.21 = (f32[48,128]{1,0:T(8,128)S(1)}, f32[48,128]{1,0:T(8,128)S(1)}, u32[]{:S(2)}, u32[]{:S(2)}) collective-permute-start(f32[48,128]{1,0:T(8,128)S(1)} %copy-done.19), channel_id=1, source_target_pairs={{0,120},{8,0},{16,8},{24,16},{32,24},{40,32},{48,40},{56,48},{64,5... | collective-permute-start | bytes 73736 | tf_op jit(solution)/shard_map/ppermute | solution.py:521
  105.7 5.4 %collective-permute-start.19 = (f32[48,128]{1,0:T(8,128)S(1)}, f32[48,128]{1,0:T(8,128)S(1)}, u32[]{:S(2)}, u32[]{:S(2)}) collective-permute-start(f32[48,128]{1,0:T(8,128)S(1)} %copy-done.19), channel_id=1, source_target_pairs={{0,1},{1,2},{2,3},{3,4},{4,5},{5,6},{6,7},{7,0},{8,9},{9,10},{10,1... | collective-permute-start | bytes 73736 | tf_op jit(solution)/shard_map/ppermute | solution.py:521
  107.5 5.1 %collective-permute-start.20 = (f32[48,128]{1,0:T(8,128)S(1)}, f32[48,128]{1,0:T(8,128)S(1)}, u32[]{:S(2)}, u32[]{:S(2)}) collective-permute-start(f32[48,128]{1,0:T(8,128)S(1)} %copy-done.19), channel_id=1, source_target_pairs={{0,7},{1,0},{2,1},{3,2},{4,3},{5,4},{6,5},{7,6},{8,15},{9,8},{10,9... | collective-permute-start | bytes 73736 | tf_op jit(solution)/shard_map/ppermute | solution.py:521
  107.5 5.1 %collective-permute-start.17 = (f32[48,128]{1,0:T(8,128)S(1)}, f32[48,128]{1,0:T(8,128)S(1)}, u32[]{:S(2)}, u32[]{:S(2)}) collective-permute-start(f32[48,128]{1,0:T(8,128)S(1)} %collective-permute-done.16.refs_10_), channel_id=1, source_target_pairs={{0,1},{1,2},{2,3},{3,4},{4,5},{5,6},{6,7},{7,0},{8,9},{9,10},{10,1... | collective-permute-start | bytes 73736 | tf_op jit(solution)/shard_map/ppermute | solution.py:521
  109.4 3.3 %collective-permute-start.18 = (f32[48,128]{1,0:T(8,128)S(1)}, f32[48,128]{1,0:T(8,128)S(1)}, u32[]{:S(2)}, u32[]{:S(2)}) collective-permute-start(f32[48,128]{1,0:T(8,128)S(1)} %collective-permute-done.16.refs_10_), channel_id=1, source_target_pairs={{0,7},{1,0},{2,1},{3,2},{4,3},{5,4},{6,5},{7,6},{8,15},{9,8},{10,9... | collective-permute-start | bytes 73736 | tf_op jit(solution)/shard_map/ppermute | solution.py:521
  109.7 3.6 %collective-permute-start.22 = (f32[48,128]{1,0:T(8,128)S(1)}, f32[48,128]{1,0:T(8,128)S(1)}, u32[]{:S(2)}, u32[]{:S(2)}) collective-permute-start(f32[48,128]{1,0:T(8,128)S(1)} %collective-permute-done.21.refs_16_), channel_id=1, source_target_pairs={{0,1},{1,2},{2,3},{3,4},{4,5},{5,6},{6,7},{7,0},{8,9},{9,10},{10,1... | collective-permute-start | bytes 73736 | tf_op jit(solution)/shard_map/ppermute | solution.py:521
  111.2 3.3 %collective-permute-start.23 = (f32[48,128]{1,0:T(8,128)S(1)}, f32[48,128]{1,0:T(8,128)S(1)}, u32[]{:S(2)}, u32[]{:S(2)}) collective-permute-start(f32[48,128]{1,0:T(8,128)S(1)} %collective-permute-done.21.refs_16_), channel_id=1, source_target_pairs={{0,7},{1,0},{2,1},{3,2},{4,3},{5,4},{6,5},{7,6},{8,15},{9,8},{10,9... | collective-permute-start | bytes 73736 | tf_op jit(solution)/shard_map/ppermute | solution.py:521
  (22 other events, 65.5 us)

commit v2 on v1

--- a/solution.py
+++ b/solution.py
@@ -17,7 +17,7 @@
 def lookup_kernel(asked_ref, table_ref, found_ref, split_ref, turned_ref, result_ref):
     for block in range(5):
         lanes = slice(block * 128, block * 128 + 128)
-        turned_ref[lanes, :] = asked_ref[:, lanes].T
+        turned_ref[lanes, :] = asked_ref[:, 0, lanes].T
     for pair in range(TABLE // (2 * COLS)):
         start = pair * 2 * COLS
         rows = jnp.concatenate(
@@ -64,14 +64,14 @@
 
     lax.fori_loop(0, 16, step, 0)
     group([512, 520, 528, 536], None, 128)
-    found_ref[:, :128] = result_ref[:128, :].T
-    found_ref[:, 128:] = result_ref[128:, :].T
+    found_ref[:, 0, :128] = result_ref[:128, :].T
+    found_ref[:, 0, 128:] = result_ref[128:, :].T
 
 
 def lookup(asked, table):
     return pl.pallas_call(
         lookup_kernel,
-        out_shape=jax.ShapeDtypeStruct((SRC, SLOTS), jnp.float32),
+        out_shape=jax.ShapeDtypeStruct((SRC, 1, SLOTS), jnp.float32),
         scratch_shapes=[
             pltpu.VMEM((8 * TABLE // COLS, 2 * COLS), jnp.bfloat16),
             pltpu.VMEM((640, 128), jnp.float32),
@@ -82,9 +82,9 @@
 
 
 def place_kernel(found_ref, point_ref, size_ref, value_ref, row_ref, lane_ref):
-    value_ref[:128, :] = found_ref[:, :128].T
-    value_ref[128:, :] = found_ref[:, 128:].T
-    point = jnp.concatenate([point_ref[:, :128].T, point_ref[:, 128:].T], axis=0)
+    value_ref[:128, :] = found_ref[:, 0, :128].T
+    value_ref[128:, :] = found_ref[:, 0, 128:].T
+    point = point_ref[...]
     line = (point * 10923) >> 21
     qx = point - line * 192
     qz = (line * 43) >> 8
@@ -135,7 +135,29 @@
 
 HALF_GAP = float(np.sqrt(0.15))
 OUTER, MIDDLE = 5.0 / 18.0, 8.0 / 18.0
-NEIGHBOURS = [(z, y) for z in (-1, 0, 1) for y in (-1, 0, 1)]
+
+
+def field_pieces(refs):
+    own, y_low, y_high, z_low, z_high, corner_low, corner_high = refs
+    return {
+        (0, -1): (y_low, 0),
+        (0, 0): (own, 0),
+        (0, 1): (y_high, 0),
+        (-1, 0): (z_low, 0),
+        (1, 0): (z_high, 0),
+        (-1, -1): (corner_low, 0),
+        (1, -1): (corner_low, 48),
+        (-1, 1): (corner_high, 0),
+        (1, 1): (corner_high, 48),
+    }
+
+
+def size_pieces(refs):
+    own, y_low, y_high, side, corner_low, corner_high = refs
+    pieces = {(0, -1): (y_low, 0), (0, 0): (own, 0), (0, 1): (y_high, 0)}
+    for z in (-1, 1):
+        pieces.update({(z, -1): (corner_low, 0), (z, 0): (side, 0), (z, 1): (corner_high, 0)})
+    return pieces
 
 
 def lane_index():
@@ -305,35 +327,36 @@
     places = ((-1, 1), (0, 0), (0, 1), (1, 0)) if not y_shift else ((0, 0), (0, 1), (1, 0), (1, 1))
     for upper in range(2):
         for y, (piece_y, row) in enumerate(places):
-            rows = pl.ds(row, count, stride=2)
-            here = pieces[0, piece_y]
-            above = pieces[1, piece_y]
+            here, below, above = (
+                ref[pl.ds(at + row, count, stride=2), :] for ref, at in (pieces[z, piece_y] for z in (0, -1, 1))
+            )
             if z_shift:
-                here = pltpu.roll(here[rows, :], 64, 1)
-                above = pltpu.roll(above[rows, :], 64, 1)
+                here = pltpu.roll(here, 64, 1)
+                above = pltpu.roll(above, 64, 1)
                 value = jnp.where(low, above, here) if upper else jnp.where(low, here, above)
             elif upper:
-                value = jnp.where(low, above[rows, :], pieces[-1, piece_y][rows, :])
+                value = jnp.where(low, above, below)
             else:
-                value = here[rows, :]
+                value = here
             out_ref[pl.ds(out_at + upper * 4 + y, count, stride=8), :] = value
 
 
 def pass_kernel(first, *refs):
     refs = list(refs)
-    field = {at: refs.pop(0) for at in NEIGHBOURS}
+    field_refs = [refs.pop(0) for _ in range(7)]
     if not first:
-        shift = {at: refs.pop(0) for at in NEIGHBOURS}
-    sizes = {at: refs.pop(0) for at in NEIGHBOURS}
+        shift_refs = [refs.pop(0) for _ in range(7)]
+    sizes = size_pieces([refs.pop(0) for _ in range(6)])
     if first:
         move_ref, terms_out, nodes_ref, size_ref, jac_ref, part_ref, turn_ref = refs
+        field = field_pieces(field_refs)
     else:
         terms_in, move_ref, terms_out, own_ref, nodes_ref, size_ref, jac_ref, part_ref, turn_ref, sum_ref = refs
         step = newton_step(add_up(terms_in))
-        for i, at in enumerate(NEIGHBOURS):
-            sum_ref[i] = field[at][...] + step * shift[at][...]
-        field = {at: sum_ref.at[i] for i, at in enumerate(NEIGHBOURS)}
-        own_ref[...] = field[0, 0][...]
+        for i, (field_ref, shift_ref) in enumerate(zip(field_refs, shift_refs)):
+            sum_ref[i, : field_ref.shape[0], :] = field_ref[...] + step * shift_ref[...]
+        field = field_pieces([sum_ref.at[i] for i in range(7)])
+        own_ref[...] = sum_ref[0, :48, :]
     for z_shift in range(2):
         for y_shift in range(2):
             ring(field, 24, nodes_ref, (z_shift * 2 + y_shift) * 192, z_shift, y_shift)
@@ -421,7 +444,7 @@
         pltpu.VMEM((243 * 8, 128), jnp.float32),
         pltpu.VMEM((243 * 8, 128), jnp.float32),
         pltpu.VMEM((24 * 8, 128), jnp.float32),
-    ] + ([] if first else [pltpu.VMEM((9, 48, 128), jnp.float32)])
+    ] + ([] if first else [pltpu.VMEM((7, 96, 128), jnp.float32)])
     args = list(field) + ([] if first else list(shift)) + list(sizes) + ([] if first else [terms])
     return pl.pallas_call(
         functools.partial(pass_kernel, first),
@@ -495,19 +518,16 @@
 
 
 def pack_kernel(elem_ref, coord_ref, out_ref):
-    elem = elem_ref[...].astype(jnp.float32)
-    out_ref[:, :128] = elem[:, :128]
-    tails = [elem[:, 128:]]
-    for j in range(3):
-        coord = coord_ref[:, j, :]
-        out_ref[:, 128 + j * 128 : 256 + j * 128] = coord[:, :128]
-        tails.append(coord[:, 128:])
-    out_ref[:, 512:] = jnp.concatenate(tails + [jnp.zeros((SRC, 96), jnp.float32)], axis=1)
+    parts = [elem_ref[...].astype(jnp.float32)] + [coord_ref[j] for j in range(3)]
+    for j, part in enumerate(parts):
+        out_ref[:, 0, j * 128 : j * 128 + 128] = part[:128].T
+    tails = jnp.concatenate([part[128:] for part in parts] + [jnp.zeros((96, 128), jnp.float32)], axis=0)
+    out_ref[:, 0, 512:] = tails.T
 
 
 def pack(elem, coord):
     return pl.pallas_call(
-        pack_kernel, out_shape=jax.ShapeDtypeStruct((SRC, 640), jnp.float32), name="pack"
+        pack_kernel, out_shape=jax.ShapeDtypeStruct((SRC, 1, 640), jnp.float32), name="pack"
     )(elem, coord)
 
 
@@ -515,29 +535,30 @@
     return lax.all_to_all(values, ("mesh", "bg"), split_axis=0, concat_axis=0, tiled=True)
 
 
-def around(block):
-    def moved(values, axis, by):
-        count = lax.axis_size(axis)
-        return lax.ppermute(values, axis, [(i, (i - by) % count) for i in range(count)])
-
-    pieces = {(0, 0): block}
-    for z in (-1, 1):
-        pieces[z, 0] = moved(block, "mesh", z)
-    for z in (0, -1, 1):
-        for y in (-1, 1):
-            pieces[z, y] = moved(pieces[z, 0], "bg", y)
-    return [pieces[at] for at in NEIGHBOURS]
+def moved(values, axis, by):
+    count = lax.axis_size(axis)
+    return lax.ppermute(values, axis, [(i, (i - by) % count) for i in range(count)])
+
+
+def around(block, merge):
+    z_low, z_high = moved(block, "mesh", -1), moved(block, "mesh", 1)
+    y_low, y_high = moved(block, "bg", -1), moved(block, "bg", 1)
+    if merge:
+        side = jnp.where(lax.broadcasted_iota(jnp.int32, block.shape, 1) < 64, z_high, z_low)
+        return [block, y_low, y_high, side, moved(side, "bg", -1), moved(side, "bg", 1)]
+    sides = jnp.concatenate([z_low, z_high], axis=0)
+    return [block, y_low, y_high, z_low, z_high, moved(sides, "bg", -1), moved(sides, "bg", 1)]
 
 
 def shards(displacement, bg_coef, query_elem, query_point, query_coord):
-    own = split_nodes(displacement)
-    asked = exchange(pack(query_elem.reshape(SRC, SLOTS), query_coord.reshape(SRC, 3, SLOTS)))
-    field = around(own)
+    asked = exchange(pack(query_elem[0].T, query_coord[0].transpose(1, 2, 0)))
+    field = around(split_nodes(displacement), False)
+    asked, field = lax.optimization_barrier((asked, field))
     found = exchange(lookup(asked, bg_coef))
-    sizes = around(place(found, query_point.reshape(SRC, SLOTS)))
+    sizes = around(place(found, query_point[0].T), True)
     move, terms = newton_pass(field, None, sizes, None)
     first_terms = exchange(terms)
-    last_move, last_terms, last_own = newton_pass(field, around(move), sizes, first_terms)
+    last_move, last_terms, last_own = newton_pass(field, around(move, False), sizes, first_terms)
     return finish(last_own, last_move, first_terms, exchange(last_terms))
 
 

time: 143 us -> 140 us (0.979)
  waiting for transfers between devices: 4.19 us -> 19.1 us
  starting transfers between devices: 47.9 us -> 39.8 us
  local copies, waits for them, and re-layouts: 9.61 us -> 3.82 us
  blocking collectives: 40.8 us -> 36.9 us
    ppermute x24 -> x18, starting transfers between devices: 37.9 us -> 23.2 us  [moved(): lax.ppermute(values, axis, [(i, (i - by) % count) for i in range(count)])]
    ppermute x24 -> x18, waiting for transfers between devices: 4.18 us -> 17 us  [moved(): lax.ppermute(values, axis, [(i, (i - by) % count) for i in range(count)])]
    all_to_all x2, starting transfers between devices: 9.98 us -> 16.6 us  [exchange(): lax.all_to_all(values, ('mesh', 'bg'), split_axis=0, concat_axis=0, tiled...]
    all_to_all x2, blocking collectives: 40.8 us -> 36.9 us  [exchange(): lax.all_to_all(values, ('mesh', 'bg'), split_axis=0, concat_axis=0, tiled...]
    all_to_all x3 -> x0, local copies, waits for them, and re-layouts: 3.66 us -> none  [exchange(): lax.all_to_all(values, ('mesh', 'bg'), split_axis=0, concat_axis=0, tiled...]
    unnamed x60 -> x44, local copies, waits for them, and re-layouts: 5.95 us -> 3.81 us
    all_to_all x2, waiting for transfers between devices: 0.01 us -> 2.12 us  [exchange(): lax.all_to_all(values, ('mesh', 'bg'), split_axis=0, concat_axis=0, tiled...]
  transfers between devices with their start and end apart: 26 -> 20, of which waited for: 5 -> 9; matrix products, arithmetic and copies ran while one was open for 1% -> 0% of each run, Pallas kernels for 6% -> 1%
where the time goes in v2:
time: 140 us; the launch traced here: 139 us
  starting transfers between devices  39.8 us (28%)
  Pallas kernels  38.5 us (28%)
  blocking collectives  36.9 us (26%)
  waiting for transfers between devices  19.1 us (14%)
  local copies, waits for them, and re-layouts  3.82 us (3%)
    all_to_all x2, blocking collectives, exchange(): lax.all_to_all(values, ('mesh', 'bg'), split_axis=0, concat_axis=0, tiled...  36.9 us
    ppermute x18, starting transfers between devices, moved(): lax.ppermute(values, axis, [(i, (i - by) % count) for i in range(count)])  23.2 us
    ppermute x18, waiting for transfers between devices, moved(): lax.ppermute(values, axis, [(i, (i - by) % count) for i in range(count)])  17 us
    all_to_all x2, starting transfers between devices, exchange(): lax.all_to_all(values, ('mesh', 'bg'), split_axis=0, concat_axis=0, tiled...  16.6 us
    pallas_call x1, Pallas kernels, lookup(): pl.pallas_call(lookup_kernel, out_shape=jax.ShapeDtypeStruct((SRC, 1, SLO...  15.2 us
    pallas_call x2, Pallas kernels, newton_pass(): pl.pallas_call(functools.partial(pass_kernel, first), out_shape=outs, scr...  10.5 us
    pallas_call x1, Pallas kernels, place(): pl.pallas_call(place_kernel, out_shape=jax.ShapeDtypeStruct((54, 128), jn...  6.25 us
    unnamed x44, local copies, waits for them, and re-layouts  3.81 us
  transfers between devices with their start and end apart: 20, of which 9 were waited for; matrix products, arithmetic and copies ran while one was open for 0% of the time, Pallas kernels for 1%

profile of v2, /device:TPU:1, one launch (start us, length us, event | category | flops | bytes accessed | tf_op | source)
XLA Modules:
  0.0 139.0 jit_solution(13006599858583220618)
XLA Ops:
  0.6 1.9 %pack.1 = f32[128,1,640]{2,1,0:T(1,128)} custom-call(s32[136,128]{1,0:T(8,128)} %bitcast.21, f32[3,136,128]{2,1,0:T(8,128)} %bitcast.20), custom_call_target="tpu_custom_call" | custom-call | tf_op jit(solution)/shard_map/pack/pallas_call | solution.py:529
  2.6 11.5 %all-to-all-start = ((f32[128,1,640]{2,1,0:T(1,128)}), f32[128,1,640]{2,1,0:T(1,128)S(1)}, u32[]{:S(2)}, u32[]{:S(2)}) async-start(f32[128,1,640]{2,1,0:T(1,128)} %pack.1), calls=%async_computation | async-start | bytes 655360 | tf_op jit(solution)/shard_map/all_to_all | solution.py:535
  14.1 1.6 %split_nodes.1.refs_0_ = f32[48,128]{1,0:T(8,128)} custom-call(f32[3,4,4,128]{3,2,1,0:T(4,128)} %nodes_ref.1), custom_call_target="tpu_custom_call" | custom-call | tf_op jit(solution)/shard_map/split_nodes/pallas_call | solution.py:482
  15.7 1.4 collective-permute-start.2
  17.1 4.0 %collective-permute-start.3 = (f32[48,128]{1,0:T(8,128)}, f32[48,128]{1,0:T(8,128)S(1)}, u32[]{:S(2)}, u32[]{:S(2)}) collective-permute-start(f32[48,128]{1,0:T(8,128)} %split_nodes.1.refs_0_), channel_id=1, source_target_pairs={{0,120},{8,0},{16,8},{24,16},{32,24},{40,32},{48,40},{56,48},{64,5... | collective-permute-start | bytes 73736 | tf_op jit(solution)/shard_map/ppermute | solution.py:540
  21.1 2.6 %collective-permute-done.2.refs_3_ = f32[48,128]{1,0:T(8,128)S(1)} collective-permute-done((f32[48,128]{1,0:T(8,128)}, f32[48,128]{1,0:T(8,128)S(1)}, u32[]{:S(2)}, u32[]{:S(2)}) %collective-permute-start.2) | collective-permute-done | bytes 24608 | tf_op jit(solution)/shard_map/ppermute | solution.py:540
  24.9 2.1 %collective-permute-start.4 = (f32[96,128]{1,0:T(8,128)S(1)}, f32[96,128]{1,0:T(8,128)S(1)}, u32[]{:S(2)}, u32[]{:S(2)}) collective-permute-start(f32[96,128]{1,0:T(8,128)S(1)} %constant_dynamic-update-slice_fusion), channel_id=1, source_target_pairs={{0,1},{1,2},{2,3},{3,4},{4,5},{5,6},{6,7},{7,0},{8,9},{9,10},{10,1... | collective-permute-start | bytes 147464 | tf_op jit(solution)/shard_map/ppermute | solution.py:540
  27.0 1.7 %collective-permute-start = (f32[48,128]{1,0:T(8,128)S(1)}, f32[48,128]{1,0:T(8,128)S(1)}, u32[]{:S(2)}, u32[]{:S(2)}) collective-permute-start(f32[48,128]{1,0:T(8,128)S(1)} %copy-done.3), channel_id=1, source_target_pairs={{0,1},{1,2},{2,3},{3,4},{4,5},{5,6},{6,7},{7,0},{8,9},{9,10},{10,1... | collective-permute-start | bytes 73736 | tf_op jit(solution)/shard_map/ppermute | solution.py:540
  28.8 0.9 collective-permute-done.refs_1_
  29.6 2.6 %collective-permute-done.1.refs_2_ = f32[48,128]{1,0:T(8,128)S(1)} collective-permute-done((f32[48,128]{1,0:T(8,128)S(1)}, f32[48,128]{1,0:T(8,128)S(1)}, u32[]{:S(2)}, u32[]{:S(2)}) %collective-permute-start.1) | collective-permute-done | bytes 24608 | tf_op jit(solution)/shard_map/ppermute | solution.py:540
  32.3 0.7 copy-done
  33.0 15.2 %lookup.1 = f32[128,1,136]{2,1,0:T(1,128)} custom-call(f32[128,1,640]{2,1,0:T(1,128)} %copy-done, f32[8,16384]{1,0:T(8,128)} %table_ref.1), custom_call_target="tpu_custom_call" | custom-call | tf_op jit(solution)/shard_map/lookup/pallas_call | solution.py:72
  48.2 18.8 %all_to_all.32.found_ref = f32[128,1,136]{2,1,0:T(1,128)} all-to-all(f32[128,1,136]{2,1,0:T(1,128)} %lookup.1), channel_id=1, replica_groups=mesh['mesh'=16,'bg'=8] {'mesh','bg'}, dimensions={0} | all-to-all | bytes 139264 | tf_op jit(solution)/shard_map/all_to_all | solution.py:535
  67.1 6.3 %place.1.refs_7_.refs_14_ = f32[54,128]{1,0:T(8,128)} custom-call(f32[128,1,136]{2,1,0:T(1,128)} %all_to_all.32.found_ref, s32[136,128]{1,0:T(8,128)} %bitcast.22), custom_call_target="tpu_custom_call" | custom-call | tf_op jit(solution)/shard_map/place/pallas_call | solution.py:124
  73.3 1.2 collective-permute-start.8
  74.8 1.4 %collective-permute-start.6 = (f32[54,128]{1,0:T(8,128)}, f32[54,128]{1,0:T(8,128)S(1)}, u32[]{:S(2)}, u32[]{:S(2)}) collective-permute-start(f32[54,128]{1,0:T(8,128)} %place.1.refs_7_.refs_14_), channel_id=1, source_target_pairs={{0,1},{1,2},{2,3},{3,4},{4,5},{5,6},{6,7},{7,0},{8,9},{9,10},{10,1... | collective-permute-start | bytes 82952 | tf_op jit(solution)/shard_map/ppermute | solution.py:540
  76.2 4.6 %collective-permute-done.9 = f32[54,128]{1,0:T(8,128)S(1)} collective-permute-done((f32[54,128]{1,0:T(8,128)}, f32[54,128]{1,0:T(8,128)S(1)}, u32[]{:S(2)}, u32[]{:S(2)}) %collective-permute-start.9) | collective-permute-done | bytes 27680 | tf_op jit(solution)/shard_map/ppermute | solution.py:540
  80.8 2.1 %collective-permute-start.10 = (f32[54,128]{1,0:T(8,128)S(1)}, f32[54,128]{1,0:T(8,128)S(1)}, u32[]{:S(2)}, u32[]{:S(2)}) collective-permute-start(f32[54,128]{1,0:T(8,128)S(1)} %broadcast_select_fusion.refs_10_.refs_17_), channel_id=1, source_target_pairs={{0,1},{1,2},{2,3},{3,4},{4,5},{5,6},{6,7},{7,0},{8,9},{9,10},{10,1... | collective-permute-start | bytes 82952 | tf_op jit(solution)/shard_map/ppermute | solution.py:540
  82.9 1.0 collective-permute-done.10.refs_11_.refs_18_
  83.9 2.6 %collective-permute-done.11.refs_12_.refs_19_ = f32[54,128]{1,0:T(8,128)S(1)} collective-permute-done((f32[54,128]{1,0:T(8,128)S(1)}, f32[54,128]{1,0:T(8,128)S(1)}, u32[]{:S(2)}, u32[]{:S(2)}) %collective-permute-start.11) | collective-permute-done | bytes 27680 | tf_op jit(solution)/shard_map/ppermute | solution.py:540
  87.1 4.5 %pass_one.1 = (f32[48,128]{1,0:T(8,128)}, f32[128,128]{1,0:T(8,128)}) custom-call(f32[48,128]{1,0:T(8,128)} %split_nodes.1.refs_0_, f32[48,128]{1,0:T(8,128)} %copy-done.12, f32[48,128]{1,0:T(8,128)} %copy-done.13, f32[48,128]{1,0:T(8,128)} %copy-done.4, f32[48,128]{1,0:T(8,128)} %copy-done.5, f32[96,128]{1,0:T(8,128)} %copy-done.6, f32[96,128]{1,0:T(8,128)} %copy-done.7, ...), custom_call_target="tpu_custom_call" | custom-call | tf_op jit(solution)/shard_map/pass_one/pallas_call | solution.py:449
  91.6 4.8 %collective-permute-start.15 = (f32[48,128]{1,0:T(8,128)}, f32[48,128]{1,0:T(8,128)S(1)}, u32[]{:S(2)}, u32[]{:S(2)}) collective-permute-start(f32[48,128]{1,0:T(8,128)} %get-tuple-element.23.refs_7_), channel_id=1, source_target_pairs={{0,120},{8,0},{16,8},{24,16},{32,24},{40,32},{48,40},{56,48},{64,5... | collective-permute-start | bytes 73736 | tf_op jit(solution)/shard_map/ppermute | solution.py:540
  96.4 5.1 %all-to-all-start.2 = ((f32[128,1,128]{2,1,0:T(1,128)}), f32[128,1,128]{2,1,0:T(1,128)S(1)}, u32[]{:S(2)}, u32[]{:S(2)}) async-start(f32[128,1,128]{2,1,0:T(1,128)} %bitcast.23), calls=%async_computation.2 | async-start | bytes 131072 | tf_op jit(solution)/shard_map/all_to_all | solution.py:535
  102.2 1.7 %collective-permute-start.16 = (f32[96,128]{1,0:T(8,128)S(1)}, f32[96,128]{1,0:T(8,128)S(1)}, u32[]{:S(2)}, u32[]{:S(2)}) collective-permute-start(f32[96,128]{1,0:T(8,128)S(1)} %constant_dynamic-update-slice_fusion.2), channel_id=1, source_target_pairs={{0,1},{1,2},{2,3},{3,4},{4,5},{5,6},{6,7},{7,0},{8,9},{9,10},{10,1... | collective-permute-start | bytes 147464 | tf_op jit(solution)/shard_map/ppermute | solution.py:540
  103.9 1.7 %collective-permute-start.12 = (f32[48,128]{1,0:T(8,128)S(1)}, f32[48,128]{1,0:T(8,128)S(1)}, u32[]{:S(2)}, u32[]{:S(2)}) collective-permute-start(f32[48,128]{1,0:T(8,128)S(1)} %copy-done.18), channel_id=1, source_target_pairs={{0,1},{1,2},{2,3},{3,4},{4,5},{5,6},{6,7},{7,0},{8,9},{9,10},{10,1... | collective-permute-start | bytes 73736 | tf_op jit(solution)/shard_map/ppermute | solution.py:540
  105.7 0.7 collective-permute-start.13
  106.4 0.7 collective-permute-done.12.refs_8_
  107.1 2.1 %collective-permute-done.13.refs_9_ = f32[48,128]{1,0:T(8,128)S(1)} collective-permute-done((f32[48,128]{1,0:T(8,128)S(1)}, f32[48,128]{1,0:T(8,128)S(1)}, u32[]{:S(2)}, u32[]{:S(2)}) %collective-permute-start.13) | collective-permute-done | bytes 24608 | tf_op jit(solution)/shard_map/ppermute | solution.py:540
  109.2 2.1 %all-to-all-done.2 = f32[128,1,128]{2,1,0:T(1,128)S(1)} async-done(((f32[128,1,128]{2,1,0:T(1,128)}), f32[128,1,128]{2,1,0:T(1,128)S(1)}, u32[]{:S(2)}, u32[]{:S(2)}) %all-to-all-start.2) | async-done | bytes 65568 | tf_op jit(solution)/shard_map/all_to_all | solution.py:535
  112.0 6.0 %pass_two.1 = (f32[48,128]{1,0:T(8,128)}, f32[128,128]{1,0:T(8,128)}, f32[48,128]{1,0:T(8,128)}) custom-call(f32[48,128]{1,0:T(8,128)} %split_nodes.1.refs_0_, f32[48,128]{1,0:T(8,128)} %copy-done.12, f32[48,128]{1,0:T(8,128)} %copy-done.13, f32[48,128]{1,0:T(8,128)} %copy-done.4, f32[48,128]{1,0:T(8,128)} %copy-done.5, f32[96,128]{1,0:T(8,128)} %copy-done.6, ...), custom_call_target="tpu_custom_call" | custom-call | tf_op jit(solution)/shard_map/pass_two/pallas_call | solution.py:449
  118.0 18.1 %all_to_all.33 = f32[128,1,128]{2,1,0:T(1,128)} all-to-all(f32[128,1,128]{2,1,0:T(1,128)} %bitcast.24), channel_id=1, replica_groups=mesh['mesh'=16,'bg'=8] {'mesh','bg'}, dimensions={0} | all-to-all | bytes 131072 | tf_op jit(solution)/shard_map/all_to_all | solution.py:535
  136.0 3.0 %finish.1 = (f32[3,4,4,128]{3,2,1,0:T(4,128)}, f32[2,5]{1,0:T(2,128)}) custom-call(f32[48,128]{1,0:T(8,128)} %get-tuple-element.25.own_ref, f32[48,128]{1,0:T(8,128)} %get-tuple-element.26.move_ref, f32[128,128]{1,0:T(8,128)} %bitcast.18, f32[128,128]{1,0:T(8,128)} %bitcast.19), custom_call_target="tpu_custom_call" | custom-call | tf_op jit(solution)/shard_map/finish/pallas_call | solution.py:512
  (65 shorter events, 3.4 us)
Async XLA Ops:
  2.6 29.7 %all-to-all-start = ((f32[128,1,640]{2,1,0:T(1,128)}), f32[128,1,640]{2,1,0:T(1,128)S(1)}, u32[]{:S(2)}, u32[]{:S(2)}) async-start(f32[128,1,640]{2,1,0:T(1,128)} %pack.1), calls=%async_computation | async-start | bytes 655360 | tf_op jit(solution)/shard_map/all_to_all | solution.py:535
  15.7 7.9 %collective-permute-start.2 = (f32[48,128]{1,0:T(8,128)}, f32[48,128]{1,0:T(8,128)S(1)}, u32[]{:S(2)}, u32[]{:S(2)}) collective-permute-start(f32[48,128]{1,0:T(8,128)} %split_nodes.1.refs_0_), channel_id=1, source_target_pairs={{0,8},{8,16},{16,24},{24,32},{32,40},{40,48},{48,56},{56,64},{64,7... | collective-permute-start | bytes 73736 | tf_op jit(solution)/shard_map/ppermute | solution.py:540
  17.1 7.2 %collective-permute-start.3 = (f32[48,128]{1,0:T(8,128)}, f32[48,128]{1,0:T(8,128)S(1)}, u32[]{:S(2)}, u32[]{:S(2)}) collective-permute-start(f32[48,128]{1,0:T(8,128)} %split_nodes.1.refs_0_), channel_id=1, source_target_pairs={{0,120},{8,0},{16,8},{24,16},{32,24},{40,32},{48,40},{56,48},{64,5... | collective-permute-start | bytes 73736 | tf_op jit(solution)/shard_map/ppermute | solution.py:540
  24.3 2.7 %copy-start.3 = (f32[48,128]{1,0:T(8,128)S(1)}, f32[48,128]{1,0:T(8,128)}, u32[]{:S(2)}) copy-start(f32[48,128]{1,0:T(8,128)} %split_nodes.1.refs_0_) | copy-start | bytes 73732
  24.9 7.4 %collective-permute-start.4 = (f32[96,128]{1,0:T(8,128)S(1)}, f32[96,128]{1,0:T(8,128)S(1)}, u32[]{:S(2)}, u32[]{:S(2)}) collective-permute-start(f32[96,128]{1,0:T(8,128)S(1)} %constant_dynamic-update-slice_fusion), channel_id=1, source_target_pairs={{0,1},{1,2},{2,3},{3,4},{4,5},{5,6},{6,7},{7,0},{8,9},{9,10},{10,1... | collective-permute-start | bytes 147464 | tf_op jit(solution)/shard_map/ppermute | solution.py:540
  26.9 5.3 %collective-permute-start.5 = (f32[96,128]{1,0:T(8,128)S(1)}, f32[96,128]{1,0:T(8,128)S(1)}, u32[]{:S(2)}, u32[]{:S(2)}) collective-permute-start(f32[96,128]{1,0:T(8,128)S(1)} %constant_dynamic-update-slice_fusion), channel_id=1, source_target_pairs={{0,7},{1,0},{2,1},{3,2},{4,3},{5,4},{6,5},{7,6},{8,15},{9,8},{10,9... | collective-permute-start | bytes 147464 | tf_op jit(solution)/shard_map/ppermute | solution.py:540
  27.0 2.7 %collective-permute-start = (f32[48,128]{1,0:T(8,128)S(1)}, f32[48,128]{1,0:T(8,128)S(1)}, u32[]{:S(2)}, u32[]{:S(2)}) collective-permute-start(f32[48,128]{1,0:T(8,128)S(1)} %copy-done.3), channel_id=1, source_target_pairs={{0,1},{1,2},{2,3},{3,4},{4,5},{5,6},{6,7},{7,0},{8,9},{9,10},{10,1... | collective-permute-start | bytes 73736 | tf_op jit(solution)/shard_map/ppermute | solution.py:540
  28.7 3.5 %collective-permute-start.1 = (f32[48,128]{1,0:T(8,128)S(1)}, f32[48,128]{1,0:T(8,128)S(1)}, u32[]{:S(2)}, u32[]{:S(2)}) collective-permute-start(f32[48,128]{1,0:T(8,128)S(1)} %copy-done.3), channel_id=1, source_target_pairs={{0,7},{1,0},{2,1},{3,2},{4,3},{5,4},{6,5},{7,6},{8,15},{9,8},{10,9... | collective-permute-start | bytes 73736 | tf_op jit(solution)/shard_map/ppermute | solution.py:540
  29.6 18.6 %copy-start.12 = (f32[48,128]{1,0:T(8,128)}, f32[48,128]{1,0:T(8,128)S(1)}, u32[]{:S(2)}) copy-start(f32[48,128]{1,0:T(8,128)S(1)} %collective-permute-done.refs_1_) | copy-start | bytes 73732
  32.2 16.0 %copy-start.13 = (f32[48,128]{1,0:T(8,128)}, f32[48,128]{1,0:T(8,128)S(1)}, u32[]{:S(2)}) copy-start(f32[48,128]{1,0:T(8,128)S(1)} %collective-permute-done.1.refs_2_) | copy-start | bytes 73732
  32.3 16.0 %copy-start.6 = (f32[96,128]{1,0:T(8,128)}, f32[96,128]{1,0:T(8,128)S(1)}, u32[]{:S(2)}) copy-start(f32[96,128]{1,0:T(8,128)S(1)} %collective-permute-done.4.refs_5_) | copy-start | bytes 147460
  32.3 16.0 %copy-start.7 = (f32[96,128]{1,0:T(8,128)}, f32[96,128]{1,0:T(8,128)S(1)}, u32[]{:S(2)}) copy-start(f32[96,128]{1,0:T(8,128)S(1)} %collective-permute-done.5.refs_6_) | copy-start | bytes 147460
  73.3 2.9 %collective-permute-start.8 = (f32[54,128]{1,0:T(8,128)}, f32[54,128]{1,0:T(8,128)S(1)}, u32[]{:S(2)}, u32[]{:S(2)}) collective-permute-start(f32[54,128]{1,0:T(8,128)} %place.1.refs_7_.refs_14_), channel_id=1, source_target_pairs={{0,120},{8,0},{16,8},{24,16},{32,24},{40,32},{48,40},{56,48},{64,5... | collective-permute-start | bytes 82952 | tf_op jit(solution)/shard_map/ppermute | solution.py:540
  74.5 6.3 %collective-permute-start.9 = (f32[54,128]{1,0:T(8,128)}, f32[54,128]{1,0:T(8,128)S(1)}, u32[]{:S(2)}, u32[]{:S(2)}) collective-permute-start(f32[54,128]{1,0:T(8,128)} %place.1.refs_7_.refs_14_), channel_id=1, source_target_pairs={{0,8},{8,16},{16,24},{24,32},{32,40},{40,48},{48,56},{56,64},{64,7... | collective-permute-start | bytes 82952 | tf_op jit(solution)/shard_map/ppermute | solution.py:540
  74.8 8.1 %collective-permute-start.6 = (f32[54,128]{1,0:T(8,128)}, f32[54,128]{1,0:T(8,128)S(1)}, u32[]{:S(2)}, u32[]{:S(2)}) collective-permute-start(f32[54,128]{1,0:T(8,128)} %place.1.refs_7_.refs_14_), channel_id=1, source_target_pairs={{0,1},{1,2},{2,3},{3,4},{4,5},{5,6},{6,7},{7,0},{8,9},{9,10},{10,1... | collective-permute-start | bytes 82952 | tf_op jit(solution)/shard_map/ppermute | solution.py:540
  76.2 6.7 %collective-permute-start.7 = (f32[54,128]{1,0:T(8,128)}, f32[54,128]{1,0:T(8,128)S(1)}, u32[]{:S(2)}, u32[]{:S(2)}) collective-permute-start(f32[54,128]{1,0:T(8,128)} %place.1.refs_7_.refs_14_), channel_id=1, source_target_pairs={{0,7},{1,0},{2,1},{3,2},{4,3},{5,4},{6,5},{7,6},{8,15},{9,8},{10,9... | collective-permute-start | bytes 82952 | tf_op jit(solution)/shard_map/ppermute | solution.py:540
  80.8 5.7 %copy-start.2 = (f32[54,128]{1,0:T(8,128)}, f32[54,128]{1,0:T(8,128)S(1)}, u32[]{:S(2)}) copy-start(f32[54,128]{1,0:T(8,128)S(1)} %broadcast_select_fusion.refs_10_.refs_17_) | copy-start | bytes 82948
  80.8 3.1 %collective-permute-start.10 = (f32[54,128]{1,0:T(8,128)S(1)}, f32[54,128]{1,0:T(8,128)S(1)}, u32[]{:S(2)}, u32[]{:S(2)}) collective-permute-start(f32[54,128]{1,0:T(8,128)S(1)} %broadcast_select_fusion.refs_10_.refs_17_), channel_id=1, source_target_pairs={{0,1},{1,2},{2,3},{3,4},{4,5},{5,6},{6,7},{7,0},{8,9},{9,10},{10,1... | collective-permute-start | bytes 82952 | tf_op jit(solution)/shard_map/ppermute | solution.py:540
  82.9 3.6 %collective-permute-start.11 = (f32[54,128]{1,0:T(8,128)S(1)}, f32[54,128]{1,0:T(8,128)S(1)}, u32[]{:S(2)}, u32[]{:S(2)}) collective-permute-start(f32[54,128]{1,0:T(8,128)S(1)} %broadcast_select_fusion.refs_10_.refs_17_), channel_id=1, source_target_pairs={{0,7},{1,0},{2,1},{3,2},{4,3},{5,4},{6,5},{7,6},{8,15},{9,8},{10,9... | collective-permute-start | bytes 82952 | tf_op jit(solution)/shard_map/ppermute | solution.py:540
  82.9 3.6 %copy-start.8 = (f32[54,128]{1,0:T(8,128)}, f32[54,128]{1,0:T(8,128)S(1)}, u32[]{:S(2)}) copy-start(f32[54,128]{1,0:T(8,128)S(1)} %collective-permute-done.6.refs_8_.refs_15_) | copy-start | bytes 82948
  82.9 3.6 %copy-start.9 = (f32[54,128]{1,0:T(8,128)}, f32[54,128]{1,0:T(8,128)S(1)}, u32[]{:S(2)}) copy-start(f32[54,128]{1,0:T(8,128)S(1)} %collective-permute-done.7.refs_9_.refs_16_) | copy-start | bytes 82948
  83.9 2.6 %copy-start.10 = (f32[54,128]{1,0:T(8,128)}, f32[54,128]{1,0:T(8,128)S(1)}, u32[]{:S(2)}) copy-start(f32[54,128]{1,0:T(8,128)S(1)} %collective-permute-done.10.refs_11_.refs_18_) | copy-start | bytes 82948
  91.6 9.9 %collective-permute-start.14 = (f32[48,128]{1,0:T(8,128)}, f32[48,128]{1,0:T(8,128)S(1)}, u32[]{:S(2)}, u32[]{:S(2)}) collective-permute-start(f32[48,128]{1,0:T(8,128)} %get-tuple-element.23.refs_7_), channel_id=1, source_target_pairs={{0,8},{8,16},{16,24},{24,32},{32,40},{40,48},{48,56},{56,64},{64,7... | collective-permute-start | bytes 73736 | tf_op jit(solution)/shard_map/ppermute | solution.py:540
  91.6 10.0 %collective-permute-start.15 = (f32[48,128]{1,0:T(8,128)}, f32[48,128]{1,0:T(8,128)S(1)}, u32[]{:S(2)}, u32[]{:S(2)}) collective-permute-start(f32[48,128]{1,0:T(8,128)} %get-tuple-element.23.refs_7_), channel_id=1, source_target_pairs={{0,120},{8,0},{16,8},{24,16},{32,24},{40,32},{48,40},{56,48},{64,5... | collective-permute-start | bytes 73736 | tf_op jit(solution)/shard_map/ppermute | solution.py:540
  96.4 14.9 %all-to-all-start.2 = ((f32[128,1,128]{2,1,0:T(1,128)}), f32[128,1,128]{2,1,0:T(1,128)S(1)}, u32[]{:S(2)}, u32[]{:S(2)}) async-start(f32[128,1,128]{2,1,0:T(1,128)} %bitcast.23), calls=%async_computation.2 | async-start | bytes 131072 | tf_op jit(solution)/shard_map/all_to_all | solution.py:535
  101.6 2.3 %copy-start.18 = (f32[48,128]{1,0:T(8,128)S(1)}, f32[48,128]{1,0:T(8,128)}, u32[]{:S(2)}) copy-start(f32[48,128]{1,0:T(8,128)} %get-tuple-element.23.refs_7_) | copy-start | bytes 73732
  102.2 9.1 %collective-permute-start.16 = (f32[96,128]{1,0:T(8,128)S(1)}, f32[96,128]{1,0:T(8,128)S(1)}, u32[]{:S(2)}, u32[]{:S(2)}) collective-permute-start(f32[96,128]{1,0:T(8,128)S(1)} %constant_dynamic-update-slice_fusion.2), channel_id=1, source_target_pairs={{0,1},{1,2},{2,3},{3,4},{4,5},{5,6},{6,7},{7,0},{8,9},{9,10},{10,1... | collective-permute-start | bytes 147464 | tf_op jit(solution)/shard_map/ppermute | solution.py:540
  103.9 7.4 %collective-permute-start.17 = (f32[96,128]{1,0:T(8,128)S(1)}, f32[96,128]{1,0:T(8,128)S(1)}, u32[]{:S(2)}, u32[]{:S(2)}) collective-permute-start(f32[96,128]{1,0:T(8,128)S(1)} %constant_dynamic-update-slice_fusion.2), channel_id=1, source_target_pairs={{0,7},{1,0},{2,1},{3,2},{4,3},{5,4},{6,5},{7,6},{8,15},{9,8},{10,9... | collective-permute-start | bytes 147464 | tf_op jit(solution)/shard_map/ppermute | solution.py:540
  103.9 3.2 %collective-permute-start.12 = (f32[48,128]{1,0:T(8,128)S(1)}, f32[48,128]{1,0:T(8,128)S(1)}, u32[]{:S(2)}, u32[]{:S(2)}) collective-permute-start(f32[48,128]{1,0:T(8,128)S(1)} %copy-done.18), channel_id=1, source_target_pairs={{0,1},{1,2},{2,3},{3,4},{4,5},{5,6},{6,7},{7,0},{8,9},{9,10},{10,1... | collective-permute-start | bytes 73736 | tf_op jit(solution)/shard_map/ppermute | solution.py:540
  105.7 3.5 %collective-permute-start.13 = (f32[48,128]{1,0:T(8,128)S(1)}, f32[48,128]{1,0:T(8,128)S(1)}, u32[]{:S(2)}, u32[]{:S(2)}) collective-permute-start(f32[48,128]{1,0:T(8,128)S(1)} %copy-done.18), channel_id=1, source_target_pairs={{0,7},{1,0},{2,1},{3,2},{4,3},{5,4},{6,5},{7,6},{8,15},{9,8},{10,9... | collective-permute-start | bytes 73736 | tf_op jit(solution)/shard_map/ppermute | solution.py:540
  107.1 4.3 %copy-start.19 = (f32[48,128]{1,0:T(8,128)}, f32[48,128]{1,0:T(8,128)S(1)}, u32[]{:S(2)}) copy-start(f32[48,128]{1,0:T(8,128)S(1)} %collective-permute-done.12.refs_8_) | copy-start | bytes 73732
  109.2 2.2 %copy-start.20 = (f32[48,128]{1,0:T(8,128)}, f32[48,128]{1,0:T(8,128)S(1)}, u32[]{:S(2)}) copy-start(f32[48,128]{1,0:T(8,128)S(1)} %collective-permute-done.13.refs_9_) | copy-start | bytes 73732
  (9 other events, 5.7 us)

commit v3 on v2

--- a/solution.py
+++ b/solution.py
@@ -14,10 +14,41 @@
 COLS = 256
 
 
-def lookup_kernel(asked_ref, table_ref, found_ref, split_ref, turned_ref, result_ref):
-    for block in range(5):
-        lanes = slice(block * 128, block * 128 + 128)
-        turned_ref[lanes, :] = asked_ref[:, 0, lanes].T
+GATHER_ROWS = 80
+ROUNDS = 10
+
+
+def in_vmem(count):
+    return [pl.BlockSpec(memory_space=pltpu.VMEM) for _ in range(count)]
+
+
+def call(kernel, outs, args, scratch, name):
+    many = isinstance(outs, list)
+    return pl.pallas_call(
+        kernel,
+        out_shape=outs,
+        in_specs=in_vmem(len(args)),
+        out_specs=in_vmem(len(outs)) if many else in_vmem(1)[0],
+        scratch_shapes=scratch,
+        name=name,
+    )(*args)
+
+
+def prepare_kernel(table_ref, split_ref, packed_ref, unit_ref):
+    top = jnp.zeros((8, 128), jnp.float32)
+    for block in range(TABLE // 128):
+        top = jnp.maximum(top, jnp.abs(table_ref[:, block * 128 : block * 128 + 128]))
+    top = jnp.maximum(jnp.max(top, keepdims=True), 1e-30)
+    unit_ref[...] = jnp.broadcast_to(top * (1.0 / 32767.0), (8, 128))
+    scale = 32767.0 / top
+
+    def whole(values):
+        return (values * scale + 32768.5).astype(jnp.int32) - 32768
+
+    for block in range(TABLE // 256):
+        low = table_ref[:, block * 128 : block * 128 + 128]
+        high = table_ref[:, TABLE // 2 + block * 128 : TABLE // 2 + block * 128 + 128]
+        packed_ref[:, block * 128 : block * 128 + 128] = (whole(high) << 16) | (whole(low) & 65535)
     for pair in range(TABLE // (2 * COLS)):
         start = pair * 2 * COLS
         rows = jnp.concatenate(
@@ -27,61 +58,106 @@
         split_ref[pair * 16 : pair * 16 + 16, :COLS] = upper
         split_ref[pair * 16 : pair * 16 + 16, COLS:] = (rows - upper.astype(jnp.float32)).astype(jnp.bfloat16)
 
-    corner = lax.broadcasted_iota(jnp.int32, (8, 256), 0)
-    bit_x = (corner & 1) == 1
-    bit_y = (corner & 2) == 2
-    bit_z = (corner & 4) == 4
-    column_at = lax.broadcasted_iota(jnp.int32, (COLS, 256), 0)
-
-    def group(main, tail, at):
-        ids = turned_ref[pl.ds(main[0], 8), :].astype(jnp.int32)
-        xs, ys, zs = (turned_ref[pl.ds(main[j], 8), :] for j in (1, 2, 3))
-        for pair in range(4):
-            def both(values):
-                return jnp.concatenate([values[2 * pair : 2 * pair + 1], values[2 * pair + 1 : 2 * pair + 2]], axis=1)
-            pair_ids = both(ids)
-            column = pair_ids & (COLS - 1)
-            row8 = jnp.broadcast_to(pair_ids >> 8, (8, 256))
-            chosen = (column_at == column).astype(jnp.float32).astype(jnp.bfloat16)
+
+def prepare(table):
+    outs = [
+        jax.ShapeDtypeStruct((8 * TABLE // COLS, 2 * COLS), jnp.bfloat16),
+        jax.ShapeDtypeStruct((8, TABLE // 2), jnp.int32),
+        jax.ShapeDtypeStruct((8, 128), jnp.float32),
+    ]
+    return call(prepare_kernel, outs, [table], [], "prepare")
+
+
+def choose(leaf, masks, first, count):
+    if count == 1:
+        return leaf(first)
+    half = count // 2
+    mask = masks[half.bit_length() - 1]
+    return jnp.where(mask, choose(leaf, masks, first + half, half), choose(leaf, masks, first, half))
+
+
+def weigh(coef, x, y, z):
+    corner = lax.broadcasted_iota(jnp.int32, coef.shape, 0)
+    weight_x = jnp.where((corner & 1) == 1, x, 1.0 - x)
+    weight_y = jnp.where((corner & 2) == 2, y, 1.0 - y)
+    weight_z = jnp.where((corner & 4) == 4, z, 1.0 - z)
+    lsize = jnp.sum(weight_x * weight_y * weight_z * coef, axis=0, keepdims=True)
+    return jnp.exp(-2.0 * lsize)
+
+
+def lookup_kernel(asked_ref, split_ref, packed_ref, unit_ref, found_ref, turned_ref, result_ref, column_ref):
+    for j in range(4):
+        turned_ref[j * SLOTS : j * SLOTS + 128, :] = asked_ref[:, 0, j * 128 : j * 128 + 128].T
+    tails = asked_ref[:, 0, 512:].T
+    for j in range(4):
+        turned_ref[j * SLOTS + 128 : (j + 1) * SLOTS, :] = tails[j * 8 : j * 8 + 8]
+    column_ref[...] = lax.broadcasted_iota(jnp.int32, (COLS, 128), 0).astype(jnp.float32).astype(jnp.bfloat16)
+    one = jnp.ones((), jnp.bfloat16)
+    zero = jnp.zeros((), jnp.bfloat16)
+
+    def step(i, carry):
+        base = pl.multiple_of(i * 8, 8)
+        ids, xs, ys, zs = (turned_ref[pl.ds(pl.multiple_of(j * SLOTS + base, 8), 8), :] for j in range(4))
+        ids = ids.astype(jnp.int32)
+        unit = unit_ref[...]
+        for r in range(8):
+            own = jnp.broadcast_to(ids[r : r + 1], (8, 128))
+            lane = own & 127
+            masks = [(own & (128 << bit)) != 0 for bit in range(6)]
+
+            def leaf(block):
+                return jnp.take_along_axis(packed_ref[:, block * 128 : block * 128 + 128], lane, axis=1)
+
+            word = choose(leaf, masks, 0, 64)
+            whole = jnp.where((own & (TABLE // 2)) != 0, word, word << 16) >> 16
+            coef = whole.astype(jnp.float32) * unit
+            result_ref[pl.ds(base + r, 1), :] = weigh(coef, xs[r : r + 1], ys[r : r + 1], zs[r : r + 1])
+
+        start = jnp.minimum(GATHER_ROWS + i * 6, SLOTS - 6)
+        for pair in range(3):
+            at = start + 2 * pair
+            pair_ids, px, py, pz = (
+                jnp.concatenate(
+                    [turned_ref[pl.ds(j * SLOTS + at, 1), :], turned_ref[pl.ds(j * SLOTS + at + 1, 1), :]], axis=1
+                )
+                for j in range(4)
+            )
+            pair_ids = pair_ids.astype(jnp.int32)
+            column = (pair_ids & (COLS - 1)).astype(jnp.float32).astype(jnp.bfloat16)
+            chosen = jnp.concatenate(
+                [
+                    jnp.where(column_ref[...] == column[:, half * 128 : half * 128 + 128], one, zero)
+                    for half in range(2)
+                ],
+                axis=1,
+            )
             picked = jnp.dot(split_ref[:, :COLS], chosen, preferred_element_type=jnp.float32) + jnp.dot(
                 split_ref[:, COLS:], chosen, preferred_element_type=jnp.float32
             )
-            coefs = [jnp.zeros((8, 256), jnp.float32) for _ in range(4)]
-            for row in range(TABLE // COLS):
-                coefs[row % 4] = jnp.where(row8 == row, picked[row * 8 : row * 8 + 8], coefs[row % 4])
-            coef = (coefs[0] + coefs[1]) + (coefs[2] + coefs[3])
-            px, py, pz = both(xs), both(ys), both(zs)
-            weight = jnp.where(bit_x, px, 1.0 - px) * jnp.where(bit_y, py, 1.0 - py) * jnp.where(bit_z, pz, 1.0 - pz)
-            lsize = jnp.sum(weight * coef, axis=0, keepdims=True)
-            value = jnp.exp(-2.0 * lsize)
-            result_ref[pl.ds(at + 2 * pair, 1), :] = value[:, :128]
-            result_ref[pl.ds(at + 2 * pair + 1, 1), :] = value[:, 128:]
-
-    def step(i, carry):
-        base = pl.multiple_of(i * 8, 8)
-        group([base, base + 128, base + 256, base + 384], None, base)
+            own = jnp.broadcast_to(pair_ids, (8, 256))
+            masks = [(own & (COLS << bit)) != 0 for bit in range(6)]
+            coef = choose(lambda row: picked[row * 8 : row * 8 + 8], masks, 0, 64)
+            value = weigh(coef, px, py, pz)
+            result_ref[pl.ds(at, 1), :] = value[:, :128]
+            result_ref[pl.ds(at + 1, 1), :] = value[:, 128:]
         return carry
 
-    lax.fori_loop(0, 16, step, 0)
-    group([512, 520, 528, 536], None, 128)
+    lax.fori_loop(0, ROUNDS, step, 0)
     found_ref[:, 0, :128] = result_ref[:128, :].T
     found_ref[:, 0, 128:] = result_ref[128:, :].T
 
 
-def lookup(asked, table):
-    return pl.pallas_call(
-        lookup_kernel,
-        out_shape=jax.ShapeDtypeStruct((SRC, 1, SLOTS), jnp.float32),
-        scratch_shapes=[
-            pltpu.VMEM((8 * TABLE // COLS, 2 * COLS), jnp.bfloat16),
-            pltpu.VMEM((640, 128), jnp.float32),
-            pltpu.VMEM((SLOTS, 128), jnp.float32),
-        ],
-        name="lookup",
-    )(asked, table)
-
-
-def place_kernel(found_ref, point_ref, size_ref, value_ref, row_ref, lane_ref):
+def lookup(asked, prepared):
+    scratch = [
+        pltpu.VMEM((4 * SLOTS, 128), jnp.float32),
+        pltpu.VMEM((SLOTS, 128), jnp.float32),
+        pltpu.VMEM((COLS, 128), jnp.bfloat16),
+    ]
+    out = jax.ShapeDtypeStruct((SRC, 1, SLOTS), jnp.float32)
+    return call(lookup_kernel, out, [asked, *prepared], scratch, "lookup")
+
+
+def place_kernel(found_ref, point_ref, size_ref, value_ref, row_ref, lane_ref, at_ref):
     value_ref[:128, :] = found_ref[:, 0, :128].T
     value_ref[128:, :] = found_ref[:, 0, 128:].T
     point = point_ref[...]
@@ -95,10 +171,11 @@
     jy = qy - ey * 3
     ez = (qz * 11) >> 5
     jz = qz - ez * 3
-    row_ref[...] = ((jz * 3 + jy) * 3 + jx) * 2 + ey
-    lane_ref[...] = ez * 64 + ex
-    lane_at = lax.broadcasted_iota(jnp.int32, (128, 128), 0)
-    row_at = lax.broadcasted_iota(jnp.int32, (56, 128), 0)
+    row_ref[...] = (((jz * 3 + jy) * 3 + jx) * 2 + ey).astype(jnp.float32)
+    lane_ref[...] = (ez * 64 + ex).astype(jnp.float32)
+    at_ref[...] = lax.broadcasted_iota(jnp.int32, (128, 128), 0).astype(jnp.float32).astype(jnp.bfloat16)
+    one = jnp.ones((), jnp.bfloat16)
+    zero = jnp.zeros((), jnp.bfloat16)
 
     def step(i, total):
         base = pl.multiple_of(i * 8, 8)
@@ -108,29 +185,22 @@
         left, right = [], []
         for r in range(8):
             value = values[r : r + 1]
-            placed = jnp.where(row_at == rows[r : r + 1], jnp.broadcast_to(value, (56, 128)), 0.0)
-            upper = placed.astype(jnp.bfloat16).astype(jnp.float32)
-            left.append(jnp.concatenate([upper, placed - upper], axis=0).astype(jnp.bfloat16))
-            right.append((lane_at == lanes[r : r + 1]).astype(jnp.float32).astype(jnp.bfloat16))
+            upper = value.astype(jnp.bfloat16)
+            lower = (value - upper.astype(jnp.float32)).astype(jnp.bfloat16)
+            row = at_ref[:64, :] == rows[r : r + 1].astype(jnp.bfloat16)
+            left.append(jnp.concatenate([jnp.where(row, upper, zero), jnp.where(row, lower, zero)], axis=0))
+            right.append(jnp.where(at_ref[...] == lanes[r : r + 1].astype(jnp.bfloat16), one, zero))
         left = jnp.concatenate(left, axis=1)
         right = jnp.concatenate(right, axis=1)
         return total + lax.dot_general(left, right, (((1,), (1,)), ((), ())), preferred_element_type=jnp.float32)
 
-    total = lax.fori_loop(0, SLOTS // 8, step, jnp.zeros((112, 128), jnp.float32))
-    size_ref[...] = (total[:56] + total[56:])[:54]
+    total = lax.fori_loop(0, SLOTS // 8, step, jnp.zeros((128, 128), jnp.float32))
+    size_ref[...] = total[:56] + total[64:120]
 
 
 def place(found, point):
-    return pl.pallas_call(
-        place_kernel,
-        out_shape=jax.ShapeDtypeStruct((54, 128), jnp.float32),
-        scratch_shapes=[
-            pltpu.VMEM((SLOTS, 128), jnp.float32),
-            pltpu.VMEM((SLOTS, 128), jnp.int32),
-            pltpu.VMEM((SLOTS, 128), jnp.int32),
-        ],
-        name="place",
-    )(found, point)
+    scratch = [pltpu.VMEM((SLOTS, 128), jnp.float32) for _ in range(3)] + [pltpu.VMEM((128, 128), jnp.bfloat16)]
+    return call(place_kernel, jax.ShapeDtypeStruct((56, 128), jnp.float32), [found, point], scratch, "place")
 
 
 HALF_GAP = float(np.sqrt(0.15))
@@ -138,26 +208,11 @@
 
 
 def field_pieces(refs):
-    own, y_low, y_high, z_low, z_high, corner_low, corner_high = refs
-    return {
-        (0, -1): (y_low, 0),
-        (0, 0): (own, 0),
-        (0, 1): (y_high, 0),
-        (-1, 0): (z_low, 0),
-        (1, 0): (z_high, 0),
-        (-1, -1): (corner_low, 0),
-        (1, -1): (corner_low, 48),
-        (-1, 1): (corner_high, 0),
-        (1, 1): (corner_high, 48),
-    }
+    return {(z, y): (refs[y], (z % 3) * 48) for z in (-1, 0, 1) for y in (-1, 0, 1)}
 
 
 def size_pieces(refs):
-    own, y_low, y_high, side, corner_low, corner_high = refs
-    pieces = {(0, -1): (y_low, 0), (0, 0): (own, 0), (0, 1): (y_high, 0)}
-    for z in (-1, 1):
-        pieces.update({(z, -1): (corner_low, 0), (z, 0): (side, 0), (z, 1): (corner_high, 0)})
-    return pieces
+    return {(z, y): (refs[y], 56 * abs(z)) for z in (-1, 0, 1) for y in (-1, 0, 1)}
 
 
 def lane_index():
@@ -225,7 +280,7 @@
     return pl.ds(pl.multiple_of(row + c * 24, 8), 8)
 
 
-def forward(c, local, out_ref):
+def forward(local, out_ref, at):
     along_z = [[spread(local(0, y, x), local(1, y, x), local(2, y, x)) for x in range(3)] for y in range(3)]
     for jz in range(3):
         value = [[along_z[y][x][0][jz] for x in range(3)] for y in range(3)]
@@ -238,7 +293,7 @@
             dz = spread(*(steep[x][jy] for x in range(3)), slopes=False)[0]
             for jx in range(3):
                 for k, part in enumerate((dx, dy, dz)):
-                    out_ref[at_point(c, k, jz, jy, jx), :] = part[jx]
+                    out_ref[at(k, jz, jy, jx), :] = part[jx]
 
 
 def backward(c, from_ref, out_ref):
@@ -343,10 +398,10 @@
 
 def pass_kernel(first, *refs):
     refs = list(refs)
-    field_refs = [refs.pop(0) for _ in range(7)]
+    field_refs = [refs.pop(0) for _ in range(3)]
     if not first:
-        shift_refs = [refs.pop(0) for _ in range(7)]
-    sizes = size_pieces([refs.pop(0) for _ in range(6)])
+        shift_refs = [refs.pop(0) for _ in range(3)]
+    sizes = size_pieces([refs.pop(0) for _ in range(3)])
     if first:
         move_ref, terms_out, nodes_ref, size_ref, jac_ref, part_ref, turn_ref = refs
         field = field_pieces(field_refs)
@@ -354,8 +409,8 @@
         terms_in, move_ref, terms_out, own_ref, nodes_ref, size_ref, jac_ref, part_ref, turn_ref, sum_ref = refs
         step = newton_step(add_up(terms_in))
         for i, (field_ref, shift_ref) in enumerate(zip(field_refs, shift_refs)):
-            sum_ref[i, : field_ref.shape[0], :] = field_ref[...] + step * shift_ref[...]
-        field = field_pieces([sum_ref.at[i] for i in range(7)])
+            sum_ref[i] = field_ref[...] + step * shift_ref[...]
+        field = field_pieces([sum_ref.at[i] for i in range(3)])
         own_ref[...] = sum_ref[0, :48, :]
     for z_shift in range(2):
         for y_shift in range(2):
@@ -369,16 +424,20 @@
             return x_up(value) if x == 2 else value
         return local
 
-    def sought(c):
-        def local(z, y, x):
-            row = ((z % 2) * 4 + (y % 2) * 2 + x % 2) * 8
-            value = turn_ref[pl.ds(pl.multiple_of(row + c * 64, 8), 8), :]
-            if x == 2:
-                value = x_up(value)
-            if y == 2:
-                value = y_up(value)
-            return z_up(value) if z == 2 else value
-        return local
+    def packed(node, upper, shift):
+        rows = [
+            turn_ref[pl.ds(node * 8 + upper * 4 + 1 + shift + ey, 4, stride=64), :] for ey in range(2)
+        ]
+        return jnp.concatenate(rows, axis=0)
+
+    def sought(z, y, x):
+        node = (z % 2) * 4 + (y % 2) * 2 + x % 2
+        shift = y // 2
+        value = packed(node, 0, shift)
+        if z == 2:
+            turned = pltpu.roll(value, 64, 1)
+            value = jnp.where(lane_index() < 64, turned, pltpu.roll(packed(node, 1, shift), 64, 1))
+        return x_up(value) if x == 2 else value
 
     def each(body):
         def run(i, carry):
@@ -389,7 +448,8 @@
     def size_at(jz, jy, jx):
         return size_ref[pl.ds(pl.multiple_of((jz * 9 + jy * 3 + jx) * 8, 8), 8), :]
 
-    each(lambda c: forward(c, known(c), jac_ref))
+    each(lambda c: forward(known(c), jac_ref, functools.partial(at_point, c)))
+    turn_ref[192:, :] = jnp.zeros((64, 128), jnp.float32)
 
     def stress(jz):
         for jy in range(3):
@@ -407,26 +467,33 @@
     each(lambda c: backward(c, part_ref, turn_ref))
     for row in range(2):
         move_ref[pl.ds(row, 24, stride=2), :] = turn_ref[pl.ds(row + 1, 24, stride=8), :]
-    each(lambda c: forward(c, sought(c), part_ref))
-
-    def line(jz, sums):
-        for jy in range(3):
-            for jx in range(3):
-                jac = jacobian_at(jac_ref, jz, jy, jx)
-                motion = load_tensor(part_ref, jz, jy, jx)
-                size = size_at(jz, jy, jx)
-                weight = weight_at(jz, jy, jx)
-                zero = strain_of(jac, size)
-                one = symmetric(lambda k, l: (column_dot(jac, motion, k, l) + column_dot(motion, jac, k, l)) * size)
-                two = symmetric(lambda k, l: column_dot(motion, motion, k, l) * size)
-                pairs = ((zero, zero), (zero, one), (zero, two), (one, two), (two, two), (one, one))
-                sums = tuple(total + weight * inner(*pair) for total, pair in zip(sums, pairs))
-        return sums
-
-    sums = lax.fori_loop(0, 3, line, tuple(jnp.zeros((8, 128), jnp.float32) for _ in range(6)))
+    forward(sought, part_ref, lambda k, jz, jy, jx: pl.ds(((jz * 9 + jy * 3 + jx) * 3 + k) * 8, 8))
+
     sub = lax.broadcasted_iota(jnp.int32, (8, 128), 0)
-    own = (sub == 1) | (sub == 2)
-    zz, zo, zt, ot, tt, gn = (jnp.sum(jnp.where(own, total, 0.0), keepdims=True) for total in sums)
+    sums = [jnp.zeros((8, 128), jnp.float32) for _ in range(6)]
+    for start, fresh in ((0, 0), (8, 8), (16, 16), (19, 24)):
+        weight = jnp.zeros((8, 128), jnp.float32)
+        for i in range(fresh - start, 8):
+            point = start + i
+            parts = [MIDDLE if (point // by) % 3 == 1 else OUTER for by in (9, 3, 1)]
+            weight = jnp.where(sub == i, (parts[0] * parts[1]) * parts[2], weight)
+        for ey in range(2):
+            jac = [
+                [jac_ref[pl.ds((start * 9 + c * 3 + k) * 8 + 1 + ey, 8, stride=72), :] for k in range(3)]
+                for c in range(3)
+            ]
+            jac = [[jac[c][k] + 1.0 if c == k else jac[c][k] for k in range(3)] for c in range(3)]
+            motion = [
+                [part_ref[pl.ds((start * 3 + k) * 8 + ey * 4 + c, 8, stride=24), :] for k in range(3)]
+                for c in range(3)
+            ]
+            size = size_ref[pl.ds(start * 8 + 1 + ey, 8, stride=8), :]
+            zero = strain_of(jac, size)
+            one = symmetric(lambda k, l: (column_dot(jac, motion, k, l) + column_dot(motion, jac, k, l)) * size)
+            two = symmetric(lambda k, l: column_dot(motion, motion, k, l) * size)
+            pairs = ((zero, zero), (zero, one), (zero, two), (one, two), (two, two), (one, one))
+            sums = [total + weight * inner(*pair) for total, pair in zip(sums, pairs)]
+    zz, zo, zt, ot, tt, gn = (jnp.sum(total, keepdims=True) for total in sums)
     lane = lax.broadcasted_iota(jnp.int32, (1, 128), 1)
     terms = jnp.zeros((1, 128), jnp.float32)
     for i, term in enumerate((zz, 2.0 * zo, gn + 2.0 * zt, 2.0 * ot, tt, gn)):
@@ -443,15 +510,10 @@
         pltpu.VMEM((27 * 8, 128), jnp.float32),
         pltpu.VMEM((243 * 8, 128), jnp.float32),
         pltpu.VMEM((243 * 8, 128), jnp.float32),
-        pltpu.VMEM((24 * 8, 128), jnp.float32),
-    ] + ([] if first else [pltpu.VMEM((7, 96, 128), jnp.float32)])
+        pltpu.VMEM((32 * 8, 128), jnp.float32),
+    ] + ([] if first else [pltpu.VMEM((3, 144, 128), jnp.float32)])
     args = list(field) + ([] if first else list(shift)) + list(sizes) + ([] if first else [terms])
-    return pl.pallas_call(
-        functools.partial(pass_kernel, first),
-        out_shape=outs,
-        scratch_shapes=scratch,
-        name="pass_one" if first else "pass_two",
-    )(*args)
+    return call(functools.partial(pass_kernel, first), outs, args, scratch, "pass_one" if first else "pass_two")
 
 
 def interleave(back):
@@ -479,42 +541,48 @@
 
 
 def split_nodes(nodes):
-    return pl.pallas_call(
-        split_kernel,
-        out_shape=jax.ShapeDtypeStruct((48, 128), jnp.float32),
-        scratch_shapes=[pltpu.VMEM((48, 128), jnp.float32)],
-        name="split_nodes",
-    )(nodes)
-
-
-def finish_kernel(own_ref, move_ref, first_ref, second_ref, out_ref, coeff_ref, rows_ref, new_ref):
-    first = add_up(first_ref)
+    out = jax.ShapeDtypeStruct((48, 128), jnp.float32)
+    return call(split_kernel, out, [nodes], [pltpu.VMEM((48, 128), jnp.float32)], "split_nodes")
+
+
+def join_kernel(first_ref, second_ref, out_first_ref, out_second_ref, rows_ref):
+    low = lax.broadcasted_iota(jnp.int32, (1, 128), 1) < 64
+    for i, new_ref in enumerate((first_ref, second_ref)):
+        for c in range(3):
+            for az in range(2):
+                for ay in range(2):
+                    for ey in range(2):
+                        at = (c * 8 + az * 4 + ay * 2) * 2 + ey
+                        even = new_ref[at : at + 1, :]
+                        odd = new_ref[at + 2 : at + 3, :]
+                        to = i * 48 + c * 16 + az * 4 + ey * 2 + ay
+                        rows_ref[to : to + 1, :] = jnp.where(low, even, pltpu.roll(odd, 64, 1))
+                        rows_ref[to + 8 : to + 9, :] = jnp.where(low, pltpu.roll(even, 64, 1), odd)
+    rows = jnp.dot(
+        rows_ref[...], interleave(True), precision=lax.Precision.HIGHEST, preferred_element_type=jnp.float32
+    )
+    out_first_ref[...] = rows[:48].reshape(3, 4, 4, 128)
+    out_second_ref[...] = rows[48:].reshape(3, 4, 4, 128)
+
+
+def join_nodes(first, second):
+    out = jax.ShapeDtypeStruct((3, 4, 4, 128), jnp.float32)
+    return call(join_kernel, [out, out], [first, second], [pltpu.VMEM((96, 128), jnp.float32)], "join_nodes")
+
+
+def finish_kernel(own_ref, move_ref, first_ref, second_ref, out_ref, coeff_ref):
     second = add_up(second_ref)
-    new_ref[...] = own_ref[...] + newton_step(second) * move_ref[...]
-    low = lax.broadcasted_iota(jnp.int32, (1, 128), 1) < 64
+    step = newton_step(second)
     for c in range(3):
-        for az in range(2):
-            for ay in range(2):
-                for ey in range(2):
-                    at = (c * 8 + az * 4 + ay * 2) * 2 + ey
-                    even = new_ref[at : at + 1, :]
-                    odd = new_ref[at + 2 : at + 3, :]
-                    to = c * 16 + az * 4 + ey * 2 + ay
-                    rows_ref[to : to + 1, :] = jnp.where(low, even, pltpu.roll(odd, 64, 1))
-                    rows_ref[to + 8 : to + 9, :] = jnp.where(low, pltpu.roll(even, 64, 1), odd)
-    rows = jnp.dot(rows_ref[...], interleave(True), precision=lax.Precision.HIGHEST, preferred_element_type=jnp.float32)
-    out_ref[...] = rows.reshape(3, 4, 4, 128)
-    coeff_ref[0:1, :] = first[:, :5] * (1.0 / 32768.0)
+        for z in range(4):
+            out_ref[c, z] = own_ref[c, z] + step * move_ref[c, z]
+    coeff_ref[0:1, :] = add_up(first_ref)[:, :5] * (1.0 / 32768.0)
     coeff_ref[1:2, :] = second[:, :5] * (1.0 / 32768.0)
 
 
 def finish(own, move, first, second):
-    return pl.pallas_call(
-        finish_kernel,
-        out_shape=[jax.ShapeDtypeStruct((3, 4, 4, 128), jnp.float32), jax.ShapeDtypeStruct((2, 5), jnp.float32)],
-        scratch_shapes=[pltpu.VMEM((48, 128), jnp.float32), pltpu.VMEM((48, 128), jnp.float32)],
-        name="finish",
-    )(own, move, first, second)
+    outs = [jax.ShapeDtypeStruct((3, 4, 4, 128), jnp.float32), jax.ShapeDtypeStruct((2, 5), jnp.float32)]
+    return call(finish_kernel, outs, [own, move, first, second], [], "finish")
 
 
 def pack_kernel(elem_ref, coord_ref, out_ref):
@@ -526,9 +594,7 @@
 
 
 def pack(elem, coord):
-    return pl.pallas_call(
-        pack_kernel, out_shape=jax.ShapeDtypeStruct((SRC, 1, 640), jnp.float32), name="pack"
-    )(elem, coord)
+    return call(pack_kernel, jax.ShapeDtypeStruct((SRC, 1, 640), jnp.float32), [elem, coord], [], "pack")
 
 
 def exchange(values):
@@ -540,26 +606,34 @@
     return lax.ppermute(values, axis, [(i, (i - by) % count) for i in range(count)])
 
 
-def around(block, merge):
-    z_low, z_high = moved(block, "mesh", -1), moved(block, "mesh", 1)
-    y_low, y_high = moved(block, "bg", -1), moved(block, "bg", 1)
+def along_mesh(block, merge):
+    low, high = moved(block, "mesh", -1), moved(block, "mesh", 1)
     if merge:
-        side = jnp.where(lax.broadcasted_iota(jnp.int32, block.shape, 1) < 64, z_high, z_low)
-        return [block, y_low, y_high, side, moved(side, "bg", -1), moved(side, "bg", 1)]
-    sides = jnp.concatenate([z_low, z_high], axis=0)
-    return [block, y_low, y_high, z_low, z_high, moved(sides, "bg", -1), moved(sides, "bg", 1)]
+        sides = [jnp.where(lax.broadcasted_iota(jnp.int32, block.shape, 1) < 64, high, low)]
+    else:
+        sides = [high, low]
+    return jnp.concatenate([block] + sides, axis=0)
+
+
+def along_bg(rows):
+    return [rows, moved(rows, "bg", 1), moved(rows, "bg", -1)]
 
 
 def shards(displacement, bg_coef, query_elem, query_point, query_coord):
     asked = exchange(pack(query_elem[0].T, query_coord[0].transpose(1, 2, 0)))
-    field = around(split_nodes(displacement), False)
-    asked, field = lax.optimization_barrier((asked, field))
-    found = exchange(lookup(asked, bg_coef))
-    sizes = around(place(found, query_point[0].T), True)
+    prepared = prepare(bg_coef)
+    rows = along_mesh(split_nodes(displacement), False)
+    asked, rows = lax.optimization_barrier((asked, rows))
+    found = exchange(lookup(asked, prepared))
+    field = along_bg(rows)
+    found, field = lax.optimization_barrier((found, field))
+    sizes = along_bg(along_mesh(place(found, query_point[0].T), True))
     move, terms = newton_pass(field, None, sizes, None)
     first_terms = exchange(terms)
-    last_move, last_terms, last_own = newton_pass(field, around(move, False), sizes, first_terms)
-    return finish(last_own, last_move, first_terms, exchange(last_terms))
+    shift = along_bg(along_mesh(move, False))
+    last_move, last_terms, last_own = newton_pass(field, shift, sizes, first_terms)
+    own, move = join_nodes(last_own, last_move)
+    return finish(own, move, first_terms, exchange(last_terms))
 
 
 def solution(mesh):

time: 140 us -> 128 us (0.914)
  blocking collectives: 36.9 us -> 28.4 us
  waiting for transfers between devices: 19.1 us -> 26.6 us
  starting transfers between devices: 39.8 us -> 32.6 us
  Pallas kernels: 38.5 us -> 34.6 us
    all_to_all x2, blocking collectives: 36.9 us -> 28.4 us  [exchange(): lax.all_to_all(values, ('mesh', 'bg'), split_axis=0, concat_axis=0, tiled...]
    ppermute x18 -> x12, starting transfers between devices: 23.2 us -> 16.6 us  [moved(): lax.ppermute(values, axis, [(i, (i - by) % count) for i in range(count)])]
    all_to_all x2, waiting for transfers between devices: 2.12 us -> 7.96 us  [exchange(): lax.all_to_all(values, ('mesh', 'bg'), split_axis=0, concat_axis=0, tiled...]
    pallas_call x7 -> x9, Pallas kernels: 38.5 us -> 34.6 us  [call(): pl.pallas_call(kernel, out_shape=outs, in_specs=in_vmem(len(args)), out_s...]
    ppermute x18 -> x12, waiting for transfers between devices: 17 us -> 18.7 us  [moved(): lax.ppermute(values, axis, [(i, (i - by) % count) for i in range(count)])]
    unnamed x44 -> x30, local copies, waits for them, and re-layouts: 3.81 us -> 3.36 us
  transfers between devices with their start and end apart: 20 -> 14, of which waited for: 9 -> 8; matrix products, arithmetic and copies ran while one was open for 0% -> 1% of each run, Pallas kernels for 1% -> 12%
where the time goes in v3:
time: 128 us; the launch traced here: 127 us
  Pallas kernels  34.6 us (27%)
  starting transfers between devices  32.6 us (25%)
  blocking collectives  28.4 us (22%)
  waiting for transfers between devices  26.6 us (21%)
  local copies, waits for them, and re-layouts  3.36 us (3%)
    pallas_call x9, Pallas kernels, call(): pl.pallas_call(kernel, out_shape=outs, in_specs=in_vmem(len(args)), out_s...  34.6 us
    all_to_all x2, blocking collectives, exchange(): lax.all_to_all(values, ('mesh', 'bg'), split_axis=0, concat_axis=0, tiled...  28.4 us
    ppermute x12, waiting for transfers between devices, moved(): lax.ppermute(values, axis, [(i, (i - by) % count) for i in range(count)])  18.7 us
    ppermute x12, starting transfers between devices, moved(): lax.ppermute(values, axis, [(i, (i - by) % count) for i in range(count)])  16.6 us
    all_to_all x2, starting transfers between devices, exchange(): lax.all_to_all(values, ('mesh', 'bg'), split_axis=0, concat_axis=0, tiled...  16 us
    all_to_all x2, waiting for transfers between devices, exchange(): lax.all_to_all(values, ('mesh', 'bg'), split_axis=0, concat_axis=0, tiled...  7.96 us
    unnamed x30, local copies, waits for them, and re-layouts  3.36 us
  transfers between devices with their start and end apart: 14, of which 8 were waited for; matrix products, arithmetic and copies ran while one was open for 1% of the time, Pallas kernels for 12%

profile of v3, /device:TPU:1, one launch (start us, length us, event | category | flops | bytes accessed | tf_op | source)
XLA Modules:
  0.0 127.0 jit_solution(17130904880595627674)
XLA Ops:
  0.6 1.9 %pack.1 = f32[128,1,640]{2,1,0:T(1,128)} custom-call(s32[136,128]{1,0:T(8,128)} %bitcast.21, f32[3,136,128]{2,1,0:T(8,128)} %bitcast.20), custom_call_target="tpu_custom_call" | custom-call | tf_op jit(solution)/shard_map/pack/pallas_call | solution.py:27
  2.6 11.5 %all-to-all-start = ((f32[128,1,640]{2,1,0:T(1,128)}), f32[128,1,640]{2,1,0:T(1,128)S(1)}, u32[]{:S(2)}, u32[]{:S(2)}) async-start(f32[128,1,640]{2,1,0:T(1,128)} %pack.1), calls=%async_computation | async-start | bytes 655360 | tf_op jit(solution)/shard_map/all_to_all | solution.py:601
  14.1 1.6 %split_nodes.1 = f32[48,128]{1,0:T(8,128)} custom-call(f32[3,4,4,128]{3,2,1,0:T(4,128)} %nodes_ref.1), custom_call_target="tpu_custom_call" | custom-call | tf_op jit(solution)/shard_map/split_nodes/pallas_call | solution.py:27
  15.7 5.4 %collective-permute-start = (f32[48,128]{1,0:T(8,128)}, f32[48,128]{1,0:T(8,128)S(1)}, u32[]{:S(2)}, u32[]{:S(2)}) collective-permute-start(f32[48,128]{1,0:T(8,128)} %split_nodes.1), channel_id=1, source_target_pairs={{0,120},{8,0},{16,8},{24,16},{32,24},{40,32},{48,40},{56,48},{64,5... | collective-permute-start | bytes 73736 | tf_op jit(solution)/shard_map/ppermute | solution.py:606
  21.1 1.2 collective-permute-done
  22.3 5.0 %collective-permute-done.1 = f32[48,128]{1,0:T(8,128)S(1)} collective-permute-done((f32[48,128]{1,0:T(8,128)}, f32[48,128]{1,0:T(8,128)S(1)}, u32[]{:S(2)}, u32[]{:S(2)}) %collective-permute-start.1) | collective-permute-done | bytes 24608 | tf_op jit(solution)/shard_map/ppermute | solution.py:606
  27.3 0.7 pad_maximum_fusion.refs_0_
  28.1 1.8 %collective-permute-start.2 = (f32[144,128]{1,0:T(8,128)S(1)}, f32[144,128]{1,0:T(8,128)S(1)}, u32[]{:S(2)}, u32[]{:S(2)}) collective-permute-start(f32[144,128]{1,0:T(8,128)S(1)} %pad_maximum_fusion.refs_0_), channel_id=1, source_target_pairs={{0,7},{1,0},{2,1},{3,2},{4,3},{5,4},{6,5},{7,6},{8,15},{9,8},{10,9... | collective-permute-start | bytes 221192 | tf_op jit(solution)/shard_map/ppermute | solution.py:606
  29.9 1.2 collective-permute-start.3
  31.1 2.3 %prepare.1 = (bf16[512,512]{1,0:T(8,128)(2,1)}, s32[8,8192]{1,0:T(8,128)}, f32[8,128]{1,0:T(8,128)}) custom-call(f32[8,16384]{1,0:T(8,128)} %table_ref.1), custom_call_target="tpu_custom_call" | custom-call | tf_op jit(solution)/shard_map/prepare/pallas_call | solution.py:27
  33.3 9.4 %lookup.1 = f32[128,1,136]{2,1,0:T(1,128)} custom-call(f32[128,1,640]{2,1,0:T(1,128)} %copy-done, bf16[512,512]{1,0:T(8,128)(2,1)} %get-tuple-element.19.split_ref, s32[8,8192]{1,0:T(8,128)} %get-tuple-element.20.packed_ref, f32[8,128]{1,0:T(8,128)} %get-tuple-element.21.unit_ref), custom_call_target="tpu_custom_call" | custom-call | tf_op jit(solution)/shard_map/lookup/pallas_call | solution.py:27
  42.7 14.6 %all_to_all.32.found_ref = f32[128,1,136]{2,1,0:T(1,128)} all-to-all(f32[128,1,136]{2,1,0:T(1,128)} %lookup.1), channel_id=1, replica_groups=mesh['mesh'=16,'bg'=8] {'mesh','bg'}, dimensions={0} | all-to-all | bytes 139264 | tf_op jit(solution)/shard_map/all_to_all | solution.py:601
  57.4 6.2 %place.1 = f32[56,128]{1,0:T(8,128)} custom-call(f32[128,1,136]{2,1,0:T(1,128)} %all_to_all.32.found_ref, s32[136,128]{1,0:T(8,128)} %bitcast.22), custom_call_target="tpu_custom_call" | custom-call | tf_op jit(solution)/shard_map/place/pallas_call | solution.py:27
  63.6 1.2 collective-permute-start.4
  65.1 1.5 %collective-permute-done.4 = f32[56,128]{1,0:T(8,128)S(1)} collective-permute-done((f32[56,128]{1,0:T(8,128)}, f32[56,128]{1,0:T(8,128)S(1)}, u32[]{:S(2)}, u32[]{:S(2)}) %collective-permute-start.4) | collective-permute-done | bytes 28704 | tf_op jit(solution)/shard_map/ppermute | solution.py:606
  66.6 4.6 %collective-permute-done.5 = f32[56,128]{1,0:T(8,128)S(1)} collective-permute-done((f32[56,128]{1,0:T(8,128)}, f32[56,128]{1,0:T(8,128)S(1)}, u32[]{:S(2)}, u32[]{:S(2)}) %collective-permute-start.5) | collective-permute-done | bytes 28704 | tf_op jit(solution)/shard_map/ppermute | solution.py:606
  71.2 1.8 %collective-permute-start.6 = (f32[112,128]{1,0:T(8,128)S(1)}, f32[112,128]{1,0:T(8,128)S(1)}, u32[]{:S(2)}, u32[]{:S(2)}) collective-permute-start(f32[112,128]{1,0:T(8,128)S(1)} %pad_maximum_fusion.1.refs_3_.refs_6_), channel_id=1, source_target_pairs={{0,7},{1,0},{2,1},{3,2},{4,3},{5,4},{6,5},{7,6},{8,15},{9,8},{10,9... | collective-permute-start | bytes 172040 | tf_op jit(solution)/shard_map/ppermute | solution.py:606
  73.1 1.8 %collective-permute-done.6.refs_4_.refs_7_ = f32[112,128]{1,0:T(8,128)S(1)} collective-permute-done((f32[112,128]{1,0:T(8,128)S(1)}, f32[112,128]{1,0:T(8,128)S(1)}, u32[]{:S(2)}, u32[]{:S(2)}) %collective-permute-start.6) | collective-permute-done | bytes 57376 | tf_op jit(solution)/shard_map/ppermute | solution.py:606
  75.6 0.6 copy-done.7
  76.2 3.6 %pass_one.1 = (f32[48,128]{1,0:T(8,128)}, f32[128,128]{1,0:T(8,128)}) custom-call(f32[144,128]{1,0:T(8,128)} %copy-done.1, f32[144,128]{1,0:T(8,128)} %copy-done.3, f32[144,128]{1,0:T(8,128)} %copy-done.4, f32[112,128]{1,0:T(8,128)} %copy-done.2, f32[112,128]{1,0:T(8,128)} %copy-done.6, f32[112,128]{1,0:T(8,128)} %copy-done.7), custom_call_target="tpu_custom_call" | custom-call | tf_op jit(solution)/shard_map/pass_one/pallas_call | solution.py:27
  79.9 0.8 constant_dynamic-update-slice_fusion.2
  80.7 1.4 %collective-permute-start.9 = (f32[48,128]{1,0:T(8,128)S(1)}, f32[48,128]{1,0:T(8,128)S(1)}, u32[]{:S(2)}, u32[]{:S(2)}) collective-permute-start(f32[48,128]{1,0:T(8,128)S(1)} %copy-done.13), channel_id=1, source_target_pairs={{0,8},{8,16},{16,24},{24,32},{32,40},{40,48},{48,56},{56,64},{64,7... | collective-permute-start | bytes 73736 | tf_op jit(solution)/shard_map/ppermute | solution.py:606
  82.1 0.6 collective-permute-done.8
  82.7 4.0 %collective-permute-done.9 = f32[48,128]{1,0:T(8,128)S(1)} collective-permute-done((f32[48,128]{1,0:T(8,128)S(1)}, f32[48,128]{1,0:T(8,128)S(1)}, u32[]{:S(2)}, u32[]{:S(2)}) %collective-permute-start.9) | collective-permute-done | bytes 24608 | tf_op jit(solution)/shard_map/ppermute | solution.py:606
  86.7 3.4 %collective-permute-start.10 = (f32[144,128]{1,0:T(8,128)S(1)}, f32[144,128]{1,0:T(8,128)S(1)}, u32[]{:S(2)}, u32[]{:S(2)}) collective-permute-start(f32[144,128]{1,0:T(8,128)S(1)} %constant_dynamic-update-slice_fusion.refs_3_), channel_id=1, source_target_pairs={{0,7},{1,0},{2,1},{3,2},{4,3},{5,4},{6,5},{7,6},{8,15},{9,8},{10,9... | collective-permute-start | bytes 221192 | tf_op jit(solution)/shard_map/ppermute | solution.py:606
  90.1 13.8 %all_to_all.33 = f32[128,1,128]{2,1,0:T(1,128)} all-to-all(f32[128,1,128]{2,1,0:T(1,128)S(1)} %bitcast.23), channel_id=1, replica_groups=mesh['mesh'=16,'bg'=8] {'mesh','bg'}, dimensions={0} | all-to-all | bytes 131072 | tf_op jit(solution)/shard_map/all_to_all | solution.py:601
  104.5 5.0 %pass_two.1 = (f32[48,128]{1,0:T(8,128)}, f32[128,128]{1,0:T(8,128)}, f32[48,128]{1,0:T(8,128)}) custom-call(f32[144,128]{1,0:T(8,128)} %copy-done.1, f32[144,128]{1,0:T(8,128)} %copy-done.3, f32[144,128]{1,0:T(8,128)} %copy-done.4, f32[144,128]{1,0:T(8,128)} %copy-done.8, f32[144,128]{1,0:T(8,128)} %copy-done.10, f32[144,128]{1,0:T(8,128)} %copy-done.11, ...), custom_call_target="tpu_custom_call" | custom-call | tf_op jit(solution)/shard_map/pass_two/pallas_call | solution.py:27
  109.5 4.5 %all-to-all-start.3 = ((f32[128,1,128]{2,1,0:T(1,128)}), f32[128,1,128]{2,1,0:T(1,128)S(1)}, u32[]{:S(2)}, u32[]{:S(2)}) async-start(f32[128,1,128]{2,1,0:T(1,128)} %bitcast.24), calls=%async_computation.3 | async-start | bytes 131072 | tf_op jit(solution)/shard_map/all_to_all | solution.py:601
  114.0 1.7 %join_nodes.1 = (f32[3,4,4,128]{3,2,1,0:T(4,128)}, f32[3,4,4,128]{3,2,1,0:T(4,128)}) custom-call(f32[48,128]{1,0:T(8,128)} %get-tuple-element.29.first_ref, f32[48,128]{1,0:T(8,128)} %get-tuple-element.30.second_ref), custom_call_target="tpu_custom_call" | custom-call | tf_op jit(solution)/shard_map/join_nodes/pallas_call | solution.py:27
  115.8 8.0 %all-to-all-done.3 = f32[128,1,128]{2,1,0:T(1,128)S(1)} async-done(((f32[128,1,128]{2,1,0:T(1,128)}), f32[128,1,128]{2,1,0:T(1,128)S(1)}, u32[]{:S(2)}, u32[]{:S(2)}) %all-to-all-start.3) | async-done | bytes 65568 | tf_op jit(solution)/shard_map/all_to_all | solution.py:601
  123.7 0.6 copy-done.5
  124.3 2.7 %finish.1 = (f32[3,4,4,128]{3,2,1,0:T(4,128)}, f32[2,5]{1,0:T(2,128)}) custom-call(f32[3,4,4,128]{3,2,1,0:T(4,128)} %get-tuple-element.31.own_ref, f32[3,4,4,128]{3,2,1,0:T(4,128)} %get-tuple-element.32.move_ref, f32[128,128]{1,0:T(8,128)} %bitcast.18, f32[128,128]{1,0:T(8,128)} %bitcast.19), custom_call_target="tpu_custom_call" | custom-call | tf_op jit(solution)/shard_map/finish/pallas_call | solution.py:27
  (42 shorter events, 1.7 us)
Async XLA Ops:
  2.6 25.5 %all-to-all-start = ((f32[128,1,640]{2,1,0:T(1,128)}), f32[128,1,640]{2,1,0:T(1,128)S(1)}, u32[]{:S(2)}, u32[]{:S(2)}) async-start(f32[128,1,640]{2,1,0:T(1,128)} %pack.1), calls=%async_computation | async-start | bytes 655360 | tf_op jit(solution)/shard_map/all_to_all | solution.py:601
  15.7 6.5 %collective-permute-start = (f32[48,128]{1,0:T(8,128)}, f32[48,128]{1,0:T(8,128)S(1)}, u32[]{:S(2)}, u32[]{:S(2)}) collective-permute-start(f32[48,128]{1,0:T(8,128)} %split_nodes.1), channel_id=1, source_target_pairs={{0,120},{8,0},{16,8},{24,16},{32,24},{40,32},{48,40},{56,48},{64,5... | collective-permute-start | bytes 73736 | tf_op jit(solution)/shard_map/ppermute | solution.py:606
  21.1 6.2 %collective-permute-start.1 = (f32[48,128]{1,0:T(8,128)}, f32[48,128]{1,0:T(8,128)S(1)}, u32[]{:S(2)}, u32[]{:S(2)}) collective-permute-start(f32[48,128]{1,0:T(8,128)} %split_nodes.1), channel_id=1, source_target_pairs={{0,8},{8,16},{16,24},{24,32},{32,40},{40,48},{48,56},{56,64},{64,7... | collective-permute-start | bytes 73736 | tf_op jit(solution)/shard_map/ppermute | solution.py:606
  28.0 5.3 %copy-start.1 = (f32[144,128]{1,0:T(8,128)}, f32[144,128]{1,0:T(8,128)S(1)}, u32[]{:S(2)}) copy-start(f32[144,128]{1,0:T(8,128)S(1)} %pad_maximum_fusion.refs_0_) | copy-start | bytes 221188
  28.1 5.3 %copy-start = (f32[128,1,640]{2,1,0:T(1,128)}, f32[128,1,640]{2,1,0:T(1,128)S(1)}, u32[]{:S(2)}) copy-start(f32[128,1,640]{2,1,0:T(1,128)S(1)} %all-to-all-done.asked_ref) | copy-start | bytes 983044
  28.1 29.3 %collective-permute-start.2 = (f32[144,128]{1,0:T(8,128)S(1)}, f32[144,128]{1,0:T(8,128)S(1)}, u32[]{:S(2)}, u32[]{:S(2)}) collective-permute-start(f32[144,128]{1,0:T(8,128)S(1)} %pad_maximum_fusion.refs_0_), channel_id=1, source_target_pairs={{0,7},{1,0},{2,1},{3,2},{4,3},{5,4},{6,5},{7,6},{8,15},{9,8},{10,9... | collective-permute-start | bytes 221192 | tf_op jit(solution)/shard_map/ppermute | solution.py:606
  29.9 27.5 %collective-permute-start.3 = (f32[144,128]{1,0:T(8,128)S(1)}, f32[144,128]{1,0:T(8,128)S(1)}, u32[]{:S(2)}, u32[]{:S(2)}) collective-permute-start(f32[144,128]{1,0:T(8,128)S(1)} %pad_maximum_fusion.refs_0_), channel_id=1, source_target_pairs={{0,1},{1,2},{2,3},{3,4},{4,5},{5,6},{6,7},{7,0},{8,9},{9,10},{10,1... | collective-permute-start | bytes 221192 | tf_op jit(solution)/shard_map/ppermute | solution.py:606
  57.4 6.2 %copy-start.3 = (f32[144,128]{1,0:T(8,128)}, f32[144,128]{1,0:T(8,128)S(1)}, u32[]{:S(2)}) copy-start(f32[144,128]{1,0:T(8,128)S(1)} %collective-permute-done.2.refs_1_) | copy-start | bytes 221188
  57.4 6.2 %copy-start.4 = (f32[144,128]{1,0:T(8,128)}, f32[144,128]{1,0:T(8,128)S(1)}, u32[]{:S(2)}) copy-start(f32[144,128]{1,0:T(8,128)S(1)} %collective-permute-done.3.refs_2_) | copy-start | bytes 221188
  63.6 2.9 %collective-permute-start.4 = (f32[56,128]{1,0:T(8,128)}, f32[56,128]{1,0:T(8,128)S(1)}, u32[]{:S(2)}, u32[]{:S(2)}) collective-permute-start(f32[56,128]{1,0:T(8,128)} %place.1), channel_id=1, source_target_pairs={{0,120},{8,0},{16,8},{24,16},{32,24},{40,32},{48,40},{56,48},{64,5... | collective-permute-start | bytes 86024 | tf_op jit(solution)/shard_map/ppermute | solution.py:606
  64.9 6.3 %collective-permute-start.5 = (f32[56,128]{1,0:T(8,128)}, f32[56,128]{1,0:T(8,128)S(1)}, u32[]{:S(2)}, u32[]{:S(2)}) collective-permute-start(f32[56,128]{1,0:T(8,128)} %place.1), channel_id=1, source_target_pairs={{0,8},{8,16},{16,24},{24,32},{32,40},{40,48},{48,56},{56,64},{64,7... | collective-permute-start | bytes 86024 | tf_op jit(solution)/shard_map/ppermute | solution.py:606
  65.1 6.0 %copy-start.9 = (f32[56,128]{1,0:T(8,128)S(1)}, f32[56,128]{1,0:T(8,128)}, u32[]{:S(2)}) copy-start(f32[56,128]{1,0:T(8,128)} %place.1) | copy-start | bytes 86020
  71.1 3.8 %copy-start.2 = (f32[112,128]{1,0:T(8,128)}, f32[112,128]{1,0:T(8,128)S(1)}, u32[]{:S(2)}) copy-start(f32[112,128]{1,0:T(8,128)S(1)} %pad_maximum_fusion.1.refs_3_.refs_6_) | copy-start | bytes 172036
  71.2 3.8 %collective-permute-start.6 = (f32[112,128]{1,0:T(8,128)S(1)}, f32[112,128]{1,0:T(8,128)S(1)}, u32[]{:S(2)}, u32[]{:S(2)}) collective-permute-start(f32[112,128]{1,0:T(8,128)S(1)} %pad_maximum_fusion.1.refs_3_.refs_6_), channel_id=1, source_target_pairs={{0,7},{1,0},{2,1},{3,2},{4,3},{5,4},{6,5},{7,6},{8,15},{9,8},{10,9... | collective-permute-start | bytes 172040 | tf_op jit(solution)/shard_map/ppermute | solution.py:606
  73.0 2.0 %collective-permute-start.7 = (f32[112,128]{1,0:T(8,128)S(1)}, f32[112,128]{1,0:T(8,128)S(1)}, u32[]{:S(2)}, u32[]{:S(2)}) collective-permute-start(f32[112,128]{1,0:T(8,128)S(1)} %pad_maximum_fusion.1.refs_3_.refs_6_), channel_id=1, source_target_pairs={{0,1},{1,2},{2,3},{3,4},{4,5},{5,6},{6,7},{7,0},{8,9},{9,10},{10,1... | collective-permute-start | bytes 172040 | tf_op jit(solution)/shard_map/ppermute | solution.py:606
  75.0 0.6 copy-start.6
  75.6 0.6 copy-start.7
  79.8 0.9 copy-start.13
  79.8 10.3 %copy-start.12 = (f32[128,128]{1,0:T(8,128)S(1)}, f32[128,128]{1,0:T(8,128)}, u32[]{:S(2)}) copy-start(f32[128,128]{1,0:T(8,128)} %get-tuple-element.28) | copy-start | bytes 196612
  79.9 2.9 %collective-permute-start.8 = (f32[48,128]{1,0:T(8,128)}, f32[48,128]{1,0:T(8,128)S(1)}, u32[]{:S(2)}, u32[]{:S(2)}) collective-permute-start(f32[48,128]{1,0:T(8,128)} %get-tuple-element.27), channel_id=1, source_target_pairs={{0,120},{8,0},{16,8},{24,16},{32,24},{40,32},{48,40},{56,48},{64,5... | collective-permute-start | bytes 73736 | tf_op jit(solution)/shard_map/ppermute | solution.py:606
  80.7 6.0 %collective-permute-start.9 = (f32[48,128]{1,0:T(8,128)S(1)}, f32[48,128]{1,0:T(8,128)S(1)}, u32[]{:S(2)}, u32[]{:S(2)}) collective-permute-start(f32[48,128]{1,0:T(8,128)S(1)} %copy-done.13), channel_id=1, source_target_pairs={{0,8},{8,16},{16,24},{24,32},{32,40},{40,48},{48,56},{56,64},{64,7... | collective-permute-start | bytes 73736 | tf_op jit(solution)/shard_map/ppermute | solution.py:606
  86.7 17.2 %copy-start.8 = (f32[144,128]{1,0:T(8,128)}, f32[144,128]{1,0:T(8,128)S(1)}, u32[]{:S(2)}) copy-start(f32[144,128]{1,0:T(8,128)S(1)} %constant_dynamic-update-slice_fusion.refs_3_) | copy-start | bytes 221188
  86.7 17.2 %collective-permute-start.10 = (f32[144,128]{1,0:T(8,128)S(1)}, f32[144,128]{1,0:T(8,128)S(1)}, u32[]{:S(2)}, u32[]{:S(2)}) collective-permute-start(f32[144,128]{1,0:T(8,128)S(1)} %constant_dynamic-update-slice_fusion.refs_3_), channel_id=1, source_target_pairs={{0,7},{1,0},{2,1},{3,2},{4,3},{5,4},{6,5},{7,6},{8,15},{9,8},{10,9... | collective-permute-start | bytes 221192 | tf_op jit(solution)/shard_map/ppermute | solution.py:606
  90.1 13.8 %collective-permute-start.11 = (f32[144,128]{1,0:T(8,128)S(1)}, f32[144,128]{1,0:T(8,128)S(1)}, u32[]{:S(2)}, u32[]{:S(2)}) collective-permute-start(f32[144,128]{1,0:T(8,128)S(1)} %constant_dynamic-update-slice_fusion.refs_3_), channel_id=1, source_target_pairs={{0,1},{1,2},{2,3},{3,4},{4,5},{5,6},{6,7},{7,0},{8,9},{9,10},{10,1... | collective-permute-start | bytes 221192 | tf_op jit(solution)/shard_map/ppermute | solution.py:606
  103.9 0.6 copy-start.10
  103.9 0.6 copy-start.11
  109.5 14.2 %all-to-all-start.3 = ((f32[128,1,128]{2,1,0:T(1,128)}), f32[128,1,128]{2,1,0:T(1,128)S(1)}, u32[]{:S(2)}, u32[]{:S(2)}) async-start(f32[128,1,128]{2,1,0:T(1,128)} %bitcast.24), calls=%async_computation.3 | async-start | bytes 131072 | tf_op jit(solution)/shard_map/all_to_all | solution.py:601
  123.7 0.6 copy-start.5

commit v4 on v3

--- a/solution.py
+++ b/solution.py
@@ -22,15 +22,17 @@
     return [pl.BlockSpec(memory_space=pltpu.VMEM) for _ in range(count)]
 
 
-def call(kernel, outs, args, scratch, name):
+def call(kernel, outs, args, scratch, far=(), last=False):
+    args = [a if i in far else pltpu.with_memory_space_constraint(a, pltpu.VMEM) for i, a in enumerate(args)]
     many = isinstance(outs, list)
+    if not last:
+        outs = [pltpu.VMEM(o.shape, o.dtype) for o in outs] if many else pltpu.VMEM(outs.shape, outs.dtype)
     return pl.pallas_call(
         kernel,
         out_shape=outs,
         in_specs=in_vmem(len(args)),
         out_specs=in_vmem(len(outs)) if many else in_vmem(1)[0],
         scratch_shapes=scratch,
-        name=name,
     )(*args)
 
 
@@ -65,7 +67,7 @@
         jax.ShapeDtypeStruct((8, TABLE // 2), jnp.int32),
         jax.ShapeDtypeStruct((8, 128), jnp.float32),
     ]
-    return call(prepare_kernel, outs, [table], [], "prepare")
+    return call(prepare_kernel, outs, [table], [], far=(0,))
 
 
 def choose(leaf, masks, first, count):
@@ -154,7 +156,7 @@
         pltpu.VMEM((COLS, 128), jnp.bfloat16),
     ]
     out = jax.ShapeDtypeStruct((SRC, 1, SLOTS), jnp.float32)
-    return call(lookup_kernel, out, [asked, *prepared], scratch, "lookup")
+    return call(lookup_kernel, out, [asked, *prepared], scratch)
 
 
 def place_kernel(found_ref, point_ref, size_ref, value_ref, row_ref, lane_ref, at_ref):
@@ -200,7 +202,7 @@
 
 def place(found, point):
     scratch = [pltpu.VMEM((SLOTS, 128), jnp.float32) for _ in range(3)] + [pltpu.VMEM((128, 128), jnp.bfloat16)]
-    return call(place_kernel, jax.ShapeDtypeStruct((56, 128), jnp.float32), [found, point], scratch, "place")
+    return call(place_kernel, jax.ShapeDtypeStruct((56, 128), jnp.float32), [found, point], scratch, far=(1,))
 
 
 HALF_GAP = float(np.sqrt(0.15))
@@ -225,20 +227,11 @@
 
 def x_down(v):
     return jnp.where((lane_index() & 63) == 0, pltpu.roll(v, 65, 1), pltpu.roll(v, 1, 1))
-
-
-def z_up(v):
-    turned = pltpu.roll(v, 64, 1)
-    return jnp.where(lane_index() < 64, turned, pltpu.roll(turned, 4, 0))
 
 
 def z_down(v):
     turned = pltpu.roll(v, 64, 1)
     return jnp.where(lane_index() < 64, pltpu.roll(turned, 4, 0), turned)
-
-
-def y_up(v):
-    return pltpu.roll(v, 7, 0)
 
 
 def y_down(v):
@@ -422,6 +415,7 @@
             row = ((z == 2) * 2 + (y == 2)) * 192 + ((z % 2) * 4 + (y % 2) * 2 + x % 2) * 8
             value = nodes_ref[pl.ds(pl.multiple_of(row + c * 64, 8), 8), :]
             return x_up(value) if x == 2 else value
+
         return local
 
     def packed(node, upper, shift):
@@ -443,6 +437,7 @@
         def run(i, carry):
             body(i)
             return carry
+
         lax.fori_loop(0, 3, run, 0)
 
     def size_at(jz, jy, jx):
@@ -513,7 +508,7 @@
         pltpu.VMEM((32 * 8, 128), jnp.float32),
     ] + ([] if first else [pltpu.VMEM((3, 144, 128), jnp.float32)])
     args = list(field) + ([] if first else list(shift)) + list(sizes) + ([] if first else [terms])
-    return call(functools.partial(pass_kernel, first), outs, args, scratch, "pass_one" if first else "pass_two")
+    return call(functools.partial(pass_kernel, first), outs, args, scratch)
 
 
 def interleave(back):
@@ -542,7 +537,7 @@
 
 def split_nodes(nodes):
     out = jax.ShapeDtypeStruct((48, 128), jnp.float32)
-    return call(split_kernel, out, [nodes], [pltpu.VMEM((48, 128), jnp.float32)], "split_nodes")
+    return call(split_kernel, out, [nodes], [pltpu.VMEM((48, 128), jnp.float32)], far=(0,))
 
 
 def join_kernel(first_ref, second_ref, out_first_ref, out_second_ref, rows_ref):
@@ -567,7 +562,7 @@
 
 def join_nodes(first, second):
     out = jax.ShapeDtypeStruct((3, 4, 4, 128), jnp.float32)
-    return call(join_kernel, [out, out], [first, second], [pltpu.VMEM((96, 128), jnp.float32)], "join_nodes")
+    return call(join_kernel, [out, out], [first, second], [pltpu.VMEM((96, 128), jnp.float32)])
 
 
 def finish_kernel(own_ref, move_ref, first_ref, second_ref, out_ref, coeff_ref):
@@ -582,7 +577,7 @@
 
 def finish(own, move, first, second):
     outs = [jax.ShapeDtypeStruct((3, 4, 4, 128), jnp.float32), jax.ShapeDtypeStruct((2, 5), jnp.float32)]
-    return call(finish_kernel, outs, [own, move, first, second], [], "finish")
+    return call(finish_kernel, outs, [own, move, first, second], [], last=True)
 
 
 def pack_kernel(elem_ref, coord_ref, out_ref):
@@ -594,7 +589,7 @@
 
 
 def pack(elem, coord):
-    return call(pack_kernel, jax.ShapeDtypeStruct((SRC, 1, 640), jnp.float32), [elem, coord], [], "pack")
+    return call(pack_kernel, jax.ShapeDtypeStruct((SRC, 1, 640), jnp.float32), [elem, coord], [], far=(0, 1))
 
 
 def exchange(values):
@@ -621,11 +616,11 @@
 
 def shards(displacement, bg_coef, query_elem, query_point, query_coord):
     asked = exchange(pack(query_elem[0].T, query_coord[0].transpose(1, 2, 0)))
-    prepared = prepare(bg_coef)
-    rows = along_mesh(split_nodes(displacement), False)
-    asked, rows = lax.optimization_barrier((asked, rows))
-    found = exchange(lookup(asked, prepared))
-    field = along_bg(rows)
+    own = split_nodes(displacement)
+    asked, prepared, own = lax.optimization_barrier((asked, prepare(bg_coef), own))
+    found, own = lax.optimization_barrier((lookup(asked, prepared), own))
+    found = exchange(found)
+    field = along_bg(along_mesh(own, False))
     found, field = lax.optimization_barrier((found, field))
     sizes = along_bg(along_mesh(place(found, query_point[0].T), True))
     move, terms = newton_pass(field, None, sizes, None)
@@ -633,7 +628,8 @@
     shift = along_bg(along_mesh(move, False))
     last_move, last_terms, last_own = newton_pass(field, shift, sizes, first_terms)
     own, move = join_nodes(last_own, last_move)
-    return finish(own, move, first_terms, exchange(last_terms))
+    last_terms = exchange(last_terms)
+    return finish(own, move, first_terms, last_terms)
 
 
 def solution(mesh):

time: 128 us -> 119 us (0.930)
  waiting for transfers between devices: 26.6 us -> 36.5 us
  Pallas kernels: 34.6 us -> 25.8 us
  starting transfers between devices: 32.6 us -> 28.6 us
  local copies, waits for them, and re-layouts: 3.36 us -> 0.02 us
  blocking collectives: 28.4 us -> 26.9 us
    all_to_all x2, waiting for transfers between devices: 7.96 us -> 18.4 us  [exchange(): lax.all_to_all(values, ('mesh', 'bg'), split_axis=0, concat_axis=0, tiled...]
    pallas_call x9, Pallas kernels: 34.6 us -> 25.8 us  [call(): pl.pallas_call(kernel, out_shape=outs, in_specs=in_vmem(len(args)), out_s...]
    ppermute x12, starting transfers between devices: 16.6 us -> 12.7 us  [moved(): lax.ppermute(values, axis, [(i, (i - by) % count) for i in range(count)])]
    unnamed x30 -> x4, local copies, waits for them, and re-layouts: 3.36 us -> 0.01 us
    all_to_all x2, blocking collectives: 28.4 us -> 26.9 us  [exchange(): lax.all_to_all(values, ('mesh', 'bg'), split_axis=0, concat_axis=0, tiled...]
  transfers between devices with their start and end apart: 14 -> 14, of which waited for: 8 -> 9; matrix products, arithmetic and copies ran while one was open for 1% -> 0% of each run, Pallas kernels for 12% -> 2%
where the time goes in v4:
time: 119 us
  waiting for transfers between devices  36.5 us (31%)
  starting transfers between devices  28.6 us (24%)
  blocking collectives  26.9 us (23%)
  Pallas kernels  25.8 us (22%)
    all_to_all x2, blocking collectives, exchange(): lax.all_to_all(values, ('mesh', 'bg'), split_axis=0, concat_axis=0, tiled...  26.9 us
    pallas_call x9, Pallas kernels, call(): pl.pallas_call(kernel, out_shape=outs, in_specs=in_vmem(len(args)), out_s...  25.8 us
    all_to_all x2, waiting for transfers between devices, exchange(): lax.all_to_all(values, ('mesh', 'bg'), split_axis=0, concat_axis=0, tiled...  18.4 us
    ppermute x12, waiting for transfers between devices, moved(): lax.ppermute(values, axis, [(i, (i - by) % count) for i in range(count)])  18.1 us
    all_to_all x2, starting transfers between devices, exchange(): lax.all_to_all(values, ('mesh', 'bg'), split_axis=0, concat_axis=0, tiled...  15.9 us
    ppermute x12, starting transfers between devices, moved(): lax.ppermute(values, axis, [(i, (i - by) % count) for i in range(count)])  12.7 us
  transfers between devices with their start and end apart: 14, of which 9 were waited for; matrix products, arithmetic and copies ran while one was open for 0% of the time, Pallas kernels for 2%

profile of v4, /device:TPU:1, one launch (start us, length us, event | category | flops | bytes accessed | tf_op | source)
XLA Modules:
  0.0 118.7 jit_solution(119018143886108658)
XLA Ops:
  0.6 1.9 %shard_map.68 = f32[128,1,640]{2,1,0:T(1,128)} custom-call(s32[136,128]{1,0:T(8,128)} %bitcast.22, f32[3,136,128]{2,1,0:T(8,128)} %bitcast.21), custom_call_target="tpu_custom_call" | custom-call | tf_op jit(solution)/shard_map/pallas_call | solution.py:30
  2.6 11.5 %all-to-all-start = ((f32[128,1,640]{2,1,0:T(1,128)}), f32[128,1,640]{2,1,0:T(1,128)S(1)}, u32[]{:S(2)}, u32[]{:S(2)}) async-start(f32[128,1,640]{2,1,0:T(1,128)} %shard_map.68), calls=%async_computation | async-start | bytes 655360 | tf_op jit(solution)/shard_map/all_to_all | solution.py:596
  14.1 1.5 %shard_map.69 = (bf16[512,512]{1,0:T(8,128)(2,1)S(1)}, s32[8,8192]{1,0:T(8,128)S(1)}, f32[8,128]{1,0:T(8,128)S(1)}) custom-call(f32[8,16384]{1,0:T(8,128)} %table_ref.1), custom_call_target="tpu_custom_call" | custom-call | tf_op jit(solution)/shard_map/pallas_call | solution.py:30
  15.5 1.0 shard_map.70
  16.6 9.1 %all-to-all-done.asked_ref = f32[128,1,640]{2,1,0:T(1,128)S(1)} async-done(((f32[128,1,640]{2,1,0:T(1,128)}), f32[128,1,640]{2,1,0:T(1,128)S(1)}, u32[]{:S(2)}, u32[]{:S(2)}) %all-to-all-start) | async-done | bytes 327712 | tf_op jit(solution)/shard_map/all_to_all | solution.py:596
  25.7 7.8 %shard_map.71 = f32[128,1,136]{2,1,0:T(1,128)S(1)} custom-call(f32[128,1,640]{2,1,0:T(1,128)S(1)} %all-to-all-done.asked_ref, bf16[512,512]{1,0:T(8,128)(2,1)S(1)} %get-tuple-element.27.split_ref, s32[8,8192]{1,0:T(8,128)S(1)} %get-tuple-element.28.packed_ref, f32[8,128]{1,0:T(8,128)S(1)} %get-tuple-element.29.unit_ref), custom_call_target="tpu_custom_call" | custom-call | tf_op jit(solution)/shard_map/pallas_call | solution.py:30
  33.5 1.4 %collective-permute-start = (f32[48,128]{1,0:T(8,128)S(1)}, f32[48,128]{1,0:T(8,128)S(1)}, u32[]{:S(2)}, u32[]{:S(2)}) collective-permute-start(f32[48,128]{1,0:T(8,128)S(1)} %shard_map.70), channel_id=1, source_target_pairs={{0,120},{8,0},{16,8},{24,16},{32,24},{40,32},{48,40},{56,48},{64,5... | collective-permute-start | bytes 73736 | tf_op jit(solution)/shard_map/ppermute | solution.py:601
  34.9 0.1 collective-permute-start.1
  35.0 1.2 %collective-permute-done = f32[48,128]{1,0:T(8,128)S(1)} collective-permute-done((f32[48,128]{1,0:T(8,128)S(1)}, f32[48,128]{1,0:T(8,128)S(1)}, u32[]{:S(2)}, u32[]{:S(2)}) %collective-permute-start) | collective-permute-done | bytes 24608 | tf_op jit(solution)/shard_map/ppermute | solution.py:601
  36.2 4.7 %collective-permute-done.1 = f32[48,128]{1,0:T(8,128)S(1)} collective-permute-done((f32[48,128]{1,0:T(8,128)S(1)}, f32[48,128]{1,0:T(8,128)S(1)}, u32[]{:S(2)}, u32[]{:S(2)}) %collective-permute-start.1) | collective-permute-done | bytes 24608 | tf_op jit(solution)/shard_map/ppermute | solution.py:601
  40.9 1.9 %collective-permute-start.2 = (f32[144,128]{1,0:T(8,128)S(1)}, f32[144,128]{1,0:T(8,128)S(1)}, u32[]{:S(2)}, u32[]{:S(2)}) collective-permute-start(f32[144,128]{1,0:T(8,128)S(1)} %constant_dynamic-update-slice_fusion.refs_0_), channel_id=1, source_target_pairs={{0,7},{1,0},{2,1},{3,2},{4,3},{5,4},{6,5},{7,6},{8,15},{9,8},{10,9... | collective-permute-start | bytes 221192 | tf_op jit(solution)/shard_map/ppermute | solution.py:601
  42.7 0.3 collective-permute-start.3
  43.0 13.7 %all_to_all.32.found_ref = f32[128,1,136]{2,1,0:T(1,128)S(1)} all-to-all(f32[128,1,136]{2,1,0:T(1,128)S(1)} %shard_map.71), channel_id=1, replica_groups=mesh['mesh'=16,'bg'=8] {'mesh','bg'}, dimensions={0} | all-to-all | bytes 139264 | tf_op jit(solution)/shard_map/all_to_all | solution.py:596
  56.7 5.6 %shard_map.72 = f32[56,128]{1,0:T(8,128)S(1)} custom-call(f32[128,1,136]{2,1,0:T(1,128)S(1)} %all_to_all.32.found_ref, s32[136,128]{1,0:T(8,128)} %bitcast.23), custom_call_target="tpu_custom_call" | custom-call | tf_op jit(solution)/shard_map/pallas_call | solution.py:30
  62.3 1.3 %collective-permute-start.4 = (f32[56,128]{1,0:T(8,128)S(1)}, f32[56,128]{1,0:T(8,128)S(1)}, u32[]{:S(2)}, u32[]{:S(2)}) collective-permute-start(f32[56,128]{1,0:T(8,128)S(1)} %shard_map.72), channel_id=1, source_target_pairs={{0,120},{8,0},{16,8},{24,16},{32,24},{40,32},{48,40},{56,48},{64,5... | collective-permute-start | bytes 86024 | tf_op jit(solution)/shard_map/ppermute | solution.py:601
  63.6 0.2 collective-permute-start.5
  63.9 1.2 %collective-permute-done.4 = f32[56,128]{1,0:T(8,128)S(1)} collective-permute-done((f32[56,128]{1,0:T(8,128)S(1)}, f32[56,128]{1,0:T(8,128)S(1)}, u32[]{:S(2)}, u32[]{:S(2)}) %collective-permute-start.4) | collective-permute-done | bytes 28704 | tf_op jit(solution)/shard_map/ppermute | solution.py:601
  65.1 4.6 %collective-permute-done.5 = f32[56,128]{1,0:T(8,128)S(1)} collective-permute-done((f32[56,128]{1,0:T(8,128)S(1)}, f32[56,128]{1,0:T(8,128)S(1)}, u32[]{:S(2)}, u32[]{:S(2)}) %collective-permute-start.5) | collective-permute-done | bytes 28704 | tf_op jit(solution)/shard_map/ppermute | solution.py:601
  69.7 1.8 %collective-permute-start.6 = (f32[112,128]{1,0:T(8,128)S(1)}, f32[112,128]{1,0:T(8,128)S(1)}, u32[]{:S(2)}, u32[]{:S(2)}) collective-permute-start(f32[112,128]{1,0:T(8,128)S(1)} %pad_maximum_fusion.refs_3_.refs_6_), channel_id=1, source_target_pairs={{0,7},{1,0},{2,1},{3,2},{4,3},{5,4},{6,5},{7,6},{8,15},{9,8},{10,9... | collective-permute-start | bytes 172040 | tf_op jit(solution)/shard_map/ppermute | solution.py:601
  71.5 0.3 collective-permute-start.7
  71.8 1.8 %collective-permute-done.6.refs_4_.refs_7_ = f32[112,128]{1,0:T(8,128)S(1)} collective-permute-done((f32[112,128]{1,0:T(8,128)S(1)}, f32[112,128]{1,0:T(8,128)S(1)}, u32[]{:S(2)}, u32[]{:S(2)}) %collective-permute-start.6) | collective-permute-done | bytes 57376 | tf_op jit(solution)/shard_map/ppermute | solution.py:601
  73.6 2.0 %shard_map.73 = (f32[48,128]{1,0:T(8,128)S(1)}, f32[128,128]{1,0:T(8,128)S(1)}) custom-call(f32[144,128]{1,0:T(8,128)S(1)} %constant_dynamic-update-slice_fusion.refs_0_, f32[144,128]{1,0:T(8,128)S(1)} %collective-permute-done.2.refs_1_, f32[144,128]{1,0:T(8,128)S(1)} %collective-permute-done.3.refs_2_, f32[112,128]{1,0:T(8,128)S(1)} %pad_maximum_fusion.refs_3_.refs_6_, ...), custom_call_target="tpu_custom_call" | custom-call | tf_op jit(solution)/shard_map/pallas_call | solution.py:30
  75.8 1.4 %collective-permute-start.9 = (f32[48,128]{1,0:T(8,128)S(1)}, f32[48,128]{1,0:T(8,128)S(1)}, u32[]{:S(2)}, u32[]{:S(2)}) collective-permute-start(f32[48,128]{1,0:T(8,128)S(1)} %get-tuple-element.37), channel_id=1, source_target_pairs={{0,8},{8,16},{16,24},{24,32},{32,40},{40,48},{48,56},{56,64},{64,7... | collective-permute-start | bytes 73736 | tf_op jit(solution)/shard_map/ppermute | solution.py:601
  77.2 1.2 %collective-permute-done.8 = f32[48,128]{1,0:T(8,128)S(1)} collective-permute-done((f32[48,128]{1,0:T(8,128)S(1)}, f32[48,128]{1,0:T(8,128)S(1)}, u32[]{:S(2)}, u32[]{:S(2)}) %collective-permute-start.8) | collective-permute-done | bytes 24608 | tf_op jit(solution)/shard_map/ppermute | solution.py:601
  78.4 3.4 %collective-permute-done.9 = f32[48,128]{1,0:T(8,128)S(1)} collective-permute-done((f32[48,128]{1,0:T(8,128)S(1)}, f32[48,128]{1,0:T(8,128)S(1)}, u32[]{:S(2)}, u32[]{:S(2)}) %collective-permute-start.9) | collective-permute-done | bytes 24608 | tf_op jit(solution)/shard_map/ppermute | solution.py:601
  81.8 3.9 %collective-permute-start.10 = (f32[144,128]{1,0:T(8,128)S(1)}, f32[144,128]{1,0:T(8,128)S(1)}, u32[]{:S(2)}, u32[]{:S(2)}) collective-permute-start(f32[144,128]{1,0:T(8,128)S(1)} %constant_dynamic-update-slice_fusion.3.refs_3_), channel_id=1, source_target_pairs={{0,7},{1,0},{2,1},{3,2},{4,3},{5,4},{6,5},{7,6},{8,15},{9,8},{10,9... | collective-permute-start | bytes 221192 | tf_op jit(solution)/shard_map/ppermute | solution.py:601
  85.7 13.3 %all_to_all.33 = f32[128,1,128]{2,1,0:T(1,128)S(1)} all-to-all(f32[128,1,128]{2,1,0:T(1,128)S(1)} %bitcast.20), channel_id=1, replica_groups=mesh['mesh'=16,'bg'=8] {'mesh','bg'}, dimensions={0} | all-to-all | bytes 131072 | tf_op jit(solution)/shard_map/all_to_all | solution.py:596
  99.0 3.9 %shard_map.74 = (f32[48,128]{1,0:T(8,128)S(1)}, f32[128,128]{1,0:T(8,128)}, f32[48,128]{1,0:T(8,128)S(1)}) custom-call(f32[144,128]{1,0:T(8,128)S(1)} %constant_dynamic-update-slice_fusion.refs_0_, f32[144,128]{1,0:T(8,128)S(1)} %collective-permute-done.2.refs_1_, f32[144,128]{1,0:T(8,128)S(1)} %collective-permute-done.3.refs_2_, ...), custom_call_target="tpu_custom_call" | custom-call | tf_op jit(solution)/shard_map/pallas_call | solution.py:30
  102.8 4.4 %all-to-all-start.3 = ((f32[128,1,128]{2,1,0:T(1,128)}), f32[128,1,128]{2,1,0:T(1,128)S(1)}, u32[]{:S(2)}, u32[]{:S(2)}) async-start(f32[128,1,128]{2,1,0:T(1,128)} %bitcast.10), calls=%async_computation.3 | async-start | bytes 131072 | tf_op jit(solution)/shard_map/all_to_all | solution.py:596
  107.2 0.3 shard_map.75
  107.6 9.3 %all-to-all-done.3 = f32[128,1,128]{2,1,0:T(1,128)S(1)} async-done(((f32[128,1,128]{2,1,0:T(1,128)}), f32[128,1,128]{2,1,0:T(1,128)S(1)}, u32[]{:S(2)}, u32[]{:S(2)}) %all-to-all-start.3) | async-done | bytes 65568 | tf_op jit(solution)/shard_map/all_to_all | solution.py:596
  116.9 1.8 %shard_map.76 = (f32[3,4,4,128]{3,2,1,0:T(4,128)}, f32[2,5]{1,0:T(2,128)}) custom-call(f32[3,4,4,128]{3,2,1,0:T(4,128)S(1)} %get-tuple-element.41.own_ref, f32[3,4,4,128]{3,2,1,0:T(4,128)S(1)} %get-tuple-element.42.move_ref, f32[128,128]{1,0:T(8,128)S(1)} %bitcast.18, f32[128,128]{1,0:T(8,128)S(1)} %bitcast.19), custom_call_target="tpu_custom_call" | custom-call | tf_op jit(solution)/shard_map/pallas_call | solution.py:30
  (16 shorter events, 0.1 us)
Async XLA Ops:
  2.6 23.1 %all-to-all-start = ((f32[128,1,640]{2,1,0:T(1,128)}), f32[128,1,640]{2,1,0:T(1,128)S(1)}, u32[]{:S(2)}, u32[]{:S(2)}) async-start(f32[128,1,640]{2,1,0:T(1,128)} %shard_map.68), calls=%async_computation | async-start | bytes 655360 | tf_op jit(solution)/shard_map/all_to_all | solution.py:596
  33.5 2.7 %collective-permute-start = (f32[48,128]{1,0:T(8,128)S(1)}, f32[48,128]{1,0:T(8,128)S(1)}, u32[]{:S(2)}, u32[]{:S(2)}) collective-permute-start(f32[48,128]{1,0:T(8,128)S(1)} %shard_map.70), channel_id=1, source_target_pairs={{0,120},{8,0},{16,8},{24,16},{32,24},{40,32},{48,40},{56,48},{64,5... | collective-permute-start | bytes 73736 | tf_op jit(solution)/shard_map/ppermute | solution.py:601
  34.9 6.0 %collective-permute-start.1 = (f32[48,128]{1,0:T(8,128)S(1)}, f32[48,128]{1,0:T(8,128)S(1)}, u32[]{:S(2)}, u32[]{:S(2)}) collective-permute-start(f32[48,128]{1,0:T(8,128)S(1)} %shard_map.70), channel_id=1, source_target_pairs={{0,8},{8,16},{16,24},{24,32},{32,40},{40,48},{48,56},{56,64},{64,7... | collective-permute-start | bytes 73736 | tf_op jit(solution)/shard_map/ppermute | solution.py:601
  40.9 15.9 %collective-permute-start.2 = (f32[144,128]{1,0:T(8,128)S(1)}, f32[144,128]{1,0:T(8,128)S(1)}, u32[]{:S(2)}, u32[]{:S(2)}) collective-permute-start(f32[144,128]{1,0:T(8,128)S(1)} %constant_dynamic-update-slice_fusion.refs_0_), channel_id=1, source_target_pairs={{0,7},{1,0},{2,1},{3,2},{4,3},{5,4},{6,5},{7,6},{8,15},{9,8},{10,9... | collective-permute-start | bytes 221192 | tf_op jit(solution)/shard_map/ppermute | solution.py:601
  42.7 14.0 %collective-permute-start.3 = (f32[144,128]{1,0:T(8,128)S(1)}, f32[144,128]{1,0:T(8,128)S(1)}, u32[]{:S(2)}, u32[]{:S(2)}) collective-permute-start(f32[144,128]{1,0:T(8,128)S(1)} %constant_dynamic-update-slice_fusion.refs_0_), channel_id=1, source_target_pairs={{0,1},{1,2},{2,3},{3,4},{4,5},{5,6},{6,7},{7,0},{8,9},{9,10},{10,1... | collective-permute-start | bytes 221192 | tf_op jit(solution)/shard_map/ppermute | solution.py:601
  62.3 2.8 %collective-permute-start.4 = (f32[56,128]{1,0:T(8,128)S(1)}, f32[56,128]{1,0:T(8,128)S(1)}, u32[]{:S(2)}, u32[]{:S(2)}) collective-permute-start(f32[56,128]{1,0:T(8,128)S(1)} %shard_map.72), channel_id=1, source_target_pairs={{0,120},{8,0},{16,8},{24,16},{32,24},{40,32},{48,40},{56,48},{64,5... | collective-permute-start | bytes 86024 | tf_op jit(solution)/shard_map/ppermute | solution.py:601
  63.6 6.0 %collective-permute-start.5 = (f32[56,128]{1,0:T(8,128)S(1)}, f32[56,128]{1,0:T(8,128)S(1)}, u32[]{:S(2)}, u32[]{:S(2)}) collective-permute-start(f32[56,128]{1,0:T(8,128)S(1)} %shard_map.72), channel_id=1, source_target_pairs={{0,8},{8,16},{16,24},{24,32},{32,40},{40,48},{48,56},{56,64},{64,7... | collective-permute-start | bytes 86024 | tf_op jit(solution)/shard_map/ppermute | solution.py:601
  69.7 4.0 %collective-permute-start.6 = (f32[112,128]{1,0:T(8,128)S(1)}, f32[112,128]{1,0:T(8,128)S(1)}, u32[]{:S(2)}, u32[]{:S(2)}) collective-permute-start(f32[112,128]{1,0:T(8,128)S(1)} %pad_maximum_fusion.refs_3_.refs_6_), channel_id=1, source_target_pairs={{0,7},{1,0},{2,1},{3,2},{4,3},{5,4},{6,5},{7,6},{8,15},{9,8},{10,9... | collective-permute-start | bytes 172040 | tf_op jit(solution)/shard_map/ppermute | solution.py:601
  71.5 2.1 %collective-permute-start.7 = (f32[112,128]{1,0:T(8,128)S(1)}, f32[112,128]{1,0:T(8,128)S(1)}, u32[]{:S(2)}, u32[]{:S(2)}) collective-permute-start(f32[112,128]{1,0:T(8,128)S(1)} %pad_maximum_fusion.refs_3_.refs_6_), channel_id=1, source_target_pairs={{0,1},{1,2},{2,3},{3,4},{4,5},{5,6},{6,7},{7,0},{8,9},{9,10},{10,1... | collective-permute-start | bytes 172040 | tf_op jit(solution)/shard_map/ppermute | solution.py:601
  75.7 2.7 %collective-permute-start.8 = (f32[48,128]{1,0:T(8,128)S(1)}, f32[48,128]{1,0:T(8,128)S(1)}, u32[]{:S(2)}, u32[]{:S(2)}) collective-permute-start(f32[48,128]{1,0:T(8,128)S(1)} %get-tuple-element.37), channel_id=1, source_target_pairs={{0,120},{8,0},{16,8},{24,16},{32,24},{40,32},{48,40},{56,48},{64,5... | collective-permute-start | bytes 73736 | tf_op jit(solution)/shard_map/ppermute | solution.py:601
  75.8 6.1 %collective-permute-start.9 = (f32[48,128]{1,0:T(8,128)S(1)}, f32[48,128]{1,0:T(8,128)S(1)}, u32[]{:S(2)}, u32[]{:S(2)}) collective-permute-start(f32[48,128]{1,0:T(8,128)S(1)} %get-tuple-element.37), channel_id=1, source_target_pairs={{0,8},{8,16},{16,24},{24,32},{32,40},{40,48},{48,56},{56,64},{64,7... | collective-permute-start | bytes 73736 | tf_op jit(solution)/shard_map/ppermute | solution.py:601
  81.8 17.1 %collective-permute-start.10 = (f32[144,128]{1,0:T(8,128)S(1)}, f32[144,128]{1,0:T(8,128)S(1)}, u32[]{:S(2)}, u32[]{:S(2)}) collective-permute-start(f32[144,128]{1,0:T(8,128)S(1)} %constant_dynamic-update-slice_fusion.3.refs_3_), channel_id=1, source_target_pairs={{0,7},{1,0},{2,1},{3,2},{4,3},{5,4},{6,5},{7,6},{8,15},{9,8},{10,9... | collective-permute-start | bytes 221192 | tf_op jit(solution)/shard_map/ppermute | solution.py:601
  85.7 13.3 %collective-permute-start.11 = (f32[144,128]{1,0:T(8,128)S(1)}, f32[144,128]{1,0:T(8,128)S(1)}, u32[]{:S(2)}, u32[]{:S(2)}) collective-permute-start(f32[144,128]{1,0:T(8,128)S(1)} %constant_dynamic-update-slice_fusion.3.refs_3_), channel_id=1, source_target_pairs={{0,1},{1,2},{2,3},{3,4},{4,5},{5,6},{6,7},{7,0},{8,9},{9,10},{10,1... | collective-permute-start | bytes 221192 | tf_op jit(solution)/shard_map/ppermute | solution.py:601
  102.8 14.0 %all-to-all-start.3 = ((f32[128,1,128]{2,1,0:T(1,128)}), f32[128,1,128]{2,1,0:T(1,128)S(1)}, u32[]{:S(2)}, u32[]{:S(2)}) async-start(f32[128,1,128]{2,1,0:T(1,128)} %bitcast.10), calls=%async_computation.3 | async-start | bytes 131072 | tf_op jit(solution)/shard_map/all_to_all | solution.py:596

commit v5 on v4

--- a/solution.py
+++ b/solution.py
@@ -14,8 +14,8 @@
 COLS = 256
 
 
-GATHER_ROWS = 80
-ROUNDS = 10
+GATHER_ROWS = 64
+ROUNDS = 8
 
 
 def in_vmem(count):
@@ -115,13 +115,12 @@
             coef = whole.astype(jnp.float32) * unit
             result_ref[pl.ds(base + r, 1), :] = weigh(coef, xs[r : r + 1], ys[r : r + 1], zs[r : r + 1])
 
-        start = jnp.minimum(GATHER_ROWS + i * 6, SLOTS - 6)
-        for pair in range(3):
+        start = GATHER_ROWS + i * 9
+        for pair in range(5):
             at = start + 2 * pair
+            wide = 2 if pair < 4 else 1
             pair_ids, px, py, pz = (
-                jnp.concatenate(
-                    [turned_ref[pl.ds(j * SLOTS + at, 1), :], turned_ref[pl.ds(j * SLOTS + at + 1, 1), :]], axis=1
-                )
+                jnp.concatenate([turned_ref[pl.ds(j * SLOTS + at + k, 1), :] for k in range(wide)], axis=1)
                 for j in range(4)
             )
             pair_ids = pair_ids.astype(jnp.int32)
@@ -129,19 +128,19 @@
             chosen = jnp.concatenate(
                 [
                     jnp.where(column_ref[...] == column[:, half * 128 : half * 128 + 128], one, zero)
-                    for half in range(2)
+                    for half in range(wide)
                 ],
                 axis=1,
             )
             picked = jnp.dot(split_ref[:, :COLS], chosen, preferred_element_type=jnp.float32) + jnp.dot(
                 split_ref[:, COLS:], chosen, preferred_element_type=jnp.float32
             )
-            own = jnp.broadcast_to(pair_ids, (8, 256))
+            own = jnp.broadcast_to(pair_ids, (8, 128 * wide))
             masks = [(own & (COLS << bit)) != 0 for bit in range(6)]
             coef = choose(lambda row: picked[row * 8 : row * 8 + 8], masks, 0, 64)
             value = weigh(coef, px, py, pz)
-            result_ref[pl.ds(at, 1), :] = value[:, :128]
-            result_ref[pl.ds(at + 1, 1), :] = value[:, 128:]
+            for k in range(wide):
+                result_ref[pl.ds(at + k, 1), :] = value[:, k * 128 : k * 128 + 128]
         return carry
 
     lax.fori_loop(0, ROUNDS, step, 0)
@@ -180,10 +179,9 @@
     zero = jnp.zeros((), jnp.bfloat16)
 
     def step(i, total):
-        base = pl.multiple_of(i * 8, 8)
-        values = value_ref[pl.ds(base, 8), :]
-        rows = row_ref[pl.ds(base, 8), :]
-        lanes = lane_ref[pl.ds(base, 8), :]
+        values = value_ref[i * 8 : i * 8 + 8, :]
+        rows = row_ref[i * 8 : i * 8 + 8, :]
+        lanes = lane_ref[i * 8 : i * 8 + 8, :]
         left, right = [], []
         for r in range(8):
             value = values[r : r + 1]
@@ -196,7 +194,9 @@
         right = jnp.concatenate(right, axis=1)
         return total + lax.dot_general(left, right, (((1,), (1,)), ((), ())), preferred_element_type=jnp.float32)
 
-    total = lax.fori_loop(0, SLOTS // 8, step, jnp.zeros((128, 128), jnp.float32))
+    total = jnp.zeros((128, 128), jnp.float32)
+    for i in range(SLOTS // 8):
+        total = step(i, total)
     size_ref[...] = total[:56] + total[64:120]
 
 
@@ -214,7 +214,8 @@
 
 
 def size_pieces(refs):
-    return {(z, y): (refs[y], 56 * abs(z)) for z in (-1, 0, 1) for y in (-1, 0, 1)}
+    own, z_low, y_low, corner = refs
+    return {(0, 0): own, (-1, 0): z_low, (0, -1): y_low, (-1, -1): corner}
 
 
 def lane_index():
@@ -372,20 +373,17 @@
 
 def ring(pieces, count, out_ref, out_at, z_shift, y_shift):
     low = lax.broadcasted_iota(jnp.int32, (count, 128), 1) < 64
-    places = ((-1, 1), (0, 0), (0, 1), (1, 0)) if not y_shift else ((0, 0), (0, 1), (1, 0), (1, 1))
+    places = ((-1, 1), (0, 0), (0, 1), (1, 0)) if y_shift else ((-1, 0), (-1, 1), (0, 0), (0, 1))
     for upper in range(2):
         for y, (piece_y, row) in enumerate(places):
-            here, below, above = (
-                ref[pl.ds(at + row, count, stride=2), :] for ref, at in (pieces[z, piece_y] for z in (0, -1, 1))
-            )
+
+            def piece(z):
+                ref, at = pieces[z, piece_y]
+                return ref[pl.ds(at + row, count, stride=2), :]
+
+            value = piece(-upper)
             if z_shift:
-                here = pltpu.roll(here, 64, 1)
-                above = pltpu.roll(above, 64, 1)
-                value = jnp.where(low, above, here) if upper else jnp.where(low, here, above)
-            elif upper:
-                value = jnp.where(low, above, below)
-            else:
-                value = here
+                value = jnp.where(low, pltpu.roll(value, 64, 1), pltpu.roll(piece(1 - upper), 64, 1))
             out_ref[pl.ds(out_at + upper * 4 + y, count, stride=8), :] = value
 
 
@@ -394,7 +392,7 @@
     field_refs = [refs.pop(0) for _ in range(3)]
     if not first:
         shift_refs = [refs.pop(0) for _ in range(3)]
-    sizes = size_pieces([refs.pop(0) for _ in range(3)])
+    sizes = {at: (ref, 0) for at, ref in size_pieces([refs.pop(0) for _ in range(4)]).items()}
     if first:
         move_ref, terms_out, nodes_ref, size_ref, jac_ref, part_ref, turn_ref = refs
         field = field_pieces(field_refs)
@@ -429,8 +427,9 @@
         shift = y // 2
         value = packed(node, 0, shift)
         if z == 2:
-            turned = pltpu.roll(value, 64, 1)
-            value = jnp.where(lane_index() < 64, turned, pltpu.roll(packed(node, 1, shift), 64, 1))
+            value = pltpu.roll(value, 64, 1)
+        else:
+            value = jnp.where(lane_index() < 64, value, packed(node, 1, shift))
         return x_up(value) if x == 2 else value
 
     def each(body):
@@ -461,8 +460,11 @@
     each(stress)
     each(lambda c: backward(c, part_ref, turn_ref))
     for row in range(2):
-        move_ref[pl.ds(row, 24, stride=2), :] = turn_ref[pl.ds(row + 1, 24, stride=8), :]
+        move_ref[pl.ds(row, 24, stride=2), :] = turn_ref[pl.ds(row + 2, 24, stride=8), :]
     forward(sought, part_ref, lambda k, jz, jy, jx: pl.ds(((jz * 9 + jy * 3 + jx) * 3 + k) * 8, 8))
+
+    def middle(ref, at, stride):
+        return jnp.where(lane_index() < 64, ref[pl.ds(at, 8, stride=stride), :], ref[pl.ds(at + 4, 8, stride=stride), :])
 
     sub = lax.broadcasted_iota(jnp.int32, (8, 128), 0)
     sums = [jnp.zeros((8, 128), jnp.float32) for _ in range(6)]
@@ -474,7 +476,7 @@
             weight = jnp.where(sub == i, (parts[0] * parts[1]) * parts[2], weight)
         for ey in range(2):
             jac = [
-                [jac_ref[pl.ds((start * 9 + c * 3 + k) * 8 + 1 + ey, 8, stride=72), :] for k in range(3)]
+                [middle(jac_ref, (start * 9 + c * 3 + k) * 8 + 1 + ey, 72) for k in range(3)]
                 for c in range(3)
             ]
             jac = [[jac[c][k] + 1.0 if c == k else jac[c][k] for k in range(3)] for c in range(3)]
@@ -482,7 +484,7 @@
                 [part_ref[pl.ds((start * 3 + k) * 8 + ey * 4 + c, 8, stride=24), :] for k in range(3)]
                 for c in range(3)
             ]
-            size = size_ref[pl.ds(start * 8 + 1 + ey, 8, stride=8), :]
+            size = middle(size_ref, start * 8 + 1 + ey, 8)
             zero = strain_of(jac, size)
             one = symmetric(lambda k, l: (column_dot(jac, motion, k, l) + column_dot(motion, jac, k, l)) * size)
             two = symmetric(lambda k, l: column_dot(motion, motion, k, l) * size)
@@ -601,13 +603,16 @@
     return lax.ppermute(values, axis, [(i, (i - by) % count) for i in range(count)])
 
 
-def along_mesh(block, merge):
-    low, high = moved(block, "mesh", -1), moved(block, "mesh", 1)
-    if merge:
-        sides = [jnp.where(lax.broadcasted_iota(jnp.int32, block.shape, 1) < 64, high, low)]
-    else:
-        sides = [high, low]
-    return jnp.concatenate([block] + sides, axis=0)
+def along_mesh(block):
+    return jnp.concatenate([block, moved(block, "mesh", 1), moved(block, "mesh", -1)], axis=0)
+
+
+def from_below(block):
+    mesh, bg = lax.axis_size("mesh"), lax.axis_size("bg")
+    steps = [
+        (z * bg + y, ((z + 1) % mesh) * bg + (y + 1) % bg) for z in range(mesh) for y in range(bg)
+    ]
+    return [block, moved(block, "mesh", -1), moved(block, "bg", -1), lax.ppermute(block, ("mesh", "bg"), steps)]
 
 
 def along_bg(rows):
@@ -617,15 +622,16 @@
 def shards(displacement, bg_coef, query_elem, query_point, query_coord):
     asked = exchange(pack(query_elem[0].T, query_coord[0].transpose(1, 2, 0)))
     own = split_nodes(displacement)
-    asked, prepared, own = lax.optimization_barrier((asked, prepare(bg_coef), own))
-    found, own = lax.optimization_barrier((lookup(asked, prepared), own))
+    rows = along_mesh(own)
+    asked, prepared, rows = lax.optimization_barrier((asked, prepare(bg_coef), rows))
+    found, rows = lax.optimization_barrier((lookup(asked, prepared), rows))
     found = exchange(found)
-    field = along_bg(along_mesh(own, False))
+    field = along_bg(rows)
     found, field = lax.optimization_barrier((found, field))
-    sizes = along_bg(along_mesh(place(found, query_point[0].T), True))
+    sizes = from_below(place(found, query_point[0].T))
     move, terms = newton_pass(field, None, sizes, None)
     first_terms = exchange(terms)
-    shift = along_bg(along_mesh(move, False))
+    shift = along_bg(along_mesh(move))
     last_move, last_terms, last_own = newton_pass(field, shift, sizes, first_terms)
     own, move = join_nodes(last_own, last_move)
     last_terms = exchange(last_terms)

time: 119 us -> 112 us (0.941)
  waiting for transfers between devices: 36.5 us -> 20 us
  blocking collectives: 26.9 us -> 35.5 us
  starting transfers between devices: 28.6 us -> 32 us
  Pallas kernels: 25.8 us -> 23 us
    ppermute x12 -> x10, waiting for transfers between devices: 18.1 us -> 2.78 us  [moved(): lax.ppermute(values, axis, [(i, (i - by) % count) for i in range(count)])]
    all_to_all x2, blocking collectives: 26.9 us -> 35.5 us  [exchange(): lax.all_to_all(values, ('mesh', 'bg'), split_axis=0, concat_axis=0, tiled...]
    all_to_all x2, waiting for transfers between devices: 18.4 us -> 11.7 us  [exchange(): lax.all_to_all(values, ('mesh', 'bg'), split_axis=0, concat_axis=0, tiled...]
    ppermute x0 -> x1, waiting for transfers between devices: none -> 5.56 us  [from_below(): lax.ppermute(block, ('mesh', 'bg'), steps)]
    pallas_call x9, Pallas kernels: 25.8 us -> 23 us  [call(): pl.pallas_call(kernel, out_shape=outs, in_specs=in_vmem(len(args)), out_s...]
    ppermute x12 -> x10, starting transfers between devices: 12.7 us -> 15.4 us  [moved(): lax.ppermute(values, axis, [(i, (i - by) % count) for i in range(count)])]
  transfers between devices with their start and end apart: 14 -> 13, of which waited for: 9 -> 7; matrix products, arithmetic and copies ran while one was open for 0% -> 0% of each run, Pallas kernels for 2% -> 3%
where the time goes in v5:
time: 112 us; the launch traced here: 111 us
  blocking collectives  35.5 us (32%)
  starting transfers between devices  32 us (29%)
  Pallas kernels  23 us (21%)
  waiting for transfers between devices  20 us (18%)
    all_to_all x2, blocking collectives, exchange(): lax.all_to_all(values, ('mesh', 'bg'), split_axis=0, concat_axis=0, tiled...  35.5 us
    pallas_call x9, Pallas kernels, call(): pl.pallas_call(kernel, out_shape=outs, in_specs=in_vmem(len(args)), out_s...  23 us
    all_to_all x2, starting transfers between devices, exchange(): lax.all_to_all(values, ('mesh', 'bg'), split_axis=0, concat_axis=0, tiled...  15.9 us
    ppermute x10, starting transfers between devices, moved(): lax.ppermute(values, axis, [(i, (i - by) % count) for i in range(count)])  15.4 us
    all_to_all x2, waiting for transfers between devices, exchange(): lax.all_to_all(values, ('mesh', 'bg'), split_axis=0, concat_axis=0, tiled...  11.7 us
    ppermute x1, waiting for transfers between devices, from_below(): lax.ppermute(block, ('mesh', 'bg'), steps)  5.56 us
    ppermute x10, waiting for transfers between devices, moved(): lax.ppermute(values, axis, [(i, (i - by) % count) for i in range(count)])  2.78 us
  transfers between devices with their start and end apart: 13, of which 7 were waited for; matrix products, arithmetic and copies ran while one was open for 0% of the time, Pallas kernels for 3%

profile of v5, /device:TPU:1, one launch (start us, length us, event | category | flops | bytes accessed | tf_op | source)
XLA Modules:
  0.0 111.3 jit_solution(7529967137664644351)
XLA Ops:
  0.6 1.9 %shard_map.68 = f32[128,1,640]{2,1,0:T(1,128)} custom-call(s32[136,128]{1,0:T(8,128)} %bitcast.22, f32[3,136,128]{2,1,0:T(8,128)} %bitcast.21), custom_call_target="tpu_custom_call" | custom-call | tf_op jit(solution)/shard_map/pallas_call | solution.py:30
  2.6 11.5 %all-to-all-start = ((f32[128,1,640]{2,1,0:T(1,128)}), f32[128,1,640]{2,1,0:T(1,128)S(1)}, u32[]{:S(2)}, u32[]{:S(2)}) async-start(f32[128,1,640]{2,1,0:T(1,128)} %shard_map.68), calls=%async_computation | async-start | bytes 655360 | tf_op jit(solution)/shard_map/all_to_all | solution.py:598
  14.1 1.0 shard_map.70
  15.1 1.4 %collective-permute-start.1 = (f32[48,128]{1,0:T(8,128)S(1)}, f32[48,128]{1,0:T(8,128)S(1)}, u32[]{:S(2)}, u32[]{:S(2)}) collective-permute-start(f32[48,128]{1,0:T(8,128)S(1)} %shard_map.70), channel_id=1, source_target_pairs={{0,8},{8,16},{16,24},{24,32},{32,40},{40,48},{48,56},{56,64},{64,7... | collective-permute-start | bytes 73736 | tf_op jit(solution)/shard_map/ppermute | solution.py:603
  16.5 4.1 %collective-permute-start = (f32[48,128]{1,0:T(8,128)S(1)}, f32[48,128]{1,0:T(8,128)S(1)}, u32[]{:S(2)}, u32[]{:S(2)}) collective-permute-start(f32[48,128]{1,0:T(8,128)S(1)} %shard_map.70), channel_id=1, source_target_pairs={{0,120},{8,0},{16,8},{24,16},{32,24},{40,32},{48,40},{56,48},{64,5... | collective-permute-start | bytes 73736 | tf_op jit(solution)/shard_map/ppermute | solution.py:603
  20.6 1.5 %shard_map.69 = (bf16[512,512]{1,0:T(8,128)(2,1)S(1)}, s32[8,8192]{1,0:T(8,128)S(1)}, f32[8,128]{1,0:T(8,128)S(1)}) custom-call(f32[8,16384]{1,0:T(8,128)} %table_ref.1), custom_call_target="tpu_custom_call" | custom-call | tf_op jit(solution)/shard_map/pallas_call | solution.py:30
  22.1 1.3 %collective-permute-done.1 = f32[48,128]{1,0:T(8,128)S(1)} collective-permute-done((f32[48,128]{1,0:T(8,128)S(1)}, f32[48,128]{1,0:T(8,128)S(1)}, u32[]{:S(2)}, u32[]{:S(2)}) %collective-permute-start.1) | collective-permute-done | bytes 24608 | tf_op jit(solution)/shard_map/ppermute | solution.py:603
  23.4 2.4 %all-to-all-done.asked_ref = f32[128,1,640]{2,1,0:T(1,128)S(1)} async-done(((f32[128,1,640]{2,1,0:T(1,128)}), f32[128,1,640]{2,1,0:T(1,128)S(1)}, u32[]{:S(2)}, u32[]{:S(2)}) %all-to-all-start) | async-done | bytes 327712 | tf_op jit(solution)/shard_map/all_to_all | solution.py:598
  25.9 7.6 %shard_map.71 = f32[128,1,136]{2,1,0:T(1,128)S(1)} custom-call(f32[128,1,640]{2,1,0:T(1,128)S(1)} %all-to-all-done.asked_ref, bf16[512,512]{1,0:T(8,128)(2,1)S(1)} %get-tuple-element.27.split_ref, s32[8,8192]{1,0:T(8,128)S(1)} %get-tuple-element.28.packed_ref, f32[8,128]{1,0:T(8,128)S(1)} %get-tuple-element.29.unit_ref), custom_call_target="tpu_custom_call" | custom-call | tf_op jit(solution)/shard_map/pallas_call | solution.py:30
  33.4 1.0 collective-permute-start.3
  34.4 0.0 collective-permute-start.2
  34.4 16.8 %all_to_all.32.found_ref = f32[128,1,136]{2,1,0:T(1,128)S(1)} all-to-all(f32[128,1,136]{2,1,0:T(1,128)S(1)} %shard_map.71), channel_id=1, replica_groups=mesh['mesh'=16,'bg'=8] {'mesh','bg'}, dimensions={0} | all-to-all | bytes 139264 | tf_op jit(solution)/shard_map/all_to_all | solution.py:598
  51.3 0.0 collective-permute-done.3.refs_2_
  51.3 2.8 %shard_map.72.refs_3_.refs_6_ = f32[56,128]{1,0:T(8,128)S(1)} custom-call(f32[128,1,136]{2,1,0:T(1,128)S(1)} %all_to_all.32.found_ref, s32[136,128]{1,0:T(8,128)} %bitcast.23), custom_call_target="tpu_custom_call" | custom-call | tf_op jit(solution)/shard_map/pallas_call | solution.py:30
  54.1 0.7 collective-permute-start.6
  54.8 0.3 collective-permute-start.5
  55.1 0.4 collective-permute-start.4
  55.5 5.6 %collective-permute-done.6.refs_6_.refs_9_ = f32[56,128]{1,0:T(8,128)S(1)} collective-permute-done((f32[56,128]{1,0:T(8,128)S(1)}, f32[56,128]{1,0:T(8,128)S(1)}, u32[]{:S(2)}, u32[]{:S(2)}) %collective-permute-start.6) | collective-permute-done | bytes 28704 | tf_op jit(solution)/shard_map/ppermute | solution.py:615
  61.1 0.2 collective-permute-done.4.refs_4_.refs_7_
  61.3 2.1 %shard_map.73 = (f32[48,128]{1,0:T(8,128)S(1)}, f32[128,128]{1,0:T(8,128)S(1)}) custom-call(f32[144,128]{1,0:T(8,128)S(1)} %pad_maximum_fusion.refs_0_, f32[144,128]{1,0:T(8,128)S(1)} %collective-permute-done.2.refs_1_, f32[144,128]{1,0:T(8,128)S(1)} %collective-permute-done.3.refs_2_, f32[56,128]{1,0:T(8,128)S(1)} %shard_map.72.refs_3_.refs_6_, ...), custom_call_target="tpu_custom_call" | custom-call | tf_op jit(solution)/shard_map/pallas_call | solution.py:30
  63.4 0.1 collective-permute-start.8
  63.5 4.8 %collective-permute-start.7 = (f32[48,128]{1,0:T(8,128)S(1)}, f32[48,128]{1,0:T(8,128)S(1)}, u32[]{:S(2)}, u32[]{:S(2)}) collective-permute-start(f32[48,128]{1,0:T(8,128)S(1)} %get-tuple-element.37), channel_id=1, source_target_pairs={{0,120},{8,0},{16,8},{24,16},{32,24},{40,32},{48,40},{56,48},{64,5... | collective-permute-start | bytes 73736 | tf_op jit(solution)/shard_map/ppermute | solution.py:603
  68.3 0.9 collective-permute-done.7
  69.2 0.3 collective-permute-done.8
  69.5 2.7 %collective-permute-start.10 = (f32[144,128]{1,0:T(8,128)S(1)}, f32[144,128]{1,0:T(8,128)S(1)}, u32[]{:S(2)}, u32[]{:S(2)}) collective-permute-start(f32[144,128]{1,0:T(8,128)S(1)} %constant_dynamic-update-slice_fusion.refs_3_), channel_id=1, source_target_pairs={{0,1},{1,2},{2,3},{3,4},{4,5},{5,6},{6,7},{7,0},{8,9},{9,10},{10,1... | collective-permute-start | bytes 221192 | tf_op jit(solution)/shard_map/ppermute | solution.py:603
  72.2 0.6 collective-permute-start.9
  72.8 18.7 %all_to_all.33 = f32[128,1,128]{2,1,0:T(1,128)S(1)} all-to-all(f32[128,1,128]{2,1,0:T(1,128)S(1)} %bitcast.20), channel_id=1, replica_groups=mesh['mesh'=16,'bg'=8] {'mesh','bg'}, dimensions={0} | all-to-all | bytes 131072 | tf_op jit(solution)/shard_map/all_to_all | solution.py:598
  91.5 3.9 %shard_map.74 = (f32[48,128]{1,0:T(8,128)S(1)}, f32[128,128]{1,0:T(8,128)}, f32[48,128]{1,0:T(8,128)S(1)}) custom-call(f32[144,128]{1,0:T(8,128)S(1)} %pad_maximum_fusion.refs_0_, f32[144,128]{1,0:T(8,128)S(1)} %collective-permute-done.2.refs_1_, f32[144,128]{1,0:T(8,128)S(1)} %collective-permute-done.3.refs_2_, ...), custom_call_target="tpu_custom_call" | custom-call | tf_op jit(solution)/shard_map/pallas_call | solution.py:30
  95.4 4.4 %all-to-all-start.3 = ((f32[128,1,128]{2,1,0:T(1,128)}), f32[128,1,128]{2,1,0:T(1,128)S(1)}, u32[]{:S(2)}, u32[]{:S(2)}) async-start(f32[128,1,128]{2,1,0:T(1,128)} %bitcast.10), calls=%async_computation.3 | async-start | bytes 131072 | tf_op jit(solution)/shard_map/all_to_all | solution.py:598
  99.8 0.3 shard_map.75
  100.2 9.3 %all-to-all-done.3 = f32[128,1,128]{2,1,0:T(1,128)S(1)} async-done(((f32[128,1,128]{2,1,0:T(1,128)}), f32[128,1,128]{2,1,0:T(1,128)S(1)}, u32[]{:S(2)}, u32[]{:S(2)}) %all-to-all-start.3) | async-done | bytes 65568 | tf_op jit(solution)/shard_map/all_to_all | solution.py:598
  109.5 1.8 %shard_map.76 = (f32[3,4,4,128]{3,2,1,0:T(4,128)}, f32[2,5]{1,0:T(2,128)}) custom-call(f32[3,4,4,128]{3,2,1,0:T(4,128)S(1)} %get-tuple-element.41.own_ref, f32[3,4,4,128]{3,2,1,0:T(4,128)S(1)} %get-tuple-element.42.move_ref, f32[128,128]{1,0:T(8,128)S(1)} %bitcast.18, f32[128,128]{1,0:T(8,128)S(1)} %bitcast.19), custom_call_target="tpu_custom_call" | custom-call | tf_op jit(solution)/shard_map/pallas_call | solution.py:30
  (9 shorter events, 0.0 us)
Async XLA Ops:
  2.6 23.3 %all-to-all-start = ((f32[128,1,640]{2,1,0:T(1,128)}), f32[128,1,640]{2,1,0:T(1,128)S(1)}, u32[]{:S(2)}, u32[]{:S(2)}) async-start(f32[128,1,640]{2,1,0:T(1,128)} %shard_map.68), calls=%async_computation | async-start | bytes 655360 | tf_op jit(solution)/shard_map/all_to_all | solution.py:598
  15.1 8.3 %collective-permute-start.1 = (f32[48,128]{1,0:T(8,128)S(1)}, f32[48,128]{1,0:T(8,128)S(1)}, u32[]{:S(2)}, u32[]{:S(2)}) collective-permute-start(f32[48,128]{1,0:T(8,128)S(1)} %shard_map.70), channel_id=1, source_target_pairs={{0,8},{8,16},{16,24},{24,32},{32,40},{40,48},{48,56},{56,64},{64,7... | collective-permute-start | bytes 73736 | tf_op jit(solution)/shard_map/ppermute | solution.py:603
  16.5 6.9 %collective-permute-start = (f32[48,128]{1,0:T(8,128)S(1)}, f32[48,128]{1,0:T(8,128)S(1)}, u32[]{:S(2)}, u32[]{:S(2)}) collective-permute-start(f32[48,128]{1,0:T(8,128)S(1)} %shard_map.70), channel_id=1, source_target_pairs={{0,120},{8,0},{16,8},{24,16},{32,24},{40,32},{48,40},{56,48},{64,5... | collective-permute-start | bytes 73736 | tf_op jit(solution)/shard_map/ppermute | solution.py:603
  33.4 17.8 %collective-permute-start.3 = (f32[144,128]{1,0:T(8,128)S(1)}, f32[144,128]{1,0:T(8,128)S(1)}, u32[]{:S(2)}, u32[]{:S(2)}) collective-permute-start(f32[144,128]{1,0:T(8,128)S(1)} %pad_maximum_fusion.refs_0_), channel_id=1, source_target_pairs={{0,1},{1,2},{2,3},{3,4},{4,5},{5,6},{6,7},{7,0},{8,9},{9,10},{10,1... | collective-permute-start | bytes 221192 | tf_op jit(solution)/shard_map/ppermute | solution.py:603
  34.4 16.8 %collective-permute-start.2 = (f32[144,128]{1,0:T(8,128)S(1)}, f32[144,128]{1,0:T(8,128)S(1)}, u32[]{:S(2)}, u32[]{:S(2)}) collective-permute-start(f32[144,128]{1,0:T(8,128)S(1)} %pad_maximum_fusion.refs_0_), channel_id=1, source_target_pairs={{0,7},{1,0},{2,1},{3,2},{4,3},{5,4},{6,5},{7,6},{8,15},{9,8},{10,9... | collective-permute-start | bytes 221192 | tf_op jit(solution)/shard_map/ppermute | solution.py:603
  54.1 7.0 %collective-permute-start.6 = (f32[56,128]{1,0:T(8,128)S(1)}, f32[56,128]{1,0:T(8,128)S(1)}, u32[]{:S(2)}, u32[]{:S(2)}) collective-permute-start(f32[56,128]{1,0:T(8,128)S(1)} %shard_map.72.refs_3_.refs_6_), channel_id=1, source_target_pairs={{0,9},{1,10},{2,11},{3,12},{4,13},{5,14},{6,15},{7,8},{8,17},{9,18... | collective-permute-start | bytes 86024 | tf_op jit(solution)/shard_map/ppermute | solution.py:615
  54.8 6.3 %collective-permute-start.5 = (f32[56,128]{1,0:T(8,128)S(1)}, f32[56,128]{1,0:T(8,128)S(1)}, u32[]{:S(2)}, u32[]{:S(2)}) collective-permute-start(f32[56,128]{1,0:T(8,128)S(1)} %shard_map.72.refs_3_.refs_6_), channel_id=1, source_target_pairs={{0,1},{1,2},{2,3},{3,4},{4,5},{5,6},{6,7},{7,0},{8,9},{9,10},{10,1... | collective-permute-start | bytes 86024 | tf_op jit(solution)/shard_map/ppermute | solution.py:603
  55.1 6.2 %collective-permute-start.4 = (f32[56,128]{1,0:T(8,128)S(1)}, f32[56,128]{1,0:T(8,128)S(1)}, u32[]{:S(2)}, u32[]{:S(2)}) collective-permute-start(f32[56,128]{1,0:T(8,128)S(1)} %shard_map.72.refs_3_.refs_6_), channel_id=1, source_target_pairs={{0,8},{8,16},{16,24},{24,32},{32,40},{40,48},{48,56},{56,64},{64,7... | collective-permute-start | bytes 86024 | tf_op jit(solution)/shard_map/ppermute | solution.py:603
  63.4 6.1 %collective-permute-start.8 = (f32[48,128]{1,0:T(8,128)S(1)}, f32[48,128]{1,0:T(8,128)S(1)}, u32[]{:S(2)}, u32[]{:S(2)}) collective-permute-start(f32[48,128]{1,0:T(8,128)S(1)} %get-tuple-element.37), channel_id=1, source_target_pairs={{0,8},{8,16},{16,24},{24,32},{32,40},{40,48},{48,56},{56,64},{64,7... | collective-permute-start | bytes 73736 | tf_op jit(solution)/shard_map/ppermute | solution.py:603
  63.5 5.7 %collective-permute-start.7 = (f32[48,128]{1,0:T(8,128)S(1)}, f32[48,128]{1,0:T(8,128)S(1)}, u32[]{:S(2)}, u32[]{:S(2)}) collective-permute-start(f32[48,128]{1,0:T(8,128)S(1)} %get-tuple-element.37), channel_id=1, source_target_pairs={{0,120},{8,0},{16,8},{24,16},{32,24},{40,32},{48,40},{56,48},{64,5... | collective-permute-start | bytes 73736 | tf_op jit(solution)/shard_map/ppermute | solution.py:603
  69.5 22.0 %collective-permute-start.10 = (f32[144,128]{1,0:T(8,128)S(1)}, f32[144,128]{1,0:T(8,128)S(1)}, u32[]{:S(2)}, u32[]{:S(2)}) collective-permute-start(f32[144,128]{1,0:T(8,128)S(1)} %constant_dynamic-update-slice_fusion.refs_3_), channel_id=1, source_target_pairs={{0,1},{1,2},{2,3},{3,4},{4,5},{5,6},{6,7},{7,0},{8,9},{9,10},{10,1... | collective-permute-start | bytes 221192 | tf_op jit(solution)/shard_map/ppermute | solution.py:603
  72.2 19.3 %collective-permute-start.9 = (f32[144,128]{1,0:T(8,128)S(1)}, f32[144,128]{1,0:T(8,128)S(1)}, u32[]{:S(2)}, u32[]{:S(2)}) collective-permute-start(f32[144,128]{1,0:T(8,128)S(1)} %constant_dynamic-update-slice_fusion.refs_3_), channel_id=1, source_target_pairs={{0,7},{1,0},{2,1},{3,2},{4,3},{5,4},{6,5},{7,6},{8,15},{9,8},{10,9... | collective-permute-start | bytes 221192 | tf_op jit(solution)/shard_map/ppermute | solution.py:603
  95.4 14.0 %all-to-all-start.3 = ((f32[128,1,128]{2,1,0:T(1,128)}), f32[128,1,128]{2,1,0:T(1,128)S(1)}, u32[]{:S(2)}, u32[]{:S(2)}) async-start(f32[128,1,128]{2,1,0:T(1,128)} %bitcast.10), calls=%async_computation.3 | async-start | bytes 131072 | tf_op jit(solution)/shard_map/all_to_all | solution.py:598

commit v6 on v5

--- a/solution.py
+++ b/solution.py
@@ -623,12 +623,12 @@
     asked = exchange(pack(query_elem[0].T, query_coord[0].transpose(1, 2, 0)))
     own = split_nodes(displacement)
     rows = along_mesh(own)
-    asked, prepared, rows = lax.optimization_barrier((asked, prepare(bg_coef), rows))
-    found, rows = lax.optimization_barrier((lookup(asked, prepared), rows))
+    asked, prepared = lax.optimization_barrier((asked, prepare(bg_coef)))
+    found = lookup(asked, prepared)
     found = exchange(found)
     field = along_bg(rows)
-    found, field = lax.optimization_barrier((found, field))
-    sizes = from_below(place(found, query_point[0].T))
+    sizes = place(found, query_point[0].T)
+    sizes = from_below(sizes)
     move, terms = newton_pass(field, None, sizes, None)
     first_terms = exchange(terms)
     shift = along_bg(along_mesh(move))

time: 112 us -> 109 us (0.973)
  blocking collectives: 35.5 us -> 15.5 us
  waiting for transfers between devices: 20 us -> 33.6 us
  starting transfers between devices: 32 us -> 35 us
    all_to_all x2 -> x1, blocking collectives: 35.5 us -> 15.5 us  [exchange(): lax.all_to_all(values, ('mesh', 'bg'), split_axis=0, concat_axis=0, tiled...]
    all_to_all x2 -> x3, waiting for transfers between devices: 11.7 us -> 21.1 us  [exchange(): lax.all_to_all(values, ('mesh', 'bg'), split_axis=0, concat_axis=0, tiled...]
    ppermute x10, waiting for transfers between devices: 2.78 us -> 10.7 us  [moved(): lax.ppermute(values, axis, [(i, (i - by) % count) for i in range(count)])]
    all_to_all x2 -> x3, starting transfers between devices: 15.9 us -> 21.7 us  [exchange(): lax.all_to_all(values, ('mesh', 'bg'), split_axis=0, concat_axis=0, tiled...]
    ppermute x1, waiting for transfers between devices: 5.56 us -> 1.8 us  [from_below(): lax.ppermute(block, ('mesh', 'bg'), steps)]
    ppermute x10, starting transfers between devices: 15.4 us -> 13.2 us  [moved(): lax.ppermute(values, axis, [(i, (i - by) % count) for i in range(count)])]
  transfers between devices with their start and end apart: 13 -> 14, of which waited for: 7 -> 7; matrix products, arithmetic and copies ran while one was open for 0% -> 0% of each run, Pallas kernels for 3% -> 13%
where the time goes in v6:
time: 109 us; the launch traced here: 108 us
  starting transfers between devices  35 us (32%)
  waiting for transfers between devices  33.6 us (31%)
  Pallas kernels  23.6 us (22%)
  blocking collectives  15.5 us (14%)
    pallas_call x9, Pallas kernels, call(): pl.pallas_call(kernel, out_shape=outs, in_specs=in_vmem(len(args)), out_s...  23.6 us
    all_to_all x3, starting transfers between devices, exchange(): lax.all_to_all(values, ('mesh', 'bg'), split_axis=0, concat_axis=0, tiled...  21.7 us
    all_to_all x3, waiting for transfers between devices, exchange(): lax.all_to_all(values, ('mesh', 'bg'), split_axis=0, concat_axis=0, tiled...  21.1 us
    all_to_all x1, blocking collectives, exchange(): lax.all_to_all(values, ('mesh', 'bg'), split_axis=0, concat_axis=0, tiled...  15.5 us
    ppermute x10, starting transfers between devices, moved(): lax.ppermute(values, axis, [(i, (i - by) % count) for i in range(count)])  13.2 us
    ppermute x10, waiting for transfers between devices, moved(): lax.ppermute(values, axis, [(i, (i - by) % count) for i in range(count)])  10.7 us
  transfers between devices with their start and end apart: 14, of which 7 were waited for; matrix products, arithmetic and copies ran while one was open for 0% of the time, Pallas kernels for 13%

profile of v6, /device:TPU:1, one launch (start us, length us, event | category | flops | bytes accessed | tf_op | source)
XLA Modules:
  0.0 108.4 jit_solution(17501036733160714608)
XLA Ops:
  0.6 1.9 %shard_map.69 = f32[128,1,640]{2,1,0:T(1,128)} custom-call(s32[136,128]{1,0:T(8,128)} %bitcast.22, f32[3,136,128]{2,1,0:T(8,128)} %bitcast.21), custom_call_target="tpu_custom_call" | custom-call | tf_op jit(solution)/shard_map/pallas_call | solution.py:30
  2.6 11.5 %all-to-all-start = ((f32[128,1,640]{2,1,0:T(1,128)}), f32[128,1,640]{2,1,0:T(1,128)S(1)}, u32[]{:S(2)}, u32[]{:S(2)}) async-start(f32[128,1,640]{2,1,0:T(1,128)} %shard_map.69), calls=%async_computation | async-start | bytes 655360 | tf_op jit(solution)/shard_map/all_to_all | solution.py:598
  14.1 1.0 shard_map.68
  15.1 5.5 %collective-permute-start = (f32[48,128]{1,0:T(8,128)S(1)}, f32[48,128]{1,0:T(8,128)S(1)}, u32[]{:S(2)}, u32[]{:S(2)}) collective-permute-start(f32[48,128]{1,0:T(8,128)S(1)} %shard_map.68), channel_id=1, source_target_pairs={{0,120},{8,0},{16,8},{24,16},{32,24},{40,32},{48,40},{56,48},{64,5... | collective-permute-start | bytes 73736 | tf_op jit(solution)/shard_map/ppermute | solution.py:603
  20.6 1.5 %shard_map.70 = (bf16[512,512]{1,0:T(8,128)(2,1)S(1)}, s32[8,8192]{1,0:T(8,128)S(1)}, f32[8,128]{1,0:T(8,128)S(1)}) custom-call(f32[8,16384]{1,0:T(8,128)} %table_ref.1), custom_call_target="tpu_custom_call" | custom-call | tf_op jit(solution)/shard_map/pallas_call | solution.py:30
  22.0 3.6 %all-to-all-done.asked_ref = f32[128,1,640]{2,1,0:T(1,128)S(1)} async-done(((f32[128,1,640]{2,1,0:T(1,128)}), f32[128,1,640]{2,1,0:T(1,128)S(1)}, u32[]{:S(2)}, u32[]{:S(2)}) %all-to-all-start) | async-done | bytes 327712 | tf_op jit(solution)/shard_map/all_to_all | solution.py:598
  25.7 8.2 %shard_map.71 = f32[128,1,136]{2,1,0:T(1,128)} custom-call(f32[128,1,640]{2,1,0:T(1,128)S(1)} %all-to-all-done.asked_ref, bf16[512,512]{1,0:T(8,128)(2,1)S(1)} %get-tuple-element.20.split_ref, s32[8,8192]{1,0:T(8,128)S(1)} %get-tuple-element.21.packed_ref, f32[8,128]{1,0:T(8,128)S(1)} %get-tuple-element.22.unit_ref), custom_call_target="tpu_custom_call" | custom-call | tf_op jit(solution)/shard_map/pallas_call | solution.py:30
  33.9 5.8 %all-to-all-start.1 = ((f32[128,1,136]{2,1,0:T(1,128)}), f32[128,1,136]{2,1,0:T(1,128)S(1)}, u32[]{:S(2)}, u32[]{:S(2)}) async-start(f32[128,1,136]{2,1,0:T(1,128)} %shard_map.71), calls=%async_computation.1 | async-start | bytes 262144 | tf_op jit(solution)/shard_map/all_to_all | solution.py:598
  39.7 0.0 collective-permute-done
  39.7 1.1 collective-permute-start.2
  40.8 0.7 collective-permute-start.3
  41.5 8.2 %all-to-all-done.1.found_ref = f32[128,1,136]{2,1,0:T(1,128)S(1)} async-done(((f32[128,1,136]{2,1,0:T(1,128)}), f32[128,1,136]{2,1,0:T(1,128)S(1)}, u32[]{:S(2)}, u32[]{:S(2)}) %all-to-all-start.1) | async-done | bytes 69664 | tf_op jit(solution)/shard_map/all_to_all | solution.py:598
  49.7 2.8 %shard_map.72.refs_3_.refs_6_ = f32[56,128]{1,0:T(8,128)S(1)} custom-call(f32[128,1,136]{2,1,0:T(1,128)S(1)} %all-to-all-done.1.found_ref, s32[136,128]{1,0:T(8,128)} %bitcast.23), custom_call_target="tpu_custom_call" | custom-call | tf_op jit(solution)/shard_map/pallas_call | solution.py:30
  52.5 0.4 collective-permute-start.4
  52.9 0.9 collective-permute-start.5
  53.8 0.1 collective-permute-start.6
  54.0 4.7 %collective-permute-done.4.refs_4_.refs_7_ = f32[56,128]{1,0:T(8,128)S(1)} collective-permute-done((f32[56,128]{1,0:T(8,128)S(1)}, f32[56,128]{1,0:T(8,128)S(1)}, u32[]{:S(2)}, u32[]{:S(2)}) %collective-permute-start.4) | collective-permute-done | bytes 28704 | tf_op jit(solution)/shard_map/ppermute | solution.py:603
  58.6 0.0 collective-permute-done.5.refs_5_.refs_8_
  58.6 1.8 %collective-permute-done.6.refs_6_.refs_9_ = f32[56,128]{1,0:T(8,128)S(1)} collective-permute-done((f32[56,128]{1,0:T(8,128)S(1)}, f32[56,128]{1,0:T(8,128)S(1)}, u32[]{:S(2)}, u32[]{:S(2)}) %collective-permute-start.6) | collective-permute-done | bytes 28704 | tf_op jit(solution)/shard_map/ppermute | solution.py:615
  60.4 2.1 %shard_map.73 = (f32[48,128]{1,0:T(8,128)S(1)}, f32[128,128]{1,0:T(8,128)S(1)}) custom-call(f32[144,128]{1,0:T(8,128)S(1)} %pad_maximum_fusion.refs_0_, f32[144,128]{1,0:T(8,128)S(1)} %collective-permute-done.2.refs_1_, f32[144,128]{1,0:T(8,128)S(1)} %collective-permute-done.3.refs_2_, f32[56,128]{1,0:T(8,128)S(1)} %shard_map.72.refs_3_.refs_6_, ...), custom_call_target="tpu_custom_call" | custom-call | tf_op jit(solution)/shard_map/pallas_call | solution.py:30
  62.5 1.6 %collective-permute-start.7 = (f32[48,128]{1,0:T(8,128)S(1)}, f32[48,128]{1,0:T(8,128)S(1)}, u32[]{:S(2)}, u32[]{:S(2)}) collective-permute-start(f32[48,128]{1,0:T(8,128)S(1)} %get-tuple-element.23), channel_id=1, source_target_pairs={{0,120},{8,0},{16,8},{24,16},{32,24},{40,32},{48,40},{56,48},{64,5... | collective-permute-start | bytes 73736 | tf_op jit(solution)/shard_map/ppermute | solution.py:603
  64.1 1.2 %collective-permute-done.7 = f32[48,128]{1,0:T(8,128)S(1)} collective-permute-done((f32[48,128]{1,0:T(8,128)S(1)}, f32[48,128]{1,0:T(8,128)S(1)}, u32[]{:S(2)}, u32[]{:S(2)}) %collective-permute-start.7) | collective-permute-done | bytes 24608 | tf_op jit(solution)/shard_map/ppermute | solution.py:603
  65.3 4.8 %collective-permute-done.8 = f32[48,128]{1,0:T(8,128)S(1)} collective-permute-done((f32[48,128]{1,0:T(8,128)S(1)}, f32[48,128]{1,0:T(8,128)S(1)}, u32[]{:S(2)}, u32[]{:S(2)}) %collective-permute-start.8) | collective-permute-done | bytes 24608 | tf_op jit(solution)/shard_map/ppermute | solution.py:603
  70.1 2.0 %collective-permute-start.10 = (f32[144,128]{1,0:T(8,128)S(1)}, f32[144,128]{1,0:T(8,128)S(1)}, u32[]{:S(2)}, u32[]{:S(2)}) collective-permute-start(f32[144,128]{1,0:T(8,128)S(1)} %constant_dynamic-update-slice_fusion.refs_3_), channel_id=1, source_target_pairs={{0,1},{1,2},{2,3},{3,4},{4,5},{5,6},{6,7},{7,0},{8,9},{9,10},{10,1... | collective-permute-start | bytes 221192 | tf_op jit(solution)/shard_map/ppermute | solution.py:603
  72.1 1.0 collective-permute-start.9
  73.2 15.5 %all_to_all.32 = f32[128,1,128]{2,1,0:T(1,128)S(1)} all-to-all(f32[128,1,128]{2,1,0:T(1,128)S(1)} %bitcast.20), channel_id=1, replica_groups=mesh['mesh'=16,'bg'=8] {'mesh','bg'}, dimensions={0} | all-to-all | bytes 131072 | tf_op jit(solution)/shard_map/all_to_all | solution.py:598
  88.6 0.0 collective-permute-done.10.refs_5_
  88.7 3.9 %shard_map.74 = (f32[48,128]{1,0:T(8,128)S(1)}, f32[128,128]{1,0:T(8,128)}, f32[48,128]{1,0:T(8,128)S(1)}) custom-call(f32[144,128]{1,0:T(8,128)S(1)} %pad_maximum_fusion.refs_0_, f32[144,128]{1,0:T(8,128)S(1)} %collective-permute-done.2.refs_1_, f32[144,128]{1,0:T(8,128)S(1)} %collective-permute-done.3.refs_2_, ...), custom_call_target="tpu_custom_call" | custom-call | tf_op jit(solution)/shard_map/pallas_call | solution.py:30
  92.6 4.4 %all-to-all-start.3 = ((f32[128,1,128]{2,1,0:T(1,128)}), f32[128,1,128]{2,1,0:T(1,128)S(1)}, u32[]{:S(2)}, u32[]{:S(2)}) async-start(f32[128,1,128]{2,1,0:T(1,128)} %bitcast.10), calls=%async_computation.3 | async-start | bytes 131072 | tf_op jit(solution)/shard_map/all_to_all | solution.py:598
  97.0 0.3 shard_map.75
  97.3 9.2 %all-to-all-done.3 = f32[128,1,128]{2,1,0:T(1,128)S(1)} async-done(((f32[128,1,128]{2,1,0:T(1,128)}), f32[128,1,128]{2,1,0:T(1,128)S(1)}, u32[]{:S(2)}, u32[]{:S(2)}) %all-to-all-start.3) | async-done | bytes 65568 | tf_op jit(solution)/shard_map/all_to_all | solution.py:598
  106.6 1.8 %shard_map.76 = (f32[3,4,4,128]{3,2,1,0:T(4,128)}, f32[2,5]{1,0:T(2,128)}) custom-call(f32[3,4,4,128]{3,2,1,0:T(4,128)S(1)} %get-tuple-element.27.own_ref, f32[3,4,4,128]{3,2,1,0:T(4,128)S(1)} %get-tuple-element.28.move_ref, f32[128,128]{1,0:T(8,128)S(1)} %bitcast.18, f32[128,128]{1,0:T(8,128)S(1)} %bitcast.19), custom_call_target="tpu_custom_call" | custom-call | tf_op jit(solution)/shard_map/pallas_call | solution.py:30
  (10 shorter events, 0.0 us)
Async XLA Ops:
  2.6 23.1 %all-to-all-start = ((f32[128,1,640]{2,1,0:T(1,128)}), f32[128,1,640]{2,1,0:T(1,128)S(1)}, u32[]{:S(2)}, u32[]{:S(2)}) async-start(f32[128,1,640]{2,1,0:T(1,128)} %shard_map.69), calls=%async_computation | async-start | bytes 655360 | tf_op jit(solution)/shard_map/all_to_all | solution.py:598
  15.1 24.6 %collective-permute-start = (f32[48,128]{1,0:T(8,128)S(1)}, f32[48,128]{1,0:T(8,128)S(1)}, u32[]{:S(2)}, u32[]{:S(2)}) collective-permute-start(f32[48,128]{1,0:T(8,128)S(1)} %shard_map.68), channel_id=1, source_target_pairs={{0,120},{8,0},{16,8},{24,16},{32,24},{40,32},{48,40},{56,48},{64,5... | collective-permute-start | bytes 73736 | tf_op jit(solution)/shard_map/ppermute | solution.py:603
  20.6 19.1 %collective-permute-start.1 = (f32[48,128]{1,0:T(8,128)S(1)}, f32[48,128]{1,0:T(8,128)S(1)}, u32[]{:S(2)}, u32[]{:S(2)}) collective-permute-start(f32[48,128]{1,0:T(8,128)S(1)} %shard_map.68), channel_id=1, source_target_pairs={{0,8},{8,16},{16,24},{24,32},{32,40},{40,48},{48,56},{56,64},{64,7... | collective-permute-start | bytes 73736 | tf_op jit(solution)/shard_map/ppermute | solution.py:603
  33.9 15.8 %all-to-all-start.1 = ((f32[128,1,136]{2,1,0:T(1,128)}), f32[128,1,136]{2,1,0:T(1,128)S(1)}, u32[]{:S(2)}, u32[]{:S(2)}) async-start(f32[128,1,136]{2,1,0:T(1,128)} %shard_map.71), calls=%async_computation.1 | async-start | bytes 262144 | tf_op jit(solution)/shard_map/all_to_all | solution.py:598
  39.7 14.2 %collective-permute-start.2 = (f32[144,128]{1,0:T(8,128)S(1)}, f32[144,128]{1,0:T(8,128)S(1)}, u32[]{:S(2)}, u32[]{:S(2)}) collective-permute-start(f32[144,128]{1,0:T(8,128)S(1)} %pad_maximum_fusion.refs_0_), channel_id=1, source_target_pairs={{0,7},{1,0},{2,1},{3,2},{4,3},{5,4},{6,5},{7,6},{8,15},{9,8},{10,9... | collective-permute-start | bytes 221192 | tf_op jit(solution)/shard_map/ppermute | solution.py:603
  40.8 13.2 %collective-permute-start.3 = (f32[144,128]{1,0:T(8,128)S(1)}, f32[144,128]{1,0:T(8,128)S(1)}, u32[]{:S(2)}, u32[]{:S(2)}) collective-permute-start(f32[144,128]{1,0:T(8,128)S(1)} %pad_maximum_fusion.refs_0_), channel_id=1, source_target_pairs={{0,1},{1,2},{2,3},{3,4},{4,5},{5,6},{6,7},{7,0},{8,9},{9,10},{10,1... | collective-permute-start | bytes 221192 | tf_op jit(solution)/shard_map/ppermute | solution.py:603
  52.5 6.1 %collective-permute-start.4 = (f32[56,128]{1,0:T(8,128)S(1)}, f32[56,128]{1,0:T(8,128)S(1)}, u32[]{:S(2)}, u32[]{:S(2)}) collective-permute-start(f32[56,128]{1,0:T(8,128)S(1)} %shard_map.72.refs_3_.refs_6_), channel_id=1, source_target_pairs={{0,8},{8,16},{16,24},{24,32},{32,40},{40,48},{48,56},{56,64},{64,7... | collective-permute-start | bytes 86024 | tf_op jit(solution)/shard_map/ppermute | solution.py:603
  52.9 5.7 %collective-permute-start.5 = (f32[56,128]{1,0:T(8,128)S(1)}, f32[56,128]{1,0:T(8,128)S(1)}, u32[]{:S(2)}, u32[]{:S(2)}) collective-permute-start(f32[56,128]{1,0:T(8,128)S(1)} %shard_map.72.refs_3_.refs_6_), channel_id=1, source_target_pairs={{0,1},{1,2},{2,3},{3,4},{4,5},{5,6},{6,7},{7,0},{8,9},{9,10},{10,1... | collective-permute-start | bytes 86024 | tf_op jit(solution)/shard_map/ppermute | solution.py:603
  53.8 6.6 %collective-permute-start.6 = (f32[56,128]{1,0:T(8,128)S(1)}, f32[56,128]{1,0:T(8,128)S(1)}, u32[]{:S(2)}, u32[]{:S(2)}) collective-permute-start(f32[56,128]{1,0:T(8,128)S(1)} %shard_map.72.refs_3_.refs_6_), channel_id=1, source_target_pairs={{0,9},{1,10},{2,11},{3,12},{4,13},{5,14},{6,15},{7,8},{8,17},{9,18... | collective-permute-start | bytes 86024 | tf_op jit(solution)/shard_map/ppermute | solution.py:615
  62.5 2.7 %collective-permute-start.7 = (f32[48,128]{1,0:T(8,128)S(1)}, f32[48,128]{1,0:T(8,128)S(1)}, u32[]{:S(2)}, u32[]{:S(2)}) collective-permute-start(f32[48,128]{1,0:T(8,128)S(1)} %get-tuple-element.23), channel_id=1, source_target_pairs={{0,120},{8,0},{16,8},{24,16},{32,24},{40,32},{48,40},{56,48},{64,5... | collective-permute-start | bytes 73736 | tf_op jit(solution)/shard_map/ppermute | solution.py:603
  64.1 6.0 %collective-permute-start.8 = (f32[48,128]{1,0:T(8,128)S(1)}, f32[48,128]{1,0:T(8,128)S(1)}, u32[]{:S(2)}, u32[]{:S(2)}) collective-permute-start(f32[48,128]{1,0:T(8,128)S(1)} %get-tuple-element.23), channel_id=1, source_target_pairs={{0,8},{8,16},{16,24},{24,32},{32,40},{40,48},{48,56},{56,64},{64,7... | collective-permute-start | bytes 73736 | tf_op jit(solution)/shard_map/ppermute | solution.py:603
  70.1 18.6 %collective-permute-start.10 = (f32[144,128]{1,0:T(8,128)S(1)}, f32[144,128]{1,0:T(8,128)S(1)}, u32[]{:S(2)}, u32[]{:S(2)}) collective-permute-start(f32[144,128]{1,0:T(8,128)S(1)} %constant_dynamic-update-slice_fusion.refs_3_), channel_id=1, source_target_pairs={{0,1},{1,2},{2,3},{3,4},{4,5},{5,6},{6,7},{7,0},{8,9},{9,10},{10,1... | collective-permute-start | bytes 221192 | tf_op jit(solution)/shard_map/ppermute | solution.py:603
  72.1 16.5 %collective-permute-start.9 = (f32[144,128]{1,0:T(8,128)S(1)}, f32[144,128]{1,0:T(8,128)S(1)}, u32[]{:S(2)}, u32[]{:S(2)}) collective-permute-start(f32[144,128]{1,0:T(8,128)S(1)} %constant_dynamic-update-slice_fusion.refs_3_), channel_id=1, source_target_pairs={{0,7},{1,0},{2,1},{3,2},{4,3},{5,4},{6,5},{7,6},{8,15},{9,8},{10,9... | collective-permute-start | bytes 221192 | tf_op jit(solution)/shard_map/ppermute | solution.py:603
  92.6 14.0 %all-to-all-start.3 = ((f32[128,1,128]{2,1,0:T(1,128)}), f32[128,1,128]{2,1,0:T(1,128)S(1)}, u32[]{:S(2)}, u32[]{:S(2)}) async-start(f32[128,1,128]{2,1,0:T(1,128)} %bitcast.10), calls=%async_computation.3 | async-start | bytes 131072 | tf_op jit(solution)/shard_map/all_to_all | solution.py:598

commit v7 on v6

--- a/solution.py
+++ b/solution.py
@@ -387,26 +387,18 @@
             out_ref[pl.ds(out_at + upper * 4 + y, count, stride=8), :] = value
 
 
-def pass_kernel(first, *refs):
-    refs = list(refs)
-    field_refs = [refs.pop(0) for _ in range(3)]
-    if not first:
-        shift_refs = [refs.pop(0) for _ in range(3)]
-    sizes = {at: (ref, 0) for at, ref in size_pieces([refs.pop(0) for _ in range(4)]).items()}
-    if first:
-        move_ref, terms_out, nodes_ref, size_ref, jac_ref, part_ref, turn_ref = refs
-        field = field_pieces(field_refs)
-    else:
-        terms_in, move_ref, terms_out, own_ref, nodes_ref, size_ref, jac_ref, part_ref, turn_ref, sum_ref = refs
-        step = newton_step(add_up(terms_in))
-        for i, (field_ref, shift_ref) in enumerate(zip(field_refs, shift_refs)):
-            sum_ref[i] = field_ref[...] + step * shift_ref[...]
-        field = field_pieces([sum_ref.at[i] for i in range(3)])
-        own_ref[...] = sum_ref[0, :48, :]
+def each(body):
+    def run(i, carry):
+        body(i)
+        return carry
+
+    lax.fori_loop(0, 3, run, 0)
+
+
+def jacobians(field, nodes_ref, jac_ref):
     for z_shift in range(2):
         for y_shift in range(2):
             ring(field, 24, nodes_ref, (z_shift * 2 + y_shift) * 192, z_shift, y_shift)
-    ring(sizes, 27, size_ref, 0, 0, 0)
 
     def known(c):
         def local(z, y, x):
@@ -416,33 +408,13 @@
 
         return local
 
-    def packed(node, upper, shift):
-        rows = [
-            turn_ref[pl.ds(node * 8 + upper * 4 + 1 + shift + ey, 4, stride=64), :] for ey in range(2)
-        ]
-        return jnp.concatenate(rows, axis=0)
-
-    def sought(z, y, x):
-        node = (z % 2) * 4 + (y % 2) * 2 + x % 2
-        shift = y // 2
-        value = packed(node, 0, shift)
-        if z == 2:
-            value = pltpu.roll(value, 64, 1)
-        else:
-            value = jnp.where(lane_index() < 64, value, packed(node, 1, shift))
-        return x_up(value) if x == 2 else value
-
-    def each(body):
-        def run(i, carry):
-            body(i)
-            return carry
-
-        lax.fori_loop(0, 3, run, 0)
-
+    each(lambda c: forward(known(c), jac_ref, functools.partial(at_point, c)))
+
+
+def descend(size_ref, jac_ref, part_ref, turn_ref, move_ref):
     def size_at(jz, jy, jx):
         return size_ref[pl.ds(pl.multiple_of((jz * 9 + jy * 3 + jx) * 8, 8), 8), :]
 
-    each(lambda c: forward(known(c), jac_ref, functools.partial(at_point, c)))
     turn_ref[192:, :] = jnp.zeros((64, 128), jnp.float32)
 
     def stress(jz):
@@ -461,6 +433,25 @@
     each(lambda c: backward(c, part_ref, turn_ref))
     for row in range(2):
         move_ref[pl.ds(row, 24, stride=2), :] = turn_ref[pl.ds(row + 2, 24, stride=8), :]
+
+
+def line_sums(size_ref, jac_ref, part_ref, turn_ref, terms_out):
+    def packed(node, upper, shift):
+        rows = [
+            turn_ref[pl.ds(node * 8 + upper * 4 + 1 + shift + ey, 4, stride=64), :] for ey in range(2)
+        ]
+        return jnp.concatenate(rows, axis=0)
+
+    def sought(z, y, x):
+        node = (z % 2) * 4 + (y % 2) * 2 + x % 2
+        shift = y // 2
+        value = packed(node, 0, shift)
+        if z == 2:
+            value = pltpu.roll(value, 64, 1)
+        else:
+            value = jnp.where(lane_index() < 64, value, packed(node, 1, shift))
+        return x_up(value) if x == 2 else value
+
     forward(sought, part_ref, lambda k, jz, jy, jx: pl.ds(((jz * 9 + jy * 3 + jx) * 3 + k) * 8, 8))
 
     def middle(ref, at, stride):
@@ -498,19 +489,62 @@
     terms_out[...] = jnp.broadcast_to(terms, (SRC, 128))
 
 
-def newton_pass(field, shift, sizes, terms):
-    first = shift is None
-    node = jax.ShapeDtypeStruct((48, 128), jnp.float32)
-    outs = [node, jax.ShapeDtypeStruct((SRC, 128), jnp.float32)] + ([] if first else [node])
-    scratch = [
-        pltpu.VMEM((4 * 192, 128), jnp.float32),
-        pltpu.VMEM((27 * 8, 128), jnp.float32),
-        pltpu.VMEM((243 * 8, 128), jnp.float32),
-        pltpu.VMEM((243 * 8, 128), jnp.float32),
-        pltpu.VMEM((32 * 8, 128), jnp.float32),
-    ] + ([] if first else [pltpu.VMEM((3, 144, 128), jnp.float32)])
-    args = list(field) + ([] if first else list(shift)) + list(sizes) + ([] if first else [terms])
-    return call(functools.partial(pass_kernel, first), outs, args, scratch)
+def jacobian_kernel(*refs):
+    jacobians(field_pieces(refs[:3]), refs[4], refs[3])
+
+
+def descent_kernel(jac_ref, own, z_low, y_low, corner, move_ref, turn_ref, size_ref, part_ref):
+    sizes = {at: (ref, 0) for at, ref in size_pieces([own, z_low, y_low, corner]).items()}
+    ring(sizes, 27, size_ref, 0, 0, 0)
+    descend(size_ref, jac_ref, part_ref, turn_ref, move_ref)
+
+
+def line_kernel(jac_ref, turn_ref, size_ref, terms_out, part_ref):
+    line_sums(size_ref, jac_ref, part_ref, turn_ref, terms_out)
+
+
+def second_kernel(*refs):
+    field_refs, shift_refs = refs[:3], refs[3:6]
+    size_ref, terms_in, move_ref, terms_out, own_ref, nodes_ref, jac_ref, part_ref, turn_ref, sum_ref = refs[6:]
+    step = newton_step(add_up(terms_in))
+    for i, (field_ref, shift_ref) in enumerate(zip(field_refs, shift_refs)):
+        sum_ref[i] = field_ref[...] + step * shift_ref[...]
+    own_ref[...] = sum_ref[0, :48, :]
+    jacobians(field_pieces([sum_ref.at[i] for i in range(3)]), nodes_ref, jac_ref)
+    descend(size_ref, jac_ref, part_ref, turn_ref, move_ref)
+    line_sums(size_ref, jac_ref, part_ref, turn_ref, terms_out)
+
+
+NODE = jax.ShapeDtypeStruct((48, 128), jnp.float32)
+TERMS = jax.ShapeDtypeStruct((SRC, 128), jnp.float32)
+NODES_ROWS, JAC_ROWS, TURN_ROWS, SIZE_ROWS = 4 * 192, 243 * 8, 32 * 8, 27 * 8
+
+
+def rows_of(count):
+    return jax.ShapeDtypeStruct((count, 128), jnp.float32)
+
+
+def scratch_of(count):
+    return pltpu.VMEM((count, 128), jnp.float32)
+
+
+def first_jacobians(field):
+    return call(jacobian_kernel, rows_of(JAC_ROWS), field, [scratch_of(NODES_ROWS)])
+
+
+def first_descent(jac, sizes):
+    outs = [NODE, rows_of(TURN_ROWS), rows_of(SIZE_ROWS)]
+    return call(descent_kernel, outs, [jac, *sizes], [scratch_of(JAC_ROWS)])
+
+
+def first_line(jac, turn, size):
+    return call(line_kernel, TERMS, [jac, turn, size], [scratch_of(81 * 8)])
+
+
+def second_pass(field, shift, size, terms):
+    scratch = [scratch_of(rows) for rows in (NODES_ROWS, JAC_ROWS, JAC_ROWS, TURN_ROWS)]
+    scratch.append(pltpu.VMEM((3, 144, 128), jnp.float32))
+    return call(second_kernel, [NODE, TERMS, NODE], [*field, *shift, size, terms], scratch)
 
 
 def interleave(back):
@@ -629,10 +663,13 @@
     field = along_bg(rows)
     sizes = place(found, query_point[0].T)
     sizes = from_below(sizes)
-    move, terms = newton_pass(field, None, sizes, None)
+    jac = first_jacobians(field)
+    move, turn, size = first_descent(jac, sizes)
+    rows = along_mesh(move)
+    terms = first_line(jac, turn, size)
     first_terms = exchange(terms)
-    shift = along_bg(along_mesh(move))
-    last_move, last_terms, last_own = newton_pass(field, shift, sizes, first_terms)
+    shift = along_bg(rows)
+    last_move, last_terms, last_own = second_pass(field, shift, size, first_terms)
     own, move = join_nodes(last_own, last_move)
     last_terms = exchange(last_terms)
     return finish(own, move, first_terms, last_terms)

time: 109 us -> 108 us (level)
  waiting for transfers between devices: 33.6 us -> 27.7 us
  blocking collectives: 15.5 us -> 18.7 us
  starting transfers between devices: 35 us -> 37 us
    ppermute x10, waiting for transfers between devices: 10.7 us -> 1.48 us  [moved(): lax.ppermute(values, axis, [(i, (i - by) % count) for i in range(count)])]
    all_to_all x1, blocking collectives: 15.5 us -> 18.7 us  [exchange(): lax.all_to_all(values, ('mesh', 'bg'), split_axis=0, concat_axis=0, tiled...]
    ppermute x1, waiting for transfers between devices: 1.8 us -> 4.84 us  [from_below(): lax.ppermute(block, ('mesh', 'bg'), steps)]
    ppermute x10, starting transfers between devices: 13.2 us -> 16.1 us  [moved(): lax.ppermute(values, axis, [(i, (i - by) % count) for i in range(count)])]
    all_to_all x3, starting transfers between devices: 21.7 us -> 20.3 us  [exchange(): lax.all_to_all(values, ('mesh', 'bg'), split_axis=0, concat_axis=0, tiled...]
    pallas_call x9 -> x11, Pallas kernels: 23.6 us -> 23.7 us  [call(): pl.pallas_call(kernel, out_shape=outs, in_specs=in_vmem(len(args)), out_s...]
  transfers between devices with their start and end apart: 14 -> 14, of which waited for: 7 -> 7; matrix products, arithmetic and copies ran while one was open for 0% -> 0% of each run, Pallas kernels for 13% -> 14%
where the time goes in v7:
time: 108 us
  starting transfers between devices  37 us (34%)
  waiting for transfers between devices  27.7 us (26%)
  Pallas kernels  23.7 us (22%)
  blocking collectives  18.7 us (17%)
    pallas_call x11, Pallas kernels, call(): pl.pallas_call(kernel, out_shape=outs, in_specs=in_vmem(len(args)), out_s...  23.7 us
    all_to_all x3, waiting for transfers between devices, exchange(): lax.all_to_all(values, ('mesh', 'bg'), split_axis=0, concat_axis=0, tiled...  21.4 us
    all_to_all x3, starting transfers between devices, exchange(): lax.all_to_all(values, ('mesh', 'bg'), split_axis=0, concat_axis=0, tiled...  20.3 us
    all_to_all x1, blocking collectives, exchange(): lax.all_to_all(values, ('mesh', 'bg'), split_axis=0, concat_axis=0, tiled...  18.7 us
    ppermute x10, starting transfers between devices, moved(): lax.ppermute(values, axis, [(i, (i - by) % count) for i in range(count)])  16.1 us
    ppermute x1, waiting for transfers between devices, from_below(): lax.ppermute(block, ('mesh', 'bg'), steps)  4.84 us
  transfers between devices with their start and end apart: 14, of which 7 were waited for; matrix products, arithmetic and copies ran while one was open for 0% of the time, Pallas kernels for 14%

profile of v7, /device:TPU:1, one launch (start us, length us, event | category | flops | bytes accessed | tf_op | source)
XLA Modules:
  0.0 107.9 jit_solution(6807312714654322891)
XLA Ops:
  0.6 1.9 %shard_map.70 = f32[128,1,640]{2,1,0:T(1,128)} custom-call(s32[136,128]{1,0:T(8,128)} %bitcast.22, f32[3,136,128]{2,1,0:T(8,128)} %bitcast.21), custom_call_target="tpu_custom_call" | custom-call | tf_op jit(solution)/shard_map/pallas_call | solution.py:30
  2.6 11.5 %all-to-all-start = ((f32[128,1,640]{2,1,0:T(1,128)}), f32[128,1,640]{2,1,0:T(1,128)S(1)}, u32[]{:S(2)}, u32[]{:S(2)}) async-start(f32[128,1,640]{2,1,0:T(1,128)} %shard_map.70), calls=%async_computation | async-start | bytes 655360 | tf_op jit(solution)/shard_map/all_to_all | solution.py:632
  14.1 1.0 shard_map.68
  15.1 1.4 %collective-permute-start.1 = (f32[48,128]{1,0:T(8,128)S(1)}, f32[48,128]{1,0:T(8,128)S(1)}, u32[]{:S(2)}, u32[]{:S(2)}) collective-permute-start(f32[48,128]{1,0:T(8,128)S(1)} %shard_map.68), channel_id=1, source_target_pairs={{0,8},{8,16},{16,24},{24,32},{32,40},{40,48},{48,56},{56,64},{64,7... | collective-permute-start | bytes 73736 | tf_op jit(solution)/shard_map/ppermute | solution.py:637
  16.5 4.1 %collective-permute-start = (f32[48,128]{1,0:T(8,128)S(1)}, f32[48,128]{1,0:T(8,128)S(1)}, u32[]{:S(2)}, u32[]{:S(2)}) collective-permute-start(f32[48,128]{1,0:T(8,128)S(1)} %shard_map.68), channel_id=1, source_target_pairs={{0,120},{8,0},{16,8},{24,16},{32,24},{40,32},{48,40},{56,48},{64,5... | collective-permute-start | bytes 73736 | tf_op jit(solution)/shard_map/ppermute | solution.py:637
  20.6 1.5 %shard_map.71 = (bf16[512,512]{1,0:T(8,128)(2,1)S(1)}, s32[8,8192]{1,0:T(8,128)S(1)}, f32[8,128]{1,0:T(8,128)S(1)}) custom-call(f32[8,16384]{1,0:T(8,128)} %table_ref.1), custom_call_target="tpu_custom_call" | custom-call | tf_op jit(solution)/shard_map/pallas_call | solution.py:30
  22.1 3.8 %all-to-all-done.asked_ref = f32[128,1,640]{2,1,0:T(1,128)S(1)} async-done(((f32[128,1,640]{2,1,0:T(1,128)}), f32[128,1,640]{2,1,0:T(1,128)S(1)}, u32[]{:S(2)}, u32[]{:S(2)}) %all-to-all-start) | async-done | bytes 327712 | tf_op jit(solution)/shard_map/all_to_all | solution.py:632
  25.9 8.2 %shard_map.72 = f32[128,1,136]{2,1,0:T(1,128)} custom-call(f32[128,1,640]{2,1,0:T(1,128)S(1)} %all-to-all-done.asked_ref, bf16[512,512]{1,0:T(8,128)(2,1)S(1)} %get-tuple-element.21.split_ref, s32[8,8192]{1,0:T(8,128)S(1)} %get-tuple-element.22.packed_ref, f32[8,128]{1,0:T(8,128)S(1)} %get-tuple-element.23.unit_ref), custom_call_target="tpu_custom_call" | custom-call | tf_op jit(solution)/shard_map/pallas_call | solution.py:30
  34.1 4.4 %all-to-all-start.1 = ((f32[128,1,136]{2,1,0:T(1,128)}), f32[128,1,136]{2,1,0:T(1,128)S(1)}, u32[]{:S(2)}, u32[]{:S(2)}) async-start(f32[128,1,136]{2,1,0:T(1,128)} %shard_map.72), calls=%async_computation.1 | async-start | bytes 262144 | tf_op jit(solution)/shard_map/all_to_all | solution.py:632
  38.5 1.6 %collective-permute-start.3 = (f32[144,128]{1,0:T(8,128)S(1)}, f32[144,128]{1,0:T(8,128)S(1)}, u32[]{:S(2)}, u32[]{:S(2)}) collective-permute-start(f32[144,128]{1,0:T(8,128)S(1)} %pad_maximum_fusion.refs_0_), channel_id=1, source_target_pairs={{0,1},{1,2},{2,3},{3,4},{4,5},{5,6},{6,7},{7,0},{8,9},{9,10},{10,1... | collective-permute-start | bytes 221192 | tf_op jit(solution)/shard_map/ppermute | solution.py:637
  40.2 8.4 %all-to-all-done.1.found_ref = f32[128,1,136]{2,1,0:T(1,128)S(1)} async-done(((f32[128,1,136]{2,1,0:T(1,128)}), f32[128,1,136]{2,1,0:T(1,128)S(1)}, u32[]{:S(2)}, u32[]{:S(2)}) %all-to-all-start.1) | async-done | bytes 69664 | tf_op jit(solution)/shard_map/all_to_all | solution.py:632
  48.6 2.8 %shard_map.73.own = f32[56,128]{1,0:T(8,128)S(1)} custom-call(f32[128,1,136]{2,1,0:T(1,128)S(1)} %all-to-all-done.1.found_ref, s32[136,128]{1,0:T(8,128)} %bitcast.23), custom_call_target="tpu_custom_call" | custom-call | tf_op jit(solution)/shard_map/pallas_call | solution.py:30
  51.4 0.7 collective-permute-start.6
  52.1 0.3 collective-permute-start.5
  52.4 0.4 collective-permute-start.4
  52.9 0.6 shard_map.69.jac_ref
  53.4 4.8 %collective-permute-done.6.corner = f32[56,128]{1,0:T(8,128)S(1)} collective-permute-done((f32[56,128]{1,0:T(8,128)S(1)}, f32[56,128]{1,0:T(8,128)S(1)}, u32[]{:S(2)}, u32[]{:S(2)}) %collective-permute-start.6) | collective-permute-done | bytes 28704 | tf_op jit(solution)/shard_map/ppermute | solution.py:649
  58.3 0.3 collective-permute-done.4.z_low
  58.5 0.9 shard_map.74
  59.4 0.1 collective-permute-start.8
  59.5 4.8 %collective-permute-start.7 = (f32[48,128]{1,0:T(8,128)S(1)}, f32[48,128]{1,0:T(8,128)S(1)}, u32[]{:S(2)}, u32[]{:S(2)}) collective-permute-start(f32[48,128]{1,0:T(8,128)S(1)} %get-tuple-element.24), channel_id=1, source_target_pairs={{0,120},{8,0},{16,8},{24,16},{32,24},{40,32},{48,40},{56,48},{64,5... | collective-permute-start | bytes 73736 | tf_op jit(solution)/shard_map/ppermute | solution.py:637
  64.3 0.9 collective-permute-done.7
  65.2 0.3 collective-permute-done.8
  65.5 2.8 %collective-permute-start.10 = (f32[144,128]{1,0:T(8,128)S(1)}, f32[144,128]{1,0:T(8,128)S(1)}, u32[]{:S(2)}, u32[]{:S(2)}) collective-permute-start(f32[144,128]{1,0:T(8,128)S(1)} %constant_dynamic-update-slice_fusion.refs_3_), channel_id=1, source_target_pairs={{0,1},{1,2},{2,3},{3,4},{4,5},{5,6},{6,7},{7,0},{8,9},{9,10},{10,1... | collective-permute-start | bytes 221192 | tf_op jit(solution)/shard_map/ppermute | solution.py:637
  68.3 0.6 collective-permute-start.9
  68.8 0.6 shard_map.75
  69.5 18.7 %all_to_all.32 = f32[128,1,128]{2,1,0:T(1,128)S(1)} all-to-all(f32[128,1,128]{2,1,0:T(1,128)S(1)} %bitcast.19), channel_id=1, replica_groups=mesh['mesh'=16,'bg'=8] {'mesh','bg'}, dimensions={0} | all-to-all | bytes 131072 | tf_op jit(solution)/shard_map/all_to_all | solution.py:632
  88.1 3.9 %shard_map.76 = (f32[48,128]{1,0:T(8,128)S(1)}, f32[128,128]{1,0:T(8,128)}, f32[48,128]{1,0:T(8,128)S(1)}) custom-call(f32[144,128]{1,0:T(8,128)S(1)} %pad_maximum_fusion.refs_0_, f32[144,128]{1,0:T(8,128)S(1)} %collective-permute-done.2.refs_1_, f32[144,128]{1,0:T(8,128)S(1)} %collective-permute-done.3.refs_2_, ...), custom_call_target="tpu_custom_call" | custom-call | tf_op jit(solution)/shard_map/pallas_call | solution.py:30
  92.0 4.4 %all-to-all-start.3 = ((f32[128,1,128]{2,1,0:T(1,128)}), f32[128,1,128]{2,1,0:T(1,128)S(1)}, u32[]{:S(2)}, u32[]{:S(2)}) async-start(f32[128,1,128]{2,1,0:T(1,128)} %bitcast.10), calls=%async_computation.3 | async-start | bytes 131072 | tf_op jit(solution)/shard_map/all_to_all | solution.py:632
  96.5 0.3 shard_map.77
  96.8 9.2 %all-to-all-done.3 = f32[128,1,128]{2,1,0:T(1,128)S(1)} async-done(((f32[128,1,128]{2,1,0:T(1,128)}), f32[128,1,128]{2,1,0:T(1,128)S(1)}, u32[]{:S(2)}, u32[]{:S(2)}) %all-to-all-start.3) | async-done | bytes 65568 | tf_op jit(solution)/shard_map/all_to_all | solution.py:632
  106.0 1.8 %shard_map.78 = (f32[3,4,4,128]{3,2,1,0:T(4,128)}, f32[2,5]{1,0:T(2,128)}) custom-call(f32[3,4,4,128]{3,2,1,0:T(4,128)S(1)} %get-tuple-element.29.own_ref, f32[3,4,4,128]{3,2,1,0:T(4,128)S(1)} %get-tuple-element.30.move_ref, f32[128,128]{1,0:T(8,128)S(1)} %bitcast.18, f32[128,128]{1,0:T(8,128)S(1)} %bitcast.20), custom_call_target="tpu_custom_call" | custom-call | tf_op jit(solution)/shard_map/pallas_call | solution.py:30
  (12 shorter events, 0.0 us)
Async XLA Ops:
  2.6 23.3 %all-to-all-start = ((f32[128,1,640]{2,1,0:T(1,128)}), f32[128,1,640]{2,1,0:T(1,128)S(1)}, u32[]{:S(2)}, u32[]{:S(2)}) async-start(f32[128,1,640]{2,1,0:T(1,128)} %shard_map.70), calls=%async_computation | async-start | bytes 655360 | tf_op jit(solution)/shard_map/all_to_all | solution.py:632
  15.1 23.4 %collective-permute-start.1 = (f32[48,128]{1,0:T(8,128)S(1)}, f32[48,128]{1,0:T(8,128)S(1)}, u32[]{:S(2)}, u32[]{:S(2)}) collective-permute-start(f32[48,128]{1,0:T(8,128)S(1)} %shard_map.68), channel_id=1, source_target_pairs={{0,8},{8,16},{16,24},{24,32},{32,40},{40,48},{48,56},{56,64},{64,7... | collective-permute-start | bytes 73736 | tf_op jit(solution)/shard_map/ppermute | solution.py:637
  16.5 22.0 %collective-permute-start = (f32[48,128]{1,0:T(8,128)S(1)}, f32[48,128]{1,0:T(8,128)S(1)}, u32[]{:S(2)}, u32[]{:S(2)}) collective-permute-start(f32[48,128]{1,0:T(8,128)S(1)} %shard_map.68), channel_id=1, source_target_pairs={{0,120},{8,0},{16,8},{24,16},{32,24},{40,32},{48,40},{56,48},{64,5... | collective-permute-start | bytes 73736 | tf_op jit(solution)/shard_map/ppermute | solution.py:637
  34.1 14.5 %all-to-all-start.1 = ((f32[128,1,136]{2,1,0:T(1,128)}), f32[128,1,136]{2,1,0:T(1,128)S(1)}, u32[]{:S(2)}, u32[]{:S(2)}) async-start(f32[128,1,136]{2,1,0:T(1,128)} %shard_map.72), calls=%async_computation.1 | async-start | bytes 262144 | tf_op jit(solution)/shard_map/all_to_all | solution.py:632
  38.5 14.3 %collective-permute-start.3 = (f32[144,128]{1,0:T(8,128)S(1)}, f32[144,128]{1,0:T(8,128)S(1)}, u32[]{:S(2)}, u32[]{:S(2)}) collective-permute-start(f32[144,128]{1,0:T(8,128)S(1)} %pad_maximum_fusion.refs_0_), channel_id=1, source_target_pairs={{0,1},{1,2},{2,3},{3,4},{4,5},{5,6},{6,7},{7,0},{8,9},{9,10},{10,1... | collective-permute-start | bytes 221192 | tf_op jit(solution)/shard_map/ppermute | solution.py:637
  40.2 12.7 %collective-permute-start.2 = (f32[144,128]{1,0:T(8,128)S(1)}, f32[144,128]{1,0:T(8,128)S(1)}, u32[]{:S(2)}, u32[]{:S(2)}) collective-permute-start(f32[144,128]{1,0:T(8,128)S(1)} %pad_maximum_fusion.refs_0_), channel_id=1, source_target_pairs={{0,7},{1,0},{2,1},{3,2},{4,3},{5,4},{6,5},{7,6},{8,15},{9,8},{10,9... | collective-permute-start | bytes 221192 | tf_op jit(solution)/shard_map/ppermute | solution.py:637
  51.4 6.8 %collective-permute-start.6 = (f32[56,128]{1,0:T(8,128)S(1)}, f32[56,128]{1,0:T(8,128)S(1)}, u32[]{:S(2)}, u32[]{:S(2)}) collective-permute-start(f32[56,128]{1,0:T(8,128)S(1)} %shard_map.73.own), channel_id=1, source_target_pairs={{0,9},{1,10},{2,11},{3,12},{4,13},{5,14},{6,15},{7,8},{8,17},{9,18... | collective-permute-start | bytes 86024 | tf_op jit(solution)/shard_map/ppermute | solution.py:649
  52.1 6.1 %collective-permute-start.5 = (f32[56,128]{1,0:T(8,128)S(1)}, f32[56,128]{1,0:T(8,128)S(1)}, u32[]{:S(2)}, u32[]{:S(2)}) collective-permute-start(f32[56,128]{1,0:T(8,128)S(1)} %shard_map.73.own), channel_id=1, source_target_pairs={{0,1},{1,2},{2,3},{3,4},{4,5},{5,6},{6,7},{7,0},{8,9},{9,10},{10,1... | collective-permute-start | bytes 86024 | tf_op jit(solution)/shard_map/ppermute | solution.py:637
  52.4 6.1 %collective-permute-start.4 = (f32[56,128]{1,0:T(8,128)S(1)}, f32[56,128]{1,0:T(8,128)S(1)}, u32[]{:S(2)}, u32[]{:S(2)}) collective-permute-start(f32[56,128]{1,0:T(8,128)S(1)} %shard_map.73.own), channel_id=1, source_target_pairs={{0,8},{8,16},{16,24},{24,32},{32,40},{40,48},{48,56},{56,64},{64,7... | collective-permute-start | bytes 86024 | tf_op jit(solution)/shard_map/ppermute | solution.py:637
  59.4 6.1 %collective-permute-start.8 = (f32[48,128]{1,0:T(8,128)S(1)}, f32[48,128]{1,0:T(8,128)S(1)}, u32[]{:S(2)}, u32[]{:S(2)}) collective-permute-start(f32[48,128]{1,0:T(8,128)S(1)} %get-tuple-element.24), channel_id=1, source_target_pairs={{0,8},{8,16},{16,24},{24,32},{32,40},{40,48},{48,56},{56,64},{64,7... | collective-permute-start | bytes 73736 | tf_op jit(solution)/shard_map/ppermute | solution.py:637
  59.5 5.7 %collective-permute-start.7 = (f32[48,128]{1,0:T(8,128)S(1)}, f32[48,128]{1,0:T(8,128)S(1)}, u32[]{:S(2)}, u32[]{:S(2)}) collective-permute-start(f32[48,128]{1,0:T(8,128)S(1)} %get-tuple-element.24), channel_id=1, source_target_pairs={{0,120},{8,0},{16,8},{24,16},{32,24},{40,32},{48,40},{56,48},{64,5... | collective-permute-start | bytes 73736 | tf_op jit(solution)/shard_map/ppermute | solution.py:637
  65.5 22.6 %collective-permute-start.10 = (f32[144,128]{1,0:T(8,128)S(1)}, f32[144,128]{1,0:T(8,128)S(1)}, u32[]{:S(2)}, u32[]{:S(2)}) collective-permute-start(f32[144,128]{1,0:T(8,128)S(1)} %constant_dynamic-update-slice_fusion.refs_3_), channel_id=1, source_target_pairs={{0,1},{1,2},{2,3},{3,4},{4,5},{5,6},{6,7},{7,0},{8,9},{9,10},{10,1... | collective-permute-start | bytes 221192 | tf_op jit(solution)/shard_map/ppermute | solution.py:637
  68.3 19.9 %collective-permute-start.9 = (f32[144,128]{1,0:T(8,128)S(1)}, f32[144,128]{1,0:T(8,128)S(1)}, u32[]{:S(2)}, u32[]{:S(2)}) collective-permute-start(f32[144,128]{1,0:T(8,128)S(1)} %constant_dynamic-update-slice_fusion.refs_3_), channel_id=1, source_target_pairs={{0,7},{1,0},{2,1},{3,2},{4,3},{5,4},{6,5},{7,6},{8,15},{9,8},{10,9... | collective-permute-start | bytes 221192 | tf_op jit(solution)/shard_map/ppermute | solution.py:637
  92.0 14.0 %all-to-all-start.3 = ((f32[128,1,128]{2,1,0:T(1,128)}), f32[128,1,128]{2,1,0:T(1,128)S(1)}, u32[]{:S(2)}, u32[]{:S(2)}) async-start(f32[128,1,128]{2,1,0:T(1,128)} %bitcast.10), calls=%async_computation.3 | async-start | bytes 131072 | tf_op jit(solution)/shard_map/all_to_all | solution.py:632

commit v8 on v7

--- a/solution.py
+++ b/solution.py
@@ -358,7 +358,7 @@
 
 
 def newton_step(totals):
-    _, linear, quadratic, cubic, quartic, floor = (totals[:, i : i + 1] for i in range(6))
+    _, linear, quadratic, cubic, quartic, floor = (jnp.broadcast_to(totals[:, i : i + 1], (8, 128)) for i in range(6))
     step = jnp.zeros_like(linear)
     for _ in range(4):
         slope = linear + step * (2.0 * quadratic + step * (3.0 * cubic + step * 4.0 * quartic))
@@ -503,14 +503,12 @@
     line_sums(size_ref, jac_ref, part_ref, turn_ref, terms_out)
 
 
-def second_kernel(*refs):
-    field_refs, shift_refs = refs[:3], refs[3:6]
-    size_ref, terms_in, move_ref, terms_out, own_ref, nodes_ref, jac_ref, part_ref, turn_ref, sum_ref = refs[6:]
+def second_kernel(before_ref, drift_ref, size_ref, terms_in, move_ref, terms_out, step_ref, jac_ref, part_ref, turn_ref):
     step = newton_step(add_up(terms_in))
-    for i, (field_ref, shift_ref) in enumerate(zip(field_refs, shift_refs)):
-        sum_ref[i] = field_ref[...] + step * shift_ref[...]
-    own_ref[...] = sum_ref[0, :48, :]
-    jacobians(field_pieces([sum_ref.at[i] for i in range(3)]), nodes_ref, jac_ref)
+    step_ref[...] = step
+    for row in range(0, JAC_ROWS, 8):
+        rows = slice(row, row + 8)
+        jac_ref[rows, :] = before_ref[rows, :] + step * drift_ref[rows, :]
     descend(size_ref, jac_ref, part_ref, turn_ref, move_ref)
     line_sums(size_ref, jac_ref, part_ref, turn_ref, terms_out)
 
@@ -528,7 +526,7 @@
     return pltpu.VMEM((count, 128), jnp.float32)
 
 
-def first_jacobians(field):
+def all_jacobians(field):
     return call(jacobian_kernel, rows_of(JAC_ROWS), field, [scratch_of(NODES_ROWS)])
 
 
@@ -541,10 +539,9 @@
     return call(line_kernel, TERMS, [jac, turn, size], [scratch_of(81 * 8)])
 
 
-def second_pass(field, shift, size, terms):
-    scratch = [scratch_of(rows) for rows in (NODES_ROWS, JAC_ROWS, JAC_ROWS, TURN_ROWS)]
-    scratch.append(pltpu.VMEM((3, 144, 128), jnp.float32))
-    return call(second_kernel, [NODE, TERMS, NODE], [*field, *shift, size, terms], scratch)
+def second_pass(jac, drift, size, terms):
+    scratch = [scratch_of(rows) for rows in (JAC_ROWS, JAC_ROWS, TURN_ROWS)]
+    return call(second_kernel, [NODE, TERMS, rows_of(8)], [jac, drift, size, terms], scratch)
 
 
 def interleave(back):
@@ -576,9 +573,10 @@
     return call(split_kernel, out, [nodes], [pltpu.VMEM((48, 128), jnp.float32)], far=(0,))
 
 
-def join_kernel(first_ref, second_ref, out_first_ref, out_second_ref, rows_ref):
+def join_kernel(count, *refs):
+    rows_ref = refs[-1]
     low = lax.broadcasted_iota(jnp.int32, (1, 128), 1) < 64
-    for i, new_ref in enumerate((first_ref, second_ref)):
+    for i, new_ref in enumerate(refs[:count]):
         for c in range(3):
             for az in range(2):
                 for ay in range(2):
@@ -592,28 +590,31 @@
     rows = jnp.dot(
         rows_ref[...], interleave(True), precision=lax.Precision.HIGHEST, preferred_element_type=jnp.float32
     )
-    out_first_ref[...] = rows[:48].reshape(3, 4, 4, 128)
-    out_second_ref[...] = rows[48:].reshape(3, 4, 4, 128)
-
-
-def join_nodes(first, second):
-    out = jax.ShapeDtypeStruct((3, 4, 4, 128), jnp.float32)
-    return call(join_kernel, [out, out], [first, second], [pltpu.VMEM((96, 128), jnp.float32)])
-
-
-def finish_kernel(own_ref, move_ref, first_ref, second_ref, out_ref, coeff_ref):
+    for i, out_ref in enumerate(refs[count : 2 * count]):
+        out_ref[...] = rows[i * 48 : i * 48 + 48].reshape(3, 4, 4, 128)
+
+
+def join_nodes(*nodes):
+    outs = [jax.ShapeDtypeStruct((3, 4, 4, 128), jnp.float32) for _ in nodes]
+    kernel = functools.partial(join_kernel, len(nodes))
+    return call(kernel, outs, list(nodes), [scratch_of(48 * len(nodes))])
+
+
+def finish_kernel(own_ref, first_move_ref, last_move_ref, step_ref, first_ref, second_ref, out_ref, coeff_ref):
     second = add_up(second_ref)
-    step = newton_step(second)
+    step = newton_step(second)[:4]
+    first_step = step_ref[:4, :]
     for c in range(3):
         for z in range(4):
-            out_ref[c, z] = own_ref[c, z] + step * move_ref[c, z]
+            field = own_ref[c, z] + first_step * first_move_ref[c, z]
+            out_ref[c, z] = field + step * last_move_ref[c, z]
     coeff_ref[0:1, :] = add_up(first_ref)[:, :5] * (1.0 / 32768.0)
     coeff_ref[1:2, :] = second[:, :5] * (1.0 / 32768.0)
 
 
-def finish(own, move, first, second):
+def finish(*args):
     outs = [jax.ShapeDtypeStruct((3, 4, 4, 128), jnp.float32), jax.ShapeDtypeStruct((2, 5), jnp.float32)]
-    return call(finish_kernel, outs, [own, move, first, second], [], last=True)
+    return call(finish_kernel, outs, list(args), [], last=True)
 
 
 def pack_kernel(elem_ref, coord_ref, out_ref):
@@ -663,16 +664,17 @@
     field = along_bg(rows)
     sizes = place(found, query_point[0].T)
     sizes = from_below(sizes)
-    jac = first_jacobians(field)
+    jac = all_jacobians(field)
     move, turn, size = first_descent(jac, sizes)
     rows = along_mesh(move)
     terms = first_line(jac, turn, size)
     first_terms = exchange(terms)
     shift = along_bg(rows)
-    last_move, last_terms, last_own = second_pass(field, shift, size, first_terms)
-    own, move = join_nodes(last_own, last_move)
+    drift = all_jacobians(shift)
+    last_move, last_terms, step = second_pass(jac, drift, size, first_terms)
     last_terms = exchange(last_terms)
-    return finish(own, move, first_terms, last_terms)
+    nodes = join_nodes(own, move, last_move)
+    return finish(*nodes, step, first_terms, last_terms)
 
 
 def solution(mesh):

time: 108 us -> 107 us (level)
  blocking collectives: 18.7 us -> 0 us
  starting transfers between devices: 37 us -> 46.2 us
  waiting for transfers between devices: 27.7 us -> 36.7 us
  Pallas kernels: 23.7 us -> 22.4 us
    all_to_all x1 -> x0, blocking collectives: 18.7 us -> none  [exchange(): lax.all_to_all(values, ('mesh', 'bg'), split_axis=0, concat_axis=0, tiled...]
    all_to_all x3 -> x4, starting transfers between devices: 20.3 us -> 29.4 us  [exchange(): lax.all_to_all(values, ('mesh', 'bg'), split_axis=0, concat_axis=0, tiled...]
    all_to_all x3 -> x4, waiting for transfers between devices: 21.4 us -> 30.4 us  [exchange(): lax.all_to_all(values, ('mesh', 'bg'), split_axis=0, concat_axis=0, tiled...]
    pallas_call x11 -> x12, Pallas kernels: 23.7 us -> 22.4 us  [call(): pl.pallas_call(kernel, out_shape=outs, in_specs=in_vmem(len(args)), out_s...]
  transfers between devices with their start and end apart: 14 -> 15, of which waited for: 7 -> 8; matrix products, arithmetic and copies ran while one was open for 0% -> 0% of each run, Pallas kernels for 14% -> 15%
where the time goes in v8:
time: 107 us; the launch traced here: 106 us
  starting transfers between devices  46.2 us (43%)
  waiting for transfers between devices  36.7 us (34%)
  Pallas kernels  22.4 us (21%)
    all_to_all x4, waiting for transfers between devices, exchange(): lax.all_to_all(values, ('mesh', 'bg'), split_axis=0, concat_axis=0, tiled...  30.4 us
    all_to_all x4, starting transfers between devices, exchange(): lax.all_to_all(values, ('mesh', 'bg'), split_axis=0, concat_axis=0, tiled...  29.4 us
    pallas_call x12, Pallas kernels, call(): pl.pallas_call(kernel, out_shape=outs, in_specs=in_vmem(len(args)), out_s...  22.4 us
    ppermute x10, starting transfers between devices, moved(): lax.ppermute(values, axis, [(i, (i - by) % count) for i in range(count)])  16 us
    ppermute x1, waiting for transfers between devices, from_below(): lax.ppermute(block, ('mesh', 'bg'), steps)  4.84 us
  transfers between devices with their start and end apart: 15, of which 8 were waited for; matrix products, arithmetic and copies ran while one was open for 0% of the time, Pallas kernels for 15%

profile of v8, /device:TPU:1, one launch (start us, length us, event | category | flops | bytes accessed | tf_op | source)
XLA Modules:
  0.0 106.1 jit_solution(9283023832316643947)
XLA Ops:
  0.6 1.9 %shard_map.70 = f32[128,1,640]{2,1,0:T(1,128)} custom-call(s32[136,128]{1,0:T(8,128)} %bitcast.21, f32[3,136,128]{2,1,0:T(8,128)} %bitcast.20), custom_call_target="tpu_custom_call" | custom-call | tf_op jit(solution)/shard_map/pallas_call | solution.py:30
  2.6 11.5 %all-to-all-start = ((f32[128,1,640]{2,1,0:T(1,128)}), f32[128,1,640]{2,1,0:T(1,128)S(1)}, u32[]{:S(2)}, u32[]{:S(2)}) async-start(f32[128,1,640]{2,1,0:T(1,128)} %shard_map.70), calls=%async_computation | async-start | bytes 655360 | tf_op jit(solution)/shard_map/all_to_all | solution.py:633
  14.1 1.0 shard_map.68.refs_0_
  15.1 1.4 %collective-permute-start.1 = (f32[48,128]{1,0:T(8,128)S(1)}, f32[48,128]{1,0:T(8,128)S(1)}, u32[]{:S(2)}, u32[]{:S(2)}) collective-permute-start(f32[48,128]{1,0:T(8,128)S(1)} %shard_map.68.refs_0_), channel_id=1, source_target_pairs={{0,8},{8,16},{16,24},{24,32},{32,40},{40,48},{48,56},{56,64},{64,7... | collective-permute-start | bytes 73736 | tf_op jit(solution)/shard_map/ppermute | solution.py:638
  16.5 4.1 %collective-permute-start = (f32[48,128]{1,0:T(8,128)S(1)}, f32[48,128]{1,0:T(8,128)S(1)}, u32[]{:S(2)}, u32[]{:S(2)}) collective-permute-start(f32[48,128]{1,0:T(8,128)S(1)} %shard_map.68.refs_0_), channel_id=1, source_target_pairs={{0,120},{8,0},{16,8},{24,16},{32,24},{40,32},{48,40},{56,48},{64,5... | collective-permute-start | bytes 73736 | tf_op jit(solution)/shard_map/ppermute | solution.py:638
  20.6 1.5 %shard_map.71 = (bf16[512,512]{1,0:T(8,128)(2,1)S(1)}, s32[8,8192]{1,0:T(8,128)S(1)}, f32[8,128]{1,0:T(8,128)S(1)}) custom-call(f32[8,16384]{1,0:T(8,128)} %table_ref.1), custom_call_target="tpu_custom_call" | custom-call | tf_op jit(solution)/shard_map/pallas_call | solution.py:30
  22.1 3.8 %all-to-all-done.asked_ref = f32[128,1,640]{2,1,0:T(1,128)S(1)} async-done(((f32[128,1,640]{2,1,0:T(1,128)}), f32[128,1,640]{2,1,0:T(1,128)S(1)}, u32[]{:S(2)}, u32[]{:S(2)}) %all-to-all-start) | async-done | bytes 327712 | tf_op jit(solution)/shard_map/all_to_all | solution.py:633
  25.9 8.2 %shard_map.72 = f32[128,1,136]{2,1,0:T(1,128)} custom-call(f32[128,1,640]{2,1,0:T(1,128)S(1)} %all-to-all-done.asked_ref, bf16[512,512]{1,0:T(8,128)(2,1)S(1)} %get-tuple-element.22.split_ref, s32[8,8192]{1,0:T(8,128)S(1)} %get-tuple-element.23.packed_ref, f32[8,128]{1,0:T(8,128)S(1)} %get-tuple-element.24.unit_ref), custom_call_target="tpu_custom_call" | custom-call | tf_op jit(solution)/shard_map/pallas_call | solution.py:30
  34.1 4.4 %all-to-all-start.1 = ((f32[128,1,136]{2,1,0:T(1,128)}), f32[128,1,136]{2,1,0:T(1,128)S(1)}, u32[]{:S(2)}, u32[]{:S(2)}) async-start(f32[128,1,136]{2,1,0:T(1,128)} %shard_map.72), calls=%async_computation.1 | async-start | bytes 262144 | tf_op jit(solution)/shard_map/all_to_all | solution.py:633
  38.5 1.6 %collective-permute-start.3 = (f32[144,128]{1,0:T(8,128)S(1)}, f32[144,128]{1,0:T(8,128)S(1)}, u32[]{:S(2)}, u32[]{:S(2)}) collective-permute-start(f32[144,128]{1,0:T(8,128)S(1)} %pad_maximum_fusion.refs_0_), channel_id=1, source_target_pairs={{0,1},{1,2},{2,3},{3,4},{4,5},{5,6},{6,7},{7,0},{8,9},{9,10},{10,1... | collective-permute-start | bytes 221192 | tf_op jit(solution)/shard_map/ppermute | solution.py:638
  40.2 8.4 %all-to-all-done.1.found_ref = f32[128,1,136]{2,1,0:T(1,128)S(1)} async-done(((f32[128,1,136]{2,1,0:T(1,128)}), f32[128,1,136]{2,1,0:T(1,128)S(1)}, u32[]{:S(2)}, u32[]{:S(2)}) %all-to-all-start.1) | async-done | bytes 69664 | tf_op jit(solution)/shard_map/all_to_all | solution.py:633
  48.5 2.8 %shard_map.73.own = f32[56,128]{1,0:T(8,128)S(1)} custom-call(f32[128,1,136]{2,1,0:T(1,128)S(1)} %all-to-all-done.1.found_ref, s32[136,128]{1,0:T(8,128)} %bitcast.22), custom_call_target="tpu_custom_call" | custom-call | tf_op jit(solution)/shard_map/pallas_call | solution.py:30
  51.4 0.7 collective-permute-start.6
  52.1 0.3 collective-permute-start.5
  52.4 0.4 collective-permute-start.4
  52.8 0.6 shard_map.69.jac_ref.before_ref
  53.4 4.8 %collective-permute-done.6.corner = f32[56,128]{1,0:T(8,128)S(1)} collective-permute-done((f32[56,128]{1,0:T(8,128)S(1)}, f32[56,128]{1,0:T(8,128)S(1)}, u32[]{:S(2)}, u32[]{:S(2)}) %collective-permute-start.6) | collective-permute-done | bytes 28704 | tf_op jit(solution)/shard_map/ppermute | solution.py:650
  58.2 0.3 collective-permute-done.4.z_low
  58.5 0.9 shard_map.74
  59.5 4.8 %collective-permute-start.7 = (f32[48,128]{1,0:T(8,128)S(1)}, f32[48,128]{1,0:T(8,128)S(1)}, u32[]{:S(2)}, u32[]{:S(2)}) collective-permute-start(f32[48,128]{1,0:T(8,128)S(1)} %get-tuple-element.25.refs_1_), channel_id=1, source_target_pairs={{0,120},{8,0},{16,8},{24,16},{32,24},{40,32},{48,40},{56,48},{64,5... | collective-permute-start | bytes 73736 | tf_op jit(solution)/shard_map/ppermute | solution.py:638
  64.3 0.9 collective-permute-done.7
  65.5 2.8 %collective-permute-start.10 = (f32[144,128]{1,0:T(8,128)S(1)}, f32[144,128]{1,0:T(8,128)S(1)}, u32[]{:S(2)}, u32[]{:S(2)}) collective-permute-start(f32[144,128]{1,0:T(8,128)S(1)} %constant_dynamic-update-slice_fusion.refs_0_), channel_id=1, source_target_pairs={{0,1},{1,2},{2,3},{3,4},{4,5},{5,6},{6,7},{7,0},{8,9},{9,10},{10,1... | collective-permute-start | bytes 221192 | tf_op jit(solution)/shard_map/ppermute | solution.py:638
  68.2 0.6 collective-permute-start.9
  68.8 1.2 %shard_map.76 = f32[128,128]{1,0:T(8,128)} custom-call(f32[1944,128]{1,0:T(8,128)S(1)} %shard_map.69.jac_ref.before_ref, f32[256,128]{1,0:T(8,128)S(1)} %get-tuple-element.27.turn_ref, f32[216,128]{1,0:T(8,128)S(1)} %get-tuple-element.26.size_ref), custom_call_target="tpu_custom_call" | custom-call | tf_op jit(solution)/shard_map/pallas_call | solution.py:30
  70.0 9.2 %all-to-all-start.2 = ((f32[128,1,128]{2,1,0:T(1,128)}), f32[128,1,128]{2,1,0:T(1,128)S(1)}, u32[]{:S(2)}, u32[]{:S(2)}) async-start(f32[128,1,128]{2,1,0:T(1,128)} %bitcast.7), calls=%async_computation.2 | async-start | bytes 131072 | tf_op jit(solution)/shard_map/all_to_all | solution.py:633
  79.3 0.6 shard_map.75.drift_ref
  79.8 9.0 %all-to-all-done.2 = f32[128,1,128]{2,1,0:T(1,128)S(1)} async-done(((f32[128,1,128]{2,1,0:T(1,128)}), f32[128,1,128]{2,1,0:T(1,128)S(1)}, u32[]{:S(2)}, u32[]{:S(2)}) %all-to-all-start.2) | async-done | bytes 65568 | tf_op jit(solution)/shard_map/all_to_all | solution.py:633
  88.9 2.4 %shard_map.77 = (f32[48,128]{1,0:T(8,128)S(1)}, f32[128,128]{1,0:T(8,128)}, f32[8,128]{1,0:T(8,128)S(1)}) custom-call(f32[1944,128]{1,0:T(8,128)S(1)} %shard_map.69.jac_ref.before_ref, f32[1944,128]{1,0:T(8,128)S(1)} %shard_map.75.drift_ref, f32[216,128]{1,0:T(8,128)S(1)} %get-tuple-element.26.size_ref, f32[128,128]{1,0:T(8,128)S(1)} %bitcast.17), custom_call_target="tpu_custom_call" | custom-call | tf_op jit(solution)/shard_map/pallas_call | solution.py:30
  91.3 4.4 %all-to-all-start.3 = ((f32[128,1,128]{2,1,0:T(1,128)}), f32[128,1,128]{2,1,0:T(1,128)S(1)}, u32[]{:S(2)}, u32[]{:S(2)}) async-start(f32[128,1,128]{2,1,0:T(1,128)} %bitcast.10), calls=%async_computation.3 | async-start | bytes 131072 | tf_op jit(solution)/shard_map/all_to_all | solution.py:633
  95.7 0.4 shard_map.78
  96.1 9.2 %all-to-all-done.3 = f32[128,1,128]{2,1,0:T(1,128)S(1)} async-done(((f32[128,1,128]{2,1,0:T(1,128)}), f32[128,1,128]{2,1,0:T(1,128)S(1)}, u32[]{:S(2)}, u32[]{:S(2)}) %all-to-all-start.3) | async-done | bytes 65568 | tf_op jit(solution)/shard_map/all_to_all | solution.py:633
  105.3 0.8 shard_map.79
  (14 shorter events, 0.4 us)
Async XLA Ops:
  2.6 23.3 %all-to-all-start = ((f32[128,1,640]{2,1,0:T(1,128)}), f32[128,1,640]{2,1,0:T(1,128)S(1)}, u32[]{:S(2)}, u32[]{:S(2)}) async-start(f32[128,1,640]{2,1,0:T(1,128)} %shard_map.70), calls=%async_computation | async-start | bytes 655360 | tf_op jit(solution)/shard_map/all_to_all | solution.py:633
  15.1 23.4 %collective-permute-start.1 = (f32[48,128]{1,0:T(8,128)S(1)}, f32[48,128]{1,0:T(8,128)S(1)}, u32[]{:S(2)}, u32[]{:S(2)}) collective-permute-start(f32[48,128]{1,0:T(8,128)S(1)} %shard_map.68.refs_0_), channel_id=1, source_target_pairs={{0,8},{8,16},{16,24},{24,32},{32,40},{40,48},{48,56},{56,64},{64,7... | collective-permute-start | bytes 73736 | tf_op jit(solution)/shard_map/ppermute | solution.py:638
  16.5 22.0 %collective-permute-start = (f32[48,128]{1,0:T(8,128)S(1)}, f32[48,128]{1,0:T(8,128)S(1)}, u32[]{:S(2)}, u32[]{:S(2)}) collective-permute-start(f32[48,128]{1,0:T(8,128)S(1)} %shard_map.68.refs_0_), channel_id=1, source_target_pairs={{0,120},{8,0},{16,8},{24,16},{32,24},{40,32},{48,40},{56,48},{64,5... | collective-permute-start | bytes 73736 | tf_op jit(solution)/shard_map/ppermute | solution.py:638
  34.1 14.4 %all-to-all-start.1 = ((f32[128,1,136]{2,1,0:T(1,128)}), f32[128,1,136]{2,1,0:T(1,128)S(1)}, u32[]{:S(2)}, u32[]{:S(2)}) async-start(f32[128,1,136]{2,1,0:T(1,128)} %shard_map.72), calls=%async_computation.1 | async-start | bytes 262144 | tf_op jit(solution)/shard_map/all_to_all | solution.py:633
  38.5 14.3 %collective-permute-start.3 = (f32[144,128]{1,0:T(8,128)S(1)}, f32[144,128]{1,0:T(8,128)S(1)}, u32[]{:S(2)}, u32[]{:S(2)}) collective-permute-start(f32[144,128]{1,0:T(8,128)S(1)} %pad_maximum_fusion.refs_0_), channel_id=1, source_target_pairs={{0,1},{1,2},{2,3},{3,4},{4,5},{5,6},{6,7},{7,0},{8,9},{9,10},{10,1... | collective-permute-start | bytes 221192 | tf_op jit(solution)/shard_map/ppermute | solution.py:638
  40.1 12.6 %collective-permute-start.2 = (f32[144,128]{1,0:T(8,128)S(1)}, f32[144,128]{1,0:T(8,128)S(1)}, u32[]{:S(2)}, u32[]{:S(2)}) collective-permute-start(f32[144,128]{1,0:T(8,128)S(1)} %pad_maximum_fusion.refs_0_), channel_id=1, source_target_pairs={{0,7},{1,0},{2,1},{3,2},{4,3},{5,4},{6,5},{7,6},{8,15},{9,8},{10,9... | collective-permute-start | bytes 221192 | tf_op jit(solution)/shard_map/ppermute | solution.py:638
  51.4 6.8 %collective-permute-start.6 = (f32[56,128]{1,0:T(8,128)S(1)}, f32[56,128]{1,0:T(8,128)S(1)}, u32[]{:S(2)}, u32[]{:S(2)}) collective-permute-start(f32[56,128]{1,0:T(8,128)S(1)} %shard_map.73.own), channel_id=1, source_target_pairs={{0,9},{1,10},{2,11},{3,12},{4,13},{5,14},{6,15},{7,8},{8,17},{9,18... | collective-permute-start | bytes 86024 | tf_op jit(solution)/shard_map/ppermute | solution.py:650
  52.1 6.1 %collective-permute-start.5 = (f32[56,128]{1,0:T(8,128)S(1)}, f32[56,128]{1,0:T(8,128)S(1)}, u32[]{:S(2)}, u32[]{:S(2)}) collective-permute-start(f32[56,128]{1,0:T(8,128)S(1)} %shard_map.73.own), channel_id=1, source_target_pairs={{0,1},{1,2},{2,3},{3,4},{4,5},{5,6},{6,7},{7,0},{8,9},{9,10},{10,1... | collective-permute-start | bytes 86024 | tf_op jit(solution)/shard_map/ppermute | solution.py:638
  52.4 6.1 %collective-permute-start.4 = (f32[56,128]{1,0:T(8,128)S(1)}, f32[56,128]{1,0:T(8,128)S(1)}, u32[]{:S(2)}, u32[]{:S(2)}) collective-permute-start(f32[56,128]{1,0:T(8,128)S(1)} %shard_map.73.own), channel_id=1, source_target_pairs={{0,8},{8,16},{16,24},{24,32},{32,40},{40,48},{48,56},{56,64},{64,7... | collective-permute-start | bytes 86024 | tf_op jit(solution)/shard_map/ppermute | solution.py:638
  59.4 6.1 %collective-permute-start.8 = (f32[48,128]{1,0:T(8,128)S(1)}, f32[48,128]{1,0:T(8,128)S(1)}, u32[]{:S(2)}, u32[]{:S(2)}) collective-permute-start(f32[48,128]{1,0:T(8,128)S(1)} %get-tuple-element.25.refs_1_), channel_id=1, source_target_pairs={{0,8},{8,16},{16,24},{24,32},{32,40},{40,48},{48,56},{56,64},{64,7... | collective-permute-start | bytes 73736 | tf_op jit(solution)/shard_map/ppermute | solution.py:638
  59.5 5.7 %collective-permute-start.7 = (f32[48,128]{1,0:T(8,128)S(1)}, f32[48,128]{1,0:T(8,128)S(1)}, u32[]{:S(2)}, u32[]{:S(2)}) collective-permute-start(f32[48,128]{1,0:T(8,128)S(1)} %get-tuple-element.25.refs_1_), channel_id=1, source_target_pairs={{0,120},{8,0},{16,8},{24,16},{32,24},{40,32},{48,40},{56,48},{64,5... | collective-permute-start | bytes 73736 | tf_op jit(solution)/shard_map/ppermute | solution.py:638
  65.5 13.8 %collective-permute-start.10 = (f32[144,128]{1,0:T(8,128)S(1)}, f32[144,128]{1,0:T(8,128)S(1)}, u32[]{:S(2)}, u32[]{:S(2)}) collective-permute-start(f32[144,128]{1,0:T(8,128)S(1)} %constant_dynamic-update-slice_fusion.refs_0_), channel_id=1, source_target_pairs={{0,1},{1,2},{2,3},{3,4},{4,5},{5,6},{6,7},{7,0},{8,9},{9,10},{10,1... | collective-permute-start | bytes 221192 | tf_op jit(solution)/shard_map/ppermute | solution.py:638
  68.2 11.0 %collective-permute-start.9 = (f32[144,128]{1,0:T(8,128)S(1)}, f32[144,128]{1,0:T(8,128)S(1)}, u32[]{:S(2)}, u32[]{:S(2)}) collective-permute-start(f32[144,128]{1,0:T(8,128)S(1)} %constant_dynamic-update-slice_fusion.refs_0_), channel_id=1, source_target_pairs={{0,7},{1,0},{2,1},{3,2},{4,3},{5,4},{6,5},{7,6},{8,15},{9,8},{10,9... | collective-permute-start | bytes 221192 | tf_op jit(solution)/shard_map/ppermute | solution.py:638
  70.0 18.8 %all-to-all-start.2 = ((f32[128,1,128]{2,1,0:T(1,128)}), f32[128,1,128]{2,1,0:T(1,128)S(1)}, u32[]{:S(2)}, u32[]{:S(2)}) async-start(f32[128,1,128]{2,1,0:T(1,128)} %bitcast.7), calls=%async_computation.2 | async-start | bytes 131072 | tf_op jit(solution)/shard_map/all_to_all | solution.py:633
  91.3 14.0 %all-to-all-start.3 = ((f32[128,1,128]{2,1,0:T(1,128)}), f32[128,1,128]{2,1,0:T(1,128)S(1)}, u32[]{:S(2)}, u32[]{:S(2)}) async-start(f32[128,1,128]{2,1,0:T(1,128)} %bitcast.10), calls=%async_computation.3 | async-start | bytes 131072 | tf_op jit(solution)/shard_map/all_to_all | solution.py:633

commit v9 on v8

--- a/solution.py
+++ b/solution.py
@@ -14,8 +14,9 @@
 COLS = 256
 
 
-GATHER_ROWS = 64
-ROUNDS = 8
+ROUNDS = 2
+GATHERED = 36
+PAIRS = 16
 
 
 def in_vmem(count):
@@ -78,6 +79,17 @@
     return jnp.where(mask, choose(leaf, masks, first + half, half), choose(leaf, masks, first, half))
 
 
+def tall(row):
+    return jnp.broadcast_to(row, (16, 128)).astype(jnp.bfloat16)
+
+
+def at_rows(index_ref, count, row, *values):
+    index = tall(row)
+    zero = jnp.zeros((16, 128), jnp.bfloat16)
+    masks = [index_ref[at : at + 16, :] == index for at in range(0, count, 16)]
+    return jnp.concatenate([jnp.where(mask, value, zero) for value in values for mask in masks], axis=0)
+
+
 def weigh(coef, x, y, z):
     corner = lax.broadcasted_iota(jnp.int32, coef.shape, 0)
     weight_x = jnp.where((corner & 1) == 1, x, 1.0 - x)
@@ -94,16 +106,13 @@
     for j in range(4):
         turned_ref[j * SLOTS + 128 : (j + 1) * SLOTS, :] = tails[j * 8 : j * 8 + 8]
     column_ref[...] = lax.broadcasted_iota(jnp.int32, (COLS, 128), 0).astype(jnp.float32).astype(jnp.bfloat16)
-    one = jnp.ones((), jnp.bfloat16)
-    zero = jnp.zeros((), jnp.bfloat16)
 
     def step(i, carry):
-        base = pl.multiple_of(i * 8, 8)
-        ids, xs, ys, zs = (turned_ref[pl.ds(pl.multiple_of(j * SLOTS + base, 8), 8), :] for j in range(4))
-        ids = ids.astype(jnp.int32)
         unit = unit_ref[...]
-        for r in range(8):
-            own = jnp.broadcast_to(ids[r : r + 1], (8, 128))
+        for r in range(GATHERED):
+            at = i * GATHERED + r
+            ids, x, y, z = (turned_ref[pl.ds(j * SLOTS + at, 1), :] for j in range(4))
+            own = jnp.broadcast_to(ids.astype(jnp.int32), (8, 128))
             lane = own & 127
             masks = [(own & (128 << bit)) != 0 for bit in range(6)]
 
@@ -113,33 +122,28 @@
             word = choose(leaf, masks, 0, 64)
             whole = jnp.where((own & (TABLE // 2)) != 0, word, word << 16) >> 16
             coef = whole.astype(jnp.float32) * unit
-            result_ref[pl.ds(base + r, 1), :] = weigh(coef, xs[r : r + 1], ys[r : r + 1], zs[r : r + 1])
-
-        start = GATHER_ROWS + i * 9
-        for pair in range(5):
-            at = start + 2 * pair
-            wide = 2 if pair < 4 else 1
+            result_ref[pl.ds(at, 1), :] = weigh(coef, x, y, z)
+
+        for pair in range(PAIRS):
+            at = ROUNDS * GATHERED + (i * PAIRS + pair) * 2
             pair_ids, px, py, pz = (
-                jnp.concatenate([turned_ref[pl.ds(j * SLOTS + at + k, 1), :] for k in range(wide)], axis=1)
+                jnp.concatenate([turned_ref[pl.ds(j * SLOTS + at + k, 1), :] for k in range(2)], axis=1)
                 for j in range(4)
             )
             pair_ids = pair_ids.astype(jnp.int32)
-            column = (pair_ids & (COLS - 1)).astype(jnp.float32).astype(jnp.bfloat16)
+            column = (pair_ids & (COLS - 1)).astype(jnp.float32)
+            ones = jnp.ones((16, 128), jnp.bfloat16)
             chosen = jnp.concatenate(
-                [
-                    jnp.where(column_ref[...] == column[:, half * 128 : half * 128 + 128], one, zero)
-                    for half in range(wide)
-                ],
-                axis=1,
+                [at_rows(column_ref, COLS, column[:, k * 128 : k * 128 + 128], ones) for k in range(2)], axis=1
             )
             picked = jnp.dot(split_ref[:, :COLS], chosen, preferred_element_type=jnp.float32) + jnp.dot(
                 split_ref[:, COLS:], chosen, preferred_element_type=jnp.float32
             )
-            own = jnp.broadcast_to(pair_ids, (8, 128 * wide))
+            own = jnp.broadcast_to(pair_ids, (8, 256))
             masks = [(own & (COLS << bit)) != 0 for bit in range(6)]
             coef = choose(lambda row: picked[row * 8 : row * 8 + 8], masks, 0, 64)
             value = weigh(coef, px, py, pz)
-            for k in range(wide):
+            for k in range(2):
                 result_ref[pl.ds(at + k, 1), :] = value[:, k * 128 : k * 128 + 128]
         return carry
 
@@ -175,8 +179,7 @@
     row_ref[...] = (((jz * 3 + jy) * 3 + jx) * 2 + ey).astype(jnp.float32)
     lane_ref[...] = (ez * 64 + ex).astype(jnp.float32)
     at_ref[...] = lax.broadcasted_iota(jnp.int32, (128, 128), 0).astype(jnp.float32).astype(jnp.bfloat16)
-    one = jnp.ones((), jnp.bfloat16)
-    zero = jnp.zeros((), jnp.bfloat16)
+    ones = jnp.ones((16, 128), jnp.bfloat16)
 
     def step(i, total):
         values = value_ref[i * 8 : i * 8 + 8, :]
@@ -185,11 +188,10 @@
         left, right = [], []
         for r in range(8):
             value = values[r : r + 1]
-            upper = value.astype(jnp.bfloat16)
-            lower = (value - upper.astype(jnp.float32)).astype(jnp.bfloat16)
-            row = at_ref[:64, :] == rows[r : r + 1].astype(jnp.bfloat16)
-            left.append(jnp.concatenate([jnp.where(row, upper, zero), jnp.where(row, lower, zero)], axis=0))
-            right.append(jnp.where(at_ref[...] == lanes[r : r + 1].astype(jnp.bfloat16), one, zero))
+            upper = tall(value)
+            lower = tall(value - upper[:1].astype(jnp.float32))
+            left.append(at_rows(at_ref, 64, rows[r : r + 1], upper, lower))
+            right.append(at_rows(at_ref, 128, lanes[r : r + 1], ones))
         left = jnp.concatenate(left, axis=1)
         right = jnp.concatenate(right, axis=1)
         return total + lax.dot_general(left, right, (((1,), (1,)), ((), ())), preferred_element_type=jnp.float32)
@@ -271,7 +273,7 @@
 
 def at_point(c, k, jz, jy, jx):
     row = (((jz * 3 + jy) * 3 + jx) * 9 + k) * 8
-    return pl.ds(pl.multiple_of(row + c * 24, 8), 8)
+    return pl.ds(row + c * 24, 8)
 
 
 def forward(local, out_ref, at):
@@ -320,7 +322,7 @@
         for y in range(2):
             for z, node in enumerate((folded[0][y] + z_down(folded[2][y]), folded[1][y])):
                 row = (z * 4 + y * 2 + x) * 8
-                out_ref[pl.ds(pl.multiple_of(row + c * 64, 8), 8), :] = node
+                out_ref[pl.ds(row + c * 64, 8), :] = node
 
 
 def symmetric(build):
@@ -353,7 +355,7 @@
 
 
 def weight_at(jz, jy, jx):
-    along_z = jnp.where(jz == 1, MIDDLE, OUTER).astype(jnp.float32)
+    along_z = MIDDLE if jz == 1 else OUTER
     return along_z * ((MIDDLE if jy == 1 else OUTER) * (MIDDLE if jx == 1 else OUTER))
 
 
@@ -388,11 +390,8 @@
 
 
 def each(body):
-    def run(i, carry):
+    for i in range(3):
         body(i)
-        return carry
-
-    lax.fori_loop(0, 3, run, 0)
 
 
 def jacobians(field, nodes_ref, jac_ref):
@@ -403,7 +402,7 @@
     def known(c):
         def local(z, y, x):
             row = ((z == 2) * 2 + (y == 2)) * 192 + ((z % 2) * 4 + (y % 2) * 2 + x % 2) * 8
-            value = nodes_ref[pl.ds(pl.multiple_of(row + c * 64, 8), 8), :]
+            value = nodes_ref[pl.ds(row + c * 64, 8), :]
             return x_up(value) if x == 2 else value
 
         return local
@@ -413,7 +412,7 @@
 
 def descend(size_ref, jac_ref, part_ref, turn_ref, move_ref):
     def size_at(jz, jy, jx):
-        return size_ref[pl.ds(pl.multiple_of((jz * 9 + jy * 3 + jx) * 8, 8), 8), :]
+        return size_ref[pl.ds((jz * 9 + jy * 3 + jx) * 8, 8), :]
 
     turn_ref[192:, :] = jnp.zeros((64, 128), jnp.float32)
 

time: 107 us -> 105 us (0.981)
  Pallas kernels: 22.4 us -> 20 us
    pallas_call x12, Pallas kernels: 22.4 us -> 20 us  [call(): pl.pallas_call(kernel, out_shape=outs, in_specs=in_vmem(len(args)), out_s...]
  transfers between devices with their start and end apart: 15 -> 15, of which waited for: 8 -> 8; matrix products, arithmetic and copies ran while one was open for 0% -> 0% of each run, Pallas kernels for 15% -> 14%
where the time goes in v9:
time: 105 us; the launch traced here: 104 us
  starting transfers between devices  46.2 us (44%)
  waiting for transfers between devices  37.1 us (35%)
  Pallas kernels  20 us (19%)
    all_to_all x4, waiting for transfers between devices, exchange(): lax.all_to_all(values, ('mesh', 'bg'), split_axis=0, concat_axis=0, tiled...  30.6 us
    all_to_all x4, starting transfers between devices, exchange(): lax.all_to_all(values, ('mesh', 'bg'), split_axis=0, concat_axis=0, tiled...  29.4 us
    pallas_call x12, Pallas kernels, call(): pl.pallas_call(kernel, out_shape=outs, in_specs=in_vmem(len(args)), out_s...  20 us
    ppermute x10, starting transfers between devices, moved(): lax.ppermute(values, axis, [(i, (i - by) % count) for i in range(count)])  16 us
    ppermute x1, waiting for transfers between devices, from_below(): lax.ppermute(block, ('mesh', 'bg'), steps)  5.03 us
  transfers between devices with their start and end apart: 15, of which 8 were waited for; matrix products, arithmetic and copies ran while one was open for 0% of the time, Pallas kernels for 14%

profile of v9, /device:TPU:1, one launch (start us, length us, event | category | flops | bytes accessed | tf_op | source)
XLA Modules:
  0.0 104.1 jit_solution(8286991565622019705)
XLA Ops:
  0.6 1.9 %shard_map.70 = f32[128,1,640]{2,1,0:T(1,128)} custom-call(s32[136,128]{1,0:T(8,128)} %bitcast.21, f32[3,136,128]{2,1,0:T(8,128)} %bitcast.20), custom_call_target="tpu_custom_call" | custom-call | tf_op jit(solution)/shard_map/pallas_call | solution.py:31
  2.6 11.5 %all-to-all-start = ((f32[128,1,640]{2,1,0:T(1,128)}), f32[128,1,640]{2,1,0:T(1,128)S(1)}, u32[]{:S(2)}, u32[]{:S(2)}) async-start(f32[128,1,640]{2,1,0:T(1,128)} %shard_map.70), calls=%async_computation | async-start | bytes 655360 | tf_op jit(solution)/shard_map/all_to_all | solution.py:632
  14.1 1.0 shard_map.68.refs_0_
  15.1 1.4 %collective-permute-start.1 = (f32[48,128]{1,0:T(8,128)S(1)}, f32[48,128]{1,0:T(8,128)S(1)}, u32[]{:S(2)}, u32[]{:S(2)}) collective-permute-start(f32[48,128]{1,0:T(8,128)S(1)} %shard_map.68.refs_0_), channel_id=1, source_target_pairs={{0,8},{8,16},{16,24},{24,32},{32,40},{40,48},{48,56},{56,64},{64,7... | collective-permute-start | bytes 73736 | tf_op jit(solution)/shard_map/ppermute | solution.py:637
  16.5 4.1 %collective-permute-start = (f32[48,128]{1,0:T(8,128)S(1)}, f32[48,128]{1,0:T(8,128)S(1)}, u32[]{:S(2)}, u32[]{:S(2)}) collective-permute-start(f32[48,128]{1,0:T(8,128)S(1)} %shard_map.68.refs_0_), channel_id=1, source_target_pairs={{0,120},{8,0},{16,8},{24,16},{32,24},{40,32},{48,40},{56,48},{64,5... | collective-permute-start | bytes 73736 | tf_op jit(solution)/shard_map/ppermute | solution.py:637
  20.6 1.5 %shard_map.71 = (bf16[512,512]{1,0:T(8,128)(2,1)S(1)}, s32[8,8192]{1,0:T(8,128)S(1)}, f32[8,128]{1,0:T(8,128)S(1)}) custom-call(f32[8,16384]{1,0:T(8,128)} %table_ref.1), custom_call_target="tpu_custom_call" | custom-call | tf_op jit(solution)/shard_map/pallas_call | solution.py:31
  22.1 3.8 %all-to-all-done.asked_ref = f32[128,1,640]{2,1,0:T(1,128)S(1)} async-done(((f32[128,1,640]{2,1,0:T(1,128)}), f32[128,1,640]{2,1,0:T(1,128)S(1)}, u32[]{:S(2)}, u32[]{:S(2)}) %all-to-all-start) | async-done | bytes 327712 | tf_op jit(solution)/shard_map/all_to_all | solution.py:632
  25.9 6.5 %shard_map.72 = f32[128,1,136]{2,1,0:T(1,128)} custom-call(f32[128,1,640]{2,1,0:T(1,128)S(1)} %all-to-all-done.asked_ref, bf16[512,512]{1,0:T(8,128)(2,1)S(1)} %get-tuple-element.22.split_ref, s32[8,8192]{1,0:T(8,128)S(1)} %get-tuple-element.23.packed_ref, f32[8,128]{1,0:T(8,128)S(1)} %get-tuple-element.24.unit_ref), custom_call_target="tpu_custom_call" | custom-call | tf_op jit(solution)/shard_map/pallas_call | solution.py:31
  32.4 4.4 %all-to-all-start.1 = ((f32[128,1,136]{2,1,0:T(1,128)}), f32[128,1,136]{2,1,0:T(1,128)S(1)}, u32[]{:S(2)}, u32[]{:S(2)}) async-start(f32[128,1,136]{2,1,0:T(1,128)} %shard_map.72), calls=%async_computation.1 | async-start | bytes 262144 | tf_op jit(solution)/shard_map/all_to_all | solution.py:632
  36.8 1.6 %collective-permute-start.3 = (f32[144,128]{1,0:T(8,128)S(1)}, f32[144,128]{1,0:T(8,128)S(1)}, u32[]{:S(2)}, u32[]{:S(2)}) collective-permute-start(f32[144,128]{1,0:T(8,128)S(1)} %pad_maximum_fusion.refs_0_), channel_id=1, source_target_pairs={{0,1},{1,2},{2,3},{3,4},{4,5},{5,6},{6,7},{7,0},{8,9},{9,10},{10,1... | collective-permute-start | bytes 221192 | tf_op jit(solution)/shard_map/ppermute | solution.py:637
  38.5 8.4 %all-to-all-done.1.found_ref = f32[128,1,136]{2,1,0:T(1,128)S(1)} async-done(((f32[128,1,136]{2,1,0:T(1,128)}), f32[128,1,136]{2,1,0:T(1,128)S(1)}, u32[]{:S(2)}, u32[]{:S(2)}) %all-to-all-start.1) | async-done | bytes 69664 | tf_op jit(solution)/shard_map/all_to_all | solution.py:632
  46.8 2.9 %shard_map.73.own = f32[56,128]{1,0:T(8,128)S(1)} custom-call(f32[128,1,136]{2,1,0:T(1,128)S(1)} %all-to-all-done.1.found_ref, s32[136,128]{1,0:T(8,128)} %bitcast.22), custom_call_target="tpu_custom_call" | custom-call | tf_op jit(solution)/shard_map/pallas_call | solution.py:31
  49.7 0.7 collective-permute-start.6
  50.5 0.3 collective-permute-start.5
  50.8 0.4 collective-permute-start.4
  51.2 0.4 shard_map.69.jac_ref.before_ref
  51.6 5.0 %collective-permute-done.6.corner = f32[56,128]{1,0:T(8,128)S(1)} collective-permute-done((f32[56,128]{1,0:T(8,128)S(1)}, f32[56,128]{1,0:T(8,128)S(1)}, u32[]{:S(2)}, u32[]{:S(2)}) %collective-permute-start.6) | collective-permute-done | bytes 28704 | tf_op jit(solution)/shard_map/ppermute | solution.py:649
  56.6 0.3 collective-permute-done.4.z_low
  56.8 0.8 shard_map.74
  57.7 4.8 %collective-permute-start.7 = (f32[48,128]{1,0:T(8,128)S(1)}, f32[48,128]{1,0:T(8,128)S(1)}, u32[]{:S(2)}, u32[]{:S(2)}) collective-permute-start(f32[48,128]{1,0:T(8,128)S(1)} %get-tuple-element.25.refs_1_), channel_id=1, source_target_pairs={{0,120},{8,0},{16,8},{24,16},{32,24},{40,32},{48,40},{56,48},{64,5... | collective-permute-start | bytes 73736 | tf_op jit(solution)/shard_map/ppermute | solution.py:637
  62.5 0.9 collective-permute-done.7
  63.7 2.8 %collective-permute-start.10 = (f32[144,128]{1,0:T(8,128)S(1)}, f32[144,128]{1,0:T(8,128)S(1)}, u32[]{:S(2)}, u32[]{:S(2)}) collective-permute-start(f32[144,128]{1,0:T(8,128)S(1)} %constant_dynamic-update-slice_fusion.refs_0_), channel_id=1, source_target_pairs={{0,1},{1,2},{2,3},{3,4},{4,5},{5,6},{6,7},{7,0},{8,9},{9,10},{10,1... | collective-permute-start | bytes 221192 | tf_op jit(solution)/shard_map/ppermute | solution.py:637
  66.5 0.6 collective-permute-start.9
  67.0 1.2 %shard_map.76 = f32[128,128]{1,0:T(8,128)} custom-call(f32[1944,128]{1,0:T(8,128)S(1)} %shard_map.69.jac_ref.before_ref, f32[256,128]{1,0:T(8,128)S(1)} %get-tuple-element.27.turn_ref, f32[216,128]{1,0:T(8,128)S(1)} %get-tuple-element.26.size_ref), custom_call_target="tpu_custom_call" | custom-call | tf_op jit(solution)/shard_map/pallas_call | solution.py:31
  68.3 9.2 %all-to-all-start.2 = ((f32[128,1,128]{2,1,0:T(1,128)}), f32[128,1,128]{2,1,0:T(1,128)S(1)}, u32[]{:S(2)}, u32[]{:S(2)}) async-start(f32[128,1,128]{2,1,0:T(1,128)} %bitcast.7), calls=%async_computation.2 | async-start | bytes 131072 | tf_op jit(solution)/shard_map/all_to_all | solution.py:632
  77.5 0.4 shard_map.75.drift_ref
  77.9 9.2 %all-to-all-done.2 = f32[128,1,128]{2,1,0:T(1,128)S(1)} async-done(((f32[128,1,128]{2,1,0:T(1,128)}), f32[128,1,128]{2,1,0:T(1,128)S(1)}, u32[]{:S(2)}, u32[]{:S(2)}) %all-to-all-start.2) | async-done | bytes 65568 | tf_op jit(solution)/shard_map/all_to_all | solution.py:632
  87.1 2.2 %shard_map.77 = (f32[48,128]{1,0:T(8,128)S(1)}, f32[128,128]{1,0:T(8,128)}, f32[8,128]{1,0:T(8,128)S(1)}) custom-call(f32[1944,128]{1,0:T(8,128)S(1)} %shard_map.69.jac_ref.before_ref, f32[1944,128]{1,0:T(8,128)S(1)} %shard_map.75.drift_ref, f32[216,128]{1,0:T(8,128)S(1)} %get-tuple-element.26.size_ref, f32[128,128]{1,0:T(8,128)S(1)} %bitcast.17), custom_call_target="tpu_custom_call" | custom-call | tf_op jit(solution)/shard_map/pallas_call | solution.py:31
  89.3 4.4 %all-to-all-start.3 = ((f32[128,1,128]{2,1,0:T(1,128)}), f32[128,1,128]{2,1,0:T(1,128)S(1)}, u32[]{:S(2)}, u32[]{:S(2)}) async-start(f32[128,1,128]{2,1,0:T(1,128)} %bitcast.10), calls=%async_computation.3 | async-start | bytes 131072 | tf_op jit(solution)/shard_map/all_to_all | solution.py:632
  93.7 0.4 shard_map.78
  94.1 9.2 %all-to-all-done.3 = f32[128,1,128]{2,1,0:T(1,128)S(1)} async-done(((f32[128,1,128]{2,1,0:T(1,128)}), f32[128,1,128]{2,1,0:T(1,128)S(1)}, u32[]{:S(2)}, u32[]{:S(2)}) %all-to-all-start.3) | async-done | bytes 65568 | tf_op jit(solution)/shard_map/all_to_all | solution.py:632
  103.3 0.8 shard_map.79
  (14 shorter events, 0.4 us)
Async XLA Ops:
  2.6 23.3 %all-to-all-start = ((f32[128,1,640]{2,1,0:T(1,128)}), f32[128,1,640]{2,1,0:T(1,128)S(1)}, u32[]{:S(2)}, u32[]{:S(2)}) async-start(f32[128,1,640]{2,1,0:T(1,128)} %shard_map.70), calls=%async_computation | async-start | bytes 655360 | tf_op jit(solution)/shard_map/all_to_all | solution.py:632
  15.1 21.7 %collective-permute-start.1 = (f32[48,128]{1,0:T(8,128)S(1)}, f32[48,128]{1,0:T(8,128)S(1)}, u32[]{:S(2)}, u32[]{:S(2)}) collective-permute-start(f32[48,128]{1,0:T(8,128)S(1)} %shard_map.68.refs_0_), channel_id=1, source_target_pairs={{0,8},{8,16},{16,24},{24,32},{32,40},{40,48},{48,56},{56,64},{64,7... | collective-permute-start | bytes 73736 | tf_op jit(solution)/shard_map/ppermute | solution.py:637
  16.5 20.3 %collective-permute-start = (f32[48,128]{1,0:T(8,128)S(1)}, f32[48,128]{1,0:T(8,128)S(1)}, u32[]{:S(2)}, u32[]{:S(2)}) collective-permute-start(f32[48,128]{1,0:T(8,128)S(1)} %shard_map.68.refs_0_), channel_id=1, source_target_pairs={{0,120},{8,0},{16,8},{24,16},{32,24},{40,32},{48,40},{56,48},{64,5... | collective-permute-start | bytes 73736 | tf_op jit(solution)/shard_map/ppermute | solution.py:637
  32.4 14.4 %all-to-all-start.1 = ((f32[128,1,136]{2,1,0:T(1,128)}), f32[128,1,136]{2,1,0:T(1,128)S(1)}, u32[]{:S(2)}, u32[]{:S(2)}) async-start(f32[128,1,136]{2,1,0:T(1,128)} %shard_map.72), calls=%async_computation.1 | async-start | bytes 262144 | tf_op jit(solution)/shard_map/all_to_all | solution.py:632
  36.8 14.4 %collective-permute-start.3 = (f32[144,128]{1,0:T(8,128)S(1)}, f32[144,128]{1,0:T(8,128)S(1)}, u32[]{:S(2)}, u32[]{:S(2)}) collective-permute-start(f32[144,128]{1,0:T(8,128)S(1)} %pad_maximum_fusion.refs_0_), channel_id=1, source_target_pairs={{0,1},{1,2},{2,3},{3,4},{4,5},{5,6},{6,7},{7,0},{8,9},{9,10},{10,1... | collective-permute-start | bytes 221192 | tf_op jit(solution)/shard_map/ppermute | solution.py:637
  38.5 12.7 %collective-permute-start.2 = (f32[144,128]{1,0:T(8,128)S(1)}, f32[144,128]{1,0:T(8,128)S(1)}, u32[]{:S(2)}, u32[]{:S(2)}) collective-permute-start(f32[144,128]{1,0:T(8,128)S(1)} %pad_maximum_fusion.refs_0_), channel_id=1, source_target_pairs={{0,7},{1,0},{2,1},{3,2},{4,3},{5,4},{6,5},{7,6},{8,15},{9,8},{10,9... | collective-permute-start | bytes 221192 | tf_op jit(solution)/shard_map/ppermute | solution.py:637
  49.7 6.8 %collective-permute-start.6 = (f32[56,128]{1,0:T(8,128)S(1)}, f32[56,128]{1,0:T(8,128)S(1)}, u32[]{:S(2)}, u32[]{:S(2)}) collective-permute-start(f32[56,128]{1,0:T(8,128)S(1)} %shard_map.73.own), channel_id=1, source_target_pairs={{0,9},{1,10},{2,11},{3,12},{4,13},{5,14},{6,15},{7,8},{8,17},{9,18... | collective-permute-start | bytes 86024 | tf_op jit(solution)/shard_map/ppermute | solution.py:649
  50.5 6.1 %collective-permute-start.5 = (f32[56,128]{1,0:T(8,128)S(1)}, f32[56,128]{1,0:T(8,128)S(1)}, u32[]{:S(2)}, u32[]{:S(2)}) collective-permute-start(f32[56,128]{1,0:T(8,128)S(1)} %shard_map.73.own), channel_id=1, source_target_pairs={{0,1},{1,2},{2,3},{3,4},{4,5},{5,6},{6,7},{7,0},{8,9},{9,10},{10,1... | collective-permute-start | bytes 86024 | tf_op jit(solution)/shard_map/ppermute | solution.py:637
  50.8 6.1 %collective-permute-start.4 = (f32[56,128]{1,0:T(8,128)S(1)}, f32[56,128]{1,0:T(8,128)S(1)}, u32[]{:S(2)}, u32[]{:S(2)}) collective-permute-start(f32[56,128]{1,0:T(8,128)S(1)} %shard_map.73.own), channel_id=1, source_target_pairs={{0,8},{8,16},{16,24},{24,32},{32,40},{40,48},{48,56},{56,64},{64,7... | collective-permute-start | bytes 86024 | tf_op jit(solution)/shard_map/ppermute | solution.py:637
  57.7 6.1 %collective-permute-start.8 = (f32[48,128]{1,0:T(8,128)S(1)}, f32[48,128]{1,0:T(8,128)S(1)}, u32[]{:S(2)}, u32[]{:S(2)}) collective-permute-start(f32[48,128]{1,0:T(8,128)S(1)} %get-tuple-element.25.refs_1_), channel_id=1, source_target_pairs={{0,8},{8,16},{16,24},{24,32},{32,40},{40,48},{48,56},{56,64},{64,7... | collective-permute-start | bytes 73736 | tf_op jit(solution)/shard_map/ppermute | solution.py:637
  57.7 5.7 %collective-permute-start.7 = (f32[48,128]{1,0:T(8,128)S(1)}, f32[48,128]{1,0:T(8,128)S(1)}, u32[]{:S(2)}, u32[]{:S(2)}) collective-permute-start(f32[48,128]{1,0:T(8,128)S(1)} %get-tuple-element.25.refs_1_), channel_id=1, source_target_pairs={{0,120},{8,0},{16,8},{24,16},{32,24},{40,32},{48,40},{56,48},{64,5... | collective-permute-start | bytes 73736 | tf_op jit(solution)/shard_map/ppermute | solution.py:637
  63.7 13.8 %collective-permute-start.10 = (f32[144,128]{1,0:T(8,128)S(1)}, f32[144,128]{1,0:T(8,128)S(1)}, u32[]{:S(2)}, u32[]{:S(2)}) collective-permute-start(f32[144,128]{1,0:T(8,128)S(1)} %constant_dynamic-update-slice_fusion.refs_0_), channel_id=1, source_target_pairs={{0,1},{1,2},{2,3},{3,4},{4,5},{5,6},{6,7},{7,0},{8,9},{9,10},{10,1... | collective-permute-start | bytes 221192 | tf_op jit(solution)/shard_map/ppermute | solution.py:637
  66.5 11.1 %collective-permute-start.9 = (f32[144,128]{1,0:T(8,128)S(1)}, f32[144,128]{1,0:T(8,128)S(1)}, u32[]{:S(2)}, u32[]{:S(2)}) collective-permute-start(f32[144,128]{1,0:T(8,128)S(1)} %constant_dynamic-update-slice_fusion.refs_0_), channel_id=1, source_target_pairs={{0,7},{1,0},{2,1},{3,2},{4,3},{5,4},{6,5},{7,6},{8,15},{9,8},{10,9... | collective-permute-start | bytes 221192 | tf_op jit(solution)/shard_map/ppermute | solution.py:637
  68.3 18.9 %all-to-all-start.2 = ((f32[128,1,128]{2,1,0:T(1,128)}), f32[128,1,128]{2,1,0:T(1,128)S(1)}, u32[]{:S(2)}, u32[]{:S(2)}) async-start(f32[128,1,128]{2,1,0:T(1,128)} %bitcast.7), calls=%async_computation.2 | async-start | bytes 131072 | tf_op jit(solution)/shard_map/all_to_all | solution.py:632
  89.3 14.0 %all-to-all-start.3 = ((f32[128,1,128]{2,1,0:T(1,128)}), f32[128,1,128]{2,1,0:T(1,128)S(1)}, u32[]{:S(2)}, u32[]{:S(2)}) async-start(f32[128,1,128]{2,1,0:T(1,128)} %bitcast.10), calls=%async_computation.3 | async-start | bytes 131072 | tf_op jit(solution)/shard_map/all_to_all | solution.py:632

commit v10 on v9

--- a/solution.py
+++ b/solution.py
@@ -15,8 +15,8 @@
 
 
 ROUNDS = 2
-GATHERED = 36
-PAIRS = 16
+GATHERED = 34
+PAIRS = 17
 
 
 def in_vmem(count):
@@ -209,6 +209,10 @@
 
 HALF_GAP = float(np.sqrt(0.15))
 OUTER, MIDDLE = 5.0 / 18.0, 8.0 / 18.0
+
+
+def shift_pieces(refs):
+    return {(z, y): (refs[z], (y % 3) * 48) for z in (-1, 0, 1) for y in (-1, 0, 1)}
 
 
 def field_pieces(refs):
@@ -488,8 +492,8 @@
     terms_out[...] = jnp.broadcast_to(terms, (SRC, 128))
 
 
-def jacobian_kernel(*refs):
-    jacobians(field_pieces(refs[:3]), refs[4], refs[3])
+def jacobian_kernel(pieces, *refs):
+    jacobians(pieces(refs[:3]), refs[4], refs[3])
 
 
 def descent_kernel(jac_ref, own, z_low, y_low, corner, move_ref, turn_ref, size_ref, part_ref):
@@ -525,8 +529,9 @@
     return pltpu.VMEM((count, 128), jnp.float32)
 
 
-def all_jacobians(field):
-    return call(jacobian_kernel, rows_of(JAC_ROWS), field, [scratch_of(NODES_ROWS)])
+def all_jacobians(field, pieces):
+    kernel = functools.partial(jacobian_kernel, pieces)
+    return call(kernel, rows_of(JAC_ROWS), field, [scratch_of(NODES_ROWS)])
 
 
 def first_descent(jac, sizes):
@@ -663,13 +668,13 @@
     field = along_bg(rows)
     sizes = place(found, query_point[0].T)
     sizes = from_below(sizes)
-    jac = all_jacobians(field)
+    jac = all_jacobians(field, field_pieces)
     move, turn, size = first_descent(jac, sizes)
-    rows = along_mesh(move)
+    rows = jnp.concatenate(along_bg(move), axis=0)
     terms = first_line(jac, turn, size)
     first_terms = exchange(terms)
-    shift = along_bg(rows)
-    drift = all_jacobians(shift)
+    shift = [rows, moved(rows, "mesh", 1), moved(rows, "mesh", -1)]
+    drift = all_jacobians(shift, shift_pieces)
     last_move, last_terms, step = second_pass(jac, drift, size, first_terms)
     last_terms = exchange(last_terms)
     nodes = join_nodes(own, move, last_move)

time: 105 us -> 101 us (0.962)
  starting transfers between devices: 46.2 us -> 41.6 us
  waiting for transfers between devices: 37.1 us -> 38.7 us
    all_to_all x4, starting transfers between devices: 29.4 us -> 25.9 us  [exchange(): lax.all_to_all(values, ('mesh', 'bg'), split_axis=0, concat_axis=0, tiled...]
    ppermute x10, waiting for transfers between devices: 1.48 us -> 2.95 us  [moved(): lax.ppermute(values, axis, [(i, (i - by) % count) for i in range(count)])]
    ppermute x10, starting transfers between devices: 16 us -> 14.9 us  [moved(): lax.ppermute(values, axis, [(i, (i - by) % count) for i in range(count)])]
  transfers between devices with their start and end apart: 15 -> 15, of which waited for: 8 -> 7; matrix products, arithmetic and copies ran while one was open for 0% -> 0% of each run, Pallas kernels for 14% -> 14%
where the time goes in v10:
time: 101 us
  starting transfers between devices  41.6 us (41%)
  waiting for transfers between devices  38.7 us (38%)
  Pallas kernels  19.8 us (20%)
    all_to_all x4, waiting for transfers between devices, exchange(): lax.all_to_all(values, ('mesh', 'bg'), split_axis=0, concat_axis=0, tiled...  30.7 us
    all_to_all x4, starting transfers between devices, exchange(): lax.all_to_all(values, ('mesh', 'bg'), split_axis=0, concat_axis=0, tiled...  25.9 us
    pallas_call x12, Pallas kernels, call(): pl.pallas_call(kernel, out_shape=outs, in_specs=in_vmem(len(args)), out_s...  19.8 us
    ppermute x10, starting transfers between devices, moved(): lax.ppermute(values, axis, [(i, (i - by) % count) for i in range(count)])  14.9 us
    ppermute x1, waiting for transfers between devices, from_below(): lax.ppermute(block, ('mesh', 'bg'), steps)  5.02 us
    ppermute x10, waiting for transfers between devices, moved(): lax.ppermute(values, axis, [(i, (i - by) % count) for i in range(count)])  2.95 us
  transfers between devices with their start and end apart: 15, of which 7 were waited for; matrix products, arithmetic and copies ran while one was open for 0% of the time, Pallas kernels for 14%

profile of v10, /device:TPU:1, one launch (start us, length us, event | category | flops | bytes accessed | tf_op | source)
XLA Modules:
  0.0 100.9 jit_solution(374728983425846556)
XLA Ops:
  0.6 1.9 %shard_map.70 = f32[128,1,640]{2,1,0:T(1,128)} custom-call(s32[136,128]{1,0:T(8,128)} %bitcast.21, f32[3,136,128]{2,1,0:T(8,128)} %bitcast.20), custom_call_target="tpu_custom_call" | custom-call | tf_op jit(solution)/shard_map/pallas_call | solution.py:31
  2.6 11.5 %all-to-all-start = ((f32[128,1,640]{2,1,0:T(1,128)}), f32[128,1,640]{2,1,0:T(1,128)S(1)}, u32[]{:S(2)}, u32[]{:S(2)}) async-start(f32[128,1,640]{2,1,0:T(1,128)} %shard_map.70), calls=%async_computation | async-start | bytes 655360 | tf_op jit(solution)/shard_map/all_to_all | solution.py:637
  14.1 1.0 %shard_map.68.refs_0_ = f32[48,128]{1,0:T(8,128)S(1)} custom-call(f32[3,4,4,128]{3,2,1,0:T(4,128)} %nodes_ref.1), custom_call_target="tpu_custom_call" | custom-call | tf_op jit(solution)/shard_map/pallas_call | solution.py:31
  15.1 1.4 %collective-permute-start.1 = (f32[48,128]{1,0:T(8,128)S(1)}, f32[48,128]{1,0:T(8,128)S(1)}, u32[]{:S(2)}, u32[]{:S(2)}) collective-permute-start(f32[48,128]{1,0:T(8,128)S(1)} %shard_map.68.refs_0_), channel_id=1, source_target_pairs={{0,8},{8,16},{16,24},{24,32},{32,40},{40,48},{48,56},{56,64},{64,7... | collective-permute-start | bytes 73736 | tf_op jit(solution)/shard_map/ppermute | solution.py:642
  16.5 4.1 %collective-permute-start = (f32[48,128]{1,0:T(8,128)S(1)}, f32[48,128]{1,0:T(8,128)S(1)}, u32[]{:S(2)}, u32[]{:S(2)}) collective-permute-start(f32[48,128]{1,0:T(8,128)S(1)} %shard_map.68.refs_0_), channel_id=1, source_target_pairs={{0,120},{8,0},{16,8},{24,16},{32,24},{40,32},{48,40},{56,48},{64,5... | collective-permute-start | bytes 73736 | tf_op jit(solution)/shard_map/ppermute | solution.py:642
  20.6 1.5 %shard_map.71 = (bf16[512,512]{1,0:T(8,128)(2,1)S(1)}, s32[8,8192]{1,0:T(8,128)S(1)}, f32[8,128]{1,0:T(8,128)S(1)}) custom-call(f32[8,16384]{1,0:T(8,128)} %table_ref.1), custom_call_target="tpu_custom_call" | custom-call | tf_op jit(solution)/shard_map/pallas_call | solution.py:31
  22.1 3.8 %all-to-all-done.asked_ref = f32[128,1,640]{2,1,0:T(1,128)S(1)} async-done(((f32[128,1,640]{2,1,0:T(1,128)}), f32[128,1,640]{2,1,0:T(1,128)S(1)}, u32[]{:S(2)}, u32[]{:S(2)}) %all-to-all-start) | async-done | bytes 327712 | tf_op jit(solution)/shard_map/all_to_all | solution.py:637
  25.9 6.3 %shard_map.72 = f32[128,1,136]{2,1,0:T(1,128)} custom-call(f32[128,1,640]{2,1,0:T(1,128)S(1)} %all-to-all-done.asked_ref, bf16[512,512]{1,0:T(8,128)(2,1)S(1)} %get-tuple-element.22.split_ref, s32[8,8192]{1,0:T(8,128)S(1)} %get-tuple-element.23.packed_ref, f32[8,128]{1,0:T(8,128)S(1)} %get-tuple-element.24.unit_ref), custom_call_target="tpu_custom_call" | custom-call | tf_op jit(solution)/shard_map/pallas_call | solution.py:31
  32.2 4.4 %all-to-all-start.1 = ((f32[128,1,136]{2,1,0:T(1,128)}), f32[128,1,136]{2,1,0:T(1,128)S(1)}, u32[]{:S(2)}, u32[]{:S(2)}) async-start(f32[128,1,136]{2,1,0:T(1,128)} %shard_map.72), calls=%async_computation.1 | async-start | bytes 262144 | tf_op jit(solution)/shard_map/all_to_all | solution.py:637
  36.6 1.6 %collective-permute-start.3 = (f32[144,128]{1,0:T(8,128)S(1)}, f32[144,128]{1,0:T(8,128)S(1)}, u32[]{:S(2)}, u32[]{:S(2)}) collective-permute-start(f32[144,128]{1,0:T(8,128)S(1)} %pad_maximum_fusion.refs_0_), channel_id=1, source_target_pairs={{0,1},{1,2},{2,3},{3,4},{4,5},{5,6},{6,7},{7,0},{8,9},{9,10},{10,1... | collective-permute-start | bytes 221192 | tf_op jit(solution)/shard_map/ppermute | solution.py:642
  38.2 8.4 %all-to-all-done.1.found_ref = f32[128,1,136]{2,1,0:T(1,128)S(1)} async-done(((f32[128,1,136]{2,1,0:T(1,128)}), f32[128,1,136]{2,1,0:T(1,128)S(1)}, u32[]{:S(2)}, u32[]{:S(2)}) %all-to-all-start.1) | async-done | bytes 69664 | tf_op jit(solution)/shard_map/all_to_all | solution.py:637
  46.6 2.9 %shard_map.73.own = f32[56,128]{1,0:T(8,128)S(1)} custom-call(f32[128,1,136]{2,1,0:T(1,128)S(1)} %all-to-all-done.1.found_ref, s32[136,128]{1,0:T(8,128)} %bitcast.22), custom_call_target="tpu_custom_call" | custom-call | tf_op jit(solution)/shard_map/pallas_call | solution.py:31
  49.5 0.7 collective-permute-start.6
  50.3 0.3 collective-permute-start.5
  50.5 0.4 collective-permute-start.4
  50.9 0.4 shard_map.69.jac_ref.before_ref
  51.3 5.0 %collective-permute-done.6.corner = f32[56,128]{1,0:T(8,128)S(1)} collective-permute-done((f32[56,128]{1,0:T(8,128)S(1)}, f32[56,128]{1,0:T(8,128)S(1)}, u32[]{:S(2)}, u32[]{:S(2)}) %collective-permute-start.6) | collective-permute-done | bytes 28704 | tf_op jit(solution)/shard_map/ppermute | solution.py:654
  56.4 0.3 collective-permute-done.4.z_low
  56.6 0.8 shard_map.74
  57.4 1.6 %collective-permute-start.8 = (f32[48,128]{1,0:T(8,128)S(1)}, f32[48,128]{1,0:T(8,128)S(1)}, u32[]{:S(2)}, u32[]{:S(2)}) collective-permute-start(f32[48,128]{1,0:T(8,128)S(1)} %get-tuple-element.25.refs_1_), channel_id=1, source_target_pairs={{0,1},{1,2},{2,3},{3,4},{4,5},{5,6},{6,7},{7,0},{8,9},{9,10},{10,1... | collective-permute-start | bytes 73736 | tf_op jit(solution)/shard_map/ppermute | solution.py:642
  59.0 0.6 collective-permute-start.7
  59.6 2.7 %collective-permute-done.7 = f32[48,128]{1,0:T(8,128)S(1)} collective-permute-done((f32[48,128]{1,0:T(8,128)S(1)}, f32[48,128]{1,0:T(8,128)S(1)}, u32[]{:S(2)}, u32[]{:S(2)}) %collective-permute-start.7) | collective-permute-done | bytes 24608 | tf_op jit(solution)/shard_map/ppermute | solution.py:642
  62.4 4.8 %collective-permute-start.9 = (f32[144,128]{1,0:T(8,128)S(1)}, f32[144,128]{1,0:T(8,128)S(1)}, u32[]{:S(2)}, u32[]{:S(2)}) collective-permute-start(f32[144,128]{1,0:T(8,128)S(1)} %constant_dynamic-update-slice_fusion.refs_0_), channel_id=1, source_target_pairs={{0,120},{8,0},{16,8},{24,16},{32,24},{40,32},{48,40},{56,48},{64,5... | collective-permute-start | bytes 221192 | tf_op jit(solution)/shard_map/ppermute | solution.py:642
  67.2 1.2 %shard_map.76 = f32[128,128]{1,0:T(8,128)} custom-call(f32[1944,128]{1,0:T(8,128)S(1)} %shard_map.69.jac_ref.before_ref, f32[256,128]{1,0:T(8,128)S(1)} %get-tuple-element.27.turn_ref, f32[216,128]{1,0:T(8,128)S(1)} %get-tuple-element.26.size_ref), custom_call_target="tpu_custom_call" | custom-call | tf_op jit(solution)/shard_map/pallas_call | solution.py:31
  68.4 5.7 %all-to-all-start.2 = ((f32[128,1,128]{2,1,0:T(1,128)}), f32[128,1,128]{2,1,0:T(1,128)S(1)}, u32[]{:S(2)}, u32[]{:S(2)}) async-start(f32[128,1,128]{2,1,0:T(1,128)} %bitcast.7), calls=%async_computation.2 | async-start | bytes 131072 | tf_op jit(solution)/shard_map/all_to_all | solution.py:637
  74.2 0.4 shard_map.75.drift_ref
  74.6 9.4 %all-to-all-done.2 = f32[128,1,128]{2,1,0:T(1,128)S(1)} async-done(((f32[128,1,128]{2,1,0:T(1,128)}), f32[128,1,128]{2,1,0:T(1,128)S(1)}, u32[]{:S(2)}, u32[]{:S(2)}) %all-to-all-start.2) | async-done | bytes 65568 | tf_op jit(solution)/shard_map/all_to_all | solution.py:637
  83.9 2.2 %shard_map.77 = (f32[48,128]{1,0:T(8,128)S(1)}, f32[128,128]{1,0:T(8,128)}, f32[8,128]{1,0:T(8,128)S(1)}) custom-call(f32[1944,128]{1,0:T(8,128)S(1)} %shard_map.69.jac_ref.before_ref, f32[1944,128]{1,0:T(8,128)S(1)} %shard_map.75.drift_ref, f32[216,128]{1,0:T(8,128)S(1)} %get-tuple-element.26.size_ref, f32[128,128]{1,0:T(8,128)S(1)} %bitcast.17), custom_call_target="tpu_custom_call" | custom-call | tf_op jit(solution)/shard_map/pallas_call | solution.py:31
  86.1 4.4 %all-to-all-start.3 = ((f32[128,1,128]{2,1,0:T(1,128)}), f32[128,1,128]{2,1,0:T(1,128)S(1)}, u32[]{:S(2)}, u32[]{:S(2)}) async-start(f32[128,1,128]{2,1,0:T(1,128)} %bitcast.10), calls=%async_computation.3 | async-start | bytes 131072 | tf_op jit(solution)/shard_map/all_to_all | solution.py:637
  90.5 0.4 shard_map.78
  90.9 9.2 %all-to-all-done.3 = f32[128,1,128]{2,1,0:T(1,128)S(1)} async-done(((f32[128,1,128]{2,1,0:T(1,128)}), f32[128,1,128]{2,1,0:T(1,128)S(1)}, u32[]{:S(2)}, u32[]{:S(2)}) %all-to-all-start.3) | async-done | bytes 65568 | tf_op jit(solution)/shard_map/all_to_all | solution.py:637
  100.1 0.8 shard_map.79
  (14 shorter events, 0.1 us)
Async XLA Ops:
  2.6 23.3 %all-to-all-start = ((f32[128,1,640]{2,1,0:T(1,128)}), f32[128,1,640]{2,1,0:T(1,128)S(1)}, u32[]{:S(2)}, u32[]{:S(2)}) async-start(f32[128,1,640]{2,1,0:T(1,128)} %shard_map.70), calls=%async_computation | async-start | bytes 655360 | tf_op jit(solution)/shard_map/all_to_all | solution.py:637
  15.1 21.5 %collective-permute-start.1 = (f32[48,128]{1,0:T(8,128)S(1)}, f32[48,128]{1,0:T(8,128)S(1)}, u32[]{:S(2)}, u32[]{:S(2)}) collective-permute-start(f32[48,128]{1,0:T(8,128)S(1)} %shard_map.68.refs_0_), channel_id=1, source_target_pairs={{0,8},{8,16},{16,24},{24,32},{32,40},{40,48},{48,56},{56,64},{64,7... | collective-permute-start | bytes 73736 | tf_op jit(solution)/shard_map/ppermute | solution.py:642
  16.5 20.0 %collective-permute-start = (f32[48,128]{1,0:T(8,128)S(1)}, f32[48,128]{1,0:T(8,128)S(1)}, u32[]{:S(2)}, u32[]{:S(2)}) collective-permute-start(f32[48,128]{1,0:T(8,128)S(1)} %shard_map.68.refs_0_), channel_id=1, source_target_pairs={{0,120},{8,0},{16,8},{24,16},{32,24},{40,32},{48,40},{56,48},{64,5... | collective-permute-start | bytes 73736 | tf_op jit(solution)/shard_map/ppermute | solution.py:642
  32.2 14.4 %all-to-all-start.1 = ((f32[128,1,136]{2,1,0:T(1,128)}), f32[128,1,136]{2,1,0:T(1,128)S(1)}, u32[]{:S(2)}, u32[]{:S(2)}) async-start(f32[128,1,136]{2,1,0:T(1,128)} %shard_map.72), calls=%async_computation.1 | async-start | bytes 262144 | tf_op jit(solution)/shard_map/all_to_all | solution.py:637
  36.6 14.4 %collective-permute-start.3 = (f32[144,128]{1,0:T(8,128)S(1)}, f32[144,128]{1,0:T(8,128)S(1)}, u32[]{:S(2)}, u32[]{:S(2)}) collective-permute-start(f32[144,128]{1,0:T(8,128)S(1)} %pad_maximum_fusion.refs_0_), channel_id=1, source_target_pairs={{0,1},{1,2},{2,3},{3,4},{4,5},{5,6},{6,7},{7,0},{8,9},{9,10},{10,1... | collective-permute-start | bytes 221192 | tf_op jit(solution)/shard_map/ppermute | solution.py:642
  38.2 12.7 %collective-permute-start.2 = (f32[144,128]{1,0:T(8,128)S(1)}, f32[144,128]{1,0:T(8,128)S(1)}, u32[]{:S(2)}, u32[]{:S(2)}) collective-permute-start(f32[144,128]{1,0:T(8,128)S(1)} %pad_maximum_fusion.refs_0_), channel_id=1, source_target_pairs={{0,7},{1,0},{2,1},{3,2},{4,3},{5,4},{6,5},{7,6},{8,15},{9,8},{10,9... | collective-permute-start | bytes 221192 | tf_op jit(solution)/shard_map/ppermute | solution.py:642
  49.5 6.8 %collective-permute-start.6 = (f32[56,128]{1,0:T(8,128)S(1)}, f32[56,128]{1,0:T(8,128)S(1)}, u32[]{:S(2)}, u32[]{:S(2)}) collective-permute-start(f32[56,128]{1,0:T(8,128)S(1)} %shard_map.73.own), channel_id=1, source_target_pairs={{0,9},{1,10},{2,11},{3,12},{4,13},{5,14},{6,15},{7,8},{8,17},{9,18... | collective-permute-start | bytes 86024 | tf_op jit(solution)/shard_map/ppermute | solution.py:654
  50.3 6.1 %collective-permute-start.5 = (f32[56,128]{1,0:T(8,128)S(1)}, f32[56,128]{1,0:T(8,128)S(1)}, u32[]{:S(2)}, u32[]{:S(2)}) collective-permute-start(f32[56,128]{1,0:T(8,128)S(1)} %shard_map.73.own), channel_id=1, source_target_pairs={{0,1},{1,2},{2,3},{3,4},{4,5},{5,6},{6,7},{7,0},{8,9},{9,10},{10,1... | collective-permute-start | bytes 86024 | tf_op jit(solution)/shard_map/ppermute | solution.py:642
  50.5 6.1 %collective-permute-start.4 = (f32[56,128]{1,0:T(8,128)S(1)}, f32[56,128]{1,0:T(8,128)S(1)}, u32[]{:S(2)}, u32[]{:S(2)}) collective-permute-start(f32[56,128]{1,0:T(8,128)S(1)} %shard_map.73.own), channel_id=1, source_target_pairs={{0,8},{8,16},{16,24},{24,32},{32,40},{40,48},{48,56},{56,64},{64,7... | collective-permute-start | bytes 86024 | tf_op jit(solution)/shard_map/ppermute | solution.py:642
  57.4 4.9 %collective-permute-start.8 = (f32[48,128]{1,0:T(8,128)S(1)}, f32[48,128]{1,0:T(8,128)S(1)}, u32[]{:S(2)}, u32[]{:S(2)}) collective-permute-start(f32[48,128]{1,0:T(8,128)S(1)} %get-tuple-element.25.refs_1_), channel_id=1, source_target_pairs={{0,1},{1,2},{2,3},{3,4},{4,5},{5,6},{6,7},{7,0},{8,9},{9,10},{10,1... | collective-permute-start | bytes 73736 | tf_op jit(solution)/shard_map/ppermute | solution.py:642
  59.0 3.3 %collective-permute-start.7 = (f32[48,128]{1,0:T(8,128)S(1)}, f32[48,128]{1,0:T(8,128)S(1)}, u32[]{:S(2)}, u32[]{:S(2)}) collective-permute-start(f32[48,128]{1,0:T(8,128)S(1)} %get-tuple-element.25.refs_1_), channel_id=1, source_target_pairs={{0,7},{1,0},{2,1},{3,2},{4,3},{5,4},{6,5},{7,6},{8,15},{9,8},{10,9... | collective-permute-start | bytes 73736 | tf_op jit(solution)/shard_map/ppermute | solution.py:642
  62.3 11.8 %collective-permute-start.10 = (f32[144,128]{1,0:T(8,128)S(1)}, f32[144,128]{1,0:T(8,128)S(1)}, u32[]{:S(2)}, u32[]{:S(2)}) collective-permute-start(f32[144,128]{1,0:T(8,128)S(1)} %constant_dynamic-update-slice_fusion.refs_0_), channel_id=1, source_target_pairs={{0,8},{8,16},{16,24},{24,32},{32,40},{40,48},{48,56},{56,64},{64,7... | collective-permute-start | bytes 221192 | tf_op jit(solution)/shard_map/ppermute | solution.py:642
  62.4 11.8 %collective-permute-start.9 = (f32[144,128]{1,0:T(8,128)S(1)}, f32[144,128]{1,0:T(8,128)S(1)}, u32[]{:S(2)}, u32[]{:S(2)}) collective-permute-start(f32[144,128]{1,0:T(8,128)S(1)} %constant_dynamic-update-slice_fusion.refs_0_), channel_id=1, source_target_pairs={{0,120},{8,0},{16,8},{24,16},{32,24},{40,32},{48,40},{56,48},{64,5... | collective-permute-start | bytes 221192 | tf_op jit(solution)/shard_map/ppermute | solution.py:642
  68.4 15.5 %all-to-all-start.2 = ((f32[128,1,128]{2,1,0:T(1,128)}), f32[128,1,128]{2,1,0:T(1,128)S(1)}, u32[]{:S(2)}, u32[]{:S(2)}) async-start(f32[128,1,128]{2,1,0:T(1,128)} %bitcast.7), calls=%async_computation.2 | async-start | bytes 131072 | tf_op jit(solution)/shard_map/all_to_all | solution.py:637
  86.1 14.0 %all-to-all-start.3 = ((f32[128,1,128]{2,1,0:T(1,128)}), f32[128,1,128]{2,1,0:T(1,128)S(1)}, u32[]{:S(2)}, u32[]{:S(2)}) async-start(f32[128,1,128]{2,1,0:T(1,128)} %bitcast.10), calls=%async_computation.3 | async-start | bytes 131072 | tf_op jit(solution)/shard_map/all_to_all | solution.py:637

commit v11 on v9

--- a/solution.py
+++ b/solution.py
@@ -15,8 +15,8 @@
 
 
 ROUNDS = 2
-GATHERED = 36
-PAIRS = 16
+GATHERED = 34
+PAIRS = 17
 
 
 def in_vmem(count):
@@ -646,7 +646,10 @@
     steps = [
         (z * bg + y, ((z + 1) % mesh) * bg + (y + 1) % bg) for z in range(mesh) for y in range(bg)
     ]
-    return [block, moved(block, "mesh", -1), moved(block, "bg", -1), lax.ppermute(block, ("mesh", "bg"), steps)]
+    corner = lax.ppermute(block, ("mesh", "bg"), steps)
+    z_low = moved(block, "mesh", -1)
+    y_low = moved(block, "bg", -1)
+    return [block, z_low, y_low, corner]
 
 
 def along_bg(rows):

time: 105 us -> 104 us (level)
  no operation moved by 1% of the time
where the time goes in v11:
time: 104 us
  starting transfers between devices  46.2 us (44%)
  waiting for transfers between devices  37.1 us (36%)
  Pallas kernels  19.8 us (19%)
    all_to_all x4, waiting for transfers between devices, exchange(): lax.all_to_all(values, ('mesh', 'bg'), split_axis=0, concat_axis=0, tiled...  30.6 us
    all_to_all x4, starting transfers between devices, exchange(): lax.all_to_all(values, ('mesh', 'bg'), split_axis=0, concat_axis=0, tiled...  29.4 us
    pallas_call x12, Pallas kernels, call(): pl.pallas_call(kernel, out_shape=outs, in_specs=in_vmem(len(args)), out_s...  19.8 us
    ppermute x10, starting transfers between devices, moved(): lax.ppermute(values, axis, [(i, (i - by) % count) for i in range(count)])  16 us
    ppermute x1, waiting for transfers between devices, from_below(): corner = lax.ppermute(block, ('mesh', 'bg'), steps)  5.02 us
  transfers between devices with their start and end apart: 15, of which 8 were waited for; matrix products, arithmetic and copies ran while one was open for 0% of the time, Pallas kernels for 14%

profile of v11, /device:TPU:1, one launch (start us, length us, event | category | flops | bytes accessed | tf_op | source)
XLA Modules:
  0.0 103.9 jit_solution(17786438656824802960)
XLA Ops:
  0.6 1.9 %shard_map.70 = f32[128,1,640]{2,1,0:T(1,128)} custom-call(s32[136,128]{1,0:T(8,128)} %bitcast.21, f32[3,136,128]{2,1,0:T(8,128)} %bitcast.20), custom_call_target="tpu_custom_call" | custom-call | tf_op jit(solution)/shard_map/pallas_call | solution.py:31
  2.6 11.5 %all-to-all-start = ((f32[128,1,640]{2,1,0:T(1,128)}), f32[128,1,640]{2,1,0:T(1,128)S(1)}, u32[]{:S(2)}, u32[]{:S(2)}) async-start(f32[128,1,640]{2,1,0:T(1,128)} %shard_map.70), calls=%async_computation | async-start | bytes 655360 | tf_op jit(solution)/shard_map/all_to_all | solution.py:632
  14.1 1.0 shard_map.68.refs_0_
  15.1 1.4 %collective-permute-start.1 = (f32[48,128]{1,0:T(8,128)S(1)}, f32[48,128]{1,0:T(8,128)S(1)}, u32[]{:S(2)}, u32[]{:S(2)}) collective-permute-start(f32[48,128]{1,0:T(8,128)S(1)} %shard_map.68.refs_0_), channel_id=1, source_target_pairs={{0,8},{8,16},{16,24},{24,32},{32,40},{40,48},{48,56},{56,64},{64,7... | collective-permute-start | bytes 73736 | tf_op jit(solution)/shard_map/ppermute | solution.py:637
  16.5 4.1 %collective-permute-start = (f32[48,128]{1,0:T(8,128)S(1)}, f32[48,128]{1,0:T(8,128)S(1)}, u32[]{:S(2)}, u32[]{:S(2)}) collective-permute-start(f32[48,128]{1,0:T(8,128)S(1)} %shard_map.68.refs_0_), channel_id=1, source_target_pairs={{0,120},{8,0},{16,8},{24,16},{32,24},{40,32},{48,40},{56,48},{64,5... | collective-permute-start | bytes 73736 | tf_op jit(solution)/shard_map/ppermute | solution.py:637
  20.6 1.5 %shard_map.71 = (bf16[512,512]{1,0:T(8,128)(2,1)S(1)}, s32[8,8192]{1,0:T(8,128)S(1)}, f32[8,128]{1,0:T(8,128)S(1)}) custom-call(f32[8,16384]{1,0:T(8,128)} %table_ref.1), custom_call_target="tpu_custom_call" | custom-call | tf_op jit(solution)/shard_map/pallas_call | solution.py:31
  22.1 3.8 %all-to-all-done.asked_ref = f32[128,1,640]{2,1,0:T(1,128)S(1)} async-done(((f32[128,1,640]{2,1,0:T(1,128)}), f32[128,1,640]{2,1,0:T(1,128)S(1)}, u32[]{:S(2)}, u32[]{:S(2)}) %all-to-all-start) | async-done | bytes 327712 | tf_op jit(solution)/shard_map/all_to_all | solution.py:632
  25.9 6.3 %shard_map.72 = f32[128,1,136]{2,1,0:T(1,128)} custom-call(f32[128,1,640]{2,1,0:T(1,128)S(1)} %all-to-all-done.asked_ref, bf16[512,512]{1,0:T(8,128)(2,1)S(1)} %get-tuple-element.22.split_ref, s32[8,8192]{1,0:T(8,128)S(1)} %get-tuple-element.23.packed_ref, f32[8,128]{1,0:T(8,128)S(1)} %get-tuple-element.24.unit_ref), custom_call_target="tpu_custom_call" | custom-call | tf_op jit(solution)/shard_map/pallas_call | solution.py:31
  32.2 4.4 %all-to-all-start.1 = ((f32[128,1,136]{2,1,0:T(1,128)}), f32[128,1,136]{2,1,0:T(1,128)S(1)}, u32[]{:S(2)}, u32[]{:S(2)}) async-start(f32[128,1,136]{2,1,0:T(1,128)} %shard_map.72), calls=%async_computation.1 | async-start | bytes 262144 | tf_op jit(solution)/shard_map/all_to_all | solution.py:632
  36.6 1.6 %collective-permute-start.3 = (f32[144,128]{1,0:T(8,128)S(1)}, f32[144,128]{1,0:T(8,128)S(1)}, u32[]{:S(2)}, u32[]{:S(2)}) collective-permute-start(f32[144,128]{1,0:T(8,128)S(1)} %pad_maximum_fusion.refs_0_), channel_id=1, source_target_pairs={{0,1},{1,2},{2,3},{3,4},{4,5},{5,6},{6,7},{7,0},{8,9},{9,10},{10,1... | collective-permute-start | bytes 221192 | tf_op jit(solution)/shard_map/ppermute | solution.py:637
  38.2 8.4 %all-to-all-done.1.found_ref = f32[128,1,136]{2,1,0:T(1,128)S(1)} async-done(((f32[128,1,136]{2,1,0:T(1,128)}), f32[128,1,136]{2,1,0:T(1,128)S(1)}, u32[]{:S(2)}, u32[]{:S(2)}) %all-to-all-start.1) | async-done | bytes 69664 | tf_op jit(solution)/shard_map/all_to_all | solution.py:632
  46.6 2.9 %shard_map.73.own = f32[56,128]{1,0:T(8,128)S(1)} custom-call(f32[128,1,136]{2,1,0:T(1,128)S(1)} %all-to-all-done.1.found_ref, s32[136,128]{1,0:T(8,128)} %bitcast.22), custom_call_target="tpu_custom_call" | custom-call | tf_op jit(solution)/shard_map/pallas_call | solution.py:31
  49.5 0.7 collective-permute-start.6
  50.3 0.3 collective-permute-start.5
  50.5 0.4 collective-permute-start.4
  50.9 0.4 shard_map.69.jac_ref.before_ref
  51.3 5.0 %collective-permute-done.6.corner = f32[56,128]{1,0:T(8,128)S(1)} collective-permute-done((f32[56,128]{1,0:T(8,128)S(1)}, f32[56,128]{1,0:T(8,128)S(1)}, u32[]{:S(2)}, u32[]{:S(2)}) %collective-permute-start.6) | collective-permute-done | bytes 28704 | tf_op jit(solution)/shard_map/ppermute | solution.py:649
  56.4 0.3 collective-permute-done.4.z_low
  56.6 0.8 shard_map.74
  57.5 4.8 %collective-permute-start.7 = (f32[48,128]{1,0:T(8,128)S(1)}, f32[48,128]{1,0:T(8,128)S(1)}, u32[]{:S(2)}, u32[]{:S(2)}) collective-permute-start(f32[48,128]{1,0:T(8,128)S(1)} %get-tuple-element.25.refs_1_), channel_id=1, source_target_pairs={{0,120},{8,0},{16,8},{24,16},{32,24},{40,32},{48,40},{56,48},{64,5... | collective-permute-start | bytes 73736 | tf_op jit(solution)/shard_map/ppermute | solution.py:637
  62.3 0.9 collective-permute-done.7
  63.5 2.8 %collective-permute-start.10 = (f32[144,128]{1,0:T(8,128)S(1)}, f32[144,128]{1,0:T(8,128)S(1)}, u32[]{:S(2)}, u32[]{:S(2)}) collective-permute-start(f32[144,128]{1,0:T(8,128)S(1)} %constant_dynamic-update-slice_fusion.refs_0_), channel_id=1, source_target_pairs={{0,1},{1,2},{2,3},{3,4},{4,5},{5,6},{6,7},{7,0},{8,9},{9,10},{10,1... | collective-permute-start | bytes 221192 | tf_op jit(solution)/shard_map/ppermute | solution.py:637
  66.3 0.6 collective-permute-start.9
  66.8 1.2 %shard_map.76 = f32[128,128]{1,0:T(8,128)} custom-call(f32[1944,128]{1,0:T(8,128)S(1)} %shard_map.69.jac_ref.before_ref, f32[256,128]{1,0:T(8,128)S(1)} %get-tuple-element.27.turn_ref, f32[216,128]{1,0:T(8,128)S(1)} %get-tuple-element.26.size_ref), custom_call_target="tpu_custom_call" | custom-call | tf_op jit(solution)/shard_map/pallas_call | solution.py:31
  68.1 9.2 %all-to-all-start.2 = ((f32[128,1,128]{2,1,0:T(1,128)}), f32[128,1,128]{2,1,0:T(1,128)S(1)}, u32[]{:S(2)}, u32[]{:S(2)}) async-start(f32[128,1,128]{2,1,0:T(1,128)} %bitcast.7), calls=%async_computation.2 | async-start | bytes 131072 | tf_op jit(solution)/shard_map/all_to_all | solution.py:632
  77.3 0.4 shard_map.75.drift_ref
  77.7 9.2 %all-to-all-done.2 = f32[128,1,128]{2,1,0:T(1,128)S(1)} async-done(((f32[128,1,128]{2,1,0:T(1,128)}), f32[128,1,128]{2,1,0:T(1,128)S(1)}, u32[]{:S(2)}, u32[]{:S(2)}) %all-to-all-start.2) | async-done | bytes 65568 | tf_op jit(solution)/shard_map/all_to_all | solution.py:632
  86.9 2.2 %shard_map.77 = (f32[48,128]{1,0:T(8,128)S(1)}, f32[128,128]{1,0:T(8,128)}, f32[8,128]{1,0:T(8,128)S(1)}) custom-call(f32[1944,128]{1,0:T(8,128)S(1)} %shard_map.69.jac_ref.before_ref, f32[1944,128]{1,0:T(8,128)S(1)} %shard_map.75.drift_ref, f32[216,128]{1,0:T(8,128)S(1)} %get-tuple-element.26.size_ref, f32[128,128]{1,0:T(8,128)S(1)} %bitcast.17), custom_call_target="tpu_custom_call" | custom-call | tf_op jit(solution)/shard_map/pallas_call | solution.py:31
  89.1 4.4 %all-to-all-start.3 = ((f32[128,1,128]{2,1,0:T(1,128)}), f32[128,1,128]{2,1,0:T(1,128)S(1)}, u32[]{:S(2)}, u32[]{:S(2)}) async-start(f32[128,1,128]{2,1,0:T(1,128)} %bitcast.10), calls=%async_computation.3 | async-start | bytes 131072 | tf_op jit(solution)/shard_map/all_to_all | solution.py:632
  93.5 0.4 shard_map.78
  93.9 9.2 %all-to-all-done.3 = f32[128,1,128]{2,1,0:T(1,128)S(1)} async-done(((f32[128,1,128]{2,1,0:T(1,128)}), f32[128,1,128]{2,1,0:T(1,128)S(1)}, u32[]{:S(2)}, u32[]{:S(2)}) %all-to-all-start.3) | async-done | bytes 65568 | tf_op jit(solution)/shard_map/all_to_all | solution.py:632
  103.1 0.8 shard_map.79
  (14 shorter events, 0.4 us)
Async XLA Ops:
  2.6 23.3 %all-to-all-start = ((f32[128,1,640]{2,1,0:T(1,128)}), f32[128,1,640]{2,1,0:T(1,128)S(1)}, u32[]{:S(2)}, u32[]{:S(2)}) async-start(f32[128,1,640]{2,1,0:T(1,128)} %shard_map.70), calls=%async_computation | async-start | bytes 655360 | tf_op jit(solution)/shard_map/all_to_all | solution.py:632
  15.1 21.5 %collective-permute-start.1 = (f32[48,128]{1,0:T(8,128)S(1)}, f32[48,128]{1,0:T(8,128)S(1)}, u32[]{:S(2)}, u32[]{:S(2)}) collective-permute-start(f32[48,128]{1,0:T(8,128)S(1)} %shard_map.68.refs_0_), channel_id=1, source_target_pairs={{0,8},{8,16},{16,24},{24,32},{32,40},{40,48},{48,56},{56,64},{64,7... | collective-permute-start | bytes 73736 | tf_op jit(solution)/shard_map/ppermute | solution.py:637
  16.5 20.0 %collective-permute-start = (f32[48,128]{1,0:T(8,128)S(1)}, f32[48,128]{1,0:T(8,128)S(1)}, u32[]{:S(2)}, u32[]{:S(2)}) collective-permute-start(f32[48,128]{1,0:T(8,128)S(1)} %shard_map.68.refs_0_), channel_id=1, source_target_pairs={{0,120},{8,0},{16,8},{24,16},{32,24},{40,32},{48,40},{56,48},{64,5... | collective-permute-start | bytes 73736 | tf_op jit(solution)/shard_map/ppermute | solution.py:637
  32.2 14.4 %all-to-all-start.1 = ((f32[128,1,136]{2,1,0:T(1,128)}), f32[128,1,136]{2,1,0:T(1,128)S(1)}, u32[]{:S(2)}, u32[]{:S(2)}) async-start(f32[128,1,136]{2,1,0:T(1,128)} %shard_map.72), calls=%async_computation.1 | async-start | bytes 262144 | tf_op jit(solution)/shard_map/all_to_all | solution.py:632
  36.6 14.4 %collective-permute-start.3 = (f32[144,128]{1,0:T(8,128)S(1)}, f32[144,128]{1,0:T(8,128)S(1)}, u32[]{:S(2)}, u32[]{:S(2)}) collective-permute-start(f32[144,128]{1,0:T(8,128)S(1)} %pad_maximum_fusion.refs_0_), channel_id=1, source_target_pairs={{0,1},{1,2},{2,3},{3,4},{4,5},{5,6},{6,7},{7,0},{8,9},{9,10},{10,1... | collective-permute-start | bytes 221192 | tf_op jit(solution)/shard_map/ppermute | solution.py:637
  38.2 12.7 %collective-permute-start.2 = (f32[144,128]{1,0:T(8,128)S(1)}, f32[144,128]{1,0:T(8,128)S(1)}, u32[]{:S(2)}, u32[]{:S(2)}) collective-permute-start(f32[144,128]{1,0:T(8,128)S(1)} %pad_maximum_fusion.refs_0_), channel_id=1, source_target_pairs={{0,7},{1,0},{2,1},{3,2},{4,3},{5,4},{6,5},{7,6},{8,15},{9,8},{10,9... | collective-permute-start | bytes 221192 | tf_op jit(solution)/shard_map/ppermute | solution.py:637
  49.5 6.8 %collective-permute-start.6 = (f32[56,128]{1,0:T(8,128)S(1)}, f32[56,128]{1,0:T(8,128)S(1)}, u32[]{:S(2)}, u32[]{:S(2)}) collective-permute-start(f32[56,128]{1,0:T(8,128)S(1)} %shard_map.73.own), channel_id=1, source_target_pairs={{0,9},{1,10},{2,11},{3,12},{4,13},{5,14},{6,15},{7,8},{8,17},{9,18... | collective-permute-start | bytes 86024 | tf_op jit(solution)/shard_map/ppermute | solution.py:649
  50.3 6.1 %collective-permute-start.5 = (f32[56,128]{1,0:T(8,128)S(1)}, f32[56,128]{1,0:T(8,128)S(1)}, u32[]{:S(2)}, u32[]{:S(2)}) collective-permute-start(f32[56,128]{1,0:T(8,128)S(1)} %shard_map.73.own), channel_id=1, source_target_pairs={{0,1},{1,2},{2,3},{3,4},{4,5},{5,6},{6,7},{7,0},{8,9},{9,10},{10,1... | collective-permute-start | bytes 86024 | tf_op jit(solution)/shard_map/ppermute | solution.py:637
  50.5 6.1 %collective-permute-start.4 = (f32[56,128]{1,0:T(8,128)S(1)}, f32[56,128]{1,0:T(8,128)S(1)}, u32[]{:S(2)}, u32[]{:S(2)}) collective-permute-start(f32[56,128]{1,0:T(8,128)S(1)} %shard_map.73.own), channel_id=1, source_target_pairs={{0,8},{8,16},{16,24},{24,32},{32,40},{40,48},{48,56},{56,64},{64,7... | collective-permute-start | bytes 86024 | tf_op jit(solution)/shard_map/ppermute | solution.py:637
  57.4 6.1 %collective-permute-start.8 = (f32[48,128]{1,0:T(8,128)S(1)}, f32[48,128]{1,0:T(8,128)S(1)}, u32[]{:S(2)}, u32[]{:S(2)}) collective-permute-start(f32[48,128]{1,0:T(8,128)S(1)} %get-tuple-element.25.refs_1_), channel_id=1, source_target_pairs={{0,8},{8,16},{16,24},{24,32},{32,40},{40,48},{48,56},{56,64},{64,7... | collective-permute-start | bytes 73736 | tf_op jit(solution)/shard_map/ppermute | solution.py:637
  57.5 5.7 %collective-permute-start.7 = (f32[48,128]{1,0:T(8,128)S(1)}, f32[48,128]{1,0:T(8,128)S(1)}, u32[]{:S(2)}, u32[]{:S(2)}) collective-permute-start(f32[48,128]{1,0:T(8,128)S(1)} %get-tuple-element.25.refs_1_), channel_id=1, source_target_pairs={{0,120},{8,0},{16,8},{24,16},{32,24},{40,32},{48,40},{56,48},{64,5... | collective-permute-start | bytes 73736 | tf_op jit(solution)/shard_map/ppermute | solution.py:637
  63.5 13.8 %collective-permute-start.10 = (f32[144,128]{1,0:T(8,128)S(1)}, f32[144,128]{1,0:T(8,128)S(1)}, u32[]{:S(2)}, u32[]{:S(2)}) collective-permute-start(f32[144,128]{1,0:T(8,128)S(1)} %constant_dynamic-update-slice_fusion.refs_0_), channel_id=1, source_target_pairs={{0,1},{1,2},{2,3},{3,4},{4,5},{5,6},{6,7},{7,0},{8,9},{9,10},{10,1... | collective-permute-start | bytes 221192 | tf_op jit(solution)/shard_map/ppermute | solution.py:637
  66.3 11.0 %collective-permute-start.9 = (f32[144,128]{1,0:T(8,128)S(1)}, f32[144,128]{1,0:T(8,128)S(1)}, u32[]{:S(2)}, u32[]{:S(2)}) collective-permute-start(f32[144,128]{1,0:T(8,128)S(1)} %constant_dynamic-update-slice_fusion.refs_0_), channel_id=1, source_target_pairs={{0,7},{1,0},{2,1},{3,2},{4,3},{5,4},{6,5},{7,6},{8,15},{9,8},{10,9... | collective-permute-start | bytes 221192 | tf_op jit(solution)/shard_map/ppermute | solution.py:637
  68.1 18.9 %all-to-all-start.2 = ((f32[128,1,128]{2,1,0:T(1,128)}), f32[128,1,128]{2,1,0:T(1,128)S(1)}, u32[]{:S(2)}, u32[]{:S(2)}) async-start(f32[128,1,128]{2,1,0:T(1,128)} %bitcast.7), calls=%async_computation.2 | async-start | bytes 131072 | tf_op jit(solution)/shard_map/all_to_all | solution.py:632
  89.1 14.0 %all-to-all-start.3 = ((f32[128,1,128]{2,1,0:T(1,128)}), f32[128,1,128]{2,1,0:T(1,128)S(1)}, u32[]{:S(2)}, u32[]{:S(2)}) async-start(f32[128,1,128]{2,1,0:T(1,128)} %bitcast.10), calls=%async_computation.3 | async-start | bytes 131072 | tf_op jit(solution)/shard_map/all_to_all | solution.py:632

commit v12 on v10

--- a/solution.py
+++ b/solution.py
@@ -651,7 +651,10 @@
     steps = [
         (z * bg + y, ((z + 1) % mesh) * bg + (y + 1) % bg) for z in range(mesh) for y in range(bg)
     ]
-    return [block, moved(block, "mesh", -1), moved(block, "bg", -1), lax.ppermute(block, ("mesh", "bg"), steps)]
+    corner = lax.ppermute(block, ("mesh", "bg"), steps)
+    z_low = moved(block, "mesh", -1)
+    y_low = moved(block, "bg", -1)
+    return [block, z_low, y_low, corner]
 
 
 def along_bg(rows):

time: 101 us -> 101 us (level)
  no operation moved by 1% of the time
where the time goes in v12:
time: 101 us
  starting transfers between devices  41.6 us (41%)
  waiting for transfers between devices  38.7 us (38%)
  Pallas kernels  19.8 us (20%)
    all_to_all x4, waiting for transfers between devices, exchange(): lax.all_to_all(values, ('mesh', 'bg'), split_axis=0, concat_axis=0, tiled...  30.7 us
    all_to_all x4, starting transfers between devices, exchange(): lax.all_to_all(values, ('mesh', 'bg'), split_axis=0, concat_axis=0, tiled...  25.9 us
    pallas_call x12, Pallas kernels, call(): pl.pallas_call(kernel, out_shape=outs, in_specs=in_vmem(len(args)), out_s...  19.8 us
    ppermute x10, starting transfers between devices, moved(): lax.ppermute(values, axis, [(i, (i - by) % count) for i in range(count)])  14.9 us
    ppermute x1, waiting for transfers between devices, from_below(): corner = lax.ppermute(block, ('mesh', 'bg'), steps)  5.02 us
    ppermute x10, waiting for transfers between devices, moved(): lax.ppermute(values, axis, [(i, (i - by) % count) for i in range(count)])  2.95 us
  transfers between devices with their start and end apart: 15, of which 7 were waited for; matrix products, arithmetic and copies ran while one was open for 0% of the time, Pallas kernels for 14%

profile of v12, /device:TPU:1, one launch (start us, length us, event | category | flops | bytes accessed | tf_op | source)
XLA Modules:
  0.0 100.9 jit_solution(374728983425846556)
XLA Ops:
  0.6 1.9 %shard_map.70 = f32[128,1,640]{2,1,0:T(1,128)} custom-call(s32[136,128]{1,0:T(8,128)} %bitcast.21, f32[3,136,128]{2,1,0:T(8,128)} %bitcast.20), custom_call_target="tpu_custom_call" | custom-call | tf_op jit(solution)/shard_map/pallas_call | solution.py:31
  2.6 11.5 %all-to-all-start = ((f32[128,1,640]{2,1,0:T(1,128)}), f32[128,1,640]{2,1,0:T(1,128)S(1)}, u32[]{:S(2)}, u32[]{:S(2)}) async-start(f32[128,1,640]{2,1,0:T(1,128)} %shard_map.70), calls=%async_computation | async-start | bytes 655360 | tf_op jit(solution)/shard_map/all_to_all | solution.py:637
  14.1 1.0 %shard_map.68.refs_0_ = f32[48,128]{1,0:T(8,128)S(1)} custom-call(f32[3,4,4,128]{3,2,1,0:T(4,128)} %nodes_ref.1), custom_call_target="tpu_custom_call" | custom-call | tf_op jit(solution)/shard_map/pallas_call | solution.py:31
  15.1 1.4 %collective-permute-start.1 = (f32[48,128]{1,0:T(8,128)S(1)}, f32[48,128]{1,0:T(8,128)S(1)}, u32[]{:S(2)}, u32[]{:S(2)}) collective-permute-start(f32[48,128]{1,0:T(8,128)S(1)} %shard_map.68.refs_0_), channel_id=1, source_target_pairs={{0,8},{8,16},{16,24},{24,32},{32,40},{40,48},{48,56},{56,64},{64,7... | collective-permute-start | bytes 73736 | tf_op jit(solution)/shard_map/ppermute | solution.py:642
  16.5 4.1 %collective-permute-start = (f32[48,128]{1,0:T(8,128)S(1)}, f32[48,128]{1,0:T(8,128)S(1)}, u32[]{:S(2)}, u32[]{:S(2)}) collective-permute-start(f32[48,128]{1,0:T(8,128)S(1)} %shard_map.68.refs_0_), channel_id=1, source_target_pairs={{0,120},{8,0},{16,8},{24,16},{32,24},{40,32},{48,40},{56,48},{64,5... | collective-permute-start | bytes 73736 | tf_op jit(solution)/shard_map/ppermute | solution.py:642
  20.6 1.5 %shard_map.71 = (bf16[512,512]{1,0:T(8,128)(2,1)S(1)}, s32[8,8192]{1,0:T(8,128)S(1)}, f32[8,128]{1,0:T(8,128)S(1)}) custom-call(f32[8,16384]{1,0:T(8,128)} %table_ref.1), custom_call_target="tpu_custom_call" | custom-call | tf_op jit(solution)/shard_map/pallas_call | solution.py:31
  22.1 3.8 %all-to-all-done.asked_ref = f32[128,1,640]{2,1,0:T(1,128)S(1)} async-done(((f32[128,1,640]{2,1,0:T(1,128)}), f32[128,1,640]{2,1,0:T(1,128)S(1)}, u32[]{:S(2)}, u32[]{:S(2)}) %all-to-all-start) | async-done | bytes 327712 | tf_op jit(solution)/shard_map/all_to_all | solution.py:637
  25.9 6.3 %shard_map.72 = f32[128,1,136]{2,1,0:T(1,128)} custom-call(f32[128,1,640]{2,1,0:T(1,128)S(1)} %all-to-all-done.asked_ref, bf16[512,512]{1,0:T(8,128)(2,1)S(1)} %get-tuple-element.22.split_ref, s32[8,8192]{1,0:T(8,128)S(1)} %get-tuple-element.23.packed_ref, f32[8,128]{1,0:T(8,128)S(1)} %get-tuple-element.24.unit_ref), custom_call_target="tpu_custom_call" | custom-call | tf_op jit(solution)/shard_map/pallas_call | solution.py:31
  32.2 4.4 %all-to-all-start.1 = ((f32[128,1,136]{2,1,0:T(1,128)}), f32[128,1,136]{2,1,0:T(1,128)S(1)}, u32[]{:S(2)}, u32[]{:S(2)}) async-start(f32[128,1,136]{2,1,0:T(1,128)} %shard_map.72), calls=%async_computation.1 | async-start | bytes 262144 | tf_op jit(solution)/shard_map/all_to_all | solution.py:637
  36.6 1.6 %collective-permute-start.3 = (f32[144,128]{1,0:T(8,128)S(1)}, f32[144,128]{1,0:T(8,128)S(1)}, u32[]{:S(2)}, u32[]{:S(2)}) collective-permute-start(f32[144,128]{1,0:T(8,128)S(1)} %pad_maximum_fusion.refs_0_), channel_id=1, source_target_pairs={{0,1},{1,2},{2,3},{3,4},{4,5},{5,6},{6,7},{7,0},{8,9},{9,10},{10,1... | collective-permute-start | bytes 221192 | tf_op jit(solution)/shard_map/ppermute | solution.py:642
  38.2 8.4 %all-to-all-done.1.found_ref = f32[128,1,136]{2,1,0:T(1,128)S(1)} async-done(((f32[128,1,136]{2,1,0:T(1,128)}), f32[128,1,136]{2,1,0:T(1,128)S(1)}, u32[]{:S(2)}, u32[]{:S(2)}) %all-to-all-start.1) | async-done | bytes 69664 | tf_op jit(solution)/shard_map/all_to_all | solution.py:637
  46.6 2.9 %shard_map.73.own = f32[56,128]{1,0:T(8,128)S(1)} custom-call(f32[128,1,136]{2,1,0:T(1,128)S(1)} %all-to-all-done.1.found_ref, s32[136,128]{1,0:T(8,128)} %bitcast.22), custom_call_target="tpu_custom_call" | custom-call | tf_op jit(solution)/shard_map/pallas_call | solution.py:31
  49.5 0.7 collective-permute-start.6
  50.3 0.3 collective-permute-start.5
  50.5 0.4 collective-permute-start.4
  50.9 0.4 shard_map.69.jac_ref.before_ref
  51.3 5.0 %collective-permute-done.6.corner = f32[56,128]{1,0:T(8,128)S(1)} collective-permute-done((f32[56,128]{1,0:T(8,128)S(1)}, f32[56,128]{1,0:T(8,128)S(1)}, u32[]{:S(2)}, u32[]{:S(2)}) %collective-permute-start.6) | collective-permute-done | bytes 28704 | tf_op jit(solution)/shard_map/ppermute | solution.py:654
  56.4 0.3 collective-permute-done.4.z_low
  56.6 0.8 shard_map.74
  57.4 1.6 %collective-permute-start.8 = (f32[48,128]{1,0:T(8,128)S(1)}, f32[48,128]{1,0:T(8,128)S(1)}, u32[]{:S(2)}, u32[]{:S(2)}) collective-permute-start(f32[48,128]{1,0:T(8,128)S(1)} %get-tuple-element.25.refs_1_), channel_id=1, source_target_pairs={{0,1},{1,2},{2,3},{3,4},{4,5},{5,6},{6,7},{7,0},{8,9},{9,10},{10,1... | collective-permute-start | bytes 73736 | tf_op jit(solution)/shard_map/ppermute | solution.py:642
  59.0 0.6 collective-permute-start.7
  59.6 2.7 %collective-permute-done.7 = f32[48,128]{1,0:T(8,128)S(1)} collective-permute-done((f32[48,128]{1,0:T(8,128)S(1)}, f32[48,128]{1,0:T(8,128)S(1)}, u32[]{:S(2)}, u32[]{:S(2)}) %collective-permute-start.7) | collective-permute-done | bytes 24608 | tf_op jit(solution)/shard_map/ppermute | solution.py:642
  62.4 4.8 %collective-permute-start.9 = (f32[144,128]{1,0:T(8,128)S(1)}, f32[144,128]{1,0:T(8,128)S(1)}, u32[]{:S(2)}, u32[]{:S(2)}) collective-permute-start(f32[144,128]{1,0:T(8,128)S(1)} %constant_dynamic-update-slice_fusion.refs_0_), channel_id=1, source_target_pairs={{0,120},{8,0},{16,8},{24,16},{32,24},{40,32},{48,40},{56,48},{64,5... | collective-permute-start | bytes 221192 | tf_op jit(solution)/shard_map/ppermute | solution.py:642
  67.2 1.2 %shard_map.76 = f32[128,128]{1,0:T(8,128)} custom-call(f32[1944,128]{1,0:T(8,128)S(1)} %shard_map.69.jac_ref.before_ref, f32[256,128]{1,0:T(8,128)S(1)} %get-tuple-element.27.turn_ref, f32[216,128]{1,0:T(8,128)S(1)} %get-tuple-element.26.size_ref), custom_call_target="tpu_custom_call" | custom-call | tf_op jit(solution)/shard_map/pallas_call | solution.py:31
  68.4 5.7 %all-to-all-start.2 = ((f32[128,1,128]{2,1,0:T(1,128)}), f32[128,1,128]{2,1,0:T(1,128)S(1)}, u32[]{:S(2)}, u32[]{:S(2)}) async-start(f32[128,1,128]{2,1,0:T(1,128)} %bitcast.7), calls=%async_computation.2 | async-start | bytes 131072 | tf_op jit(solution)/shard_map/all_to_all | solution.py:637
  74.2 0.4 shard_map.75.drift_ref
  74.6 9.4 %all-to-all-done.2 = f32[128,1,128]{2,1,0:T(1,128)S(1)} async-done(((f32[128,1,128]{2,1,0:T(1,128)}), f32[128,1,128]{2,1,0:T(1,128)S(1)}, u32[]{:S(2)}, u32[]{:S(2)}) %all-to-all-start.2) | async-done | bytes 65568 | tf_op jit(solution)/shard_map/all_to_all | solution.py:637
  83.9 2.2 %shard_map.77 = (f32[48,128]{1,0:T(8,128)S(1)}, f32[128,128]{1,0:T(8,128)}, f32[8,128]{1,0:T(8,128)S(1)}) custom-call(f32[1944,128]{1,0:T(8,128)S(1)} %shard_map.69.jac_ref.before_ref, f32[1944,128]{1,0:T(8,128)S(1)} %shard_map.75.drift_ref, f32[216,128]{1,0:T(8,128)S(1)} %get-tuple-element.26.size_ref, f32[128,128]{1,0:T(8,128)S(1)} %bitcast.17), custom_call_target="tpu_custom_call" | custom-call | tf_op jit(solution)/shard_map/pallas_call | solution.py:31
  86.1 4.4 %all-to-all-start.3 = ((f32[128,1,128]{2,1,0:T(1,128)}), f32[128,1,128]{2,1,0:T(1,128)S(1)}, u32[]{:S(2)}, u32[]{:S(2)}) async-start(f32[128,1,128]{2,1,0:T(1,128)} %bitcast.10), calls=%async_computation.3 | async-start | bytes 131072 | tf_op jit(solution)/shard_map/all_to_all | solution.py:637
  90.5 0.4 shard_map.78
  90.9 9.2 %all-to-all-done.3 = f32[128,1,128]{2,1,0:T(1,128)S(1)} async-done(((f32[128,1,128]{2,1,0:T(1,128)}), f32[128,1,128]{2,1,0:T(1,128)S(1)}, u32[]{:S(2)}, u32[]{:S(2)}) %all-to-all-start.3) | async-done | bytes 65568 | tf_op jit(solution)/shard_map/all_to_all | solution.py:637
  100.1 0.8 shard_map.79
  (14 shorter events, 0.1 us)
Async XLA Ops:
  2.6 23.3 %all-to-all-start = ((f32[128,1,640]{2,1,0:T(1,128)}), f32[128,1,640]{2,1,0:T(1,128)S(1)}, u32[]{:S(2)}, u32[]{:S(2)}) async-start(f32[128,1,640]{2,1,0:T(1,128)} %shard_map.70), calls=%async_computation | async-start | bytes 655360 | tf_op jit(solution)/shard_map/all_to_all | solution.py:637
  15.1 21.5 %collective-permute-start.1 = (f32[48,128]{1,0:T(8,128)S(1)}, f32[48,128]{1,0:T(8,128)S(1)}, u32[]{:S(2)}, u32[]{:S(2)}) collective-permute-start(f32[48,128]{1,0:T(8,128)S(1)} %shard_map.68.refs_0_), channel_id=1, source_target_pairs={{0,8},{8,16},{16,24},{24,32},{32,40},{40,48},{48,56},{56,64},{64,7... | collective-permute-start | bytes 73736 | tf_op jit(solution)/shard_map/ppermute | solution.py:642
  16.5 20.0 %collective-permute-start = (f32[48,128]{1,0:T(8,128)S(1)}, f32[48,128]{1,0:T(8,128)S(1)}, u32[]{:S(2)}, u32[]{:S(2)}) collective-permute-start(f32[48,128]{1,0:T(8,128)S(1)} %shard_map.68.refs_0_), channel_id=1, source_target_pairs={{0,120},{8,0},{16,8},{24,16},{32,24},{40,32},{48,40},{56,48},{64,5... | collective-permute-start | bytes 73736 | tf_op jit(solution)/shard_map/ppermute | solution.py:642
  32.2 14.4 %all-to-all-start.1 = ((f32[128,1,136]{2,1,0:T(1,128)}), f32[128,1,136]{2,1,0:T(1,128)S(1)}, u32[]{:S(2)}, u32[]{:S(2)}) async-start(f32[128,1,136]{2,1,0:T(1,128)} %shard_map.72), calls=%async_computation.1 | async-start | bytes 262144 | tf_op jit(solution)/shard_map/all_to_all | solution.py:637
  36.6 14.4 %collective-permute-start.3 = (f32[144,128]{1,0:T(8,128)S(1)}, f32[144,128]{1,0:T(8,128)S(1)}, u32[]{:S(2)}, u32[]{:S(2)}) collective-permute-start(f32[144,128]{1,0:T(8,128)S(1)} %pad_maximum_fusion.refs_0_), channel_id=1, source_target_pairs={{0,1},{1,2},{2,3},{3,4},{4,5},{5,6},{6,7},{7,0},{8,9},{9,10},{10,1... | collective-permute-start | bytes 221192 | tf_op jit(solution)/shard_map/ppermute | solution.py:642
  38.2 12.7 %collective-permute-start.2 = (f32[144,128]{1,0:T(8,128)S(1)}, f32[144,128]{1,0:T(8,128)S(1)}, u32[]{:S(2)}, u32[]{:S(2)}) collective-permute-start(f32[144,128]{1,0:T(8,128)S(1)} %pad_maximum_fusion.refs_0_), channel_id=1, source_target_pairs={{0,7},{1,0},{2,1},{3,2},{4,3},{5,4},{6,5},{7,6},{8,15},{9,8},{10,9... | collective-permute-start | bytes 221192 | tf_op jit(solution)/shard_map/ppermute | solution.py:642
  49.5 6.8 %collective-permute-start.6 = (f32[56,128]{1,0:T(8,128)S(1)}, f32[56,128]{1,0:T(8,128)S(1)}, u32[]{:S(2)}, u32[]{:S(2)}) collective-permute-start(f32[56,128]{1,0:T(8,128)S(1)} %shard_map.73.own), channel_id=1, source_target_pairs={{0,9},{1,10},{2,11},{3,12},{4,13},{5,14},{6,15},{7,8},{8,17},{9,18... | collective-permute-start | bytes 86024 | tf_op jit(solution)/shard_map/ppermute | solution.py:654
  50.3 6.1 %collective-permute-start.5 = (f32[56,128]{1,0:T(8,128)S(1)}, f32[56,128]{1,0:T(8,128)S(1)}, u32[]{:S(2)}, u32[]{:S(2)}) collective-permute-start(f32[56,128]{1,0:T(8,128)S(1)} %shard_map.73.own), channel_id=1, source_target_pairs={{0,1},{1,2},{2,3},{3,4},{4,5},{5,6},{6,7},{7,0},{8,9},{9,10},{10,1... | collective-permute-start | bytes 86024 | tf_op jit(solution)/shard_map/ppermute | solution.py:642
  50.5 6.1 %collective-permute-start.4 = (f32[56,128]{1,0:T(8,128)S(1)}, f32[56,128]{1,0:T(8,128)S(1)}, u32[]{:S(2)}, u32[]{:S(2)}) collective-permute-start(f32[56,128]{1,0:T(8,128)S(1)} %shard_map.73.own), channel_id=1, source_target_pairs={{0,8},{8,16},{16,24},{24,32},{32,40},{40,48},{48,56},{56,64},{64,7... | collective-permute-start | bytes 86024 | tf_op jit(solution)/shard_map/ppermute | solution.py:642
  57.4 4.9 %collective-permute-start.8 = (f32[48,128]{1,0:T(8,128)S(1)}, f32[48,128]{1,0:T(8,128)S(1)}, u32[]{:S(2)}, u32[]{:S(2)}) collective-permute-start(f32[48,128]{1,0:T(8,128)S(1)} %get-tuple-element.25.refs_1_), channel_id=1, source_target_pairs={{0,1},{1,2},{2,3},{3,4},{4,5},{5,6},{6,7},{7,0},{8,9},{9,10},{10,1... | collective-permute-start | bytes 73736 | tf_op jit(solution)/shard_map/ppermute | solution.py:642
  59.0 3.3 %collective-permute-start.7 = (f32[48,128]{1,0:T(8,128)S(1)}, f32[48,128]{1,0:T(8,128)S(1)}, u32[]{:S(2)}, u32[]{:S(2)}) collective-permute-start(f32[48,128]{1,0:T(8,128)S(1)} %get-tuple-element.25.refs_1_), channel_id=1, source_target_pairs={{0,7},{1,0},{2,1},{3,2},{4,3},{5,4},{6,5},{7,6},{8,15},{9,8},{10,9... | collective-permute-start | bytes 73736 | tf_op jit(solution)/shard_map/ppermute | solution.py:642
  62.3 11.8 %collective-permute-start.10 = (f32[144,128]{1,0:T(8,128)S(1)}, f32[144,128]{1,0:T(8,128)S(1)}, u32[]{:S(2)}, u32[]{:S(2)}) collective-permute-start(f32[144,128]{1,0:T(8,128)S(1)} %constant_dynamic-update-slice_fusion.refs_0_), channel_id=1, source_target_pairs={{0,8},{8,16},{16,24},{24,32},{32,40},{40,48},{48,56},{56,64},{64,7... | collective-permute-start | bytes 221192 | tf_op jit(solution)/shard_map/ppermute | solution.py:642
  62.4 11.8 %collective-permute-start.9 = (f32[144,128]{1,0:T(8,128)S(1)}, f32[144,128]{1,0:T(8,128)S(1)}, u32[]{:S(2)}, u32[]{:S(2)}) collective-permute-start(f32[144,128]{1,0:T(8,128)S(1)} %constant_dynamic-update-slice_fusion.refs_0_), channel_id=1, source_target_pairs={{0,120},{8,0},{16,8},{24,16},{32,24},{40,32},{48,40},{56,48},{64,5... | collective-permute-start | bytes 221192 | tf_op jit(solution)/shard_map/ppermute | solution.py:642
  68.4 15.5 %all-to-all-start.2 = ((f32[128,1,128]{2,1,0:T(1,128)}), f32[128,1,128]{2,1,0:T(1,128)S(1)}, u32[]{:S(2)}, u32[]{:S(2)}) async-start(f32[128,1,128]{2,1,0:T(1,128)} %bitcast.7), calls=%async_computation.2 | async-start | bytes 131072 | tf_op jit(solution)/shard_map/all_to_all | solution.py:637
  86.1 14.0 %all-to-all-start.3 = ((f32[128,1,128]{2,1,0:T(1,128)}), f32[128,1,128]{2,1,0:T(1,128)S(1)}, u32[]{:S(2)}, u32[]{:S(2)}) async-start(f32[128,1,128]{2,1,0:T(1,128)} %bitcast.10), calls=%async_computation.3 | async-start | bytes 131072 | tf_op jit(solution)/shard_map/all_to_all | solution.py:637
